TPU v7x, 512 devices: a whole 4x4x16 slice. The times are simulated.
512 devices in a mesh: axial: 32 (over z, core), circ: 16 (over y, x).
Axes of the slice: x: 4, y: 4, z: 16, core: 2. Of those that a mesh axis runs over, the one named last changes fastest.
Arguments:
- load_terms: float32 [32, 16, 128, 512], P('axial', 'circ'), may hold values from -19 to 19
- diffusivity: float32 [32, 16, 512], P('axial', 'circ'), may hold values from 0.1 to 10
- interface_diag: float32 [32, 16, 512], P('axial', 'circ'), may hold values from 4 to 8
- coupling: float32 [32, 16, 512, 512], P('axial', 'circ'), may hold values from -0.125 to 0.125
- interior_inverse: float32 [32, 16, 4, 128, 128], P('axial', 'circ'), may hold values from -1 to 3, as said below
- neumann_solve: float32 [32, 16, 512, 512], P('axial', 'circ'), may hold values from -1 to 3, as said below
- row_coarse: float32 [32, 8, 8], P('axial'), may hold values from -1 to 3, as said below
- lower_coef: float32 [32, 8], P('axial'), may hold values from 0.1 to 1
- upper_coef: float32 [32, 8], P('axial'), may hold values from 0.1 to 1
- face_order: int32 [32, 16, 512], P('axial', 'circ'), may hold values from 0 to 511, as said below
- primal_lists: int32 [32, 16, 8, 64], P('axial', 'circ'), may hold values from 0 to 511, as said below
Outputs:
- solution_field: float32 [32, 16, 128, 512], P('axial', 'circ')
- residual: float32 [32, 16, 128, 512], P('axial', 'circ')
Inputs may be any that keep to these rules, and one draw needn't show every extreme that they name: `face_order`: in each subdomain the values on face f (points f * 128 to f * 128 + 127) are those same numbers in some order; equal values on the two sides of a face name the same point. `primal_lists`: lists 2f and 2f + 1 together name every point of face f once. `interior_inverse`: symmetric in the last two dimensions. `neumann_solve`: symmetric in the last two dimensions. `row_coarse`: Symmetric, each diagonal entry larger than the sum of its row's other magnitudes.
All inputs are finite; a program needn't handle non-finite values.
Results may differ from a plain program's by a relative error of at most 0.0003.
Values sent between devices are 32-bit elements; how exact they have to be, the bound alone decides.
No kernel may reach another device: no remote copies, remote signals or barrier semaphores. Data moves between devices by JAX's collectives and lax.ppermute only.
A program may use at most 64 MiB of HBM per device.

v0:
```python
import jax
import jax.numpy as jnp
from jax import lax
from jax.sharding import PartitionSpec as P

ITERS = 3


def with_halo(block, sides, width, periodic):
    for axis, dim in sides:
        count = lax.axis_size(axis)
        forward = [(i, i + 1) for i in range(count - 1)]
        if periodic:
            forward.append((count - 1, 0))
        backward = [(target, source) for source, target in forward]
        low = lax.ppermute(
            lax.slice_in_dim(block, block.shape[dim] - width, None, axis=dim), axis, forward
        )
        high = lax.ppermute(lax.slice_in_dim(block, 0, width, axis=dim), axis, backward)
        block = jnp.concatenate([low, block, high], axis=dim)
    return block


def invert_order(order):
    size = order.shape[0]
    return jnp.zeros((size,), jnp.int32).at[order].set(jnp.arange(size, dtype=jnp.int32))


def assemble(values, order, inverse):
    width = order.shape[0] // 4
    shared = jnp.take(values, inverse, axis=-1)
    south = shared[..., :width]
    north = shared[..., width : 2 * width]
    west = shared[..., 2 * width : 3 * width]
    east = shared[..., 3 * width :]
    axial_pair = with_halo(jnp.stack([south, north]), (("axial", 0),), 1, False)
    circ_pair = with_halo(jnp.stack([west, east]), (("circ", 0),), 1, True)
    below = axial_pair[0]
    above = axial_pair[3]
    left_side = circ_pair[0]
    right_side = circ_pair[3]
    summed = jnp.concatenate(
        [south + below, north + above, west + left_side, east + right_side], axis=-1
    )
    return jnp.take(summed, order, axis=-1)


def forward_step(carry, inputs):
    factor, value = inputs
    carry = factor * carry + (1.0 - factor) * value
    return (carry, carry)


def top_level(row_total, lower_local, upper_local):
    all_rows, all_lower, all_upper = (
        lax.all_gather(row_total[None], "axial", axis=0, tiled=True),
        lax.all_gather(lower_local, "axial", axis=0, tiled=True),
        lax.all_gather(upper_local, "axial", axis=0, tiled=True),
    )
    start = jnp.zeros_like(row_total)
    _, smoothed = lax.scan(forward_step, start, (all_lower[:, None, :], all_rows))
    _, tops = lax.scan(forward_step, start, (all_upper[:, None, :], smoothed), reverse=True)
    return lax.dynamic_index_in_dim(tops, lax.axis_index("axial"), 0, keepdims=False)


def local(
    load_terms,
    diffusivity,
    interface_diag,
    coupling,
    interior_inverse,
    neumann_solve,
    row_coarse,
    lower_coef,
    upper_coef,
    face_order,
    primal_lists,
):
    highest = lax.Precision.HIGHEST
    rhs_local = load_terms[0, 0]
    rho_local = diffusivity[0, 0]
    diag_local = interface_diag[0, 0]
    couple_local = coupling[0, 0]
    blocks_local = interior_inverse[0, 0]
    neumann_local = neumann_solve[0, 0]
    coarse_local = row_coarse[0]
    order = face_order[0, 0]
    lists = primal_lists[0, 0]
    points = order.shape[0]
    width = points // 4
    count_rhs = rhs_local.shape[0]
    block_count = blocks_local.shape[0]
    block_size = blocks_local.shape[1]
    list_len = lists.shape[1]
    inverse = invert_order(order)
    lower_flag = (lax.axis_index("axial") > 0).astype(jnp.float32)
    upper_flag = (lax.axis_index("axial") < lax.axis_size("axial") - 1).astype(jnp.float32)
    keep = jnp.concatenate(
        [
            jnp.full((width,), 1.0, jnp.float32) * lower_flag,
            jnp.full((width,), 1.0, jnp.float32) * upper_flag,
            jnp.ones((2 * width,), jnp.float32),
        ]
    )
    share = rho_local / assemble(rho_local, order, inverse)
    positions = jnp.arange(points, dtype=jnp.int32)
    averaging = (
        jnp.sum((lists[:, :, None] == positions[None, None, :]).astype(jnp.float32), axis=1)
        / list_len
    )

    def precondition(residual):
        weighted = share * residual
        local_part = jnp.dot(weighted, neumann_local, precision=highest)
        primal = lax.dot_general(weighted, averaging, (((1,), (1,)), ((), ())), precision=highest)
        row_total = lax.psum(primal, "circ")
        row_part = jnp.dot(row_total, coarse_local, precision=highest)
        top_part = top_level(row_total, lower_coef, upper_coef)
        coarse_part = jnp.dot(row_part + top_part, averaging, precision=highest)
        return assemble(share * (local_part + coarse_part), order, inverse) * keep

    def inner_product(first, second):
        return 0.5 * lax.psum(jnp.sum(first * second, axis=1), ("axial", "circ"))

    residual = assemble(rhs_local, order, inverse) * keep
    solution_field = jnp.zeros_like(residual)
    precond = precondition(residual)
    direction = precond
    rz_value = inner_product(residual, precond)
    for iteration in range(ITERS):
        inner = jnp.dot(direction, couple_local, precision=highest)
        blocked = inner.reshape(count_rhs, block_count, block_size)
        solved = jnp.einsum("rnk,nkl->rnl", blocked, blocks_local, precision=highest).reshape(
            count_rhs, block_count * block_size
        )
        back = lax.dot_general(solved, couple_local, (((1,), (1,)), ((), ())), precision=highest)
        image = assemble(diag_local * direction - back, order, inverse) * keep
        alpha = rz_value / inner_product(direction, image)
        solution_field = solution_field + alpha[:, None] * direction
        residual = residual - alpha[:, None] * image
        if iteration + 1 < ITERS:
            precond = precondition(residual)
            new_value = inner_product(residual, precond)
            direction = precond + (new_value / rz_value)[:, None] * direction
            rz_value = new_value
    return (solution_field[None, None], residual[None, None])


def solution(mesh):
    in_specs = (
        P("axial", "circ", None, None),
        P("axial", "circ", None),
        P("axial", "circ", None),
        P("axial", "circ", None, None),
        P("axial", "circ", None, None, None),
        P("axial", "circ", None, None),
        P("axial", None, None),
        P("axial", None),
        P("axial", None),
        P("axial", "circ", None),
        P("axial", "circ", None, None),
    )
    out_specs = (P("axial", "circ", None, None), P("axial", "circ", None, None))
    return jax.shard_map(local, mesh=mesh, in_specs=in_specs, out_specs=out_specs, check_vma=False)
```

profile of v0, /device:TPU:1, one launch (start us, length us, event | category | flops | bytes accessed | tf_op | source)
XLA Modules:
  0.0 1201.1 jit_solution(1127212635862563293)
XLA Ops:
  1.4 2.4 scatter_custom_fusion
  4.6 3.5 gather_fusion.2
  9.4 4.9 collective-permute-start
  18.6 34.3 %all-gather.4 = f32[32,1,8]{2,1,0:T(1,128)S(1)} all-gather(f32[1,1,8]{2,1,0:T(1,128)S(1)} %bitcast.378), channel_id=1, replica_groups=mesh['axial'=32,'circ'=16] {'axial'}, dimensions={0}, use_global_device_ids=true | all-gather | bytes 1056 | tf_op jit(solution)/shard_map/all_gather | solution.py:57
  52.9 2.1 collective-permute-start.5
  55.0 3.1 collective-permute-start.6
  58.1 5.6 collective-permute-start.7
  63.8 29.8 %all-gather.3 = f32[32,1,8]{2,1,0:T(1,128)S(1)} all-gather(f32[1,1,8]{2,1,0:T(1,128)S(1)} %bitcast.379), channel_id=1, replica_groups=mesh['axial'=32,'circ'=16] {'axial'}, dimensions={0}, use_global_device_ids=true | all-gather | bytes 1056 | tf_op jit(solution)/shard_map/all_gather | solution.py:58
  93.6 3.5 gather_fusion.3
  97.2 2.1 collective-permute-start.1
  101.2 6.7 collective-permute-start.3
  111.2 34.1 %psum.63 = f32[128,8]{0,1:T(8,128)S(1)} all-reduce(f32[128,8]{0,1:T(8,128)S(1)} %fusion.42), channel_id=1, replica_groups=mesh['axial'=32,'circ'=16] {'circ'}, use_global_device_ids=true, to_apply=%region_2.0 | all-reduce | flops 1024 | bytes 8192 | tf_op jit(solution)/shard_map/psum | solution.py:116
  145.3 36.7 %all-gather = f32[4096,8]{0,1:T(8,128)S(1)} all-gather(f32[128,8]{0,1:T(8,128)S(1)} %psum.63), channel_id=2, replica_groups=mesh['axial'=32,'circ'=16] {'axial'}, dimensions={0}, use_global_device_ids=true | all-gather | bytes 135168 | tf_op jit(solution)/shard_map/all_gather | solution.py:56
  181.9 2.6 while.90
  184.5 2.6 while.91
  189.9 2.1 collective-permute-start.8
  195.8 6.7 collective-permute-start.11
  202.5 2.5 collective-permute-start.9
  205.4 4.2 collective-permute-done.9
  215.8 2.0 convolution_subtract_fusion.2
  225.5 2.0 collective-permute-start.13
  227.4 1.9 collective-permute-start.14
  229.4 6.7 collective-permute-start.15
  243.8 105.5 %all-reduce = (f32[128]{0:T(128)S(1)}, f32[128]{0:T(128)S(1)}) all-reduce(f32[128]{0:T(128)S(1)} %get-tuple-element.509, f32[128]{0:T(128)S(1)} %get-tuple-element.508), channel_id=1, replica_groups=mesh['axial'=32,'circ'=16] {'axial','circ'}, use_global_device_ids=true, to_apply=%region_10.13 | all-reduce | flops 256 | bytes 2048 | tf_op jit(solution)/shard_map/psum | solution.py:123
  352.9 29.8 %psum.66 = f32[128,8]{0,1:T(8,128)S(1)} all-reduce(f32[128,8]{0,1:T(8,128)S(1)} %fusion.39), channel_id=1, replica_groups=mesh['axial'=32,'circ'=16] {'circ'}, use_global_device_ids=true, to_apply=%region_11.14 | all-reduce | flops 1024 | bytes 8192 | tf_op jit(solution)/shard_map/psum | solution.py:116
  382.7 40.6 %all-gather.1 = f32[4096,8]{0,1:T(8,128)} all-gather(f32[128,8]{0,1:T(8,128)S(1)} %psum.66), channel_id=3, replica_groups=mesh['axial'=32,'circ'=16] {'axial'}, dimensions={0}, use_global_device_ids=true | all-gather | bytes 135168 | tf_op jit(solution)/shard_map/all_gather | solution.py:56
  424.0 43.0 %while.92 = (s32[]{:T(128)}, f32[128,8]{0,1:T(8,128)S(1)}, f32[32,128,8]{1,2,0:T(8,128)}, f32[32,1,8]{2,1,0:T(1,128)S(1)}, f32[32,128,8]{1,2,0:T(8,128)}, /*index=5*/s32[]{:T(128)}, s32[]{:T(128)}) while((s32[]{:T(128)}, f32[128,8]{0,1:T(8,128)S(1)}, f32[32,128,8]{1,2,0:T(8,128)}, f32[32,1,8]{2,1,0:T(1,128)S(1)}, ...), condition=%wide.region_13.16_spmd.clone, body=%wide.region_12.15_spmd.clone.sunk | while | flops 4107 | bytes 17147 | solution.py:61
  467.7 43.1 %while.93 = (s32[]{:T(128)}, f32[128,8]{0,1:T(8,128)S(1)}, f32[32,128,8]{1,2,0:T(8,128)}, f32[32,1,8]{2,1,0:T(1,128)S(1)}, f32[32,128,8]{1,2,0:T(8,128)}, /*index=5*/s32[]{:T(128)}, s32[]{:T(128)}, s32[]{:T(128)}) while((s32[]{:T(128)}, f32[128,8]{0,1:T(8,128)S(1)}, f32[32,128,8]{1,2,0:T(8,128)}, f32[32,1,8]{2,1,0:T(1,128)S(1)}, ...), condition=%wide.region_15.18_spmd.clone, body=%wide.region_14.17_spmd.clone.sunk | while | flops 4108 | bytes 16659 | solution.py:62
  519.9 2.0 collective-permute-start.17
  521.8 2.2 collective-permute-start.18
  524.0 6.4 collective-permute-start.19
  536.9 104.1 %psum.67 = f32[128]{0:T(128)S(1)} all-reduce(f32[128]{0:T(128)S(1)} %multiply_reduce_fusion.3), channel_id=1, replica_groups=mesh['axial'=32,'circ'=16] {'axial','circ'}, use_global_device_ids=true, to_apply=%region_17.20 | all-reduce | flops 128 | bytes 1024 | tf_op jit(solution)/shard_map/psum | solution.py:123
  644.6 2.0 convolution_subtract_fusion.1
  650.4 4.2 collective-permute-start.20
  658.5 1.9 collective-permute-start.22
  660.5 6.7 collective-permute-start.23
  674.3 106.3 %psum.68 = f32[128]{0:T(128)S(1)} all-reduce(f32[128]{0:T(128)S(1)} %multiply_reduce_fusion.2), channel_id=1, replica_groups=mesh['axial'=32,'circ'=16] {'axial','circ'}, use_global_device_ids=true, to_apply=%region_19.22 | all-reduce | flops 128 | bytes 1024 | tf_op jit(solution)/shard_map/psum | solution.py:123
  783.8 29.7 %psum.69 = f32[128,8]{0,1:T(8,128)S(1)} all-reduce(f32[128,8]{0,1:T(8,128)S(1)} %fusion.36), channel_id=1, replica_groups=mesh['axial'=32,'circ'=16] {'circ'}, use_global_device_ids=true, to_apply=%region_20.23 | all-reduce | flops 1024 | bytes 8192 | tf_op jit(solution)/shard_map/psum | solution.py:116
  813.4 38.4 %all-gather.2 = f32[4096,8]{0,1:T(8,128)} all-gather(f32[128,8]{0,1:T(8,128)S(1)} %psum.69), channel_id=4, replica_groups=mesh['axial'=32,'circ'=16] {'axial'}, dimensions={0}, use_global_device_ids=true | all-gather | bytes 135168 | tf_op jit(solution)/shard_map/all_gather | solution.py:56
  852.5 42.9 %while.94 = (s32[]{:T(128)}, f32[128,8]{0,1:T(8,128)S(1)}, f32[32,128,8]{1,2,0:T(8,128)}, f32[32,1,8]{2,1,0:T(1,128)S(1)}, f32[32,128,8]{1,2,0:T(8,128)}, /*index=5*/s32[]{:T(128)}, s32[]{:T(128)}) while((s32[]{:T(128)}, f32[128,8]{0,1:T(8,128)S(1)}, f32[32,128,8]{1,2,0:T(8,128)}, f32[32,1,8]{2,1,0:T(1,128)S(1)}, ...), condition=%wide.region_22.25_spmd.clone, body=%wide.region_21.24_spmd.clone.sunk | while | flops 4107 | bytes 17147 | solution.py:61
  896.1 43.1 %while.95 = (s32[]{:T(128)}, f32[128,8]{0,1:T(8,128)S(1)}, f32[32,128,8]{1,2,0:T(8,128)}, f32[32,1,8]{2,1,0:T(1,128)S(1)}, f32[32,128,8]{1,2,0:T(8,128)}, /*index=5*/s32[]{:T(128)}, s32[]{:T(128)}, s32[]{:T(128)}) while((s32[]{:T(128)}, f32[128,8]{0,1:T(8,128)S(1)}, f32[32,128,8]{1,2,0:T(8,128)}, f32[32,1,8]{2,1,0:T(1,128)S(1)}, ...), condition=%wide.region_24.27_spmd.clone, body=%wide.region_23.26_spmd.clone.sunk | while | flops 4108 | bytes 16659 | solution.py:62
  945.0 2.8 collective-permute-start.24
  951.1 2.6 collective-permute-start.26
  953.7 6.3 collective-permute-start.27
  965.7 103.7 %psum.70 = f32[128]{0:T(128)S(1)} all-reduce(f32[128]{0:T(128)S(1)} %multiply_reduce_fusion.1), channel_id=1, replica_groups=mesh['axial'=32,'circ'=16] {'axial','circ'}, use_global_device_ids=true, to_apply=%region_26.29 | all-reduce | flops 128 | bytes 1024 | tf_op jit(solution)/shard_map/psum | solution.py:123
  1075.0 4.2 collective-permute-start.28
  1084.5 6.7 collective-permute-start.31
  1094.6 104.8 %psum.71 = f32[128]{0:T(128)S(1)} all-reduce(f32[128]{0:T(128)S(1)} %multiply_reduce_fusion), channel_id=1, replica_groups=mesh['axial'=32,'circ'=16] {'axial','circ'}, use_global_device_ids=true, to_apply=%region_28.31 | all-reduce | flops 128 | bytes 1024 | tf_op jit(solution)/shard_map/psum | solution.py:123
  (630 shorter events, 291.0 us)
Async XLA Ops:
  0.6 186.5 %copy-start = (f32[1,1,512,512]{3,2,1,0:T(8,128)S(1)}, f32[1,1,512,512]{3,2,1,0:T(8,128)}, u32[]{:S(2)}) copy-start(f32[1,1,512,512]{3,2,1,0:T(8,128)} %param.32) | copy-start | bytes 3145732
  4.6 3.5 copy-start.20
  9.4 87.7 %collective-permute-start = (f32[1,128,128]{1,2,0:T(8,128)S(1)}, f32[1,128,128]{1,2,0:T(8,128)S(1)}, u32[]{:S(2)}, u32[]{:S(2)}) collective-permute-start(f32[1,128,128]{1,2,0:T(8,128)S(1)} %slice_bitcast_fusion.26), channel_id=1, source_target_pairs={{0,16},{16,32},{32,48},{48,64},{64,80},{80,96},{96,112},{112,128},... | collective-permute-start | bytes 196616 | tf_op jit(solution)/shard_map/ppermute | solution.py:16
  14.4 38.5 %collective-permute-start.4 = (f32[1,128]{1,0:T(1,128)S(1)}, f32[1,128]{1,0:T(1,128)S(1)}, u32[]{:S(2)}, u32[]{:S(2)}) collective-permute-start(f32[1,128]{1,0:T(1,128)S(1)} %slice_bitcast_fusion.30), channel_id=1, source_target_pairs={{0,16},{16,32},{32,48},{48,64},{64,80},{80,96},{96,112},{112,128},... | collective-permute-start | bytes 1544 | tf_op jit(solution)/shard_map/ppermute | solution.py:16
  52.9 40.7 %collective-permute-start.5 = (f32[1,128]{1,0:T(1,128)S(1)}, f32[1,128]{1,0:T(1,128)S(1)}, u32[]{:S(2)}, u32[]{:S(2)}) collective-permute-start(f32[1,128]{1,0:T(1,128)S(1)} %get-tuple-element.652), channel_id=1, source_target_pairs={{16,0},{32,16},{48,32},{64,48},{80,64},{96,80},{112,96},{128,112},... | collective-permute-start | bytes 1544 | tf_op jit(solution)/shard_map/ppermute | solution.py:19
  55.0 38.6 %collective-permute-start.6 = (f32[1,128]{1,0:T(1,128)S(1)}, f32[1,128]{1,0:T(1,128)S(1)}, u32[]{:S(2)}, u32[]{:S(2)}) collective-permute-start(f32[1,128]{1,0:T(1,128)S(1)} %get-tuple-element.654), channel_id=1, source_target_pairs={{0,1},{1,2},{2,3},{3,4},{4,5},{5,6},{6,7},{7,8},{8,9},{9,10},{10,1... | collective-permute-start | bytes 1544 | tf_op jit(solution)/shard_map/ppermute | solution.py:16
  58.1 5.7 copy-start.31
  58.1 35.5 %collective-permute-start.7 = (f32[1,128]{1,0:T(1,128)S(1)}, f32[1,128]{1,0:T(1,128)S(1)}, u32[]{:S(2)}, u32[]{:S(2)}) collective-permute-start(f32[1,128]{1,0:T(1,128)S(1)} %get-tuple-element.653), channel_id=1, source_target_pairs={{1,0},{2,1},{3,2},{4,3},{5,4},{6,5},{7,6},{8,7},{9,8},{10,9},{11,1... | collective-permute-start | bytes 1544 | tf_op jit(solution)/shard_map/ppermute | solution.py:19
  97.2 10.8 collective-permute-start.1
  99.3 9.0 collective-permute-start.2
  101.2 8.5 collective-permute-start.3
  110.9 76.2 %copy-start.13 = (f32[512,128]{0,1:T(8,128)}, f32[512,128]{0,1:T(8,128)S(1)}, u32[]{:S(2)}) copy-start(f32[512,128]{0,1:T(8,128)S(1)} %copy.68) | copy-start | bytes 786436
  189.7 15.4 %copy-start.2 = (f32[1,1,512,512]{3,2,1,0:T(8,128)S(1)}, f32[1,1,512,512]{3,2,1,0:T(8,128)}, u32[]{:S(2)}) copy-start(f32[1,1,512,512]{3,2,1,0:T(8,128)} %param.30) | copy-start | bytes 3145732
  189.9 3.4 collective-permute-start.8
  193.9 11.5 collective-permute-start.10
  195.8 9.6 collective-permute-start.11
  202.5 7.1 collective-permute-start.9
  221.6 3.2 collective-permute-start.12
  225.5 10.6 collective-permute-start.13
  227.4 9.3 collective-permute-start.14
  229.4 8.8 collective-permute-start.15
  467.7 43.1 %copy-start.33 = (f32[1,8,8]{2,1,0:T(8,128)S(1)}, f32[1,8,8]{2,1,0:T(8,128)}, u32[]{:S(2)}) copy-start(f32[1,8,8]{2,1,0:T(8,128)} %param.33) | copy-start | bytes 772
  516.6 3.2 collective-permute-start.16
  519.9 10.6 collective-permute-start.17
  521.8 9.0 collective-permute-start.18
  524.0 8.2 collective-permute-start.19
  535.7 105.9 %copy-start.5 = (f32[512,128]{0,1:T(8,128)S(1)}, f32[512,128]{0,1:T(8,128)}, u32[]{:S(2)}) copy-start(f32[512,128]{0,1:T(8,128)} %copy-done.3) | copy-start | bytes 786436
  536.9 104.2 %copy-start.39 = (f32[128]{0:T(128)S(1)}, f32[128]{0:T(128)}, u32[]{:S(2)}) copy-start(f32[128]{0:T(128)} %copy-done.38) | copy-start | bytes 1540
  642.6 1.8 copy-start.7
  650.4 5.6 collective-permute-start.20
  656.6 10.6 collective-permute-start.21
  658.5 8.7 collective-permute-start.22
  660.5 8.3 collective-permute-start.23
  674.3 106.3 %copy-start.36 = (f32[128]{0:T(128)S(1)}, f32[128]{0:T(128)}, u32[]{:S(2)}) copy-start(f32[128]{0:T(128)} %copy-done.35) | copy-start | bytes 1540
  896.1 43.1 %copy-start.34 = (f32[1,8,8]{2,1,0:T(8,128)S(1)}, f32[1,8,8]{2,1,0:T(8,128)}, u32[]{:S(2)}) copy-start(f32[1,8,8]{2,1,0:T(8,128)} %param.33) | copy-start | bytes 772
  945.0 4.1 collective-permute-start.24
  949.2 10.8 collective-permute-start.25
  951.1 8.9 collective-permute-start.26
  953.7 7.3 collective-permute-start.27
  964.5 105.0 %copy-start.9 = (f32[128,512]{1,0:T(8,128)S(1)}, f32[128,512]{1,0:T(8,128)}, u32[]{:S(2)}) copy-start(f32[128,512]{1,0:T(8,128)} %copy-done.7) | copy-start | bytes 786436
  965.7 103.8 %copy-start.37 = (f32[128]{0:T(128)S(1)}, f32[128]{0:T(128)}, u32[]{:S(2)}) copy-start(f32[128]{0:T(128)} %copy-done.35) | copy-start | bytes 1540
  1075.0 5.6 collective-permute-start.28
  1080.6 10.5 collective-permute-start.29
  1082.5 8.6 collective-permute-start.30
  1084.5 8.0 collective-permute-start.31
  1093.6 105.9 %copy-start.12 = (f32[128,512]{1,0:T(8,128)S(1)}, f32[128,512]{1,0:T(8,128)}, u32[]{:S(2)}) copy-start(f32[128,512]{1,0:T(8,128)} %copy-done.11) | copy-start | bytes 786436
  1094.5 105.0 %copy-start.6 = (f32[512,128]{0,1:T(8,128)S(1)}, f32[512,128]{0,1:T(8,128)}, u32[]{:S(2)}) copy-start(f32[512,128]{0,1:T(8,128)} %copy-done.3) | copy-start | bytes 786436
  1094.5 105.0 %copy-start.10 = (f32[128,512]{1,0:T(8,128)S(1)}, f32[128,512]{1,0:T(8,128)}, u32[]{:S(2)}) copy-start(f32[128,512]{1,0:T(8,128)} %copy-done.7) | copy-start | bytes 786436
  (24 other events, 23.3 us)
where the time goes:
time: 1210 us; the launch traced here: 1200 us
  blocking collectives  798 us (66%)
  other arithmetic  198 us (16%)
  starting transfers between devices  110 us (9%)
  local copies, waits for them, and re-layouts  53.7 us (4%)
  waiting for transfers between devices  21.5 us (2%)
  matrix products  18.2 us (2%)
    psum x5, blocking collectives, inner_product(): return 0.5 * lax.psum(jnp.sum(first * second, axis=1), ('axial', 'circ'))  525 us
    dynamic_update_slice x192, other arithmetic, top_level(): lax.scan(forward_step, start, (all_lower[:, None, :], all_rows))  176 us
    all_gather x3, blocking collectives, top_level(): lax.all_gather(row_total[None], 'axial', axis=0, tiled=True)  116 us
    psum x3, blocking collectives, precondition(): row_total = lax.psum(primal, 'circ')  93.5 us
    ppermute x16, starting transfers between devices, with_halo(): lax.ppermute(lax.slice_in_dim(block, 0, width, axis=dim), axis, backward)  68.2 us
    ppermute x16, starting transfers between devices, with_halo(): lax.ppermute(lax.slice_in_dim(block, block.shape[dim] - width, None, axis...  41.5 us
    all_gather x1, blocking collectives, top_level(): lax.all_gather(lower_local, 'axial', axis=0, tiled=True)  34.3 us
    all_gather x1, blocking collectives, top_level(): lax.all_gather(upper_local, 'axial', axis=0, tiled=True)  29.8 us
  transfers between devices with their start and end apart: 32, of which 16 were waited for; matrix products, arithmetic and copies ran while one was open for 0% of the time, Pallas kernels for 0%

commit v1 on v0

v1 whole, which is shorter than its diff:
```python
import functools

import jax
import jax.numpy as jnp
from jax import lax
from jax.experimental import pallas as pl
from jax.experimental.pallas import tpu as pltpu
from jax.sharding import PartitionSpec as P

SHIFT = 12.0
HIGHEST = lax.Precision.HIGHEST
F32 = jnp.float32
LANES = 128


def mm(a, b):
    return lax.dot_general(
        a, b, (((1,), (0,)), ((), ())), precision=HIGHEST, preferred_element_type=F32
    )


def mm_t(a, b):
    return lax.dot_general(
        a, b, (((1,), (1,)), ((), ())), precision=HIGHEST, preferred_element_type=F32
    )


def faces_of(full):
    return [full[:, f * LANES : (f + 1) * LANES] for f in range(4)]


def one_hot_faces(order):
    rows = lax.broadcasted_iota(jnp.int32, (LANES, LANES), 0)
    return [
        jnp.where(order[:, f * LANES : (f + 1) * LANES] - f * LANES == rows, 1.0, 0.0).astype(F32)
        for f in range(4)
    ]


def to_shared(full, hots):
    return jnp.concatenate([mm_t(part, hot) for part, hot in zip(faces_of(full), hots)], axis=1)


def to_points(full, hots):
    return jnp.concatenate([mm(part, hot) for part, hot in zip(faces_of(full), hots)], axis=1)


class Place:
    def __init__(self, place):
        row, rows, column = place[0], place[1], place[2]
        self.row = row
        self.even_row = lax.rem(row, 2) == 0
        self.even_column = lax.rem(column, 2) == 0
        self.keep_south = jnp.where(row > 0, 1.0, 0.0).astype(F32)
        self.keep_north = jnp.where(row < rows - 1, 1.0, 0.0).astype(F32)


def put_sends(sends, full, at):
    south, north, west, east = faces_of(full)
    sends[0][...] = jnp.where(at.even_row, north, south)
    sends[1][...] = jnp.where(at.even_row, south, north)
    sends[2][...] = jnp.where(at.even_column, east, west)
    sends[3][...] = jnp.where(at.even_column, west, east)


def neighbours(got, at):
    core, link, near, far = [ref[...] for ref in got]
    above = jnp.where(at.even_row, core, link)
    below = jnp.where(at.even_row, link, core)
    right = jnp.where(at.even_column, near, far)
    left = jnp.where(at.even_column, far, near)
    return below, above, left, right


def assembled(full, got, at, rhs, keep=True):
    count = full.shape[0]
    extra = count - rhs
    own = faces_of(full)
    other = neighbours(got, at)
    scale = (at.keep_south, at.keep_north, None, None)
    shift = (0, 16, 8, 8)
    out = []
    for f in range(4):
        part = own[f][:rhs] + other[f][:rhs]
        if extra:
            zero = jnp.zeros((8, LANES), F32)
            mine = jnp.concatenate([zero, own[f][rhs:], zero], axis=0)
            pieces = [jnp.zeros((shift[f], LANES), F32)] if shift[f] else []
            pieces.append(other[f][rhs:])
            if shift[f] < 16:
                pieces.append(jnp.zeros((16 - shift[f], LANES), F32))
            part = jnp.concatenate([part, mine + jnp.concatenate(pieces, axis=0)], axis=0)
        if keep and scale[f] is not None:
            part = part * scale[f]
        out.append(part)
    return jnp.concatenate(out, axis=1)


def schur(z, diag, couple, blocks):
    inner = mm(z, couple)
    solved = jnp.concatenate([mm(part, blocks[n]) for n, part in enumerate(faces_of(inner))], axis=1)
    return diag * z - mm_t(solved, couple)


def k_prepare(place, load, rho, order, shared_o, *sends):
    at = Place(place)
    hots = one_hot_faces(order[...])
    pad = jnp.zeros((7, rho.shape[1]), F32)
    full = to_shared(jnp.concatenate([load[...], rho[...], pad], axis=0), hots)
    shared_o[...] = full
    put_sends(sends, full, at)


def k_matrices(order, diag, couple, neumann, lists, diag_o, couple_o, neumann_o, avg_o):
    hots = one_hot_faces(order[...])
    diag_o[...] = to_shared(jnp.broadcast_to(diag[...], (8, diag.shape[1])), hots)[:1]
    for f in range(4):
        rows = slice(f * LANES, (f + 1) * LANES)
        couple_o[rows, :] = mm(hots[f], couple[rows, :])
        neumann_o[rows, :] = to_shared(mm(hots[f], neumann[rows, :]), hots)
    points = order.shape[1]
    named = lists[...]
    position = lax.broadcasted_iota(jnp.int32, (8, points), 1)
    total = jnp.zeros((8, points), F32)
    length = named.shape[1]
    for item in range(length):
        total = total + jnp.where(named[:, item : item + 1] == position, 1.0, 0.0)
    avg_o[...] = to_shared(total * (1.0 / length), hots)


def k_first(place, shared, g0, g1, g2, g3, neumann, avg, r_o, share_o, prim_o, t_o, *sends):
    at = Place(place)
    rhs = r_o.shape[0]
    full = assembled(shared[...], (g0, g1, g2, g3), at, shared.shape[0], keep=False)
    share = shared[rhs : rhs + 1, :] / full[rhs : rhs + 1]
    south, north, west, east = faces_of(full[:rhs])
    r = jnp.concatenate([south * at.keep_south, north * at.keep_north, west, east], axis=1)
    r_o[...] = r
    share_o[...] = share
    weighted = share * r
    prim_o[...] = mm_t(avg[...], weighted)
    t = jnp.concatenate([share * mm(weighted, neumann[...]), share * avg[...]], axis=0)
    t_o[...] = t
    put_sends(sends, t, at)


def k_schur(place, t, g0, g1, g2, g3, diag, couple, blocks, z_o, q_o, *sends, rhs):
    at = Place(place)
    z = assembled(t[...], (g0, g1, g2, g3), at, rhs)
    z_o[...] = z
    q = schur(z, diag[...], couple[...], blocks)
    q_o[...] = q
    put_sends(sends, q, at)


def k_second(place, q, g0, g1, g2, g3, r, share, neumann, avg, v_o, t_o, pr_o, *sends):
    at = Place(place)
    rhs = r.shape[0]
    w = assembled(q[...], (g0, g1, g2, g3), at, rhs)
    v = jnp.concatenate([w[:rhs] - SHIFT * r[...], w[rhs:]], axis=0)
    v_o[...] = v
    weighted = share[...] * v
    pr_o[...] = jnp.concatenate(
        [mm_t(avg[...], weighted[:rhs]), mm_t(avg[...], weighted[rhs:])], axis=1
    )
    t = share[...] * mm(weighted, neumann[...])
    t_o[...] = t
    put_sends(sends, t, at)


def k_third(place, q, g0, g1, g2, g3, v, share, avg, prim0, prim1, v2_o, pay_o):
    at = Place(place)
    rhs = prim0.shape[1]
    w = assembled(q[...], (g0, g1, g2, g3), at, rhs)
    zero = jnp.zeros((16, w.shape[1]), F32)
    older = jnp.concatenate([v[...][:rhs], zero, v[...][rhs:], zero], axis=0)
    v2 = w - SHIFT * older
    v2_o[...] = v2
    weighted = share[...] * v2
    prim2 = mm_t(avg[...], weighted[:rhs])
    reach2 = mm_t(avg[...], weighted[rhs:])
    reach1 = prim1[...][:, rhs:]
    spare = jnp.zeros((8, LANES - reach1.shape[1] - reach2.shape[1]), F32)
    tail = jnp.concatenate([reach1, reach2, spare], axis=1)
    pay_o[...] = jnp.concatenate([prim0[...], prim1[...][:, :rhs], prim2, tail], axis=0)


def k_sum_spread(got, coefs, out):
    total = got[0]
    for item in range(1, got.shape[0]):
        total = total + got[item]
    total = total + coefs[...]
    for item in range(out.shape[0]):
        out[item] = total


def coarse_rows(totals, lowers, uppers):
    carry = jnp.zeros_like(totals[0])
    smooth = []
    for low, value in zip(lowers, totals):
        carry = low * carry + (1.0 - low) * value
        smooth.append(carry)
    carry = jnp.zeros_like(totals[0])
    tops = []
    for up, value in zip(uppers[::-1], smooth[::-1]):
        carry = up * carry + (1.0 - up) * value
        tops.append(carry)
    return tops[::-1]


def k_coarse(
    place, got, v2, v1, share, neumann,
    v_o, t_o, c0_o, c1_o, c2_o, s0, s1, s2, s3,
    band0, band1, band2, c0_s, c1_s, c2_s,
):
    at = Place(place)
    rhs = v_o.shape[0]
    rows = got.shape[0]
    width = band0.shape[1]
    lane = lax.broadcasted_iota(jnp.int32, (8, width), 1)
    lowers, uppers = [], []
    for ref in (band0, band1, band2):
        if ref.shape[0] > rows * 8:
            ref[rows * 8 :, :] = jnp.zeros((ref.shape[0] - rows * 8, width), F32)
    for k in range(rows):
        tail = got[k, 24:32, :]
        lowers.append(jnp.broadcast_to(tail[:, 120:121], (8, rhs)))
        uppers.append(jnp.broadcast_to(tail[:, 121:122], (8, rhs)))
        wide = tail
        if width > LANES:
            wide = jnp.concatenate([tail, jnp.zeros((8, width - LANES), F32)], axis=1)
        for ref, first, last, to in (
            (band1, 0, 40, 8 * (k - 2)),
            (band2, 40, 112, 8 * (k - 4)),
            (band0, 112, 120, 8 * k),
        ):
            picked = jnp.where((lane >= first) & (lane < last), wide, 0.0)
            ref[8 * k : 8 * k + 8, :] = pltpu.roll(picked, (to - first) % width, 1)

    def stacked(tiles):
        if width > rows * 8:
            tiles = tiles + [jnp.zeros((width - rows * 8, rhs), F32)]
        return jnp.concatenate(tiles, axis=0)

    def solve(total):
        tiles = [total[8 * k : 8 * k + 8] for k in range(rows)]
        return stacked(coarse_rows(tiles, lowers, uppers)) + mm(band0[...], total)

    edge = jnp.zeros((32, rhs), F32)
    c0 = solve(stacked([got[k, 0:8, :] for k in range(rows)]))
    c1 = solve(stacked([got[k, 8:16, :] for k in range(rows)]) + mm(band1[...], c0))
    c2 = solve(
        stacked([got[k, 16:24, :] for k in range(rows)]) + mm(band2[...], c0) + mm(band1[...], c1)
    )
    for ref, value in ((c0_s, c0), (c1_s, c1), (c2_s, c2)):
        ref[0:32, :] = edge
        ref[32 : 32 + width, :] = value
        ref[32 + width :, :] = edge
    start = at.row * 8
    c0w = c0_s[pl.ds(pl.multiple_of(start, 8), 72), :]
    c1w = c1_s[pl.ds(pl.multiple_of(start + 16, 8), 40), :]
    c2w = c2_s[pl.ds(pl.multiple_of(start + 24, 8), 24), :]
    c0_o[...] = c0w
    c1_o[...] = c1w
    c2_o[...] = c2w
    v = v2[:rhs, :] + mm_first(jnp.concatenate([c0w, c1w], axis=0),
                               jnp.concatenate([v2[rhs:, :], v1[rhs:, :]], axis=0))
    v_o[...] = v
    t = share[...] * mm(share[...] * v, neumann[...])
    t_o[...] = t
    put_sends((s0, s1, s2, s3), t, at)


def mm_first(a, b):
    return lax.dot_general(
        a, b, (((0,), (0,)), ((), ())), precision=HIGHEST, preferred_element_type=F32
    )


def dot_rows(pairs):
    rows = lax.broadcasted_iota(jnp.int32, (16, LANES), 0)
    total = jnp.zeros((16, LANES), F32)
    for index, (a, b) in pairs:
        part = sum(faces_of(a * b)[1:], faces_of(a * b)[0])
        total = total + mm_t(jnp.where(rows == index, 1.0, 0.0).astype(F32), part)
    return total


def k_known(r, z0, v1, z1, v2, vv2, c0, c1, z0_o, w0_o, z1_o, w1_o, dots_o):
    rhs = r.shape[0]
    c0, c1 = c0[...], c1[...]
    z0f = z0[:rhs, :] + mm_first(c0[24:48], z0[rhs:, :])
    v1f = v1[:rhs, :] + mm_first(c0[16:56], v1[rhs:, :])
    z1f = z1[:rhs, :] + mm_first(
        jnp.concatenate([c0[8:64], c1[8:32]], axis=0),
        jnp.concatenate([z1[rhs:, :], z0[rhs:, :]], axis=0),
    )
    v2f = vv2[...]
    z0_o[...] = z0f
    z1_o[...] = z1f
    w0_o[...] = v1f + SHIFT * r[...]
    w1_o[...] = v2f + SHIFT * v1f
    vs = (r[...], v1f, v2f)
    dots_o[...] = dot_rows([(3 * i + j, (vs[i], (z0f, z1f)[j])) for i in range(3) for j in range(2)])


def k_last_schur(place, t, g0, g1, g2, g3, pbasis, c2, diag, couple, blocks, z_o, q_o, *sends):
    at = Place(place)
    rhs = z_o.shape[0]
    z = assembled(t[...], (g0, g1, g2, g3), at, rhs) + mm_first(c2[...], pbasis[rhs:, :])
    z_o[...] = z
    q = schur(z, diag[...], couple[...], blocks)
    q_o[...] = q
    put_sends(sends, q, at)


def k_dots(place, q, g0, g1, g2, g3, r, w0, vv2, z0, z1, z2, dots, w2_o, pay_o):
    at = Place(place)
    w2 = assembled(q[...], (g0, g1, g2, g3), at, q.shape[0])
    w2_o[...] = w2
    v1 = w0[...] - SHIFT * r[...]
    vs = (r[...], v1, vv2[...])
    pairs = [(3 * i + 2, (vs[i], z2[...])) for i in range(3)]
    pairs += [(9 + i, (z, w2)) for i, z in enumerate((z0[...], z1[...], z2[...]))]
    pay_o[...] = dots[...] + dot_rows(pairs)


def k_final(got, order, r0, z0, z1, z2, w0, w1, w2, x_o, r_o):
    total = got[0]
    for item in range(1, got.shape[0]):
        total = total + got[item]
    vz = [[total[3 * i + j : 3 * i + j + 1] for j in range(3)] for i in range(3)]
    zw = [[None] * 3 for _ in range(3)]
    for i in range(3):
        for j in range(2):
            zw[i][j] = vz[j + 1][i] + SHIFT * vz[j][i]
        zw[i][2] = total[9 + i : 10 + i]

    def form(left, table, right):
        value = None
        for i, a in enumerate(left):
            for j, b in enumerate(right):
                if a is None or b is None:
                    continue
                term = a * table[i][j] * b
                value = term if value is None else value + term
        return value

    one = jnp.ones_like(vz[0][0])
    zero = jnp.zeros_like(one)
    toward = [one, None, None]
    steps = [zero, zero, zero]
    drops = [zero, zero, zero]
    rz = vz[0][0]
    for iteration in range(3):
        alpha = rz / form(toward, zw, toward)
        for j in range(3):
            if toward[j] is not None:
                steps[j] = steps[j] + alpha * toward[j]
                drops[j] = drops[j] - alpha * toward[j]
        if iteration < 2:
            mix = [one + SHIFT * drops[0], drops[0] + SHIFT * drops[1], None]
            if iteration == 1:
                mix[2] = drops[1]
            new = form(mix, vz, mix)
            beta = new / rz
            toward = [
                m if d is None else (beta * d if m is None else m + beta * d)
                for m, d in zip(mix, toward)
            ]
            rz = new
    table = jnp.concatenate(steps + drops + [zero, zero], axis=0)
    eye = jnp.where(
        lax.broadcasted_iota(jnp.int32, (LANES, LANES), 0)
        == lax.broadcasted_iota(jnp.int32, (LANES, LANES), 1),
        1.0,
        0.0,
    ).astype(F32)
    columns = mm_t(eye, table)
    col = [columns[:, i : i + 1] for i in range(6)]
    hots = one_hot_faces(order[...])
    x = col[0] * z0[...] + col[1] * z1[...] + col[2] * z2[...]
    r = r0[...] + col[3] * w0[...] + col[4] * w1[...] + col[5] * w2[...]
    x_o[...] = to_points(x, hots)
    r_o[...] = to_points(r, hots)


def call(body, outs, place, *args, scratch=(), flops=1_000_000):
    specs = [pl.BlockSpec(memory_space=pltpu.VMEM) for _ in args]
    if place is not None:
        specs = [pl.BlockSpec(memory_space=pltpu.SMEM)] + specs
        args = (place,) + args
    return pl.pallas_call(
        body,
        out_shape=[jax.ShapeDtypeStruct(shape, F32) for shape in outs],
        in_specs=specs,
        out_specs=[pl.BlockSpec(memory_space=pltpu.VMEM) for _ in outs],
        scratch_shapes=list(scratch),
        compiler_params=pltpu.CompilerParams(vmem_limit_bytes=32 * 1024 * 1024),
        cost_estimate=pl.CostEstimate(flops=flops, bytes_accessed=1_000_000, transcendentals=0),
    )(*args)


def exchange(sends, rows, columns):
    core = [(i, i ^ 1) for i in range(rows)]
    link = [(i, i + 1 if i % 2 else i - 1) for i in range(1, rows - 1)]
    near = [(i, i ^ 1) for i in range(columns)]
    far = [(i, (i + 1 if i % 2 else i - 1) % columns) for i in range(columns)]
    return [
        lax.ppermute(sends[0], "axial", core),
        lax.ppermute(sends[1], "axial", link),
        lax.ppermute(sends[2], "circ", near),
        lax.ppermute(sends[3], "circ", far),
    ]


def spread(value, axis):
    return lax.all_to_all(value, axis, split_axis=0, concat_axis=0, tiled=True)


def local(
    load_terms, diffusivity, interface_diag, coupling, interior_inverse, neumann_solve,
    row_coarse, lower_coef, upper_coef, face_order, primal_lists,
):
    rows, columns = lax.axis_size("axial"), lax.axis_size("circ")
    rhs, points = load_terms.shape[2], load_terms.shape[3]
    place = jnp.stack(
        [lax.axis_index("axial"), jnp.int32(rows), lax.axis_index("circ")]
    ).astype(jnp.int32)
    order = face_order[0]
    blocks = interior_inverse[0, 0]
    swap = functools.partial(exchange, rows=rows, columns=columns)

    def face(n):
        return [(n, LANES)] * 4

    shared, *sends = call(
        k_prepare, [(rhs + 8, points)] + face(rhs + 8), place, load_terms[0, 0], diffusivity[0], order
    )
    got = swap(sends)
    diag, couple, neumann, avg = call(
        k_matrices,
        [(1, points), (points, points), (points, points), (8, points)],
        None, order, interface_diag[0], coupling[0, 0], neumann_solve[0, 0], primal_lists[0, 0],
        flops=2_000_000_000,
    )
    r0, share, prim0, t0, *sends = call(
        k_first,
        [(rhs, points), (1, points), (8, rhs), (rhs + 8, points)] + face(rhs + 8),
        place, shared, *got, neumann, avg,
    )
    got = swap(sends)
    n = rhs + 24
    z0, q0, *sends = call(
        functools.partial(k_schur, rhs=rhs), [(n, points)] * 2 + face(n),
        place, t0, *got, diag, couple, blocks,
    )
    got = swap(sends)
    n = rhs + 40
    v1, t1, prim1, *sends = call(
        k_second, [(n, points)] * 2 + [(8, n)] + face(n), place, q0, *got, r0, share, neumann, avg
    )
    got = swap(sends)
    n = rhs + 56
    z1, q1, *sends = call(
        functools.partial(k_schur, rhs=rhs), [(n, points)] * 2 + face(n),
        place, t1, *got, diag, couple, blocks,
    )
    got = swap(sends)
    n = rhs + 72
    v2, pay = call(
        k_third, [(n, points), (32, LANES)], place, q1, *got, v1, share, avg, prim0, prim1
    )
    coefs = jnp.concatenate(
        [jnp.swapaxes(row_coarse[0], 0, 1), lower_coef[0][:, None], upper_coef[0][:, None]], axis=1
    )
    coefs = jnp.pad(coefs, ((24, 0), (112, LANES - 112 - coefs.shape[1])))
    got = spread(jnp.broadcast_to(pay[None], (columns, 32, LANES)), "circ")
    (pay,) = call(k_sum_spread, [(rows, 32, LANES)], None, got, coefs)
    got = spread(pay, "axial")
    width = max(LANES, 8 * rows)
    vv2, t2, c0, c1, c2, *sends = call(
        k_coarse,
        [(rhs, points)] * 2 + [(72, rhs), (40, rhs), (24, rhs)] + face(rhs),
        place, got, v2, v1, share, neumann,
        scratch=[pltpu.VMEM((width, width), F32)] * 3 + [pltpu.VMEM((width + 64, rhs), F32)] * 3,
    )
    got = swap(sends)
    z0f, w0f, z1f, w1f, dots = call(
        k_known, [(rhs, points)] * 4 + [(16, rhs)], None, r0, z0, v1, z1, v2, vv2, c0, c1
    )
    z2f, q2, *sends = call(
        k_last_schur, [(rhs, points)] * 2 + face(rhs),
        place, t2, *got, z0, c2, diag, couple, blocks,
    )
    got = swap(sends)
    w2f, pay = call(
        k_dots, [(rhs, points), (16, rhs)],
        place, q2, *got, r0, w0f, vv2, z0f, z1f, z2f, dots,
    )
    got = spread(jnp.broadcast_to(pay[None], (columns, 16, rhs)), "circ")
    (pay,) = call(k_sum_spread, [(rows, 16, rhs)], None, got, jnp.zeros((16, rhs), F32))
    got = spread(pay, "axial")
    x, r = call(
        k_final, [(rhs, points)] * 2, None, got, order, r0, z0f, z1f, z2f, w0f, w1f, w2f
    )
    return (x[None, None], r[None, None])


def solution(mesh):
    in_specs = (
        P("axial", "circ", None, None),
        P("axial", "circ", None),
        P("axial", "circ", None),
        P("axial", "circ", None, None),
        P("axial", "circ", None, None, None),
        P("axial", "circ", None, None),
        P("axial", None, None),
        P("axial", None),
        P("axial", None),
        P("axial", "circ", None),
        P("axial", "circ", None, None),
    )
    out_specs = (P("axial", "circ", None, None), P("axial", "circ", None, None))
    return jax.shard_map(local, mesh=mesh, in_specs=in_specs, out_specs=out_specs, check_vma=False)
```

time: 1210 us -> 250 us (0.21)
  blocking collectives: 798 us -> 88.5 us
  other arithmetic: 198 us -> 0.16 us
  local copies, waits for them, and re-layouts: 53.7 us -> 8.6 us
  Pallas kernels: 0 us -> 30.2 us
  matrix products: 18.2 us -> 0 us
  starting transfers between devices: 110 us -> 92.7 us
    psum x8 -> x0, blocking collectives: 618 us -> none  [the longest x5 525 us: inner_product(): return 0.5 * lax.psum(jnp.sum(first * second, axis=1), ('axial', 'circ'))]
    all_gather x5 -> x0, blocking collectives: 180 us -> none  [the longest x3 116 us: top_level(): lax.all_gather(row_total[None], 'axial', axis=0, tiled=True)]
    dynamic_update_slice x192 -> x0, other arithmetic: 176 us -> none  [top_level(): lax.scan(forward_step, start, (all_lower[:, None, :], all_rows))]
    all_to_all x0 -> x3, blocking collectives: none -> 88.5 us  [spread(): return lax.all_to_all(value, axis, split_axis=0, concat_axis=0, tiled=True)]
    gather x23 -> x0, local copies, waits for them, and re-layouts: 35.6 us -> none  [the longest x15 22.4 us: assemble(): return jnp.take(summed, order, axis=-1)]
    pallas_call x0 -> x14, Pallas kernels: none -> 30.2 us  [call(): pl.pallas_call(body, out_shape=[jax.ShapeDtypeStruct(shape, F32) for shap...]
    ppermute x32 -> x28, starting transfers between devices: 110 us -> 88.4 us  [the longest x7 29.1 us: exchange(): lax.ppermute(sends[3], 'circ', far)]
    dot_general x21 -> x0, matrix products: 18.2 us -> none  [the longest x3 5.23 us: local(): lax.dot_general(solved, couple_local, (((1,), (1,)), ((), ())), precision...]
  transfers between devices with their start and end apart: 32 -> 29, of which waited for: 16 -> 7; matrix products, arithmetic and copies ran while one was open for 0% -> 0% of each run, Pallas kernels for 0% -> 3%
where the time goes in v1:
time: 250 us; the launch traced here: 249 us
  starting transfers between devices  92.7 us (37%)
  blocking collectives  88.5 us (35%)
  Pallas kernels  30.2 us (12%)
  waiting for transfers between devices  27.3 us (11%)
  local copies, waits for them, and re-layouts  8.6 us (3%)
    all_to_all x3, blocking collectives, spread(): return lax.all_to_all(value, axis, split_axis=0, concat_axis=0, tiled=True)  88.5 us
    pallas_call x14, Pallas kernels, call(): pl.pallas_call(body, out_shape=[jax.ShapeDtypeStruct(shape, F32) for shap...  30.2 us
    ppermute x7, starting transfers between devices, exchange(): lax.ppermute(sends[3], 'circ', far)  29.1 us
    ppermute x7, starting transfers between devices, exchange(): lax.ppermute(sends[1], 'axial', link)  24.5 us
    ppermute x7, starting transfers between devices, exchange(): lax.ppermute(sends[0], 'axial', core)  21 us
    ppermute x7, waiting for transfers between devices, exchange(): lax.ppermute(sends[3], 'circ', far)  18.9 us
    ppermute x7, starting transfers between devices, exchange(): lax.ppermute(sends[2], 'circ', near)  13.7 us
    unnamed x30, local copies, waits for them, and re-layouts  7.57 us
  transfers between devices with their start and end apart: 29, of which 7 were waited for; matrix products, arithmetic and copies ran while one was open for 0% of the time, Pallas kernels for 3%

profile of v1, /device:TPU:1, one launch (start us, length us, event | category | flops | bytes accessed | tf_op | source)
XLA Modules:
  0.0 248.6 jit_solution(3818976607293683980)
XLA Ops:
  3.5 8.8 %collective-permute-start = (f32[136,128]{1,0:T(8,128)S(1)}, f32[136,128]{1,0:T(8,128)S(1)}, u32[]{:S(2)}, u32[]{:S(2)}) collective-permute-start(f32[136,128]{1,0:T(8,128)S(1)} %get-tuple-element.65), channel_id=1, source_target_pairs={{0,16},{16,0},{32,48},{48,32},{64,80},{80,64},{96,112},{112,96},{1... | collective-permute-start | bytes 208904 | tf_op jit(solution)/shard_map/ppermute | solution.py:410
  12.3 1.9 collective-permute-start.1
  14.2 1.9 collective-permute-start.2
  16.2 3.5 %collective-permute-start.3 = (f32[136,128]{1,0:T(8,128)S(1)}, f32[136,128]{1,0:T(8,128)S(1)}, u32[]{:S(2)}, u32[]{:S(2)}) collective-permute-start(f32[136,128]{1,0:T(8,128)S(1)} %get-tuple-element.68), channel_id=1, source_target_pairs={{0,15},{1,2},{2,1},{3,4},{4,3},{5,6},{6,5},{7,8},{8,7},{9,10},{10,... | collective-permute-start | bytes 208904 | tf_op jit(solution)/shard_map/ppermute | solution.py:413
  22.8 5.0 %shard_map.123 = (f32[1,512]{1,0:T(1,128)S(1)}, f32[512,512]{1,0:T(8,128)S(1)}, f32[512,512]{1,0:T(8,128)S(1)}, f32[8,512]{1,0:T(8,128)S(1)}) custom-call(s32[1,512]{1,0:T(1,128)S(1)} %bitcast.21, f32[1,512]{1,0:T(1,128)S(1)} %bitcast.27, f32[512,512]{1,0:T(8,128)S(1)} %bitcast.24, f32[512,512]{1,0:T(8,128)S(1)} %bitcast.25, s32[8,64]{1,0:T(8,128)S(1)} %bitcast.26), custom_call_target="tpu_custom_call" | custom-call | flops 2000000000 | bytes 1000000 | tf_op jit(solution)/shard_map/pallas_call | solution.py:393
  27.9 1.4 shard_map.124
  29.3 1.9 collective-permute-start.4
  31.2 3.9 %collective-permute-start.5 = (f32[136,128]{1,0:T(8,128)S(1)}, f32[136,128]{1,0:T(8,128)S(1)}, u32[]{:S(2)}, u32[]{:S(2)}) collective-permute-start(f32[136,128]{1,0:T(8,128)S(1)} %get-tuple-element.73), channel_id=1, source_target_pairs={{16,32},{32,16},{48,64},{64,48},{80,96},{96,80},{112,128},{128,112... | collective-permute-start | bytes 208904 | tf_op jit(solution)/shard_map/ppermute | solution.py:411
  35.2 1.9 collective-permute-start.6
  37.1 5.1 %collective-permute-start.7 = (f32[136,128]{1,0:T(8,128)S(1)}, f32[136,128]{1,0:T(8,128)S(1)}, u32[]{:S(2)}, u32[]{:S(2)}) collective-permute-start(f32[136,128]{1,0:T(8,128)S(1)} %get-tuple-element.75), channel_id=1, source_target_pairs={{0,15},{1,2},{2,1},{3,4},{4,3},{5,6},{6,5},{7,8},{8,7},{9,10},{10,... | collective-permute-start | bytes 208904 | tf_op jit(solution)/shard_map/ppermute | solution.py:413
  42.2 3.2 %collective-permute-done.7.g3 = f32[136,128]{1,0:T(8,128)S(1)} collective-permute-done((f32[136,128]{1,0:T(8,128)S(1)}, f32[136,128]{1,0:T(8,128)S(1)}, u32[]{:S(2)}, u32[]{:S(2)}) %collective-permute-start.7) | collective-permute-done | bytes 69664 | tf_op jit(solution)/shard_map/ppermute | solution.py:413
  45.5 3.1 %shard_map.125 = (f32[152,512]{1,0:T(8,128)S(1)}, f32[152,512]{1,0:T(8,128)S(1)}, f32[152,128]{1,0:T(8,128)S(1)}, f32[152,128]{1,0:T(8,128)S(1)}, f32[152,128]{1,0:T(8,128)S(1)}, /*index=5*/f32[152,128]{1,0:T(8,128)S(1)}) custom-call(s32[3]{0:T(128)S(1)} %pad_add_fusion.place, f32[136,512]{1,0:T(8,128)S(1)} %get-tuple-element.71.t, ...), custom_call_target="tpu_custom_call" | custom-call | flops 1000000 | bytes 1000000 | tf_op jit(solution)/shard_map/pallas_call | solution.py:393
  49.3 1.9 collective-permute-start.10
  51.2 5.1 %collective-permute-start.11 = (f32[152,128]{1,0:T(8,128)S(1)}, f32[152,128]{1,0:T(8,128)S(1)}, u32[]{:S(2)}, u32[]{:S(2)}) collective-permute-start(f32[152,128]{1,0:T(8,128)S(1)} %get-tuple-element.82), channel_id=1, source_target_pairs={{0,15},{1,2},{2,1},{3,4},{4,3},{5,6},{6,5},{7,8},{8,7},{9,10},{10,... | collective-permute-start | bytes 233480 | tf_op jit(solution)/shard_map/ppermute | solution.py:413
  56.3 1.9 collective-permute-start.8
  58.2 3.6 %collective-permute-start.9 = (f32[152,128]{1,0:T(8,128)S(1)}, f32[152,128]{1,0:T(8,128)S(1)}, u32[]{:S(2)}, u32[]{:S(2)}) collective-permute-start(f32[152,128]{1,0:T(8,128)S(1)} %get-tuple-element.80), channel_id=1, source_target_pairs={{16,32},{32,16},{48,64},{64,48},{80,96},{96,80},{112,128},{128,112... | collective-permute-start | bytes 233480 | tf_op jit(solution)/shard_map/ppermute | solution.py:411
  61.9 2.1 collective-permute-done.9.g1
  63.9 1.6 shard_map.126
  65.5 1.9 collective-permute-start.12
  67.4 4.4 %collective-permute-start.13 = (f32[168,128]{1,0:T(8,128)S(1)}, f32[168,128]{1,0:T(8,128)S(1)}, u32[]{:S(2)}, u32[]{:S(2)}) collective-permute-start(f32[168,128]{1,0:T(8,128)S(1)} %get-tuple-element.87), channel_id=1, source_target_pairs={{16,32},{32,16},{48,64},{64,48},{80,96},{96,80},{112,128},{128,112... | collective-permute-start | bytes 258056 | tf_op jit(solution)/shard_map/ppermute | solution.py:411
  71.8 1.9 collective-permute-start.14
  73.8 4.6 %collective-permute-start.15 = (f32[168,128]{1,0:T(8,128)S(1)}, f32[168,128]{1,0:T(8,128)S(1)}, u32[]{:S(2)}, u32[]{:S(2)}) collective-permute-start(f32[168,128]{1,0:T(8,128)S(1)} %get-tuple-element.89), channel_id=1, source_target_pairs={{0,15},{1,2},{2,1},{3,4},{4,3},{5,6},{6,5},{7,8},{8,7},{9,10},{10,... | collective-permute-start | bytes 258056 | tf_op jit(solution)/shard_map/ppermute | solution.py:413
  78.4 4.0 %collective-permute-done.15.g3 = f32[168,128]{1,0:T(8,128)S(1)} collective-permute-done((f32[168,128]{1,0:T(8,128)S(1)}, f32[168,128]{1,0:T(8,128)S(1)}, u32[]{:S(2)}, u32[]{:S(2)}) %collective-permute-start.15) | collective-permute-done | bytes 86048 | tf_op jit(solution)/shard_map/ppermute | solution.py:413
  82.3 3.2 %shard_map.127 = (f32[184,512]{1,0:T(8,128)S(1)}, f32[184,512]{1,0:T(8,128)S(1)}, f32[184,128]{1,0:T(8,128)S(1)}, f32[184,128]{1,0:T(8,128)S(1)}, f32[184,128]{1,0:T(8,128)S(1)}, /*index=5*/f32[184,128]{1,0:T(8,128)S(1)}) custom-call(s32[3]{0:T(128)S(1)} %pad_add_fusion.place, f32[168,512]{1,0:T(8,128)S(1)} %get-tuple-element.85.t, ...), custom_call_target="tpu_custom_call" | custom-call | flops 1000000 | bytes 1000000 | tf_op jit(solution)/shard_map/pallas_call | solution.py:393
  86.3 1.9 collective-permute-start.16
  88.2 4.1 %collective-permute-start.17 = (f32[184,128]{1,0:T(8,128)S(1)}, f32[184,128]{1,0:T(8,128)S(1)}, u32[]{:S(2)}, u32[]{:S(2)}) collective-permute-start(f32[184,128]{1,0:T(8,128)S(1)} %get-tuple-element.92), channel_id=1, source_target_pairs={{16,32},{32,16},{48,64},{64,48},{80,96},{96,80},{112,128},{128,112... | collective-permute-start | bytes 282632 | tf_op jit(solution)/shard_map/ppermute | solution.py:411
  92.3 1.9 collective-permute-start.18
  94.2 4.5 %collective-permute-start.19 = (f32[184,128]{1,0:T(8,128)S(1)}, f32[184,128]{1,0:T(8,128)S(1)}, u32[]{:S(2)}, u32[]{:S(2)}) collective-permute-start(f32[184,128]{1,0:T(8,128)S(1)} %get-tuple-element.94), channel_id=1, source_target_pairs={{0,15},{1,2},{2,1},{3,4},{4,3},{5,6},{6,5},{7,8},{8,7},{9,10},{10,... | collective-permute-start | bytes 282632 | tf_op jit(solution)/shard_map/ppermute | solution.py:413
  98.8 4.1 %collective-permute-done.19.g3 = f32[184,128]{1,0:T(8,128)S(1)} collective-permute-done((f32[184,128]{1,0:T(8,128)S(1)}, f32[184,128]{1,0:T(8,128)S(1)}, u32[]{:S(2)}, u32[]{:S(2)}) %collective-permute-start.19) | collective-permute-done | bytes 94240 | tf_op jit(solution)/shard_map/ppermute | solution.py:413
  104.7 4.3 %all-to-all-start = ((f32[16,32,128]{2,1,0:T(8,128)}), f32[16,32,128]{2,1,0:T(8,128)}, u32[]{:S(2)}, u32[]{:S(2)}) async-start(f32[16,32,128]{2,1,0:T(8,128)} %broadcast_in_dim.10), calls=%async_computation | async-start | bytes 524288 | tf_op jit(solution)/shard_map/all_to_all | solution.py:418
  110.6 6.2 %all-to-all-done.got = f32[16,32,128]{2,1,0:T(8,128)} async-done(((f32[16,32,128]{2,1,0:T(8,128)}), f32[16,32,128]{2,1,0:T(8,128)}, u32[]{:S(2)}, u32[]{:S(2)}) %all-to-all-start) | async-done | bytes 262176 | tf_op jit(solution)/shard_map/all_to_all | solution.py:418
  117.9 50.6 %all_to_all.20.got = f32[32,32,128]{2,1,0:T(8,128)S(1)} all-to-all(f32[32,32,128]{2,1,0:T(8,128)S(1)} %shard_map.129), channel_id=1, replica_groups=mesh['axial'=32,'circ'=16] {'axial'}, dimensions={0} | all-to-all | bytes 1048576 | tf_op jit(solution)/shard_map/all_to_all | solution.py:418
  168.4 3.9 %shard_map.130 = (f32[128,512]{1,0:T(8,128)S(1)}, f32[128,512]{1,0:T(8,128)S(1)}, f32[72,128]{1,0:T(8,128)S(1)}, f32[40,128]{1,0:T(8,128)S(1)}, f32[24,128]{1,0:...) custom-call(s32[3]{0:T(128)S(1)} %pad_add_fusion.place, ...), custom_call_target="tpu_custom_call" | custom-call | flops 1000000 | bytes 1000000 | tf_op jit(solution)/shard_map/pallas_call | solution.py:393
  172.3 2.4 collective-permute-start.20
  174.7 1.9 collective-permute-start.21
  176.7 2.2 collective-permute-start.22
  178.9 3.2 %collective-permute-start.23 = (f32[128,128]{1,0:T(8,128)S(1)}, f32[128,128]{1,0:T(8,128)S(1)}, u32[]{:S(2)}, u32[]{:S(2)}) collective-permute-start(f32[128,128]{1,0:T(8,128)S(1)} %get-tuple-element.104), channel_id=1, source_target_pairs={{0,15},{1,2},{2,1},{3,4},{4,3},{5,6},{6,5},{7,8},{8,7},{9,10},{10,... | collective-permute-start | bytes 196616 | tf_op jit(solution)/shard_map/ppermute | solution.py:413
  182.1 5.3 %collective-permute-done.23.g3 = f32[128,128]{1,0:T(8,128)S(1)} collective-permute-done((f32[128,128]{1,0:T(8,128)S(1)}, f32[128,128]{1,0:T(8,128)S(1)}, u32[]{:S(2)}, u32[]{:S(2)}) %collective-permute-start.23) | collective-permute-done | bytes 65568 | tf_op jit(solution)/shard_map/ppermute | solution.py:413
  187.4 3.0 %shard_map.131 = (f32[128,512]{1,0:T(8,128)S(1)}, f32[128,512]{1,0:T(8,128)S(1)}, f32[128,128]{1,0:T(8,128)S(1)}, f32[128,128]{1,0:T(8,128)S(1)}, f32[128,128]{1,0:T(8,128)S(1)}, /*index=5*/f32[128,128]{1,0:T(8,128)S(1)}) custom-call(s32[3]{0:T(128)S(1)} %pad_add_fusion.place, f32[128,512]{1,0:T(8,128)S(1)} %get-tuple-element.100.t, ...), custom_call_target="tpu_custom_call" | custom-call | flops 1000000 | bytes 1000000 | tf_op jit(solution)/shard_map/pallas_call | solution.py:393
  190.4 2.2 collective-permute-start.24
  192.6 4.6 %collective-permute-start.25 = (f32[128,128]{1,0:T(8,128)S(1)}, f32[128,128]{1,0:T(8,128)S(1)}, u32[]{:S(2)}, u32[]{:S(2)}) collective-permute-start(f32[128,128]{1,0:T(8,128)S(1)} %get-tuple-element.109), channel_id=1, source_target_pairs={{16,32},{32,16},{48,64},{64,48},{80,96},{96,80},{112,128},{128,112... | collective-permute-start | bytes 196616 | tf_op jit(solution)/shard_map/ppermute | solution.py:411
  197.2 1.9 collective-permute-start.26
  199.2 3.2 %collective-permute-start.27 = (f32[128,128]{1,0:T(8,128)S(1)}, f32[128,128]{1,0:T(8,128)S(1)}, u32[]{:S(2)}, u32[]{:S(2)}) collective-permute-start(f32[128,128]{1,0:T(8,128)S(1)} %get-tuple-element.111), channel_id=1, source_target_pairs={{0,15},{1,2},{2,1},{3,4},{4,3},{5,6},{6,5},{7,8},{8,7},{9,10},{10,... | collective-permute-start | bytes 196616 | tf_op jit(solution)/shard_map/ppermute | solution.py:413
  202.3 2.7 %shard_map.132 = (f32[128,512]{1,0:T(8,128)S(1)}, f32[128,512]{1,0:T(8,128)S(1)}, f32[128,512]{1,0:T(8,128)S(1)}, f32[128,512]{1,0:T(8,128)S(1)}, f32[16,128]{1,0:T(8,128)S(1)}) custom-call(f32[128,512]{1,0:T(8,128)S(1)} %get-tuple-element.83.r.r0, f32[152,512]{1,0:T(8,128)S(1)} %copy-done.2, f32[168,512]{1,0:T(8,128)S(1)} %get-tuple-element.95.v.v1, ...), custom_call_target="tpu_custom_call" | custom-call | flops 1000000 | bytes 1000000 | tf_op jit(solution)/shard_map/pallas_call | solution.py:393
  205.1 2.4 collective-permute-done.27.g3
  208.8 9.4 %all_to_all.21.got = f32[16,16,128]{2,1,0:T(8,128)S(1)} all-to-all(f32[16,16,128]{2,1,0:T(8,128)S(1)} %broadcast_in_dim.22), channel_id=1, replica_groups=mesh['axial'=32,'circ'=16] {'circ'}, dimensions={0} | all-to-all | bytes 262144 | tf_op jit(solution)/shard_map/all_to_all | solution.py:418
  218.3 28.6 %all_to_all.22.got = f32[32,16,128]{2,1,0:T(8,128)S(1)} all-to-all(f32[32,16,128]{2,1,0:T(8,128)S(1)} %shard_map.134), channel_id=1, replica_groups=mesh['axial'=32,'circ'=16] {'axial'}, dimensions={0} | all-to-all | bytes 524288 | tf_op jit(solution)/shard_map/all_to_all | solution.py:418
  246.9 1.8 shard_map.135
  (65 shorter events, 13.4 us)
Async XLA Ops:
  0.7 0.7 copy-start.7
  0.7 0.7 copy-start.6
  1.4 0.9 copy-start.5
  3.5 24.3 %collective-permute-start = (f32[136,128]{1,0:T(8,128)S(1)}, f32[136,128]{1,0:T(8,128)S(1)}, u32[]{:S(2)}, u32[]{:S(2)}) collective-permute-start(f32[136,128]{1,0:T(8,128)S(1)} %get-tuple-element.65), channel_id=1, source_target_pairs={{0,16},{16,0},{32,48},{48,32},{64,80},{80,64},{96,112},{112,96},{1... | collective-permute-start | bytes 208904 | tf_op jit(solution)/shard_map/ppermute | solution.py:410
  12.3 15.5 %collective-permute-start.1 = (f32[136,128]{1,0:T(8,128)S(1)}, f32[136,128]{1,0:T(8,128)S(1)}, u32[]{:S(2)}, u32[]{:S(2)}) collective-permute-start(f32[136,128]{1,0:T(8,128)S(1)} %get-tuple-element.66), channel_id=1, source_target_pairs={{16,32},{32,16},{48,64},{64,48},{80,96},{96,80},{112,128},{128,112... | collective-permute-start | bytes 208904 | tf_op jit(solution)/shard_map/ppermute | solution.py:411
  14.2 13.6 %collective-permute-start.2 = (f32[136,128]{1,0:T(8,128)S(1)}, f32[136,128]{1,0:T(8,128)S(1)}, u32[]{:S(2)}, u32[]{:S(2)}) collective-permute-start(f32[136,128]{1,0:T(8,128)S(1)} %get-tuple-element.67), channel_id=1, source_target_pairs={{0,1},{1,0},{2,3},{3,2},{4,5},{5,4},{6,7},{7,6},{8,9},{9,8},{10,11... | collective-permute-start | bytes 208904 | tf_op jit(solution)/shard_map/ppermute | solution.py:412
  16.2 3.6 %copy-start.10 = (s32[1,1,8,64]{3,2,1,0:T(8,128)S(1)}, s32[1,1,8,64]{3,2,1,0:T(8,128)}, u32[]{:S(2)}) copy-start(s32[1,1,8,64]{3,2,1,0:T(8,128)} %param.21) | copy-start | bytes 6148
  16.2 11.7 %collective-permute-start.3 = (f32[136,128]{1,0:T(8,128)S(1)}, f32[136,128]{1,0:T(8,128)S(1)}, u32[]{:S(2)}, u32[]{:S(2)}) collective-permute-start(f32[136,128]{1,0:T(8,128)S(1)} %get-tuple-element.68), channel_id=1, source_target_pairs={{0,15},{1,2},{2,1},{3,4},{4,3},{5,6},{6,5},{7,8},{8,7},{9,10},{10,... | collective-permute-start | bytes 208904 | tf_op jit(solution)/shard_map/ppermute | solution.py:413
  19.7 0.7 copy-start.11
  20.4 1.2 copy-start.8
  21.6 1.2 copy-start.9
  27.8 17.6 %copy-start = (f32[1,1,4,128,128]{4,3,2,1,0:T(8,128)S(1)}, f32[1,1,4,128,128]{4,3,2,1,0:T(8,128)}, u32[]{:S(2)}) copy-start(f32[1,1,4,128,128]{4,3,2,1,0:T(8,128)} %param.15) | copy-start | bytes 786436
  29.3 12.9 %collective-permute-start.4 = (f32[136,128]{1,0:T(8,128)S(1)}, f32[136,128]{1,0:T(8,128)S(1)}, u32[]{:S(2)}, u32[]{:S(2)}) collective-permute-start(f32[136,128]{1,0:T(8,128)S(1)} %get-tuple-element.72), channel_id=1, source_target_pairs={{0,16},{16,0},{32,48},{48,32},{64,80},{80,64},{96,112},{112,96},{1... | collective-permute-start | bytes 208904 | tf_op jit(solution)/shard_map/ppermute | solution.py:410
  31.2 11.0 %collective-permute-start.5 = (f32[136,128]{1,0:T(8,128)S(1)}, f32[136,128]{1,0:T(8,128)S(1)}, u32[]{:S(2)}, u32[]{:S(2)}) collective-permute-start(f32[136,128]{1,0:T(8,128)S(1)} %get-tuple-element.73), channel_id=1, source_target_pairs={{16,32},{32,16},{48,64},{64,48},{80,96},{96,80},{112,128},{128,112... | collective-permute-start | bytes 208904 | tf_op jit(solution)/shard_map/ppermute | solution.py:411
  35.2 7.0 %collective-permute-start.6 = (f32[136,128]{1,0:T(8,128)S(1)}, f32[136,128]{1,0:T(8,128)S(1)}, u32[]{:S(2)}, u32[]{:S(2)}) collective-permute-start(f32[136,128]{1,0:T(8,128)S(1)} %get-tuple-element.74), channel_id=1, source_target_pairs={{0,1},{1,0},{2,3},{3,2},{4,5},{5,4},{6,7},{7,6},{8,9},{9,8},{10,11... | collective-permute-start | bytes 208904 | tf_op jit(solution)/shard_map/ppermute | solution.py:412
  37.1 8.4 %collective-permute-start.7 = (f32[136,128]{1,0:T(8,128)S(1)}, f32[136,128]{1,0:T(8,128)S(1)}, u32[]{:S(2)}, u32[]{:S(2)}) collective-permute-start(f32[136,128]{1,0:T(8,128)S(1)} %get-tuple-element.75), channel_id=1, source_target_pairs={{0,15},{1,2},{2,1},{3,4},{4,3},{5,6},{6,5},{7,8},{8,7},{9,10},{10,... | collective-permute-start | bytes 208904 | tf_op jit(solution)/shard_map/ppermute | solution.py:413
  48.5 0.7 copy-start.1
  49.3 12.6 %collective-permute-start.10 = (f32[152,128]{1,0:T(8,128)S(1)}, f32[152,128]{1,0:T(8,128)S(1)}, u32[]{:S(2)}, u32[]{:S(2)}) collective-permute-start(f32[152,128]{1,0:T(8,128)S(1)} %get-tuple-element.81), channel_id=1, source_target_pairs={{0,1},{1,0},{2,3},{3,2},{4,5},{5,4},{6,7},{7,6},{8,9},{9,8},{10,11... | collective-permute-start | bytes 233480 | tf_op jit(solution)/shard_map/ppermute | solution.py:412
  51.2 10.7 %collective-permute-start.11 = (f32[152,128]{1,0:T(8,128)S(1)}, f32[152,128]{1,0:T(8,128)S(1)}, u32[]{:S(2)}, u32[]{:S(2)}) collective-permute-start(f32[152,128]{1,0:T(8,128)S(1)} %get-tuple-element.82), channel_id=1, source_target_pairs={{0,15},{1,2},{2,1},{3,4},{4,3},{5,6},{6,5},{7,8},{8,7},{9,10},{10,... | collective-permute-start | bytes 233480 | tf_op jit(solution)/shard_map/ppermute | solution.py:413
  56.3 5.6 %collective-permute-start.8 = (f32[152,128]{1,0:T(8,128)S(1)}, f32[152,128]{1,0:T(8,128)S(1)}, u32[]{:S(2)}, u32[]{:S(2)}) collective-permute-start(f32[152,128]{1,0:T(8,128)S(1)} %get-tuple-element.79), channel_id=1, source_target_pairs={{0,16},{16,0},{32,48},{48,32},{64,80},{80,64},{96,112},{112,96},{1... | collective-permute-start | bytes 233480 | tf_op jit(solution)/shard_map/ppermute | solution.py:410
  58.2 5.7 %collective-permute-start.9 = (f32[152,128]{1,0:T(8,128)S(1)}, f32[152,128]{1,0:T(8,128)S(1)}, u32[]{:S(2)}, u32[]{:S(2)}) collective-permute-start(f32[152,128]{1,0:T(8,128)S(1)} %get-tuple-element.80), channel_id=1, source_target_pairs={{16,32},{32,16},{48,64},{64,48},{80,96},{96,80},{112,128},{128,112... | collective-permute-start | bytes 233480 | tf_op jit(solution)/shard_map/ppermute | solution.py:411
  65.5 12.8 %collective-permute-start.12 = (f32[168,128]{1,0:T(8,128)S(1)}, f32[168,128]{1,0:T(8,128)S(1)}, u32[]{:S(2)}, u32[]{:S(2)}) collective-permute-start(f32[168,128]{1,0:T(8,128)S(1)} %get-tuple-element.86), channel_id=1, source_target_pairs={{0,16},{16,0},{32,48},{48,32},{64,80},{80,64},{96,112},{112,96},{1... | collective-permute-start | bytes 258056 | tf_op jit(solution)/shard_map/ppermute | solution.py:410
  67.4 10.9 %collective-permute-start.13 = (f32[168,128]{1,0:T(8,128)S(1)}, f32[168,128]{1,0:T(8,128)S(1)}, u32[]{:S(2)}, u32[]{:S(2)}) collective-permute-start(f32[168,128]{1,0:T(8,128)S(1)} %get-tuple-element.87), channel_id=1, source_target_pairs={{16,32},{32,16},{48,64},{64,48},{80,96},{96,80},{112,128},{128,112... | collective-permute-start | bytes 258056 | tf_op jit(solution)/shard_map/ppermute | solution.py:411
  71.8 6.5 %collective-permute-start.14 = (f32[168,128]{1,0:T(8,128)S(1)}, f32[168,128]{1,0:T(8,128)S(1)}, u32[]{:S(2)}, u32[]{:S(2)}) collective-permute-start(f32[168,128]{1,0:T(8,128)S(1)} %get-tuple-element.88), channel_id=1, source_target_pairs={{0,1},{1,0},{2,3},{3,2},{4,5},{5,4},{6,7},{7,6},{8,9},{9,8},{10,11... | collective-permute-start | bytes 258056 | tf_op jit(solution)/shard_map/ppermute | solution.py:412
  73.8 8.5 %collective-permute-start.15 = (f32[168,128]{1,0:T(8,128)S(1)}, f32[168,128]{1,0:T(8,128)S(1)}, u32[]{:S(2)}, u32[]{:S(2)}) collective-permute-start(f32[168,128]{1,0:T(8,128)S(1)} %get-tuple-element.89), channel_id=1, source_target_pairs={{0,15},{1,2},{2,1},{3,4},{4,3},{5,6},{6,5},{7,8},{8,7},{9,10},{10,... | collective-permute-start | bytes 258056 | tf_op jit(solution)/shard_map/ppermute | solution.py:413
  85.5 0.8 copy-start.3
  86.3 12.5 %collective-permute-start.16 = (f32[184,128]{1,0:T(8,128)S(1)}, f32[184,128]{1,0:T(8,128)S(1)}, u32[]{:S(2)}, u32[]{:S(2)}) collective-permute-start(f32[184,128]{1,0:T(8,128)S(1)} %get-tuple-element.91), channel_id=1, source_target_pairs={{0,16},{16,0},{32,48},{48,32},{64,80},{80,64},{96,112},{112,96},{1... | collective-permute-start | bytes 282632 | tf_op jit(solution)/shard_map/ppermute | solution.py:410
  88.2 10.6 %collective-permute-start.17 = (f32[184,128]{1,0:T(8,128)S(1)}, f32[184,128]{1,0:T(8,128)S(1)}, u32[]{:S(2)}, u32[]{:S(2)}) collective-permute-start(f32[184,128]{1,0:T(8,128)S(1)} %get-tuple-element.92), channel_id=1, source_target_pairs={{16,32},{32,16},{48,64},{64,48},{80,96},{96,80},{112,128},{128,112... | collective-permute-start | bytes 282632 | tf_op jit(solution)/shard_map/ppermute | solution.py:411
  92.3 6.5 %collective-permute-start.18 = (f32[184,128]{1,0:T(8,128)S(1)}, f32[184,128]{1,0:T(8,128)S(1)}, u32[]{:S(2)}, u32[]{:S(2)}) collective-permute-start(f32[184,128]{1,0:T(8,128)S(1)} %get-tuple-element.93), channel_id=1, source_target_pairs={{0,1},{1,0},{2,3},{3,2},{4,5},{5,4},{6,7},{7,6},{8,9},{9,8},{10,11... | collective-permute-start | bytes 282632 | tf_op jit(solution)/shard_map/ppermute | solution.py:412
  94.2 8.6 %collective-permute-start.19 = (f32[184,128]{1,0:T(8,128)S(1)}, f32[184,128]{1,0:T(8,128)S(1)}, u32[]{:S(2)}, u32[]{:S(2)}) collective-permute-start(f32[184,128]{1,0:T(8,128)S(1)} %get-tuple-element.94), channel_id=1, source_target_pairs={{0,15},{1,2},{2,1},{3,4},{4,3},{5,6},{6,5},{7,8},{8,7},{9,10},{10,... | collective-permute-start | bytes 282632 | tf_op jit(solution)/shard_map/ppermute | solution.py:413
  104.7 4.3 %copy-start.12 = (f32[1,8,8]{2,1,0:T(8,128)S(1)}, f32[1,8,8]{2,1,0:T(8,128)}, u32[]{:S(2)}) copy-start(f32[1,8,8]{2,1,0:T(8,128)} %param.17) | copy-start | bytes 772
  104.7 12.2 %all-to-all-start = ((f32[16,32,128]{2,1,0:T(8,128)}), f32[16,32,128]{2,1,0:T(8,128)}, u32[]{:S(2)}, u32[]{:S(2)}) async-start(f32[16,32,128]{2,1,0:T(8,128)} %broadcast_in_dim.10), calls=%async_computation | async-start | bytes 524288 | tf_op jit(solution)/shard_map/all_to_all | solution.py:418
  109.1 0.7 copy-start.13
  109.8 0.7 copy-start.14
  168.4 19.0 %copy-start.2 = (f32[152,512]{1,0:T(8,128)S(1)}, f32[152,512]{1,0:T(8,128)}, u32[]{:S(2)}) copy-start(f32[152,512]{1,0:T(8,128)} %copy-done.1) | copy-start | bytes 933892
  172.3 9.7 %collective-permute-start.20 = (f32[128,128]{1,0:T(8,128)S(1)}, f32[128,128]{1,0:T(8,128)S(1)}, u32[]{:S(2)}, u32[]{:S(2)}) collective-permute-start(f32[128,128]{1,0:T(8,128)S(1)} %get-tuple-element.101), channel_id=1, source_target_pairs={{0,16},{16,0},{32,48},{48,32},{64,80},{80,64},{96,112},{112,96},{1... | collective-permute-start | bytes 196616 | tf_op jit(solution)/shard_map/ppermute | solution.py:410
  174.7 7.3 %collective-permute-start.21 = (f32[128,128]{1,0:T(8,128)S(1)}, f32[128,128]{1,0:T(8,128)S(1)}, u32[]{:S(2)}, u32[]{:S(2)}) collective-permute-start(f32[128,128]{1,0:T(8,128)S(1)} %get-tuple-element.102), channel_id=1, source_target_pairs={{16,32},{32,16},{48,64},{64,48},{80,96},{96,80},{112,128},{128,112... | collective-permute-start | bytes 196616 | tf_op jit(solution)/shard_map/ppermute | solution.py:411
  176.7 5.4 %collective-permute-start.22 = (f32[128,128]{1,0:T(8,128)S(1)}, f32[128,128]{1,0:T(8,128)S(1)}, u32[]{:S(2)}, u32[]{:S(2)}) collective-permute-start(f32[128,128]{1,0:T(8,128)S(1)} %get-tuple-element.103), channel_id=1, source_target_pairs={{0,1},{1,0},{2,3},{3,2},{4,5},{5,4},{6,7},{7,6},{8,9},{9,8},{10,11... | collective-permute-start | bytes 196616 | tf_op jit(solution)/shard_map/ppermute | solution.py:412
  178.9 8.5 %collective-permute-start.23 = (f32[128,128]{1,0:T(8,128)S(1)}, f32[128,128]{1,0:T(8,128)S(1)}, u32[]{:S(2)}, u32[]{:S(2)}) collective-permute-start(f32[128,128]{1,0:T(8,128)S(1)} %get-tuple-element.104), channel_id=1, source_target_pairs={{0,15},{1,2},{2,1},{3,4},{4,3},{5,6},{6,5},{7,8},{8,7},{9,10},{10,... | collective-permute-start | bytes 196616 | tf_op jit(solution)/shard_map/ppermute | solution.py:413
  187.4 14.9 %copy-start.4 = (f32[184,512]{1,0:T(8,128)S(1)}, f32[184,512]{1,0:T(8,128)}, u32[]{:S(2)}) copy-start(f32[184,512]{1,0:T(8,128)} %copy-done.3) | copy-start | bytes 1130500
  190.4 14.6 %collective-permute-start.24 = (f32[128,128]{1,0:T(8,128)S(1)}, f32[128,128]{1,0:T(8,128)S(1)}, u32[]{:S(2)}, u32[]{:S(2)}) collective-permute-start(f32[128,128]{1,0:T(8,128)S(1)} %get-tuple-element.108), channel_id=1, source_target_pairs={{0,16},{16,0},{32,48},{48,32},{64,80},{80,64},{96,112},{112,96},{1... | collective-permute-start | bytes 196616 | tf_op jit(solution)/shard_map/ppermute | solution.py:410
  192.6 12.5 %collective-permute-start.25 = (f32[128,128]{1,0:T(8,128)S(1)}, f32[128,128]{1,0:T(8,128)S(1)}, u32[]{:S(2)}, u32[]{:S(2)}) collective-permute-start(f32[128,128]{1,0:T(8,128)S(1)} %get-tuple-element.109), channel_id=1, source_target_pairs={{16,32},{32,16},{48,64},{64,48},{80,96},{96,80},{112,128},{128,112... | collective-permute-start | bytes 196616 | tf_op jit(solution)/shard_map/ppermute | solution.py:411
  197.2 7.9 %collective-permute-start.26 = (f32[128,128]{1,0:T(8,128)S(1)}, f32[128,128]{1,0:T(8,128)S(1)}, u32[]{:S(2)}, u32[]{:S(2)}) collective-permute-start(f32[128,128]{1,0:T(8,128)S(1)} %get-tuple-element.110), channel_id=1, source_target_pairs={{0,1},{1,0},{2,3},{3,2},{4,5},{5,4},{6,7},{7,6},{8,9},{9,8},{10,11... | collective-permute-start | bytes 196616 | tf_op jit(solution)/shard_map/ppermute | solution.py:412
  199.2 8.3 %collective-permute-start.27 = (f32[128,128]{1,0:T(8,128)S(1)}, f32[128,128]{1,0:T(8,128)S(1)}, u32[]{:S(2)}, u32[]{:S(2)}) collective-permute-start(f32[128,128]{1,0:T(8,128)S(1)} %get-tuple-element.111), channel_id=1, source_target_pairs={{0,15},{1,2},{2,1},{3,4},{4,3},{5,6},{6,5},{7,8},{8,7},{9,10},{10,... | collective-permute-start | bytes 196616 | tf_op jit(solution)/shard_map/ppermute | solution.py:413

commit v2 on v1

--- a/solution.py
+++ b/solution.py
@@ -10,7 +10,9 @@
 SHIFT = 12.0
 HIGHEST = lax.Precision.HIGHEST
 F32 = jnp.float32
+BF16 = jnp.bfloat16
 LANES = 128
+PIECES = 2
 
 
 def mm(a, b):
@@ -25,6 +27,52 @@
     )
 
 
+def cut(value, count):
+    pieces = []
+    for _ in range(count):
+        piece = value.astype(BF16)
+        pieces.append(piece)
+        value = value - piece.astype(F32)
+    return pieces
+
+
+def narrow(a, b, transposed=False):
+    return lax.dot_general(
+        a, b, (((1,), (1 if transposed else 0,)), ((), ())), preferred_element_type=F32
+    )
+
+
+def product(a, pieces, transposed=False):
+    count = a.shape[0]
+    levels = len(pieces)
+    if count % 16:
+        a = jnp.concatenate([a, jnp.zeros((16 - count % 16, a.shape[1]), F32)], axis=0)
+    tall = a.shape[0]
+    left = cut(a, levels)
+    by_level = [None] * levels
+    for n, piece in enumerate(pieces):
+        used = left[: levels - n]
+        stack = used[0] if len(used) == 1 else jnp.concatenate(used, axis=0)
+        out = narrow(stack, piece, transposed)
+        for m in range(len(used)):
+            part = out[m * tall : (m + 1) * tall]
+            level = n + m
+            by_level[level] = part if by_level[level] is None else by_level[level] + part
+    total = by_level[-1]
+    for part in by_level[-2::-1]:
+        total = total + part
+    return total[:count]
+
+
+def select_columns(a, hot, transposed):
+    count = a.shape[0]
+    if count % 16:
+        a = jnp.concatenate([a, jnp.zeros((16 - count % 16, a.shape[1]), F32)], axis=0)
+    tall = a.shape[0]
+    out = narrow(jnp.concatenate(cut(a, 3), axis=0), hot, transposed)
+    return ((out[2 * tall :] + out[tall : 2 * tall]) + out[:tall])[:count]
+
+
 def faces_of(full):
     return [full[:, f * LANES : (f + 1) * LANES] for f in range(4)]
 
@@ -32,17 +80,23 @@
 def one_hot_faces(order):
     rows = lax.broadcasted_iota(jnp.int32, (LANES, LANES), 0)
     return [
-        jnp.where(order[:, f * LANES : (f + 1) * LANES] - f * LANES == rows, 1.0, 0.0).astype(F32)
+        jnp.where(order[:, f * LANES : (f + 1) * LANES] - f * LANES == rows, 1.0, 0.0)
+        .astype(F32)
+        .astype(BF16)
         for f in range(4)
     ]
 
 
 def to_shared(full, hots):
-    return jnp.concatenate([mm_t(part, hot) for part, hot in zip(faces_of(full), hots)], axis=1)
+    return jnp.concatenate(
+        [select_columns(part, hot, True) for part, hot in zip(faces_of(full), hots)], axis=1
+    )
 
 
 def to_points(full, hots):
-    return jnp.concatenate([mm(part, hot) for part, hot in zip(faces_of(full), hots)], axis=1)
+    return jnp.concatenate(
+        [select_columns(part, hot, False) for part, hot in zip(faces_of(full), hots)], axis=1
+    )
 
 
 class Place:
@@ -96,28 +150,47 @@
     return jnp.concatenate(out, axis=1)
 
 
+def held(ref):
+    return [ref[n] for n in range(ref.shape[0])]
+
+
 def schur(z, diag, couple, blocks):
-    inner = mm(z, couple)
-    solved = jnp.concatenate([mm(part, blocks[n]) for n, part in enumerate(faces_of(inner))], axis=1)
-    return diag * z - mm_t(solved, couple)
-
-
-def k_prepare(place, load, rho, order, shared_o, *sends):
-    at = Place(place)
+    inner = product(z, couple)
+    solved = jnp.concatenate(
+        [
+            product(part, [piece[n] for piece in blocks])
+            for n, part in enumerate(faces_of(inner))
+        ],
+        axis=1,
+    )
+    return diag * z - product(solved, couple, True)
+
+
+def k_prepare(place, load, rho, order, shared_o, order_o, s0, s1, s2, s3, load_s, rho_s, sem):
+    at = Place(place)
+    copies = [
+        pltpu.make_async_copy(source, target, sem.at[n])
+        for n, (source, target) in enumerate(((order, order_o), (load, load_s), (rho, rho_s)))
+    ]
+    for copy in copies:
+        copy.start()
+    copies[0].wait()
+    hots = one_hot_faces(order_o[...])
+    copies[1].wait()
+    copies[2].wait()
+    pad = jnp.zeros((7, rho_s.shape[1]), F32)
+    full = to_shared(jnp.concatenate([load_s[...], rho_s[...], pad], axis=0), hots)
+    shared_o[...] = full
+    put_sends((s0, s1, s2, s3), full, at)
+
+
+def k_neumann(order, neumann, lists, neumann_o, avg_o, neumann_s, sem):
+    copies = []
+    for f in range(4):
+        rows = pl.ds(f * LANES, LANES)
+        copies.append(pltpu.make_async_copy(neumann.at[rows], neumann_s.at[rows], sem.at[f]))
+        copies[f].start()
     hots = one_hot_faces(order[...])
-    pad = jnp.zeros((7, rho.shape[1]), F32)
-    full = to_shared(jnp.concatenate([load[...], rho[...], pad], axis=0), hots)
-    shared_o[...] = full
-    put_sends(sends, full, at)
-
-
-def k_matrices(order, diag, couple, neumann, lists, diag_o, couple_o, neumann_o, avg_o):
-    hots = one_hot_faces(order[...])
-    diag_o[...] = to_shared(jnp.broadcast_to(diag[...], (8, diag.shape[1])), hots)[:1]
-    for f in range(4):
-        rows = slice(f * LANES, (f + 1) * LANES)
-        couple_o[rows, :] = mm(hots[f], couple[rows, :])
-        neumann_o[rows, :] = to_shared(mm(hots[f], neumann[rows, :]), hots)
     points = order.shape[1]
     named = lists[...]
     position = lax.broadcasted_iota(jnp.int32, (8, points), 1)
@@ -126,6 +199,35 @@
     for item in range(length):
         total = total + jnp.where(named[:, item : item + 1] == position, 1.0, 0.0)
     avg_o[...] = to_shared(total * (1.0 / length), hots)
+    for f in range(4):
+        rows = slice(f * LANES, (f + 1) * LANES)
+        copies[f].wait()
+        for n, piece in enumerate(cut(neumann_s[rows, :], PIECES)):
+            half = narrow(hots[f], piece).astype(BF16)
+            neumann_o[n, rows, :] = jnp.concatenate(
+                [narrow(part, hot, True) for part, hot in zip(faces_of(half), hots)], axis=1
+            ).astype(BF16)
+
+
+def k_couple(order, diag, after, couple, blocks, diag_o, couple_o, blocks_o, couple_s, blocks_s, sem):
+    copies = []
+    for f in range(4):
+        rows = pl.ds(f * LANES, LANES)
+        copies.append(pltpu.make_async_copy(couple.at[rows], couple_s.at[rows], sem.at[f]))
+    copies.append(pltpu.make_async_copy(blocks, blocks_s, sem.at[4]))
+    for copy in copies:
+        copy.start()
+    hots = one_hot_faces(order[...])
+    diag_o[...] = to_shared(jnp.broadcast_to(diag[...], (8, diag.shape[1])), hots)[:1]
+    for f in range(4):
+        rows = slice(f * LANES, (f + 1) * LANES)
+        copies[f].wait()
+        for n, piece in enumerate(cut(couple_s[rows, :], PIECES)):
+            couple_o[n, rows, :] = narrow(hots[f], piece).astype(BF16)
+    copies[4].wait()
+    for f in range(4):
+        for n, piece in enumerate(cut(blocks_s[f], PIECES)):
+            blocks_o[n, f] = piece
 
 
 def k_first(place, shared, g0, g1, g2, g3, neumann, avg, r_o, share_o, prim_o, t_o, *sends):
@@ -139,7 +241,7 @@
     share_o[...] = share
     weighted = share * r
     prim_o[...] = mm_t(avg[...], weighted)
-    t = jnp.concatenate([share * mm(weighted, neumann[...]), share * avg[...]], axis=0)
+    t = jnp.concatenate([share * product(weighted, held(neumann)), share * avg[...]], axis=0)
     t_o[...] = t
     put_sends(sends, t, at)
 
@@ -148,7 +250,7 @@
     at = Place(place)
     z = assembled(t[...], (g0, g1, g2, g3), at, rhs)
     z_o[...] = z
-    q = schur(z, diag[...], couple[...], blocks)
+    q = schur(z, diag[...], held(couple), held(blocks))
     q_o[...] = q
     put_sends(sends, q, at)
 
@@ -163,7 +265,7 @@
     pr_o[...] = jnp.concatenate(
         [mm_t(avg[...], weighted[:rhs]), mm_t(avg[...], weighted[rhs:])], axis=1
     )
-    t = share[...] * mm(weighted, neumann[...])
+    t = share[...] * product(weighted, held(neumann))
     t_o[...] = t
     put_sends(sends, t, at)
 
@@ -185,11 +287,22 @@
     pay_o[...] = jnp.concatenate([prim0[...], prim1[...][:, :rhs], prim2, tail], axis=0)
 
 
-def k_sum_spread(got, coefs, out):
+def summed(got):
     total = got[0]
     for item in range(1, got.shape[0]):
         total = total + got[item]
-    total = total + coefs[...]
+    return total
+
+
+def k_sum_halves(got, coefs, out):
+    total = summed(got) + coefs[...]
+    half = total.shape[0] // 2
+    for item in range(out.shape[0]):
+        out[item] = total[half * (item % 2) : half * (item % 2) + half]
+
+
+def k_sum_spread(got, out):
+    total = summed(got)
     for item in range(out.shape[0]):
         out[item] = total
 
@@ -209,21 +322,23 @@
 
 
 def k_coarse(
-    place, got, v2, v1, share, neumann,
+    place, mine, other, v2, v1, share, neumann,
     v_o, t_o, c0_o, c1_o, c2_o, s0, s1, s2, s3,
     band0, band1, band2, c0_s, c1_s, c2_s,
 ):
     at = Place(place)
     rhs = v_o.shape[0]
-    rows = got.shape[0]
+    rows = mine.shape[0]
     width = band0.shape[1]
     lane = lax.broadcasted_iota(jnp.int32, (8, width), 1)
     lowers, uppers = [], []
     for ref in (band0, band1, band2):
         if ref.shape[0] > rows * 8:
             ref[rows * 8 :, :] = jnp.zeros((ref.shape[0] - rows * 8, width), F32)
+    upper = [jnp.where(at.even_row, mine[k], other[k]) for k in range(rows)]
+    lower = [jnp.where(at.even_row, other[k], mine[k]) for k in range(rows)]
     for k in range(rows):
-        tail = got[k, 24:32, :]
+        tail = lower[k][8:16]
         lowers.append(jnp.broadcast_to(tail[:, 120:121], (8, rhs)))
         uppers.append(jnp.broadcast_to(tail[:, 121:122], (8, rhs)))
         wide = tail
@@ -247,10 +362,10 @@
         return stacked(coarse_rows(tiles, lowers, uppers)) + mm(band0[...], total)
 
     edge = jnp.zeros((32, rhs), F32)
-    c0 = solve(stacked([got[k, 0:8, :] for k in range(rows)]))
-    c1 = solve(stacked([got[k, 8:16, :] for k in range(rows)]) + mm(band1[...], c0))
+    c0 = solve(stacked([part[0:8] for part in upper]))
+    c1 = solve(stacked([part[8:16] for part in upper]) + mm(band1[...], c0))
     c2 = solve(
-        stacked([got[k, 16:24, :] for k in range(rows)]) + mm(band2[...], c0) + mm(band1[...], c1)
+        stacked([part[0:8] for part in lower]) + mm(band2[...], c0) + mm(band1[...], c1)
     )
     for ref, value in ((c0_s, c0), (c1_s, c1), (c2_s, c2)):
         ref[0:32, :] = edge
@@ -266,7 +381,7 @@
     v = v2[:rhs, :] + mm_first(jnp.concatenate([c0w, c1w], axis=0),
                                jnp.concatenate([v2[rhs:, :], v1[rhs:, :]], axis=0))
     v_o[...] = v
-    t = share[...] * mm(share[...] * v, neumann[...])
+    t = share[...] * product(share[...] * v, held(neumann))
     t_o[...] = t
     put_sends((s0, s1, s2, s3), t, at)
 
@@ -301,7 +416,9 @@
     w0_o[...] = v1f + SHIFT * r[...]
     w1_o[...] = v2f + SHIFT * v1f
     vs = (r[...], v1f, v2f)
-    dots_o[...] = dot_rows([(3 * i + j, (vs[i], (z0f, z1f)[j])) for i in range(3) for j in range(2)])
+    dots_o[...] = dot_rows(
+        [(0, (vs[0], z0f)), (1, (vs[0], z1f)), (2, (vs[1], z0f)), (3, (vs[1], z1f)), (4, (v2f, z1f))]
+    )
 
 
 def k_last_schur(place, t, g0, g1, g2, g3, pbasis, c2, diag, couple, blocks, z_o, q_o, *sends):
@@ -309,32 +426,36 @@
     rhs = z_o.shape[0]
     z = assembled(t[...], (g0, g1, g2, g3), at, rhs) + mm_first(c2[...], pbasis[rhs:, :])
     z_o[...] = z
-    q = schur(z, diag[...], couple[...], blocks)
+    q = schur(z, diag[...], held(couple), held(blocks))
     q_o[...] = q
     put_sends(sends, q, at)
 
 
-def k_dots(place, q, g0, g1, g2, g3, r, w0, vv2, z0, z1, z2, dots, w2_o, pay_o):
+def k_dots(place, q, g0, g1, g2, g3, r, w0, vv2, z2, dots, w2_o, pay_o):
     at = Place(place)
     w2 = assembled(q[...], (g0, g1, g2, g3), at, q.shape[0])
     w2_o[...] = w2
     v1 = w0[...] - SHIFT * r[...]
     vs = (r[...], v1, vv2[...])
-    pairs = [(3 * i + 2, (vs[i], z2[...])) for i in range(3)]
-    pairs += [(9 + i, (z, w2)) for i, z in enumerate((z0[...], z1[...], z2[...]))]
-    pay_o[...] = dots[...] + dot_rows(pairs)
+    pairs = [(5 + i, (vs[i], z2[...])) for i in range(3)] + [(8, (z2[...], w2))]
+    table = dots[...] + dot_rows(pairs)
+    pay_o[...] = jnp.concatenate([table[i : i + 1] for i in range(9)], axis=1)
 
 
 def k_final(got, order, r0, z0, z1, z2, w0, w1, w2, x_o, r_o):
-    total = got[0]
-    for item in range(1, got.shape[0]):
-        total = total + got[item]
-    vz = [[total[3 * i + j : 3 * i + j + 1] for j in range(3)] for i in range(3)]
-    zw = [[None] * 3 for _ in range(3)]
-    for i in range(3):
-        for j in range(2):
-            zw[i][j] = vz[j + 1][i] + SHIFT * vz[j][i]
-        zw[i][2] = total[9 + i : 10 + i]
+    total = summed(got)
+    v0z0, v0z1, v1z0, v1z1, v2z1, v0z2, v1z2, v2z2, z2w2 = [
+        total[:, i * LANES : (i + 1) * LANES] for i in range(9)
+    ]
+    z1w0 = v1z1 + SHIFT * v0z1
+    z2w0 = v1z2 + SHIFT * v0z2
+    z2w1 = v2z2 + SHIFT * v1z2
+    zw = [
+        [v1z0 + SHIFT * v0z0, z1w0, z2w0],
+        [z1w0, v2z1 + SHIFT * v1z1, z2w1],
+        [z2w0, z2w1, z2w2],
+    ]
+    vz = [[v0z0, v0z1, v0z2], [v1z0, v1z1, v1z2], [z1w0 - SHIFT * v1z0, v2z1, v2z2]]
 
     def form(left, table, right):
         value = None
@@ -381,18 +502,24 @@
     hots = one_hot_faces(order[...])
     x = col[0] * z0[...] + col[1] * z1[...] + col[2] * z2[...]
     r = r0[...] + col[3] * w0[...] + col[4] * w1[...] + col[5] * w2[...]
-    x_o[...] = to_points(x, hots)
-    r_o[...] = to_points(r, hots)
-
-
-def call(body, outs, place, *args, scratch=(), flops=1_000_000):
-    specs = [pl.BlockSpec(memory_space=pltpu.VMEM) for _ in args]
+    both = to_points(jnp.concatenate([x, r], axis=0), hots)
+    rhs = x.shape[0]
+    x_o[...] = both[:rhs]
+    r_o[...] = both[rhs:]
+
+
+def call(body, outs, place, *args, scratch=(), raw=(), flops=1_000_000):
+    space = [pl.ANY if n in raw else pltpu.VMEM for n in range(len(args))]
+    specs = [pl.BlockSpec(memory_space=kind) for kind in space]
     if place is not None:
         specs = [pl.BlockSpec(memory_space=pltpu.SMEM)] + specs
         args = (place,) + args
     return pl.pallas_call(
         body,
-        out_shape=[jax.ShapeDtypeStruct(shape, F32) for shape in outs],
+        out_shape=[
+            out if isinstance(out, jax.ShapeDtypeStruct) else jax.ShapeDtypeStruct(out, F32)
+            for out in outs
+        ],
         in_specs=specs,
         out_specs=[pl.BlockSpec(memory_space=pltpu.VMEM) for _ in outs],
         scratch_shapes=list(scratch),
@@ -406,12 +533,11 @@
     link = [(i, i + 1 if i % 2 else i - 1) for i in range(1, rows - 1)]
     near = [(i, i ^ 1) for i in range(columns)]
     far = [(i, (i + 1 if i % 2 else i - 1) % columns) for i in range(columns)]
-    return [
-        lax.ppermute(sends[0], "axial", core),
-        lax.ppermute(sends[1], "axial", link),
-        lax.ppermute(sends[2], "circ", near),
-        lax.ppermute(sends[3], "circ", far),
-    ]
+    got3 = lax.ppermute(sends[3], "circ", far)
+    got2 = lax.ppermute(sends[2], "circ", near)
+    got1 = lax.ppermute(sends[1], "axial", link)
+    got0 = lax.ppermute(sends[0], "axial", core)
+    return [got0, got1, got2, got3]
 
 
 def spread(value, axis):
@@ -427,21 +553,29 @@
     place = jnp.stack(
         [lax.axis_index("axial"), jnp.int32(rows), lax.axis_index("circ")]
     ).astype(jnp.int32)
-    order = face_order[0]
-    blocks = interior_inverse[0, 0]
     swap = functools.partial(exchange, rows=rows, columns=columns)
+    dma = pltpu.SemaphoreType.DMA
 
     def face(n):
         return [(n, LANES)] * 4
 
-    shared, *sends = call(
-        k_prepare, [(rhs + 8, points)] + face(rhs + 8), place, load_terms[0, 0], diffusivity[0], order
+    def bf16(*shape):
+        return jax.ShapeDtypeStruct((PIECES,) + shape, BF16)
+
+    shared, order, *sends = call(
+        k_prepare,
+        [(rhs + 8, points), jax.ShapeDtypeStruct((1, points), jnp.int32)] + face(rhs + 8),
+        place, load_terms[0, 0], diffusivity[0], face_order[0],
+        raw=(0, 1, 2),
+        scratch=[pltpu.VMEM((rhs, points), F32), pltpu.VMEM((1, points), F32), dma((3,))],
     )
     got = swap(sends)
-    diag, couple, neumann, avg = call(
-        k_matrices,
-        [(1, points), (points, points), (points, points), (8, points)],
-        None, order, interface_diag[0], coupling[0, 0], neumann_solve[0, 0], primal_lists[0, 0],
+    neumann, avg = call(
+        k_neumann,
+        [bf16(points, points), (8, points)],
+        None, order, neumann_solve[0, 0], primal_lists[0, 0],
+        raw=(1,),
+        scratch=[pltpu.VMEM((points, points), F32), dma((4,))],
         flops=2_000_000_000,
     )
     r0, share, prim0, t0, *sends = call(
@@ -450,6 +584,15 @@
         place, shared, *got, neumann, avg,
     )
     got = swap(sends)
+    inner = interior_inverse.shape[2:]
+    diag, couple, blocks = call(
+        k_couple,
+        [(1, points), bf16(points, points), bf16(*inner)],
+        None, order, interface_diag[0], share, coupling[0, 0], interior_inverse[0, 0],
+        raw=(3, 4),
+        scratch=[pltpu.VMEM((points, points), F32), pltpu.VMEM(inner, F32), dma((5,))],
+        flops=2_000_000_000,
+    )
     n = rhs + 24
     z0, q0, *sends = call(
         functools.partial(k_schur, rhs=rhs), [(n, points)] * 2 + face(n),
@@ -476,13 +619,14 @@
     )
     coefs = jnp.pad(coefs, ((24, 0), (112, LANES - 112 - coefs.shape[1])))
     got = spread(jnp.broadcast_to(pay[None], (columns, 32, LANES)), "circ")
-    (pay,) = call(k_sum_spread, [(rows, 32, LANES)], None, got, coefs)
-    got = spread(pay, "axial")
+    (pay,) = call(k_sum_halves, [(rows, 16, LANES)], None, got, coefs)
+    mine = spread(pay, "axial")
+    other = lax.ppermute(mine, "axial", [(i, i ^ 1) for i in range(rows)])
     width = max(LANES, 8 * rows)
     vv2, t2, c0, c1, c2, *sends = call(
         k_coarse,
         [(rhs, points)] * 2 + [(72, rhs), (40, rhs), (24, rhs)] + face(rhs),
-        place, got, v2, v1, share, neumann,
+        place, mine, other, v2, v1, share, neumann,
         scratch=[pltpu.VMEM((width, width), F32)] * 3 + [pltpu.VMEM((width + 64, rhs), F32)] * 3,
     )
     got = swap(sends)
@@ -495,11 +639,10 @@
     )
     got = swap(sends)
     w2f, pay = call(
-        k_dots, [(rhs, points), (16, rhs)],
-        place, q2, *got, r0, w0f, vv2, z0f, z1f, z2f, dots,
-    )
-    got = spread(jnp.broadcast_to(pay[None], (columns, 16, rhs)), "circ")
-    (pay,) = call(k_sum_spread, [(rows, 16, rhs)], None, got, jnp.zeros((16, rhs), F32))
+        k_dots, [(rhs, points), (1, 9 * LANES)], place, q2, *got, r0, w0f, vv2, z2f, dots
+    )
+    got = spread(jnp.broadcast_to(pay[None], (columns,) + pay.shape), "circ")
+    (pay,) = call(k_sum_spread, [(rows,) + pay.shape], None, got)
     got = spread(pay, "axial")
     x, r = call(
         k_final, [(rhs, points)] * 2, None, got, order, r0, z0f, z1f, z2f, w0f, w1f, w2f

time: 250 us -> 229 us (0.916)
  blocking collectives: 88.5 us -> 70.7 us
  Pallas kernels: 30.2 us -> 23.1 us
  waiting for transfers between devices: 27.3 us -> 33.9 us
    all_to_all x3, blocking collectives: 88.5 us -> 70.7 us  [spread(): return lax.all_to_all(value, axis, split_axis=0, concat_axis=0, tiled=True)]
    pallas_call x14 -> x15, Pallas kernels: 30.2 us -> 23.1 us  [call(): pl.pallas_call(body, out_shape=[out if isinstance(out, jax.ShapeDtypeStru...]
    ppermute x28 -> x29, waiting for transfers between devices: 21.1 us -> 27.6 us  [the longest x7 26.4 us: exchange(): got3 = lax.ppermute(sends[3], 'circ', far)]
    ppermute x28 -> x29, starting transfers between devices: 88.4 us -> 86.9 us  [the longest x7 24.7 us: exchange(): got1 = lax.ppermute(sends[1], 'axial', link)]
  transfers between devices with their start and end apart: 29 -> 30, of which waited for: 7 -> 9; matrix products, arithmetic and copies ran while one was open for 0% -> 0% of each run, Pallas kernels for 3% -> 3%
where the time goes in v2:
time: 229 us; the launch traced here: 228 us
  starting transfers between devices  91.2 us (40%)
  blocking collectives  70.7 us (31%)
  waiting for transfers between devices  33.9 us (15%)
  Pallas kernels  23.1 us (10%)
  local copies, waits for them, and re-layouts  7.36 us (3%)
    all_to_all x3, blocking collectives, spread(): return lax.all_to_all(value, axis, split_axis=0, concat_axis=0, tiled=True)  70.7 us
    ppermute x7, waiting for transfers between devices, exchange(): got3 = lax.ppermute(sends[3], 'circ', far)  26.4 us
    ppermute x7, starting transfers between devices, exchange(): got1 = lax.ppermute(sends[1], 'axial', link)  24.7 us
    ppermute x7, starting transfers between devices, exchange(): got3 = lax.ppermute(sends[3], 'circ', far)  24.6 us
    pallas_call x15, Pallas kernels, call(): pl.pallas_call(body, out_shape=[out if isinstance(out, jax.ShapeDtypeStru...  23.1 us
    ppermute x7, starting transfers between devices, exchange(): got0 = lax.ppermute(sends[0], 'axial', core)  21 us
    ppermute x7, starting transfers between devices, exchange(): got2 = lax.ppermute(sends[2], 'circ', near)  13.7 us
    unnamed x30, local copies, waits for them, and re-layouts  6.33 us
  transfers between devices with their start and end apart: 30, of which 9 were waited for; matrix products, arithmetic and copies ran while one was open for 0% of the time, Pallas kernels for 3%

profile of v2, /device:TPU:1, one launch (start us, length us, event | category | flops | bytes accessed | tf_op | source)
XLA Modules:
  0.0 227.7 jit_solution(733003517396037420)
XLA Ops:
  3.4 8.8 %collective-permute-start = (f32[136,128]{1,0:T(8,128)S(1)}, f32[136,128]{1,0:T(8,128)S(1)}, u32[]{:S(2)}, u32[]{:S(2)}) collective-permute-start(f32[136,128]{1,0:T(8,128)S(1)} %get-tuple-element.67), channel_id=1, source_target_pairs={{0,16},{16,0},{32,48},{48,32},{64,80},{80,64},{96,112},{112,96},{1... | collective-permute-start | bytes 208904 | tf_op jit(solution)/shard_map/ppermute | solution.py:539
  12.2 1.9 collective-permute-start.1
  14.1 1.9 collective-permute-start.2
  16.0 3.5 %collective-permute-start.3 = (f32[136,128]{1,0:T(8,128)S(1)}, f32[136,128]{1,0:T(8,128)S(1)}, u32[]{:S(2)}, u32[]{:S(2)}) collective-permute-start(f32[136,128]{1,0:T(8,128)S(1)} %get-tuple-element.70), channel_id=1, source_target_pairs={{0,15},{1,2},{2,1},{3,4},{4,3},{5,6},{6,5},{7,8},{8,7},{9,10},{10,... | collective-permute-start | bytes 208904 | tf_op jit(solution)/shard_map/ppermute | solution.py:536
  20.8 2.5 %shard_map.123 = (bf16[2,512,512]{2,1,0:T(8,128)(2,1)S(1)}, f32[8,512]{1,0:T(8,128)S(1)}) custom-call(s32[1,512]{1,0:T(1,128)S(1)} %get-tuple-element.71.order, f32[512,512]{1,0:T(8,128)S(1)} %bitcast.19, s32[8,64]{1,0:T(8,128)S(1)} %bitcast.22), custom_call_target="tpu_custom_call" | custom-call | flops 2000000000 | bytes 1000000 | tf_op jit(solution)/shard_map/pallas_call | solution.py:517
  25.5 1.9 collective-permute-start.4
  27.5 4.8 %collective-permute-start.5 = (f32[136,128]{1,0:T(8,128)S(1)}, f32[136,128]{1,0:T(8,128)S(1)}, u32[]{:S(2)}, u32[]{:S(2)}) collective-permute-start(f32[136,128]{1,0:T(8,128)S(1)} %get-tuple-element.76), channel_id=1, source_target_pairs={{16,32},{32,16},{48,64},{64,48},{80,96},{96,80},{112,128},{128,112... | collective-permute-start | bytes 208904 | tf_op jit(solution)/shard_map/ppermute | solution.py:538
  32.3 1.9 collective-permute-start.6
  34.2 3.2 %collective-permute-start.7 = (f32[136,128]{1,0:T(8,128)S(1)}, f32[136,128]{1,0:T(8,128)S(1)}, u32[]{:S(2)}, u32[]{:S(2)}) collective-permute-start(f32[136,128]{1,0:T(8,128)S(1)} %get-tuple-element.78), channel_id=1, source_target_pairs={{0,15},{1,2},{2,1},{3,4},{4,3},{5,6},{6,5},{7,8},{8,7},{9,10},{10,... | collective-permute-start | bytes 208904 | tf_op jit(solution)/shard_map/ppermute | solution.py:536
  39.3 3.2 %collective-permute-done.7.g3 = f32[136,128]{1,0:T(8,128)S(1)} collective-permute-done((f32[136,128]{1,0:T(8,128)S(1)}, f32[136,128]{1,0:T(8,128)S(1)}, u32[]{:S(2)}, u32[]{:S(2)}) %collective-permute-start.7) | collective-permute-done | bytes 69664 | tf_op jit(solution)/shard_map/ppermute | solution.py:536
  42.6 1.6 shard_map.126
  44.9 1.9 collective-permute-start.8
  46.8 3.3 %collective-permute-start.9 = (f32[152,128]{1,0:T(8,128)S(1)}, f32[152,128]{1,0:T(8,128)S(1)}, u32[]{:S(2)}, u32[]{:S(2)}) collective-permute-start(f32[152,128]{1,0:T(8,128)S(1)} %get-tuple-element.85), channel_id=1, source_target_pairs={{16,32},{32,16},{48,64},{64,48},{80,96},{96,80},{112,128},{128,112... | collective-permute-start | bytes 233480 | tf_op jit(solution)/shard_map/ppermute | solution.py:538
  50.1 1.9 collective-permute-start.10
  52.1 3.4 %collective-permute-start.11 = (f32[152,128]{1,0:T(8,128)S(1)}, f32[152,128]{1,0:T(8,128)S(1)}, u32[]{:S(2)}, u32[]{:S(2)}) collective-permute-start(f32[152,128]{1,0:T(8,128)S(1)} %get-tuple-element.87), channel_id=1, source_target_pairs={{0,15},{1,2},{2,1},{3,4},{4,3},{5,6},{6,5},{7,8},{8,7},{9,10},{10,... | collective-permute-start | bytes 233480 | tf_op jit(solution)/shard_map/ppermute | solution.py:536
  55.5 5.0 %collective-permute-done.11.g3 = f32[152,128]{1,0:T(8,128)S(1)} collective-permute-done((f32[152,128]{1,0:T(8,128)S(1)}, f32[152,128]{1,0:T(8,128)S(1)}, u32[]{:S(2)}, u32[]{:S(2)}) %collective-permute-start.11) | collective-permute-done | bytes 77856 | tf_op jit(solution)/shard_map/ppermute | solution.py:536
  60.5 1.3 shard_map.127
  61.8 1.9 collective-permute-start.12
  63.7 4.6 %collective-permute-start.13 = (f32[168,128]{1,0:T(8,128)S(1)}, f32[168,128]{1,0:T(8,128)S(1)}, u32[]{:S(2)}, u32[]{:S(2)}) collective-permute-start(f32[168,128]{1,0:T(8,128)S(1)} %get-tuple-element.91), channel_id=1, source_target_pairs={{16,32},{32,16},{48,64},{64,48},{80,96},{96,80},{112,128},{128,112... | collective-permute-start | bytes 258056 | tf_op jit(solution)/shard_map/ppermute | solution.py:538
  68.3 1.9 collective-permute-start.14
  70.2 3.8 %collective-permute-start.15 = (f32[168,128]{1,0:T(8,128)S(1)}, f32[168,128]{1,0:T(8,128)S(1)}, u32[]{:S(2)}, u32[]{:S(2)}) collective-permute-start(f32[168,128]{1,0:T(8,128)S(1)} %get-tuple-element.93), channel_id=1, source_target_pairs={{0,15},{1,2},{2,1},{3,4},{4,3},{5,6},{6,5},{7,8},{8,7},{9,10},{10,... | collective-permute-start | bytes 258056 | tf_op jit(solution)/shard_map/ppermute | solution.py:536
  74.1 4.7 %collective-permute-done.15.g3 = f32[168,128]{1,0:T(8,128)S(1)} collective-permute-done((f32[168,128]{1,0:T(8,128)S(1)}, f32[168,128]{1,0:T(8,128)S(1)}, u32[]{:S(2)}, u32[]{:S(2)}) %collective-permute-start.15) | collective-permute-done | bytes 86048 | tf_op jit(solution)/shard_map/ppermute | solution.py:536
  78.8 1.7 shard_map.128
  81.2 1.9 collective-permute-start.16
  83.1 3.8 %collective-permute-start.17 = (f32[184,128]{1,0:T(8,128)S(1)}, f32[184,128]{1,0:T(8,128)S(1)}, u32[]{:S(2)}, u32[]{:S(2)}) collective-permute-start(f32[184,128]{1,0:T(8,128)S(1)} %get-tuple-element.96), channel_id=1, source_target_pairs={{16,32},{32,16},{48,64},{64,48},{80,96},{96,80},{112,128},{128,112... | collective-permute-start | bytes 282632 | tf_op jit(solution)/shard_map/ppermute | solution.py:538
  87.0 1.9 collective-permute-start.18
  88.9 4.1 %collective-permute-start.19 = (f32[184,128]{1,0:T(8,128)S(1)}, f32[184,128]{1,0:T(8,128)S(1)}, u32[]{:S(2)}, u32[]{:S(2)}) collective-permute-start(f32[184,128]{1,0:T(8,128)S(1)} %get-tuple-element.98), channel_id=1, source_target_pairs={{0,15},{1,2},{2,1},{3,4},{4,3},{5,6},{6,5},{7,8},{8,7},{9,10},{10,... | collective-permute-start | bytes 282632 | tf_op jit(solution)/shard_map/ppermute | solution.py:536
  93.0 4.5 %collective-permute-done.19.g3 = f32[184,128]{1,0:T(8,128)S(1)} collective-permute-done((f32[184,128]{1,0:T(8,128)S(1)}, f32[184,128]{1,0:T(8,128)S(1)}, u32[]{:S(2)}, u32[]{:S(2)}) %collective-permute-start.19) | collective-permute-done | bytes 94240 | tf_op jit(solution)/shard_map/ppermute | solution.py:536
  99.3 4.3 %all-to-all-start = ((f32[16,32,128]{2,1,0:T(8,128)}), f32[16,32,128]{2,1,0:T(8,128)}, u32[]{:S(2)}, u32[]{:S(2)}) async-start(f32[16,32,128]{2,1,0:T(8,128)} %broadcast_in_dim.20), calls=%async_computation | async-start | bytes 524288 | tf_op jit(solution)/shard_map/all_to_all | solution.py:544
  105.3 6.3 %all-to-all-done.got = f32[16,32,128]{2,1,0:T(8,128)} async-done(((f32[16,32,128]{2,1,0:T(8,128)}), f32[16,32,128]{2,1,0:T(8,128)}, u32[]{:S(2)}, u32[]{:S(2)}) %all-to-all-start) | async-done | bytes 262176 | tf_op jit(solution)/shard_map/all_to_all | solution.py:544
  112.6 38.7 %all_to_all.20.mine = f32[32,16,128]{2,1,0:T(8,128)S(1)} all-to-all(f32[32,16,128]{2,1,0:T(8,128)S(1)} %shard_map.130), channel_id=1, replica_groups=mesh['axial'=32,'circ'=16] {'axial'}, dimensions={0} | all-to-all | bytes 524288 | tf_op jit(solution)/shard_map/all_to_all | solution.py:544
  151.3 2.9 %collective-permute-start.20 = (f32[32,16,128]{2,1,0:T(8,128)S(1)}, f32[32,16,128]{2,1,0:T(8,128)S(1)}, u32[]{:S(2)}, u32[]{:S(2)}) collective-permute-start(f32[32,16,128]{2,1,0:T(8,128)S(1)} %all_to_all.20.mine), channel_id=1, source_target_pairs={{0,16},{16,0},{32,48},{48,32},{64,80},{80,64},{96,112},{112,96},{1... | collective-permute-start | bytes 786440 | tf_op jit(solution)/shard_map/ppermute | solution.py:624
  155.3 3.6 %shard_map.131 = (f32[128,512]{1,0:T(8,128)S(1)}, f32[128,512]{1,0:T(8,128)S(1)}, f32[72,128]{1,0:T(8,128)S(1)}, f32[40,128]{1,0:T(8,128)S(1)}, f32[24,128]{1,0:...) custom-call(s32[3]{0:T(128)S(1)} %pad_add_fusion.place, ...), custom_call_target="tpu_custom_call" | custom-call | flops 1000000 | bytes 1000000 | tf_op jit(solution)/shard_map/pallas_call | solution.py:517
  159.0 2.3 %collective-permute-start.21 = (f32[128,128]{1,0:T(8,128)S(1)}, f32[128,128]{1,0:T(8,128)S(1)}, u32[]{:S(2)}, u32[]{:S(2)}) collective-permute-start(f32[128,128]{1,0:T(8,128)S(1)} %get-tuple-element.105), channel_id=1, source_target_pairs={{0,16},{16,0},{32,48},{48,32},{64,80},{80,64},{96,112},{112,96},{1... | collective-permute-start | bytes 196616 | tf_op jit(solution)/shard_map/ppermute | solution.py:539
  161.2 1.9 collective-permute-start.22
  163.2 2.2 collective-permute-start.23
  165.4 3.2 %collective-permute-start.24 = (f32[128,128]{1,0:T(8,128)S(1)}, f32[128,128]{1,0:T(8,128)S(1)}, u32[]{:S(2)}, u32[]{:S(2)}) collective-permute-start(f32[128,128]{1,0:T(8,128)S(1)} %get-tuple-element.108), channel_id=1, source_target_pairs={{0,15},{1,2},{2,1},{3,4},{4,3},{5,6},{6,5},{7,8},{8,7},{9,10},{10,... | collective-permute-start | bytes 196616 | tf_op jit(solution)/shard_map/ppermute | solution.py:536
  168.6 5.4 %collective-permute-done.24.g3 = f32[128,128]{1,0:T(8,128)S(1)} collective-permute-done((f32[128,128]{1,0:T(8,128)S(1)}, f32[128,128]{1,0:T(8,128)S(1)}, u32[]{:S(2)}, u32[]{:S(2)}) %collective-permute-start.24) | collective-permute-done | bytes 65568 | tf_op jit(solution)/shard_map/ppermute | solution.py:536
  174.0 1.8 shard_map.132
  175.8 2.3 %collective-permute-start.25 = (f32[128,128]{1,0:T(8,128)S(1)}, f32[128,128]{1,0:T(8,128)S(1)}, u32[]{:S(2)}, u32[]{:S(2)}) collective-permute-start(f32[128,128]{1,0:T(8,128)S(1)} %get-tuple-element.112), channel_id=1, source_target_pairs={{0,16},{16,0},{32,48},{48,32},{64,80},{80,64},{96,112},{112,96},{1... | collective-permute-start | bytes 196616 | tf_op jit(solution)/shard_map/ppermute | solution.py:539
  178.1 4.4 %collective-permute-start.26 = (f32[128,128]{1,0:T(8,128)S(1)}, f32[128,128]{1,0:T(8,128)S(1)}, u32[]{:S(2)}, u32[]{:S(2)}) collective-permute-start(f32[128,128]{1,0:T(8,128)S(1)} %get-tuple-element.113), channel_id=1, source_target_pairs={{16,32},{32,16},{48,64},{64,48},{80,96},{96,80},{112,128},{128,112... | collective-permute-start | bytes 196616 | tf_op jit(solution)/shard_map/ppermute | solution.py:538
  182.5 1.9 collective-permute-start.27
  184.5 3.3 %collective-permute-start.28 = (f32[128,128]{1,0:T(8,128)S(1)}, f32[128,128]{1,0:T(8,128)S(1)}, u32[]{:S(2)}, u32[]{:S(2)}) collective-permute-start(f32[128,128]{1,0:T(8,128)S(1)} %get-tuple-element.115), channel_id=1, source_target_pairs={{0,15},{1,2},{2,1},{3,4},{4,3},{5,6},{6,5},{7,8},{8,7},{9,10},{10,... | collective-permute-start | bytes 196616 | tf_op jit(solution)/shard_map/ppermute | solution.py:536
  187.8 2.4 %shard_map.133 = (f32[128,512]{1,0:T(8,128)S(1)}, f32[128,512]{1,0:T(8,128)S(1)}, f32[128,512]{1,0:T(8,128)S(1)}, f32[128,512]{1,0:T(8,128)S(1)}, f32[16,128]{1,0:T(8,128)S(1)}) custom-call(f32[128,512]{1,0:T(8,128)S(1)} %get-tuple-element.88.r.r0, f32[152,512]{1,0:T(8,128)S(1)} %copy-done.1, f32[168,512]{1,0:T(8,128)S(1)} %get-tuple-element.99.v.v1, ...), custom_call_target="tpu_custom_call" | custom-call | flops 1000000 | bytes 1000000 | tf_op jit(solution)/shard_map/pallas_call | solution.py:517
  190.3 2.5 %collective-permute-done.28.g3 = f32[128,128]{1,0:T(8,128)S(1)} collective-permute-done((f32[128,128]{1,0:T(8,128)S(1)}, f32[128,128]{1,0:T(8,128)S(1)}, u32[]{:S(2)}, u32[]{:S(2)}) %collective-permute-start.28) | collective-permute-done | bytes 65568 | tf_op jit(solution)/shard_map/ppermute | solution.py:536
  194.0 9.1 %all_to_all.21.got = f32[16,1,1152]{2,1,0:T(1,128)S(1)} all-to-all(f32[16,1,1152]{2,1,0:T(1,128)S(1)} %broadcast_in_dim.22), channel_id=1, replica_groups=mesh['axial'=32,'circ'=16] {'circ'}, dimensions={0} | all-to-all | bytes 147456 | tf_op jit(solution)/shard_map/all_to_all | solution.py:544
  203.1 22.9 %all_to_all.22.got = f32[32,1,1152]{2,1,0:T(1,128)S(1)} all-to-all(f32[32,1,1152]{2,1,0:T(1,128)S(1)} %shard_map.135), channel_id=1, replica_groups=mesh['axial'=32,'circ'=16] {'axial'}, dimensions={0} | all-to-all | bytes 294912 | tf_op jit(solution)/shard_map/all_to_all | solution.py:544
  226.1 1.7 shard_map.136
  (68 shorter events, 16.4 us)
Async XLA Ops:
  0.7 0.7 copy-start.6
  0.7 0.7 copy-start.5
  1.4 0.9 copy-start.4
  3.4 19.9 %collective-permute-start = (f32[136,128]{1,0:T(8,128)S(1)}, f32[136,128]{1,0:T(8,128)S(1)}, u32[]{:S(2)}, u32[]{:S(2)}) collective-permute-start(f32[136,128]{1,0:T(8,128)S(1)} %get-tuple-element.67), channel_id=1, source_target_pairs={{0,16},{16,0},{32,48},{48,32},{64,80},{80,64},{96,112},{112,96},{1... | collective-permute-start | bytes 208904 | tf_op jit(solution)/shard_map/ppermute | solution.py:539
  12.2 11.1 %collective-permute-start.1 = (f32[136,128]{1,0:T(8,128)S(1)}, f32[136,128]{1,0:T(8,128)S(1)}, u32[]{:S(2)}, u32[]{:S(2)}) collective-permute-start(f32[136,128]{1,0:T(8,128)S(1)} %get-tuple-element.68), channel_id=1, source_target_pairs={{16,32},{32,16},{48,64},{64,48},{80,96},{96,80},{112,128},{128,112... | collective-permute-start | bytes 208904 | tf_op jit(solution)/shard_map/ppermute | solution.py:538
  14.1 5.5 %copy-start.10 = (s32[1,1,8,64]{3,2,1,0:T(8,128)S(1)}, s32[1,1,8,64]{3,2,1,0:T(8,128)}, u32[]{:S(2)}) copy-start(s32[1,1,8,64]{3,2,1,0:T(8,128)} %param.21) | copy-start | bytes 6148
  14.1 9.2 %collective-permute-start.2 = (f32[136,128]{1,0:T(8,128)S(1)}, f32[136,128]{1,0:T(8,128)S(1)}, u32[]{:S(2)}, u32[]{:S(2)}) collective-permute-start(f32[136,128]{1,0:T(8,128)S(1)} %get-tuple-element.69), channel_id=1, source_target_pairs={{0,1},{1,0},{2,3},{3,2},{4,5},{5,4},{6,7},{7,6},{8,9},{9,8},{10,11... | collective-permute-start | bytes 208904 | tf_op jit(solution)/shard_map/ppermute | solution.py:537
  16.0 8.4 %collective-permute-start.3 = (f32[136,128]{1,0:T(8,128)S(1)}, f32[136,128]{1,0:T(8,128)S(1)}, u32[]{:S(2)}, u32[]{:S(2)}) collective-permute-start(f32[136,128]{1,0:T(8,128)S(1)} %get-tuple-element.70), channel_id=1, source_target_pairs={{0,15},{1,2},{2,1},{3,4},{4,3},{5,6},{6,5},{7,8},{8,7},{9,10},{10,... | collective-permute-start | bytes 208904 | tf_op jit(solution)/shard_map/ppermute | solution.py:536
  19.6 1.2 copy-start.7
  23.3 14.1 %copy-start.8 = (f32[1,1,512,512]{3,2,1,0:T(8,128)S(1)}, f32[1,1,512,512]{3,2,1,0:T(8,128)}, u32[]{:S(2)}) copy-start(f32[1,1,512,512]{3,2,1,0:T(8,128)} %param.14) | copy-start | bytes 3145732
  24.4 13.0 %copy-start.9 = (f32[1,1,4,128,128]{4,3,2,1,0:T(8,128)S(1)}, f32[1,1,4,128,128]{4,3,2,1,0:T(8,128)}, u32[]{:S(2)}) copy-start(f32[1,1,4,128,128]{4,3,2,1,0:T(8,128)} %param.15) | copy-start | bytes 786436
  25.5 13.8 %collective-permute-start.4 = (f32[136,128]{1,0:T(8,128)S(1)}, f32[136,128]{1,0:T(8,128)S(1)}, u32[]{:S(2)}, u32[]{:S(2)}) collective-permute-start(f32[136,128]{1,0:T(8,128)S(1)} %get-tuple-element.75), channel_id=1, source_target_pairs={{0,16},{16,0},{32,48},{48,32},{64,80},{80,64},{96,112},{112,96},{1... | collective-permute-start | bytes 208904 | tf_op jit(solution)/shard_map/ppermute | solution.py:539
  27.5 11.8 %collective-permute-start.5 = (f32[136,128]{1,0:T(8,128)S(1)}, f32[136,128]{1,0:T(8,128)S(1)}, u32[]{:S(2)}, u32[]{:S(2)}) collective-permute-start(f32[136,128]{1,0:T(8,128)S(1)} %get-tuple-element.76), channel_id=1, source_target_pairs={{16,32},{32,16},{48,64},{64,48},{80,96},{96,80},{112,128},{128,112... | collective-permute-start | bytes 208904 | tf_op jit(solution)/shard_map/ppermute | solution.py:538
  32.3 7.1 %collective-permute-start.6 = (f32[136,128]{1,0:T(8,128)S(1)}, f32[136,128]{1,0:T(8,128)S(1)}, u32[]{:S(2)}, u32[]{:S(2)}) collective-permute-start(f32[136,128]{1,0:T(8,128)S(1)} %get-tuple-element.77), channel_id=1, source_target_pairs={{0,1},{1,0},{2,3},{3,2},{4,5},{5,4},{6,7},{7,6},{8,9},{9,8},{10,11... | collective-permute-start | bytes 208904 | tf_op jit(solution)/shard_map/ppermute | solution.py:537
  34.2 8.4 %collective-permute-start.7 = (f32[136,128]{1,0:T(8,128)S(1)}, f32[136,128]{1,0:T(8,128)S(1)}, u32[]{:S(2)}, u32[]{:S(2)}) collective-permute-start(f32[136,128]{1,0:T(8,128)S(1)} %get-tuple-element.78), channel_id=1, source_target_pairs={{0,15},{1,2},{2,1},{3,4},{4,3},{5,6},{6,5},{7,8},{8,7},{9,10},{10,... | collective-permute-start | bytes 208904 | tf_op jit(solution)/shard_map/ppermute | solution.py:536
  37.3 0.7 copy-start.11
  44.1 0.7 copy-start
  44.9 10.6 %collective-permute-start.8 = (f32[152,128]{1,0:T(8,128)S(1)}, f32[152,128]{1,0:T(8,128)S(1)}, u32[]{:S(2)}, u32[]{:S(2)}) collective-permute-start(f32[152,128]{1,0:T(8,128)S(1)} %get-tuple-element.84), channel_id=1, source_target_pairs={{0,16},{16,0},{32,48},{48,32},{64,80},{80,64},{96,112},{112,96},{1... | collective-permute-start | bytes 233480 | tf_op jit(solution)/shard_map/ppermute | solution.py:539
  46.8 8.7 %collective-permute-start.9 = (f32[152,128]{1,0:T(8,128)S(1)}, f32[152,128]{1,0:T(8,128)S(1)}, u32[]{:S(2)}, u32[]{:S(2)}) collective-permute-start(f32[152,128]{1,0:T(8,128)S(1)} %get-tuple-element.85), channel_id=1, source_target_pairs={{16,32},{32,16},{48,64},{64,48},{80,96},{96,80},{112,128},{128,112... | collective-permute-start | bytes 233480 | tf_op jit(solution)/shard_map/ppermute | solution.py:538
  50.1 5.4 %collective-permute-start.10 = (f32[152,128]{1,0:T(8,128)S(1)}, f32[152,128]{1,0:T(8,128)S(1)}, u32[]{:S(2)}, u32[]{:S(2)}) collective-permute-start(f32[152,128]{1,0:T(8,128)S(1)} %get-tuple-element.86), channel_id=1, source_target_pairs={{0,1},{1,0},{2,3},{3,2},{4,5},{5,4},{6,7},{7,6},{8,9},{9,8},{10,11... | collective-permute-start | bytes 233480 | tf_op jit(solution)/shard_map/ppermute | solution.py:537
  52.1 8.5 %collective-permute-start.11 = (f32[152,128]{1,0:T(8,128)S(1)}, f32[152,128]{1,0:T(8,128)S(1)}, u32[]{:S(2)}, u32[]{:S(2)}) collective-permute-start(f32[152,128]{1,0:T(8,128)S(1)} %get-tuple-element.87), channel_id=1, source_target_pairs={{0,15},{1,2},{2,1},{3,4},{4,3},{5,6},{6,5},{7,8},{8,7},{9,10},{10,... | collective-permute-start | bytes 233480 | tf_op jit(solution)/shard_map/ppermute | solution.py:536
  61.8 12.3 %collective-permute-start.12 = (f32[168,128]{1,0:T(8,128)S(1)}, f32[168,128]{1,0:T(8,128)S(1)}, u32[]{:S(2)}, u32[]{:S(2)}) collective-permute-start(f32[168,128]{1,0:T(8,128)S(1)} %get-tuple-element.90), channel_id=1, source_target_pairs={{0,16},{16,0},{32,48},{48,32},{64,80},{80,64},{96,112},{112,96},{1... | collective-permute-start | bytes 258056 | tf_op jit(solution)/shard_map/ppermute | solution.py:539
  63.7 10.3 %collective-permute-start.13 = (f32[168,128]{1,0:T(8,128)S(1)}, f32[168,128]{1,0:T(8,128)S(1)}, u32[]{:S(2)}, u32[]{:S(2)}) collective-permute-start(f32[168,128]{1,0:T(8,128)S(1)} %get-tuple-element.91), channel_id=1, source_target_pairs={{16,32},{32,16},{48,64},{64,48},{80,96},{96,80},{112,128},{128,112... | collective-permute-start | bytes 258056 | tf_op jit(solution)/shard_map/ppermute | solution.py:538
  68.3 5.8 %collective-permute-start.14 = (f32[168,128]{1,0:T(8,128)S(1)}, f32[168,128]{1,0:T(8,128)S(1)}, u32[]{:S(2)}, u32[]{:S(2)}) collective-permute-start(f32[168,128]{1,0:T(8,128)S(1)} %get-tuple-element.92), channel_id=1, source_target_pairs={{0,1},{1,0},{2,3},{3,2},{4,5},{5,4},{6,7},{7,6},{8,9},{9,8},{10,11... | collective-permute-start | bytes 258056 | tf_op jit(solution)/shard_map/ppermute | solution.py:537
  70.2 8.5 %collective-permute-start.15 = (f32[168,128]{1,0:T(8,128)S(1)}, f32[168,128]{1,0:T(8,128)S(1)}, u32[]{:S(2)}, u32[]{:S(2)}) collective-permute-start(f32[168,128]{1,0:T(8,128)S(1)} %get-tuple-element.93), channel_id=1, source_target_pairs={{0,15},{1,2},{2,1},{3,4},{4,3},{5,6},{6,5},{7,8},{8,7},{9,10},{10,... | collective-permute-start | bytes 258056 | tf_op jit(solution)/shard_map/ppermute | solution.py:536
  80.5 0.8 copy-start.2
  81.2 11.8 %collective-permute-start.16 = (f32[184,128]{1,0:T(8,128)S(1)}, f32[184,128]{1,0:T(8,128)S(1)}, u32[]{:S(2)}, u32[]{:S(2)}) collective-permute-start(f32[184,128]{1,0:T(8,128)S(1)} %get-tuple-element.95), channel_id=1, source_target_pairs={{0,16},{16,0},{32,48},{48,32},{64,80},{80,64},{96,112},{112,96},{1... | collective-permute-start | bytes 282632 | tf_op jit(solution)/shard_map/ppermute | solution.py:539
  83.1 9.9 %collective-permute-start.17 = (f32[184,128]{1,0:T(8,128)S(1)}, f32[184,128]{1,0:T(8,128)S(1)}, u32[]{:S(2)}, u32[]{:S(2)}) collective-permute-start(f32[184,128]{1,0:T(8,128)S(1)} %get-tuple-element.96), channel_id=1, source_target_pairs={{16,32},{32,16},{48,64},{64,48},{80,96},{96,80},{112,128},{128,112... | collective-permute-start | bytes 282632 | tf_op jit(solution)/shard_map/ppermute | solution.py:538
  87.0 6.1 %collective-permute-start.18 = (f32[184,128]{1,0:T(8,128)S(1)}, f32[184,128]{1,0:T(8,128)S(1)}, u32[]{:S(2)}, u32[]{:S(2)}) collective-permute-start(f32[184,128]{1,0:T(8,128)S(1)} %get-tuple-element.97), channel_id=1, source_target_pairs={{0,1},{1,0},{2,3},{3,2},{4,5},{5,4},{6,7},{7,6},{8,9},{9,8},{10,11... | collective-permute-start | bytes 282632 | tf_op jit(solution)/shard_map/ppermute | solution.py:537
  88.9 8.6 %collective-permute-start.19 = (f32[184,128]{1,0:T(8,128)S(1)}, f32[184,128]{1,0:T(8,128)S(1)}, u32[]{:S(2)}, u32[]{:S(2)}) collective-permute-start(f32[184,128]{1,0:T(8,128)S(1)} %get-tuple-element.98), channel_id=1, source_target_pairs={{0,15},{1,2},{2,1},{3,4},{4,3},{5,6},{6,5},{7,8},{8,7},{9,10},{10,... | collective-permute-start | bytes 282632 | tf_op jit(solution)/shard_map/ppermute | solution.py:536
  99.3 4.3 %copy-start.12 = (f32[1,8,8]{2,1,0:T(8,128)S(1)}, f32[1,8,8]{2,1,0:T(8,128)}, u32[]{:S(2)}) copy-start(f32[1,8,8]{2,1,0:T(8,128)} %param.17) | copy-start | bytes 772
  99.3 12.3 %all-to-all-start = ((f32[16,32,128]{2,1,0:T(8,128)}), f32[16,32,128]{2,1,0:T(8,128)}, u32[]{:S(2)}, u32[]{:S(2)}) async-start(f32[16,32,128]{2,1,0:T(8,128)} %broadcast_in_dim.20), calls=%async_computation | async-start | bytes 524288 | tf_op jit(solution)/shard_map/all_to_all | solution.py:544
  103.7 0.7 copy-start.13
  104.5 0.7 copy-start.14
  151.3 4.0 %collective-permute-start.20 = (f32[32,16,128]{2,1,0:T(8,128)S(1)}, f32[32,16,128]{2,1,0:T(8,128)S(1)}, u32[]{:S(2)}, u32[]{:S(2)}) collective-permute-start(f32[32,16,128]{2,1,0:T(8,128)S(1)} %all_to_all.20.mine), channel_id=1, source_target_pairs={{0,16},{16,0},{32,48},{48,32},{64,80},{80,64},{96,112},{112,96},{1... | collective-permute-start | bytes 786440 | tf_op jit(solution)/shard_map/ppermute | solution.py:624
  155.3 18.7 %copy-start.1 = (f32[152,512]{1,0:T(8,128)S(1)}, f32[152,512]{1,0:T(8,128)}, u32[]{:S(2)}) copy-start(f32[152,512]{1,0:T(8,128)} %copy-done) | copy-start | bytes 933892
  159.0 9.6 %collective-permute-start.21 = (f32[128,128]{1,0:T(8,128)S(1)}, f32[128,128]{1,0:T(8,128)S(1)}, u32[]{:S(2)}, u32[]{:S(2)}) collective-permute-start(f32[128,128]{1,0:T(8,128)S(1)} %get-tuple-element.105), channel_id=1, source_target_pairs={{0,16},{16,0},{32,48},{48,32},{64,80},{80,64},{96,112},{112,96},{1... | collective-permute-start | bytes 196616 | tf_op jit(solution)/shard_map/ppermute | solution.py:539
  161.2 7.3 %collective-permute-start.22 = (f32[128,128]{1,0:T(8,128)S(1)}, f32[128,128]{1,0:T(8,128)S(1)}, u32[]{:S(2)}, u32[]{:S(2)}) collective-permute-start(f32[128,128]{1,0:T(8,128)S(1)} %get-tuple-element.106), channel_id=1, source_target_pairs={{16,32},{32,16},{48,64},{64,48},{80,96},{96,80},{112,128},{128,112... | collective-permute-start | bytes 196616 | tf_op jit(solution)/shard_map/ppermute | solution.py:538
  163.2 5.4 %collective-permute-start.23 = (f32[128,128]{1,0:T(8,128)S(1)}, f32[128,128]{1,0:T(8,128)S(1)}, u32[]{:S(2)}, u32[]{:S(2)}) collective-permute-start(f32[128,128]{1,0:T(8,128)S(1)} %get-tuple-element.107), channel_id=1, source_target_pairs={{0,1},{1,0},{2,3},{3,2},{4,5},{5,4},{6,7},{7,6},{8,9},{9,8},{10,11... | collective-permute-start | bytes 196616 | tf_op jit(solution)/shard_map/ppermute | solution.py:537
  165.4 8.6 %collective-permute-start.24 = (f32[128,128]{1,0:T(8,128)S(1)}, f32[128,128]{1,0:T(8,128)S(1)}, u32[]{:S(2)}, u32[]{:S(2)}) collective-permute-start(f32[128,128]{1,0:T(8,128)S(1)} %get-tuple-element.108), channel_id=1, source_target_pairs={{0,15},{1,2},{2,1},{3,4},{4,3},{5,6},{6,5},{7,8},{8,7},{9,10},{10,... | collective-permute-start | bytes 196616 | tf_op jit(solution)/shard_map/ppermute | solution.py:536
  174.0 13.8 %copy-start.3 = (f32[184,512]{1,0:T(8,128)S(1)}, f32[184,512]{1,0:T(8,128)}, u32[]{:S(2)}) copy-start(f32[184,512]{1,0:T(8,128)} %copy-done.2) | copy-start | bytes 1130500
  175.8 14.4 %collective-permute-start.25 = (f32[128,128]{1,0:T(8,128)S(1)}, f32[128,128]{1,0:T(8,128)S(1)}, u32[]{:S(2)}, u32[]{:S(2)}) collective-permute-start(f32[128,128]{1,0:T(8,128)S(1)} %get-tuple-element.112), channel_id=1, source_target_pairs={{0,16},{16,0},{32,48},{48,32},{64,80},{80,64},{96,112},{112,96},{1... | collective-permute-start | bytes 196616 | tf_op jit(solution)/shard_map/ppermute | solution.py:539
  178.1 12.1 %collective-permute-start.26 = (f32[128,128]{1,0:T(8,128)S(1)}, f32[128,128]{1,0:T(8,128)S(1)}, u32[]{:S(2)}, u32[]{:S(2)}) collective-permute-start(f32[128,128]{1,0:T(8,128)S(1)} %get-tuple-element.113), channel_id=1, source_target_pairs={{16,32},{32,16},{48,64},{64,48},{80,96},{96,80},{112,128},{128,112... | collective-permute-start | bytes 196616 | tf_op jit(solution)/shard_map/ppermute | solution.py:538
  182.5 7.7 %collective-permute-start.27 = (f32[128,128]{1,0:T(8,128)S(1)}, f32[128,128]{1,0:T(8,128)S(1)}, u32[]{:S(2)}, u32[]{:S(2)}) collective-permute-start(f32[128,128]{1,0:T(8,128)S(1)} %get-tuple-element.114), channel_id=1, source_target_pairs={{0,1},{1,0},{2,3},{3,2},{4,5},{5,4},{6,7},{7,6},{8,9},{9,8},{10,11... | collective-permute-start | bytes 196616 | tf_op jit(solution)/shard_map/ppermute | solution.py:537
  184.5 8.3 %collective-permute-start.28 = (f32[128,128]{1,0:T(8,128)S(1)}, f32[128,128]{1,0:T(8,128)S(1)}, u32[]{:S(2)}, u32[]{:S(2)}) collective-permute-start(f32[128,128]{1,0:T(8,128)S(1)} %get-tuple-element.115), channel_id=1, source_target_pairs={{0,15},{1,2},{2,1},{3,4},{4,3},{5,6},{6,5},{7,8},{8,7},{9,10},{10,... | collective-permute-start | bytes 196616 | tf_op jit(solution)/shard_map/ppermute | solution.py:536

commit v3 on v2

--- a/solution.py
+++ b/solution.py
@@ -111,14 +111,14 @@
 
 def put_sends(sends, full, at):
     south, north, west, east = faces_of(full)
-    sends[0][...] = jnp.where(at.even_row, north, south)
-    sends[1][...] = jnp.where(at.even_row, south, north)
-    sends[2][...] = jnp.where(at.even_column, east, west)
-    sends[3][...] = jnp.where(at.even_column, west, east)
+    sends[0][...] = jnp.where(at.even_column, west, east)
+    sends[1][...] = jnp.where(at.even_column, east, west)
+    sends[2][...] = jnp.where(at.even_row, south, north)
+    sends[3][...] = jnp.where(at.even_row, north, south)
 
 
 def neighbours(got, at):
-    core, link, near, far = [ref[...] for ref in got]
+    far, near, link, core = [ref[...] for ref in got]
     above = jnp.where(at.even_row, core, link)
     below = jnp.where(at.even_row, link, core)
     right = jnp.where(at.even_column, near, far)
@@ -184,7 +184,9 @@
     put_sends((s0, s1, s2, s3), full, at)
 
 
-def k_neumann(order, neumann, lists, neumann_o, avg_o, neumann_s, sem):
+def k_neumann(order, neumann, lists, neumann_o, avg_o, neumann_s, lists_s, sem):
+    listed = pltpu.make_async_copy(lists, lists_s, sem.at[4])
+    listed.start()
     copies = []
     for f in range(4):
         rows = pl.ds(f * LANES, LANES)
@@ -192,7 +194,8 @@
         copies[f].start()
     hots = one_hot_faces(order[...])
     points = order.shape[1]
-    named = lists[...]
+    listed.wait()
+    named = lists_s[...]
     position = lax.broadcasted_iota(jnp.int32, (8, points), 1)
     total = jnp.zeros((8, points), F32)
     length = named.shape[1]
@@ -209,16 +212,20 @@
             ).astype(BF16)
 
 
-def k_couple(order, diag, after, couple, blocks, diag_o, couple_o, blocks_o, couple_s, blocks_s, sem):
+def k_couple(
+    order, after, diag, couple, blocks, diag_o, couple_o, blocks_o, diag_s, couple_s, blocks_s, sem
+):
     copies = []
     for f in range(4):
         rows = pl.ds(f * LANES, LANES)
         copies.append(pltpu.make_async_copy(couple.at[rows], couple_s.at[rows], sem.at[f]))
     copies.append(pltpu.make_async_copy(blocks, blocks_s, sem.at[4]))
+    copies.append(pltpu.make_async_copy(diag, diag_s, sem.at[5]))
     for copy in copies:
         copy.start()
     hots = one_hot_faces(order[...])
-    diag_o[...] = to_shared(jnp.broadcast_to(diag[...], (8, diag.shape[1])), hots)[:1]
+    copies[5].wait()
+    diag_o[...] = to_shared(jnp.broadcast_to(diag_s[...], (8, diag_s.shape[1])), hots)[:1]
     for f in range(4):
         rows = slice(f * LANES, (f + 1) * LANES)
         copies[f].wait()
@@ -246,13 +253,18 @@
     put_sends(sends, t, at)
 
 
-def k_schur(place, t, g0, g1, g2, g3, diag, couple, blocks, z_o, q_o, *sends, rhs):
+def k_schur(
+    place, t, g0, g1, g2, g3, diag, couple, blocks, z_o, q_o, s0, s1, s2, s3, z_s, sem, *, rhs
+):
     at = Place(place)
     z = assembled(t[...], (g0, g1, g2, g3), at, rhs)
-    z_o[...] = z
+    z_s[...] = z
+    copy = pltpu.make_async_copy(z_s, z_o, sem.at[0])
+    copy.start()
     q = schur(z, diag[...], held(couple), held(blocks))
     q_o[...] = q
-    put_sends(sends, q, at)
+    put_sends((s0, s1, s2, s3), q, at)
+    copy.wait()
 
 
 def k_second(place, q, g0, g1, g2, g3, r, share, neumann, avg, v_o, t_o, pr_o, *sends):
@@ -284,7 +296,9 @@
     reach1 = prim1[...][:, rhs:]
     spare = jnp.zeros((8, LANES - reach1.shape[1] - reach2.shape[1]), F32)
     tail = jnp.concatenate([reach1, reach2, spare], axis=1)
-    pay_o[...] = jnp.concatenate([prim0[...], prim1[...][:, :rhs], prim2, tail], axis=0)
+    pay = jnp.concatenate([prim0[...], prim1[...][:, :rhs], prim2, tail], axis=0)
+    for item in range(pay_o.shape[0]):
+        pay_o[item] = pay
 
 
 def summed(got):
@@ -307,16 +321,22 @@
         out[item] = total
 
 
+def banded_product(pieces, value):
+    first, second = cut(value, 2)
+    return (narrow(pieces[1], first) + narrow(pieces[0], second)) + narrow(pieces[0], first)
+
+
 def coarse_rows(totals, lowers, uppers):
     carry = jnp.zeros_like(totals[0])
     smooth = []
-    for low, value in zip(lowers, totals):
-        carry = low * carry + (1.0 - low) * value
+    for low, value in zip(lowers, [(1.0 - low) * value for low, value in zip(lowers, totals)]):
+        carry = low * carry + value
         smooth.append(carry)
     carry = jnp.zeros_like(totals[0])
     tops = []
+    smooth = [(1.0 - up) * value for up, value in zip(uppers, smooth)]
     for up, value in zip(uppers[::-1], smooth[::-1]):
-        carry = up * carry + (1.0 - up) * value
+        carry = up * carry + value
         tops.append(carry)
     return tops[::-1]
 
@@ -357,15 +377,19 @@
             tiles = tiles + [jnp.zeros((width - rows * 8, rhs), F32)]
         return jnp.concatenate(tiles, axis=0)
 
+    own, near, wide = [cut(ref[...], 2) for ref in (band0, band1, band2)]
+
     def solve(total):
         tiles = [total[8 * k : 8 * k + 8] for k in range(rows)]
-        return stacked(coarse_rows(tiles, lowers, uppers)) + mm(band0[...], total)
+        return stacked(coarse_rows(tiles, lowers, uppers)) + banded_product(own, total)
 
     edge = jnp.zeros((32, rhs), F32)
     c0 = solve(stacked([part[0:8] for part in upper]))
-    c1 = solve(stacked([part[8:16] for part in upper]) + mm(band1[...], c0))
+    c1 = solve(stacked([part[8:16] for part in upper]) + banded_product(near, c0))
     c2 = solve(
-        stacked([part[0:8] for part in lower]) + mm(band2[...], c0) + mm(band1[...], c1)
+        stacked([part[0:8] for part in lower])
+        + banded_product(wide, c0)
+        + banded_product(near, c1)
     )
     for ref, value in ((c0_s, c0), (c1_s, c1), (c2_s, c2)):
         ref[0:32, :] = edge
@@ -421,28 +445,27 @@
     )
 
 
-def k_last_schur(place, t, g0, g1, g2, g3, pbasis, c2, diag, couple, blocks, z_o, q_o, *sends):
+def k_last_schur(
+    place, t, g0, g1, g2, g3, pbasis, c2, diag, couple, blocks, r, w0, vv2, dots,
+    z_o, q_o, pay_o, s0, s1, s2, s3,
+):
     at = Place(place)
     rhs = z_o.shape[0]
     z = assembled(t[...], (g0, g1, g2, g3), at, rhs) + mm_first(c2[...], pbasis[rhs:, :])
     z_o[...] = z
     q = schur(z, diag[...], held(couple), held(blocks))
     q_o[...] = q
-    put_sends(sends, q, at)
-
-
-def k_dots(place, q, g0, g1, g2, g3, r, w0, vv2, z2, dots, w2_o, pay_o):
-    at = Place(place)
-    w2 = assembled(q[...], (g0, g1, g2, g3), at, q.shape[0])
-    w2_o[...] = w2
+    put_sends((s0, s1, s2, s3), q, at)
     v1 = w0[...] - SHIFT * r[...]
-    vs = (r[...], v1, vv2[...])
-    pairs = [(5 + i, (vs[i], z2[...])) for i in range(3)] + [(8, (z2[...], w2))]
-    table = dots[...] + dot_rows(pairs)
-    pay_o[...] = jnp.concatenate([table[i : i + 1] for i in range(9)], axis=1)
-
-
-def k_final(got, order, r0, z0, z1, z2, w0, w1, w2, x_o, r_o):
+    pairs = [(5 + i, (v, z)) for i, v in enumerate((r[...], v1, vv2[...]))]
+    table = dots[...] + dot_rows(pairs + [(8, (z, q + q))])
+    line = jnp.concatenate([table[i : i + 1] for i in range(9)], axis=1)
+    for item in range(pay_o.shape[0]):
+        pay_o[item] = line
+
+
+def k_final(place, got, q, g0, g1, g2, g3, order, r0, z0, z1, z2, w0, w1, x_o, r_o):
+    w2 = assembled(q[...], (g0, g1, g2, g3), Place(place), q.shape[0])
     total = summed(got)
     v0z0, v0z1, v1z0, v1z1, v2z1, v0z2, v1z2, v2z2, z2w2 = [
         total[:, i * LANES : (i + 1) * LANES] for i in range(9)
@@ -501,15 +524,19 @@
     col = [columns[:, i : i + 1] for i in range(6)]
     hots = one_hot_faces(order[...])
     x = col[0] * z0[...] + col[1] * z1[...] + col[2] * z2[...]
-    r = r0[...] + col[3] * w0[...] + col[4] * w1[...] + col[5] * w2[...]
+    r = r0[...] + col[3] * w0[...] + col[4] * w1[...] + col[5] * w2
     both = to_points(jnp.concatenate([x, r], axis=0), hots)
     rhs = x.shape[0]
     x_o[...] = both[:rhs]
     r_o[...] = both[rhs:]
 
 
-def call(body, outs, place, *args, scratch=(), raw=(), flops=1_000_000):
-    space = [pl.ANY if n in raw else pltpu.VMEM for n in range(len(args))]
+def call(body, outs, place, *args, scratch=(), raw=(), raw_outs=(), flops=1_000_000):
+    args = tuple(
+        pltpu.with_memory_space_constraint(arg, pltpu.HBM) if n in raw else arg
+        for n, arg in enumerate(args)
+    )
+    space = [pltpu.HBM if n in raw else pltpu.VMEM for n in range(len(args))]
     specs = [pl.BlockSpec(memory_space=kind) for kind in space]
     if place is not None:
         specs = [pl.BlockSpec(memory_space=pltpu.SMEM)] + specs
@@ -517,13 +544,18 @@
     return pl.pallas_call(
         body,
         out_shape=[
-            out if isinstance(out, jax.ShapeDtypeStruct) else jax.ShapeDtypeStruct(out, F32)
-            for out in outs
+            out
+            if isinstance(out, jax.ShapeDtypeStruct)
+            else (pltpu.HBM(out, F32) if n in raw_outs else jax.ShapeDtypeStruct(out, F32))
+            for n, out in enumerate(outs)
         ],
         in_specs=specs,
-        out_specs=[pl.BlockSpec(memory_space=pltpu.VMEM) for _ in outs],
+        out_specs=[
+            pl.BlockSpec(memory_space=pltpu.HBM if n in raw_outs else pltpu.VMEM)
+            for n in range(len(outs))
+        ],
         scratch_shapes=list(scratch),
-        compiler_params=pltpu.CompilerParams(vmem_limit_bytes=32 * 1024 * 1024),
+        compiler_params=pltpu.CompilerParams(vmem_limit_bytes=16 * 1024 * 1024),
         cost_estimate=pl.CostEstimate(flops=flops, bytes_accessed=1_000_000, transcendentals=0),
     )(*args)
 
@@ -533,11 +565,12 @@
     link = [(i, i + 1 if i % 2 else i - 1) for i in range(1, rows - 1)]
     near = [(i, i ^ 1) for i in range(columns)]
     far = [(i, (i + 1 if i % 2 else i - 1) % columns) for i in range(columns)]
-    got3 = lax.ppermute(sends[3], "circ", far)
-    got2 = lax.ppermute(sends[2], "circ", near)
-    got1 = lax.ppermute(sends[1], "axial", link)
-    got0 = lax.ppermute(sends[0], "axial", core)
-    return [got0, got1, got2, got3]
+    return [
+        lax.ppermute(sends[0], "circ", far),
+        lax.ppermute(sends[1], "circ", near),
+        lax.ppermute(sends[2], "axial", link),
+        lax.ppermute(sends[3], "axial", core),
+    ]
 
 
 def spread(value, axis):
@@ -574,8 +607,12 @@
         k_neumann,
         [bf16(points, points), (8, points)],
         None, order, neumann_solve[0, 0], primal_lists[0, 0],
-        raw=(1,),
-        scratch=[pltpu.VMEM((points, points), F32), dma((4,))],
+        raw=(1, 2),
+        scratch=[
+            pltpu.VMEM((points, points), F32),
+            pltpu.VMEM(primal_lists.shape[2:], jnp.int32),
+            dma((5,)),
+        ],
         flops=2_000_000_000,
     )
     r0, share, prim0, t0, *sends = call(
@@ -588,15 +625,21 @@
     diag, couple, blocks = call(
         k_couple,
         [(1, points), bf16(points, points), bf16(*inner)],
-        None, order, interface_diag[0], share, coupling[0, 0], interior_inverse[0, 0],
-        raw=(3, 4),
-        scratch=[pltpu.VMEM((points, points), F32), pltpu.VMEM(inner, F32), dma((5,))],
+        None, order, share, interface_diag[0], coupling[0, 0], interior_inverse[0, 0],
+        raw=(2, 3, 4),
+        scratch=[
+            pltpu.VMEM((1, points), F32),
+            pltpu.VMEM((points, points), F32),
+            pltpu.VMEM(inner, F32),
+            dma((6,)),
+        ],
         flops=2_000_000_000,
     )
     n = rhs + 24
     z0, q0, *sends = call(
         functools.partial(k_schur, rhs=rhs), [(n, points)] * 2 + face(n),
         place, t0, *got, diag, couple, blocks,
+        raw_outs=(0,), scratch=[pltpu.VMEM((n, points), F32), dma((1,))],
     )
     got = swap(sends)
     n = rhs + 40
@@ -608,17 +651,18 @@
     z1, q1, *sends = call(
         functools.partial(k_schur, rhs=rhs), [(n, points)] * 2 + face(n),
         place, t1, *got, diag, couple, blocks,
+        raw_outs=(0,), scratch=[pltpu.VMEM((n, points), F32), dma((1,))],
     )
     got = swap(sends)
     n = rhs + 72
     v2, pay = call(
-        k_third, [(n, points), (32, LANES)], place, q1, *got, v1, share, avg, prim0, prim1
+        k_third, [(n, points), (columns, 32, LANES)], place, q1, *got, v1, share, avg, prim0, prim1
     )
     coefs = jnp.concatenate(
         [jnp.swapaxes(row_coarse[0], 0, 1), lower_coef[0][:, None], upper_coef[0][:, None]], axis=1
     )
     coefs = jnp.pad(coefs, ((24, 0), (112, LANES - 112 - coefs.shape[1])))
-    got = spread(jnp.broadcast_to(pay[None], (columns, 32, LANES)), "circ")
+    got = spread(pay, "circ")
     (pay,) = call(k_sum_halves, [(rows, 16, LANES)], None, got, coefs)
     mine = spread(pay, "axial")
     other = lax.ppermute(mine, "axial", [(i, i ^ 1) for i in range(rows)])
@@ -633,19 +677,17 @@
     z0f, w0f, z1f, w1f, dots = call(
         k_known, [(rhs, points)] * 4 + [(16, rhs)], None, r0, z0, v1, z1, v2, vv2, c0, c1
     )
-    z2f, q2, *sends = call(
-        k_last_schur, [(rhs, points)] * 2 + face(rhs),
-        place, t2, *got, z0, c2, diag, couple, blocks,
-    )
+    z2f, q2, pay, *sends = call(
+        k_last_schur, [(rhs, points)] * 2 + [(columns, 1, 9 * LANES)] + face(rhs),
+        place, t2, *got, z0, c2, diag, couple, blocks, r0, w0f, vv2, dots,
+    )
+    dots = spread(pay, "circ")
     got = swap(sends)
-    w2f, pay = call(
-        k_dots, [(rhs, points), (1, 9 * LANES)], place, q2, *got, r0, w0f, vv2, z2f, dots
-    )
-    got = spread(jnp.broadcast_to(pay[None], (columns,) + pay.shape), "circ")
-    (pay,) = call(k_sum_spread, [(rows,) + pay.shape], None, got)
-    got = spread(pay, "axial")
+    (pay,) = call(k_sum_spread, [(rows, 1, 9 * LANES)], None, dots)
+    dots = spread(pay, "axial")
     x, r = call(
-        k_final, [(rhs, points)] * 2, None, got, order, r0, z0f, z1f, z2f, w0f, w1f, w2f
+        k_final, [(rhs, points)] * 2,
+        place, dots, q2, *got, order, r0, z0f, z1f, z2f, w0f, w1f,
     )
     return (x[None, None], r[None, None])
 

time: 229 us -> 199 us (0.87)
  blocking collectives: 70.7 us -> 48.9 us
  waiting for transfers between devices: 33.9 us -> 17 us
  starting transfers between devices: 91.2 us -> 100 us
  Pallas kernels: 23.1 us -> 26.3 us
  local copies, waits for them, and re-layouts: 7.36 us -> 4.42 us
    all_to_all x3 -> x2, blocking collectives: 70.7 us -> 48.9 us  [spread(): return lax.all_to_all(value, axis, split_axis=0, concat_axis=0, tiled=True)]
    ppermute x28, waiting for transfers between devices: 26.5 us -> 4.93 us  [the longest x7 3.54 us: exchange(): lax.ppermute(sends[3], 'axial', core)]
    all_to_all x1 -> x2, starting transfers between devices: 4.32 us -> 11.4 us  [spread(): return lax.all_to_all(value, axis, split_axis=0, concat_axis=0, tiled=True)]
    all_to_all x1 -> x2, waiting for transfers between devices: 6.29 us -> 10.9 us  [spread(): return lax.all_to_all(value, axis, split_axis=0, concat_axis=0, tiled=True)]
    pallas_call x15 -> x14, Pallas kernels: 23.1 us -> 26.3 us  [call(): pl.pallas_call(body, out_shape=[out if isinstance(out, jax.ShapeDtypeStru...]
    unnamed x30 -> x24, local copies, waits for them, and re-layouts: 6.33 us -> 4.19 us
  transfers between devices with their start and end apart: 30 -> 31, of which waited for: 9 -> 11; matrix products, arithmetic and copies ran while one was open for 0% -> 0% of each run, Pallas kernels for 3% -> 4%
where the time goes in v3:
time: 199 us; the launch traced here: 198 us
  starting transfers between devices  100 us (50%)
  blocking collectives  48.9 us (25%)
  Pallas kernels  26.3 us (13%)
  waiting for transfers between devices  17 us (9%)
  local copies, waits for them, and re-layouts  4.42 us (2%)
    all_to_all x2, blocking collectives, spread(): return lax.all_to_all(value, axis, split_axis=0, concat_axis=0, tiled=True)  48.9 us
    ppermute x7, starting transfers between devices, exchange(): lax.ppermute(sends[0], 'circ', far)  31.9 us
    ppermute x7, starting transfers between devices, exchange(): lax.ppermute(sends[2], 'axial', link)  27 us
    pallas_call x14, Pallas kernels, call(): pl.pallas_call(body, out_shape=[out if isinstance(out, jax.ShapeDtypeStru...  26.3 us
    ppermute x7, starting transfers between devices, exchange(): lax.ppermute(sends[1], 'circ', near)  13.4 us
    ppermute x7, starting transfers between devices, exchange(): lax.ppermute(sends[3], 'axial', core)  13.4 us
    all_to_all x2, starting transfers between devices, spread(): return lax.all_to_all(value, axis, split_axis=0, concat_axis=0, tiled=True)  11.4 us
    all_to_all x2, waiting for transfers between devices, spread(): return lax.all_to_all(value, axis, split_axis=0, concat_axis=0, tiled=True)  10.9 us
  transfers between devices with their start and end apart: 31, of which 11 were waited for; matrix products, arithmetic and copies ran while one was open for 0% of the time, Pallas kernels for 4%

profile of v3, /device:TPU:1, one launch (start us, length us, event | category | flops | bytes accessed | tf_op | source)
XLA Modules:
  0.0 198.1 jit_solution(1378036349879549439)
XLA Ops:
  0.7 1.9 shard_map.122
  2.6 7.7 %collective-permute-start = (f32[136,128]{1,0:T(8,128)S(1)}, f32[136,128]{1,0:T(8,128)S(1)}, u32[]{:S(2)}, u32[]{:S(2)}) collective-permute-start(f32[136,128]{1,0:T(8,128)S(1)} %get-tuple-element.66), channel_id=1, source_target_pairs={{0,15},{1,2},{2,1},{3,4},{4,3},{5,6},{6,5},{7,8},{8,7},{9,10},{10,... | collective-permute-start | bytes 208904 | tf_op jit(solution)/shard_map/ppermute | solution.py:569
  10.3 1.9 collective-permute-start.1
  12.2 4.4 %collective-permute-start.2 = (f32[136,128]{1,0:T(8,128)S(1)}, f32[136,128]{1,0:T(8,128)S(1)}, u32[]{:S(2)}, u32[]{:S(2)}) collective-permute-start(f32[136,128]{1,0:T(8,128)S(1)} %get-tuple-element.68), channel_id=1, source_target_pairs={{16,32},{32,16},{48,64},{64,48},{80,96},{96,80},{112,128},{128,112... | collective-permute-start | bytes 208904 | tf_op jit(solution)/shard_map/ppermute | solution.py:571
  16.6 1.9 collective-permute-start.3
  18.6 3.1 %shard_map.123 = (bf16[2,512,512]{2,1,0:T(8,128)(2,1)S(1)}, f32[8,512]{1,0:T(8,128)S(1)}) custom-call(s32[1,512]{1,0:T(1,128)S(1)} %get-tuple-element.70.order, f32[512,512]{1,0:T(8,128)} %bitcast.23, s32[8,64]{1,0:T(8,128)} %bitcast.28), custom_call_target="tpu_custom_call" | custom-call | flops 2000000000 | bytes 1000000 | tf_op jit(solution)/shard_map/pallas_call | solution.py:544
  21.7 1.1 shard_map.124
  22.8 4.4 %collective-permute-start.4 = (f32[136,128]{1,0:T(8,128)S(1)}, f32[136,128]{1,0:T(8,128)S(1)}, u32[]{:S(2)}, u32[]{:S(2)}) collective-permute-start(f32[136,128]{1,0:T(8,128)S(1)} %get-tuple-element.74), channel_id=1, source_target_pairs={{0,15},{1,2},{2,1},{3,4},{4,3},{5,6},{6,5},{7,8},{8,7},{9,10},{10,... | collective-permute-start | bytes 208904 | tf_op jit(solution)/shard_map/ppermute | solution.py:569
  27.2 1.9 collective-permute-start.5
  29.2 3.5 %collective-permute-start.6 = (f32[136,128]{1,0:T(8,128)S(1)}, f32[136,128]{1,0:T(8,128)S(1)}, u32[]{:S(2)}, u32[]{:S(2)}) collective-permute-start(f32[136,128]{1,0:T(8,128)S(1)} %get-tuple-element.76), channel_id=1, source_target_pairs={{16,32},{32,16},{48,64},{64,48},{80,96},{96,80},{112,128},{128,112... | collective-permute-start | bytes 208904 | tf_op jit(solution)/shard_map/ppermute | solution.py:571
  32.6 1.9 collective-permute-start.7
  34.6 2.2 %shard_map.125 = (f32[1,512]{1,0:T(1,128)S(1)}, bf16[2,512,512]{2,1,0:T(8,128)(2,1)S(1)}, bf16[2,4,128,128]{3,2,1,0:T(8,128)(2,1)S(1)}) custom-call(s32[1,512]{1,0:T(1,128)S(1)} %get-tuple-element.70.order, f32[1,512]{1,0:T(1,128)S(1)} %get-tuple-element.78.after.share, f32[1,512]{1,0:T(1,128)} %bitcast.29, f32[512,512]{1,0:T(8,128)} %bitcast.24, ...), custom_call_target="tpu_custom_call" | custom-call | flops 2000000000 | bytes 1000000 | tf_op jit(solution)/shard_map/pallas_call | solution.py:544
  36.9 2.1 %shard_map.126 = (f32[152,512]{1,0:T(8,128)}, f32[152,512]{1,0:T(8,128)S(1)}, f32[152,128]{1,0:T(8,128)S(1)}, f32[152,128]{1,0:T(8,128)S(1)}, f32[152,128]{1,0:T(8,128)S(1)}, /*index=5*/f32[152,128]{1,0:T(8,128)S(1)}) custom-call(s32[3]{0:T(128)S(1)} %pad_add_fusion.place, f32[136,512]{1,0:T(8,128)S(1)} %get-tuple-element.73.t, ...), custom_call_target="tpu_custom_call" | custom-call | flops 1000000 | bytes 1000000 | tf_op jit(solution)/shard_map/pallas_call | solution.py:544
  39.0 5.0 %collective-permute-start.8 = (f32[152,128]{1,0:T(8,128)S(1)}, f32[152,128]{1,0:T(8,128)S(1)}, u32[]{:S(2)}, u32[]{:S(2)}) collective-permute-start(f32[152,128]{1,0:T(8,128)S(1)} %get-tuple-element.83), channel_id=1, source_target_pairs={{0,15},{1,2},{2,1},{3,4},{4,3},{5,6},{6,5},{7,8},{8,7},{9,10},{10,... | collective-permute-start | bytes 233480 | tf_op jit(solution)/shard_map/ppermute | solution.py:569
  44.0 1.9 collective-permute-start.9
  45.9 4.2 %collective-permute-start.10 = (f32[152,128]{1,0:T(8,128)S(1)}, f32[152,128]{1,0:T(8,128)S(1)}, u32[]{:S(2)}, u32[]{:S(2)}) collective-permute-start(f32[152,128]{1,0:T(8,128)S(1)} %get-tuple-element.85), channel_id=1, source_target_pairs={{16,32},{32,16},{48,64},{64,48},{80,96},{96,80},{112,128},{128,112... | collective-permute-start | bytes 233480 | tf_op jit(solution)/shard_map/ppermute | solution.py:571
  50.1 1.9 collective-permute-start.11
  52.2 1.1 collective-permute-done.11.g3
  53.3 1.3 shard_map.127
  54.5 3.6 %collective-permute-start.12 = (f32[168,128]{1,0:T(8,128)S(1)}, f32[168,128]{1,0:T(8,128)S(1)}, u32[]{:S(2)}, u32[]{:S(2)}) collective-permute-start(f32[168,128]{1,0:T(8,128)S(1)} %get-tuple-element.89), channel_id=1, source_target_pairs={{0,15},{1,2},{2,1},{3,4},{4,3},{5,6},{6,5},{7,8},{8,7},{9,10},{10,... | collective-permute-start | bytes 258056 | tf_op jit(solution)/shard_map/ppermute | solution.py:569
  58.2 1.9 collective-permute-start.13
  60.1 5.1 %collective-permute-start.14 = (f32[168,128]{1,0:T(8,128)S(1)}, f32[168,128]{1,0:T(8,128)S(1)}, u32[]{:S(2)}, u32[]{:S(2)}) collective-permute-start(f32[168,128]{1,0:T(8,128)S(1)} %get-tuple-element.91), channel_id=1, source_target_pairs={{16,32},{32,16},{48,64},{64,48},{80,96},{96,80},{112,128},{128,112... | collective-permute-start | bytes 258056 | tf_op jit(solution)/shard_map/ppermute | solution.py:571
  65.2 1.9 collective-permute-start.15
  68.4 2.2 %shard_map.128 = (f32[184,512]{1,0:T(8,128)}, f32[184,512]{1,0:T(8,128)S(1)}, f32[184,128]{1,0:T(8,128)S(1)}, f32[184,128]{1,0:T(8,128)S(1)}, f32[184,128]{1,0:T(8,128)S(1)}, /*index=5*/f32[184,128]{1,0:T(8,128)S(1)}) custom-call(s32[3]{0:T(128)S(1)} %pad_add_fusion.place, f32[168,512]{1,0:T(8,128)S(1)} %get-tuple-element.88.t, ...), custom_call_target="tpu_custom_call" | custom-call | flops 1000000 | bytes 1000000 | tf_op jit(solution)/shard_map/pallas_call | solution.py:544
  70.6 4.9 %collective-permute-start.16 = (f32[184,128]{1,0:T(8,128)S(1)}, f32[184,128]{1,0:T(8,128)S(1)}, u32[]{:S(2)}, u32[]{:S(2)}) collective-permute-start(f32[184,128]{1,0:T(8,128)S(1)} %get-tuple-element.94), channel_id=1, source_target_pairs={{0,15},{1,2},{2,1},{3,4},{4,3},{5,6},{6,5},{7,8},{8,7},{9,10},{10,... | collective-permute-start | bytes 282632 | tf_op jit(solution)/shard_map/ppermute | solution.py:569
  75.6 1.9 collective-permute-start.17
  77.5 3.9 %collective-permute-start.18 = (f32[184,128]{1,0:T(8,128)S(1)}, f32[184,128]{1,0:T(8,128)S(1)}, u32[]{:S(2)}, u32[]{:S(2)}) collective-permute-start(f32[184,128]{1,0:T(8,128)S(1)} %get-tuple-element.96), channel_id=1, source_target_pairs={{16,32},{32,16},{48,64},{64,48},{80,96},{96,80},{112,128},{128,112... | collective-permute-start | bytes 282632 | tf_op jit(solution)/shard_map/ppermute | solution.py:571
  81.4 1.9 collective-permute-start.19
  86.4 4.9 %all-to-all-start = ((f32[16,32,128]{2,1,0:T(8,128)}), f32[16,32,128]{2,1,0:T(8,128)}, u32[]{:S(2)}, u32[]{:S(2)}) async-start(f32[16,32,128]{2,1,0:T(8,128)} %copy-done.2), calls=%async_computation | async-start | bytes 524288 | tf_op jit(solution)/shard_map/all_to_all | solution.py:577
  93.0 6.8 %all-to-all-done.got = f32[16,32,128]{2,1,0:T(8,128)} async-done(((f32[16,32,128]{2,1,0:T(8,128)}), f32[16,32,128]{2,1,0:T(8,128)}, u32[]{:S(2)}, u32[]{:S(2)}) %all-to-all-start) | async-done | bytes 262176 | tf_op jit(solution)/shard_map/all_to_all | solution.py:577
  100.7 36.0 %all_to_all.20.mine = f32[32,16,128]{2,1,0:T(8,128)S(1)} all-to-all(f32[32,16,128]{2,1,0:T(8,128)S(1)} %shard_map.130), channel_id=1, replica_groups=mesh['axial'=32,'circ'=16] {'axial'}, dimensions={0} | all-to-all | bytes 524288 | tf_op jit(solution)/shard_map/all_to_all | solution.py:577
  136.7 2.9 %collective-permute-start.20 = (f32[32,16,128]{2,1,0:T(8,128)S(1)}, f32[32,16,128]{2,1,0:T(8,128)S(1)}, u32[]{:S(2)}, u32[]{:S(2)}) collective-permute-start(f32[32,16,128]{2,1,0:T(8,128)S(1)} %all_to_all.20.mine), channel_id=1, source_target_pairs={{0,16},{16,0},{32,48},{48,32},{64,80},{80,64},{96,112},{112,96},{1... | collective-permute-start | bytes 786440 | tf_op jit(solution)/shard_map/ppermute | solution.py:668
  139.6 1.1 collective-permute-done.20.other
  140.8 2.5 %shard_map.131 = (f32[128,512]{1,0:T(8,128)S(1)}, f32[128,512]{1,0:T(8,128)S(1)}, f32[72,128]{1,0:T(8,128)S(1)}, f32[40,128]{1,0:T(8,128)S(1)}, f32[24,128]{1,0:...) custom-call(s32[3]{0:T(128)S(1)} %pad_add_fusion.place, ...), custom_call_target="tpu_custom_call" | custom-call | flops 1000000 | bytes 1000000 | tf_op jit(solution)/shard_map/pallas_call | solution.py:544
  143.2 2.9 %collective-permute-start.21 = (f32[128,128]{1,0:T(8,128)S(1)}, f32[128,128]{1,0:T(8,128)S(1)}, u32[]{:S(2)}, u32[]{:S(2)}) collective-permute-start(f32[128,128]{1,0:T(8,128)S(1)} %get-tuple-element.104), channel_id=1, source_target_pairs={{0,15},{1,2},{2,1},{3,4},{4,3},{5,6},{6,5},{7,8},{8,7},{9,10},{10,... | collective-permute-start | bytes 196616 | tf_op jit(solution)/shard_map/ppermute | solution.py:569
  146.1 1.9 collective-permute-start.22
  148.1 2.2 %collective-permute-start.23 = (f32[128,128]{1,0:T(8,128)S(1)}, f32[128,128]{1,0:T(8,128)S(1)}, u32[]{:S(2)}, u32[]{:S(2)}) collective-permute-start(f32[128,128]{1,0:T(8,128)S(1)} %get-tuple-element.106), channel_id=1, source_target_pairs={{16,32},{32,16},{48,64},{64,48},{80,96},{96,80},{112,128},{128,112... | collective-permute-start | bytes 196616 | tf_op jit(solution)/shard_map/ppermute | solution.py:571
  150.3 1.9 collective-permute-start.24
  152.2 2.4 %shard_map.132 = (f32[128,512]{1,0:T(8,128)S(1)}, f32[128,512]{1,0:T(8,128)S(1)}, f32[128,512]{1,0:T(8,128)S(1)}, f32[128,512]{1,0:T(8,128)S(1)}, f32[16,128]{1,0:T(8,128)S(1)}) custom-call(f32[128,512]{1,0:T(8,128)S(1)} %get-tuple-element.87.r.r0, f32[152,512]{1,0:T(8,128)S(1)} %copy-done, f32[168,512]{1,0:T(8,128)S(1)} %get-tuple-element.98.v.v1, ...), custom_call_target="tpu_custom_call" | custom-call | flops 1000000 | bytes 1000000 | tf_op jit(solution)/shard_map/pallas_call | solution.py:544
  156.8 2.5 %shard_map.133 = (f32[128,512]{1,0:T(8,128)S(1)}, f32[128,512]{1,0:T(8,128)S(1)}, f32[16,1,1152]{2,1,0:T(1,128)S(1)}, f32[128,128]{1,0:T(8,128)S(1)}, f32[128,12...) custom-call(s32[3]{0:T(128)S(1)} %pad_add_fusion.place, f32[128,512]{1,0:T(8,128)S(1)} %get-tuple-element.103.t, ...), custom_call_target="tpu_custom_call" | custom-call | flops 1000000 | bytes 1000000 | tf_op jit(solution)/shard_map/pallas_call | solution.py:544
  159.2 13.0 %all_to_all.21.got = f32[16,1,1152]{2,1,0:T(1,128)S(1)} all-to-all(f32[16,1,1152]{2,1,0:T(1,128)S(1)} %get-tuple-element.116), channel_id=1, replica_groups=mesh['axial'=32,'circ'=16] {'circ'}, dimensions={0} | all-to-all | bytes 147456 | tf_op jit(solution)/shard_map/all_to_all | solution.py:577
  172.9 6.5 %all-to-all-start.3 = ((f32[32,1,1152]{2,1,0:T(1,128)}), f32[32,1,1152]{2,1,0:T(1,128)S(1)}, u32[]{:S(2)}, u32[]{:S(2)}) async-start(f32[32,1,1152]{2,1,0:T(1,128)} %shard_map.134), calls=%async_computation.3 | async-start | bytes 294912 | tf_op jit(solution)/shard_map/all_to_all | solution.py:577
  179.3 3.4 %collective-permute-start.25 = (f32[128,128]{1,0:T(8,128)S(1)}, f32[128,128]{1,0:T(8,128)S(1)}, u32[]{:S(2)}, u32[]{:S(2)}) collective-permute-start(f32[128,128]{1,0:T(8,128)S(1)} %get-tuple-element.118), channel_id=1, source_target_pairs={{0,15},{1,2},{2,1},{3,4},{4,3},{5,6},{6,5},{7,8},{8,7},{9,10},{10,... | collective-permute-start | bytes 196616 | tf_op jit(solution)/shard_map/ppermute | solution.py:569
  182.7 1.9 collective-permute-start.26
  184.7 3.8 %collective-permute-start.27 = (f32[128,128]{1,0:T(8,128)S(1)}, f32[128,128]{1,0:T(8,128)S(1)}, u32[]{:S(2)}, u32[]{:S(2)}) collective-permute-start(f32[128,128]{1,0:T(8,128)S(1)} %get-tuple-element.120), channel_id=1, source_target_pairs={{16,32},{32,16},{48,64},{64,48},{80,96},{96,80},{112,128},{128,112... | collective-permute-start | bytes 196616 | tf_op jit(solution)/shard_map/ppermute | solution.py:571
  188.5 1.9 collective-permute-start.28
  191.7 4.2 %all-to-all-done.3.got = f32[32,1,1152]{2,1,0:T(1,128)S(1)} async-done(((f32[32,1,1152]{2,1,0:T(1,128)}), f32[32,1,1152]{2,1,0:T(1,128)S(1)}, u32[]{:S(2)}, u32[]{:S(2)}) %all-to-all-start.3) | async-done | bytes 147488 | tf_op jit(solution)/shard_map/all_to_all | solution.py:577
  195.8 2.2 %shard_map.135 = (f32[128,512]{1,0:T(8,128)}, f32[128,512]{1,0:T(8,128)}) custom-call(s32[3]{0:T(128)S(1)} %pad_add_fusion.place, f32[32,1,1152]{2,1,0:T(1,128)S(1)} %all-to-all-done.3.got, f32[128,512]{1,0:T(8,128)S(1)} %get-tuple-element.117.q, f32[128,128]{1,0:T(8,128)S(1)} %collective-permute-done.25.g0, f32[128,128]{1,0:T(8,128)S(1)} %collective-permute-done.26.g1, ...), custom_call_target="tpu_custom_call" | custom-call | flops 1000000 | bytes 1000000 | tf_op jit(solution)/shard_map/pallas_call | solution.py:544
  (59 shorter events, 11.2 us)
Async XLA Ops:
  2.6 19.0 %collective-permute-start = (f32[136,128]{1,0:T(8,128)S(1)}, f32[136,128]{1,0:T(8,128)S(1)}, u32[]{:S(2)}, u32[]{:S(2)}) collective-permute-start(f32[136,128]{1,0:T(8,128)S(1)} %get-tuple-element.66), channel_id=1, source_target_pairs={{0,15},{1,2},{2,1},{3,4},{4,3},{5,6},{6,5},{7,8},{8,7},{9,10},{10,... | collective-permute-start | bytes 208904 | tf_op jit(solution)/shard_map/ppermute | solution.py:569
  10.3 11.4 %collective-permute-start.1 = (f32[136,128]{1,0:T(8,128)S(1)}, f32[136,128]{1,0:T(8,128)S(1)}, u32[]{:S(2)}, u32[]{:S(2)}) collective-permute-start(f32[136,128]{1,0:T(8,128)S(1)} %get-tuple-element.67), channel_id=1, source_target_pairs={{0,1},{1,0},{2,3},{3,2},{4,5},{5,4},{6,7},{7,6},{8,9},{9,8},{10,11... | collective-permute-start | bytes 208904 | tf_op jit(solution)/shard_map/ppermute | solution.py:570
  12.2 9.5 %collective-permute-start.2 = (f32[136,128]{1,0:T(8,128)S(1)}, f32[136,128]{1,0:T(8,128)S(1)}, u32[]{:S(2)}, u32[]{:S(2)}) collective-permute-start(f32[136,128]{1,0:T(8,128)S(1)} %get-tuple-element.68), channel_id=1, source_target_pairs={{16,32},{32,16},{48,64},{64,48},{80,96},{96,80},{112,128},{128,112... | collective-permute-start | bytes 208904 | tf_op jit(solution)/shard_map/ppermute | solution.py:571
  16.6 5.1 %collective-permute-start.3 = (f32[136,128]{1,0:T(8,128)S(1)}, f32[136,128]{1,0:T(8,128)S(1)}, u32[]{:S(2)}, u32[]{:S(2)}) collective-permute-start(f32[136,128]{1,0:T(8,128)S(1)} %get-tuple-element.69), channel_id=1, source_target_pairs={{0,16},{16,0},{32,48},{48,32},{64,80},{80,64},{96,112},{112,96},{1... | collective-permute-start | bytes 208904 | tf_op jit(solution)/shard_map/ppermute | solution.py:572
  22.8 14.0 %collective-permute-start.4 = (f32[136,128]{1,0:T(8,128)S(1)}, f32[136,128]{1,0:T(8,128)S(1)}, u32[]{:S(2)}, u32[]{:S(2)}) collective-permute-start(f32[136,128]{1,0:T(8,128)S(1)} %get-tuple-element.74), channel_id=1, source_target_pairs={{0,15},{1,2},{2,1},{3,4},{4,3},{5,6},{6,5},{7,8},{8,7},{9,10},{10,... | collective-permute-start | bytes 208904 | tf_op jit(solution)/shard_map/ppermute | solution.py:569
  27.2 9.6 %collective-permute-start.5 = (f32[136,128]{1,0:T(8,128)S(1)}, f32[136,128]{1,0:T(8,128)S(1)}, u32[]{:S(2)}, u32[]{:S(2)}) collective-permute-start(f32[136,128]{1,0:T(8,128)S(1)} %get-tuple-element.75), channel_id=1, source_target_pairs={{0,1},{1,0},{2,3},{3,2},{4,5},{5,4},{6,7},{7,6},{8,9},{9,8},{10,11... | collective-permute-start | bytes 208904 | tf_op jit(solution)/shard_map/ppermute | solution.py:570
  29.2 7.7 %collective-permute-start.6 = (f32[136,128]{1,0:T(8,128)S(1)}, f32[136,128]{1,0:T(8,128)S(1)}, u32[]{:S(2)}, u32[]{:S(2)}) collective-permute-start(f32[136,128]{1,0:T(8,128)S(1)} %get-tuple-element.76), channel_id=1, source_target_pairs={{16,32},{32,16},{48,64},{64,48},{80,96},{96,80},{112,128},{128,112... | collective-permute-start | bytes 208904 | tf_op jit(solution)/shard_map/ppermute | solution.py:571
  32.6 4.2 %collective-permute-start.7 = (f32[136,128]{1,0:T(8,128)S(1)}, f32[136,128]{1,0:T(8,128)S(1)}, u32[]{:S(2)}, u32[]{:S(2)}) collective-permute-start(f32[136,128]{1,0:T(8,128)S(1)} %get-tuple-element.77), channel_id=1, source_target_pairs={{0,16},{16,0},{32,48},{48,32},{64,80},{80,64},{96,112},{112,96},{1... | collective-permute-start | bytes 208904 | tf_op jit(solution)/shard_map/ppermute | solution.py:572
  39.0 13.1 %collective-permute-start.8 = (f32[152,128]{1,0:T(8,128)S(1)}, f32[152,128]{1,0:T(8,128)S(1)}, u32[]{:S(2)}, u32[]{:S(2)}) collective-permute-start(f32[152,128]{1,0:T(8,128)S(1)} %get-tuple-element.83), channel_id=1, source_target_pairs={{0,15},{1,2},{2,1},{3,4},{4,3},{5,6},{6,5},{7,8},{8,7},{9,10},{10,... | collective-permute-start | bytes 233480 | tf_op jit(solution)/shard_map/ppermute | solution.py:569
  44.0 8.1 %collective-permute-start.9 = (f32[152,128]{1,0:T(8,128)S(1)}, f32[152,128]{1,0:T(8,128)S(1)}, u32[]{:S(2)}, u32[]{:S(2)}) collective-permute-start(f32[152,128]{1,0:T(8,128)S(1)} %get-tuple-element.84), channel_id=1, source_target_pairs={{0,1},{1,0},{2,3},{3,2},{4,5},{5,4},{6,7},{7,6},{8,9},{9,8},{10,11... | collective-permute-start | bytes 233480 | tf_op jit(solution)/shard_map/ppermute | solution.py:570
  45.9 6.3 %collective-permute-start.10 = (f32[152,128]{1,0:T(8,128)S(1)}, f32[152,128]{1,0:T(8,128)S(1)}, u32[]{:S(2)}, u32[]{:S(2)}) collective-permute-start(f32[152,128]{1,0:T(8,128)S(1)} %get-tuple-element.85), channel_id=1, source_target_pairs={{16,32},{32,16},{48,64},{64,48},{80,96},{96,80},{112,128},{128,112... | collective-permute-start | bytes 233480 | tf_op jit(solution)/shard_map/ppermute | solution.py:571
  50.1 3.2 %collective-permute-start.11 = (f32[152,128]{1,0:T(8,128)S(1)}, f32[152,128]{1,0:T(8,128)S(1)}, u32[]{:S(2)}, u32[]{:S(2)}) collective-permute-start(f32[152,128]{1,0:T(8,128)S(1)} %get-tuple-element.86), channel_id=1, source_target_pairs={{0,16},{16,0},{32,48},{48,32},{64,80},{80,64},{96,112},{112,96},{1... | collective-permute-start | bytes 233480 | tf_op jit(solution)/shard_map/ppermute | solution.py:572
  54.5 12.6 %collective-permute-start.12 = (f32[168,128]{1,0:T(8,128)S(1)}, f32[168,128]{1,0:T(8,128)S(1)}, u32[]{:S(2)}, u32[]{:S(2)}) collective-permute-start(f32[168,128]{1,0:T(8,128)S(1)} %get-tuple-element.89), channel_id=1, source_target_pairs={{0,15},{1,2},{2,1},{3,4},{4,3},{5,6},{6,5},{7,8},{8,7},{9,10},{10,... | collective-permute-start | bytes 258056 | tf_op jit(solution)/shard_map/ppermute | solution.py:569
  58.2 9.0 %collective-permute-start.13 = (f32[168,128]{1,0:T(8,128)S(1)}, f32[168,128]{1,0:T(8,128)S(1)}, u32[]{:S(2)}, u32[]{:S(2)}) collective-permute-start(f32[168,128]{1,0:T(8,128)S(1)} %get-tuple-element.90), channel_id=1, source_target_pairs={{0,1},{1,0},{2,3},{3,2},{4,5},{5,4},{6,7},{7,6},{8,9},{9,8},{10,11... | collective-permute-start | bytes 258056 | tf_op jit(solution)/shard_map/ppermute | solution.py:570
  60.1 7.2 %collective-permute-start.14 = (f32[168,128]{1,0:T(8,128)S(1)}, f32[168,128]{1,0:T(8,128)S(1)}, u32[]{:S(2)}, u32[]{:S(2)}) collective-permute-start(f32[168,128]{1,0:T(8,128)S(1)} %get-tuple-element.91), channel_id=1, source_target_pairs={{16,32},{32,16},{48,64},{64,48},{80,96},{96,80},{112,128},{128,112... | collective-permute-start | bytes 258056 | tf_op jit(solution)/shard_map/ppermute | solution.py:571
  65.2 3.2 %collective-permute-start.15 = (f32[168,128]{1,0:T(8,128)S(1)}, f32[168,128]{1,0:T(8,128)S(1)}, u32[]{:S(2)}, u32[]{:S(2)}) collective-permute-start(f32[168,128]{1,0:T(8,128)S(1)} %get-tuple-element.92), channel_id=1, source_target_pairs={{0,16},{16,0},{32,48},{48,32},{64,80},{80,64},{96,112},{112,96},{1... | collective-permute-start | bytes 258056 | tf_op jit(solution)/shard_map/ppermute | solution.py:572
  70.6 12.7 %collective-permute-start.16 = (f32[184,128]{1,0:T(8,128)S(1)}, f32[184,128]{1,0:T(8,128)S(1)}, u32[]{:S(2)}, u32[]{:S(2)}) collective-permute-start(f32[184,128]{1,0:T(8,128)S(1)} %get-tuple-element.94), channel_id=1, source_target_pairs={{0,15},{1,2},{2,1},{3,4},{4,3},{5,6},{6,5},{7,8},{8,7},{9,10},{10,... | collective-permute-start | bytes 282632 | tf_op jit(solution)/shard_map/ppermute | solution.py:569
  75.6 7.8 %collective-permute-start.17 = (f32[184,128]{1,0:T(8,128)S(1)}, f32[184,128]{1,0:T(8,128)S(1)}, u32[]{:S(2)}, u32[]{:S(2)}) collective-permute-start(f32[184,128]{1,0:T(8,128)S(1)} %get-tuple-element.95), channel_id=1, source_target_pairs={{0,1},{1,0},{2,3},{3,2},{4,5},{5,4},{6,7},{7,6},{8,9},{9,8},{10,11... | collective-permute-start | bytes 282632 | tf_op jit(solution)/shard_map/ppermute | solution.py:570
  77.5 6.1 %collective-permute-start.18 = (f32[184,128]{1,0:T(8,128)S(1)}, f32[184,128]{1,0:T(8,128)S(1)}, u32[]{:S(2)}, u32[]{:S(2)}) collective-permute-start(f32[184,128]{1,0:T(8,128)S(1)} %get-tuple-element.96), channel_id=1, source_target_pairs={{16,32},{32,16},{48,64},{64,48},{80,96},{96,80},{112,128},{128,112... | collective-permute-start | bytes 282632 | tf_op jit(solution)/shard_map/ppermute | solution.py:571
  81.4 3.2 %collective-permute-start.19 = (f32[184,128]{1,0:T(8,128)S(1)}, f32[184,128]{1,0:T(8,128)S(1)}, u32[]{:S(2)}, u32[]{:S(2)}) collective-permute-start(f32[184,128]{1,0:T(8,128)S(1)} %get-tuple-element.97), channel_id=1, source_target_pairs={{0,16},{16,0},{32,48},{48,32},{64,80},{80,64},{96,112},{112,96},{1... | collective-permute-start | bytes 282632 | tf_op jit(solution)/shard_map/ppermute | solution.py:572
  85.7 0.7 copy-start.2
  86.4 4.9 %copy-start.9 = (f32[1,8,8]{2,1,0:T(8,128)S(1)}, f32[1,8,8]{2,1,0:T(8,128)}, u32[]{:S(2)}) copy-start(f32[1,8,8]{2,1,0:T(8,128)} %param.17) | copy-start | bytes 772
  86.4 13.3 %all-to-all-start = ((f32[16,32,128]{2,1,0:T(8,128)}), f32[16,32,128]{2,1,0:T(8,128)}, u32[]{:S(2)}, u32[]{:S(2)}) async-start(f32[16,32,128]{2,1,0:T(8,128)} %copy-done.2), calls=%async_computation | async-start | bytes 524288 | tf_op jit(solution)/shard_map/all_to_all | solution.py:577
  91.4 0.7 copy-start.10
  92.2 0.7 copy-start.11
  136.7 4.0 %collective-permute-start.20 = (f32[32,16,128]{2,1,0:T(8,128)S(1)}, f32[32,16,128]{2,1,0:T(8,128)S(1)}, u32[]{:S(2)}, u32[]{:S(2)}) collective-permute-start(f32[32,16,128]{2,1,0:T(8,128)S(1)} %all_to_all.20.mine), channel_id=1, source_target_pairs={{0,16},{16,0},{32,48},{48,32},{64,80},{80,64},{96,112},{112,96},{1... | collective-permute-start | bytes 786440 | tf_op jit(solution)/shard_map/ppermute | solution.py:668
  140.7 11.4 %copy-start = (f32[152,512]{1,0:T(8,128)S(1)}, f32[152,512]{1,0:T(8,128)}, u32[]{:S(2)}) copy-start(f32[152,512]{1,0:T(8,128)} %get-tuple-element.108.z0.pbasis) | copy-start | bytes 933892
  140.7 11.5 %copy-start.1 = (f32[184,512]{1,0:T(8,128)S(1)}, f32[184,512]{1,0:T(8,128)}, u32[]{:S(2)}) copy-start(f32[184,512]{1,0:T(8,128)} %get-tuple-element.110.z1) | copy-start | bytes 1130500
  143.2 13.5 %collective-permute-start.21 = (f32[128,128]{1,0:T(8,128)S(1)}, f32[128,128]{1,0:T(8,128)S(1)}, u32[]{:S(2)}, u32[]{:S(2)}) collective-permute-start(f32[128,128]{1,0:T(8,128)S(1)} %get-tuple-element.104), channel_id=1, source_target_pairs={{0,15},{1,2},{2,1},{3,4},{4,3},{5,6},{6,5},{7,8},{8,7},{9,10},{10,... | collective-permute-start | bytes 196616 | tf_op jit(solution)/shard_map/ppermute | solution.py:569
  146.1 10.6 %collective-permute-start.22 = (f32[128,128]{1,0:T(8,128)S(1)}, f32[128,128]{1,0:T(8,128)S(1)}, u32[]{:S(2)}, u32[]{:S(2)}) collective-permute-start(f32[128,128]{1,0:T(8,128)S(1)} %get-tuple-element.105), channel_id=1, source_target_pairs={{0,1},{1,0},{2,3},{3,2},{4,5},{5,4},{6,7},{7,6},{8,9},{9,8},{10,11... | collective-permute-start | bytes 196616 | tf_op jit(solution)/shard_map/ppermute | solution.py:570
  148.1 8.7 %collective-permute-start.23 = (f32[128,128]{1,0:T(8,128)S(1)}, f32[128,128]{1,0:T(8,128)S(1)}, u32[]{:S(2)}, u32[]{:S(2)}) collective-permute-start(f32[128,128]{1,0:T(8,128)S(1)} %get-tuple-element.106), channel_id=1, source_target_pairs={{16,32},{32,16},{48,64},{64,48},{80,96},{96,80},{112,128},{128,112... | collective-permute-start | bytes 196616 | tf_op jit(solution)/shard_map/ppermute | solution.py:571
  150.3 6.5 %collective-permute-start.24 = (f32[128,128]{1,0:T(8,128)S(1)}, f32[128,128]{1,0:T(8,128)S(1)}, u32[]{:S(2)}, u32[]{:S(2)}) collective-permute-start(f32[128,128]{1,0:T(8,128)S(1)} %get-tuple-element.107), channel_id=1, source_target_pairs={{0,16},{16,0},{32,48},{48,32},{64,80},{80,64},{96,112},{112,96},{1... | collective-permute-start | bytes 196616 | tf_op jit(solution)/shard_map/ppermute | solution.py:572
  154.6 0.7 copy-start.3
  155.3 0.7 copy-start.5
  156.0 0.7 copy-start.7
  156.7 39.1 %copy-start.8 = (f32[128,512]{1,0:T(8,128)S(1)}, f32[128,512]{1,0:T(8,128)}, u32[]{:S(2)}) copy-start(f32[128,512]{1,0:T(8,128)} %copy-done.7) | copy-start | bytes 786436
  172.2 23.7 %copy-start.4 = (f32[128,512]{1,0:T(8,128)S(1)}, f32[128,512]{1,0:T(8,128)}, u32[]{:S(2)}) copy-start(f32[128,512]{1,0:T(8,128)} %copy-done.3) | copy-start | bytes 786436
  172.2 23.7 %copy-start.6 = (f32[128,512]{1,0:T(8,128)S(1)}, f32[128,512]{1,0:T(8,128)}, u32[]{:S(2)}) copy-start(f32[128,512]{1,0:T(8,128)} %copy-done.5) | copy-start | bytes 786436
  172.9 22.9 %all-to-all-start.3 = ((f32[32,1,1152]{2,1,0:T(1,128)}), f32[32,1,1152]{2,1,0:T(1,128)S(1)}, u32[]{:S(2)}, u32[]{:S(2)}) async-start(f32[32,1,1152]{2,1,0:T(1,128)} %shard_map.134), calls=%async_computation.3 | async-start | bytes 294912 | tf_op jit(solution)/shard_map/all_to_all | solution.py:577
  179.3 11.1 %collective-permute-start.25 = (f32[128,128]{1,0:T(8,128)S(1)}, f32[128,128]{1,0:T(8,128)S(1)}, u32[]{:S(2)}, u32[]{:S(2)}) collective-permute-start(f32[128,128]{1,0:T(8,128)S(1)} %get-tuple-element.118), channel_id=1, source_target_pairs={{0,15},{1,2},{2,1},{3,4},{4,3},{5,6},{6,5},{7,8},{8,7},{9,10},{10,... | collective-permute-start | bytes 196616 | tf_op jit(solution)/shard_map/ppermute | solution.py:569
  182.7 7.7 %collective-permute-start.26 = (f32[128,128]{1,0:T(8,128)S(1)}, f32[128,128]{1,0:T(8,128)S(1)}, u32[]{:S(2)}, u32[]{:S(2)}) collective-permute-start(f32[128,128]{1,0:T(8,128)S(1)} %get-tuple-element.119), channel_id=1, source_target_pairs={{0,1},{1,0},{2,3},{3,2},{4,5},{5,4},{6,7},{7,6},{8,9},{9,8},{10,11... | collective-permute-start | bytes 196616 | tf_op jit(solution)/shard_map/ppermute | solution.py:570
  184.7 6.5 %collective-permute-start.27 = (f32[128,128]{1,0:T(8,128)S(1)}, f32[128,128]{1,0:T(8,128)S(1)}, u32[]{:S(2)}, u32[]{:S(2)}) collective-permute-start(f32[128,128]{1,0:T(8,128)S(1)} %get-tuple-element.120), channel_id=1, source_target_pairs={{16,32},{32,16},{48,64},{64,48},{80,96},{96,80},{112,128},{128,112... | collective-permute-start | bytes 196616 | tf_op jit(solution)/shard_map/ppermute | solution.py:571
  188.5 3.1 %collective-permute-start.28 = (f32[128,128]{1,0:T(8,128)S(1)}, f32[128,128]{1,0:T(8,128)S(1)}, u32[]{:S(2)}, u32[]{:S(2)}) collective-permute-start(f32[128,128]{1,0:T(8,128)S(1)} %get-tuple-element.121), channel_id=1, source_target_pairs={{0,16},{16,0},{32,48},{48,32},{64,80},{80,64},{96,112},{112,96},{1... | collective-permute-start | bytes 196616 | tf_op jit(solution)/shard_map/ppermute | solution.py:572

commit v4 on v3

--- a/solution.py
+++ b/solution.py
@@ -13,12 +13,6 @@
 BF16 = jnp.bfloat16
 LANES = 128
 PIECES = 2
-
-
-def mm(a, b):
-    return lax.dot_general(
-        a, b, (((1,), (0,)), ((), ())), precision=HIGHEST, preferred_element_type=F32
-    )
 
 
 def mm_t(a, b):
@@ -213,7 +207,9 @@
 
 
 def k_couple(
-    order, after, diag, couple, blocks, diag_o, couple_o, blocks_o, diag_s, couple_s, blocks_s, sem
+    order, after, diag, couple, blocks, row_coarse, lower, upper,
+    diag_o, couple_o, blocks_o, coefs_o,
+    diag_s, couple_s, blocks_s, rows_s, lower_s, upper_s, sem,
 ):
     copies = []
     for f in range(4):
@@ -221,6 +217,9 @@
         copies.append(pltpu.make_async_copy(couple.at[rows], couple_s.at[rows], sem.at[f]))
     copies.append(pltpu.make_async_copy(blocks, blocks_s, sem.at[4]))
     copies.append(pltpu.make_async_copy(diag, diag_s, sem.at[5]))
+    copies.append(pltpu.make_async_copy(row_coarse, rows_s, sem.at[6]))
+    copies.append(pltpu.make_async_copy(lower, lower_s, sem.at[7]))
+    copies.append(pltpu.make_async_copy(upper, upper_s, sem.at[8]))
     for copy in copies:
         copy.start()
     hots = one_hot_faces(order[...])
@@ -235,6 +234,23 @@
     for f in range(4):
         for n, piece in enumerate(cut(blocks_s[f], PIECES)):
             blocks_o[n, f] = piece
+    for n in (6, 7, 8):
+        copies[n].wait()
+    count = lower_s.shape[1]
+    lane = lax.broadcasted_iota(jnp.int32, (count, LANES), 1)
+    eye = lax.broadcasted_iota(jnp.int32, (count, count), 0) == lax.broadcasted_iota(
+        jnp.int32, (count, count), 1
+    )
+    tile = jnp.zeros((count, LANES), F32)
+    for n in range(count):
+        tile = tile + jnp.where(lane == 112 + n, rows_s[:, n : n + 1], 0.0)
+    for n, ref in ((120, lower_s), (121, upper_s)):
+        column = jnp.sum(
+            jnp.where(eye, jnp.broadcast_to(ref[...], (count, count)), 0.0), axis=1, keepdims=True
+        )
+        tile = tile + jnp.where(lane == n, column, 0.0)
+    coefs_o[0:24, :] = jnp.zeros((24, LANES), F32)
+    coefs_o[24:32, :] = tile
 
 
 def k_first(place, shared, g0, g1, g2, g3, neumann, avg, r_o, share_o, prim_o, t_o, *sends):
@@ -282,14 +298,16 @@
     put_sends(sends, t, at)
 
 
-def k_third(place, q, g0, g1, g2, g3, v, share, avg, prim0, prim1, v2_o, pay_o):
+def k_third(place, q, g0, g1, g2, g3, v, share, avg, prim0, prim1, v2_o, pay_o, v2_s, sem):
     at = Place(place)
     rhs = prim0.shape[1]
     w = assembled(q[...], (g0, g1, g2, g3), at, rhs)
     zero = jnp.zeros((16, w.shape[1]), F32)
     older = jnp.concatenate([v[...][:rhs], zero, v[...][rhs:], zero], axis=0)
     v2 = w - SHIFT * older
-    v2_o[...] = v2
+    v2_s[...] = v2
+    copy = pltpu.make_async_copy(v2_s, v2_o, sem.at[0])
+    copy.start()
     weighted = share[...] * v2
     prim2 = mm_t(avg[...], weighted[:rhs])
     reach2 = mm_t(avg[...], weighted[rhs:])
@@ -299,6 +317,7 @@
     pay = jnp.concatenate([prim0[...], prim1[...][:, :rhs], prim2, tail], axis=0)
     for item in range(pay_o.shape[0]):
         pay_o[item] = pay
+    copy.wait()
 
 
 def summed(got):
@@ -341,13 +360,33 @@
     return tops[::-1]
 
 
-def k_coarse(
-    place, mine, other, v2, v1, share, neumann,
-    v_o, t_o, c0_o, c1_o, c2_o, s0, s1, s2, s3,
-    band0, band1, band2, c0_s, c1_s, c2_s,
+def k_fourth(place, v2, share, neumann, after, t_o, *sends):
+    at = Place(place)
+    t = share[...] * product(share[...] * v2[...], held(neumann))
+    t_o[...] = t
+    put_sends(sends, t, at)
+
+
+def lift(coefs, basis):
+    spare = -coefs.shape[0] % 16
+    if spare:
+        coefs = jnp.concatenate([coefs, jnp.zeros((spare, coefs.shape[1]), F32)], axis=0)
+        basis = jnp.concatenate([basis, jnp.zeros((spare, basis.shape[1]), F32)], axis=0)
+    c, b = cut(coefs, 2), cut(basis, 2)
+
+    def times(x, y):
+        return lax.dot_general(x, y, (((0,), (0,)), ((), ())), preferred_element_type=F32)
+
+    return (times(c[1], b[0]) + times(c[0], b[1])) + times(c[0], b[0])
+
+
+def k_core(
+    place, mine, other, t, g0, g1, g2, g3, z0, v1, z1, v2, r, diag, couple, blocks,
+    z0_o, z1_o, z2_o, w0_o, w1_o, q_o, pay_o, s0, s1, s2, s3,
+    band0, band1, band2, c0_s, c1_s, c2_s, full_s, sem,
 ):
     at = Place(place)
-    rhs = v_o.shape[0]
+    rhs = r.shape[0]
     rows = mine.shape[0]
     width = band0.shape[1]
     lane = lax.broadcasted_iota(jnp.int32, (8, width), 1)
@@ -383,7 +422,7 @@
         tiles = [total[8 * k : 8 * k + 8] for k in range(rows)]
         return stacked(coarse_rows(tiles, lowers, uppers)) + banded_product(own, total)
 
-    edge = jnp.zeros((32, rhs), F32)
+    edge = jnp.zeros((40, rhs), F32)
     c0 = solve(stacked([part[0:8] for part in upper]))
     c1 = solve(stacked([part[8:16] for part in upper]) + banded_product(near, c0))
     c2 = solve(
@@ -392,76 +431,63 @@
         + banded_product(near, c1)
     )
     for ref, value in ((c0_s, c0), (c1_s, c1), (c2_s, c2)):
-        ref[0:32, :] = edge
-        ref[32 : 32 + width, :] = value
-        ref[32 + width :, :] = edge
+        ref[0:40, :] = edge
+        ref[40 : 40 + width, :] = value
+        ref[40 + width :, :] = edge
     start = at.row * 8
-    c0w = c0_s[pl.ds(pl.multiple_of(start, 8), 72), :]
-    c1w = c1_s[pl.ds(pl.multiple_of(start + 16, 8), 40), :]
-    c2w = c2_s[pl.ds(pl.multiple_of(start + 24, 8), 24), :]
-    c0_o[...] = c0w
-    c1_o[...] = c1w
-    c2_o[...] = c2w
-    v = v2[:rhs, :] + mm_first(jnp.concatenate([c0w, c1w], axis=0),
-                               jnp.concatenate([v2[rhs:, :], v1[rhs:, :]], axis=0))
-    v_o[...] = v
-    t = share[...] * product(share[...] * v, held(neumann))
-    t_o[...] = t
-    put_sends((s0, s1, s2, s3), t, at)
-
-
-def mm_first(a, b):
-    return lax.dot_general(
-        a, b, (((0,), (0,)), ((), ())), precision=HIGHEST, preferred_element_type=F32
-    )
-
-
-def dot_rows(pairs):
-    rows = lax.broadcasted_iota(jnp.int32, (16, LANES), 0)
-    total = jnp.zeros((16, LANES), F32)
-    for index, (a, b) in pairs:
-        part = sum(faces_of(a * b)[1:], faces_of(a * b)[0])
-        total = total + mm_t(jnp.where(rows == index, 1.0, 0.0).astype(F32), part)
-    return total
-
-
-def k_known(r, z0, v1, z1, v2, vv2, c0, c1, z0_o, w0_o, z1_o, w1_o, dots_o):
-    rhs = r.shape[0]
-    c0, c1 = c0[...], c1[...]
-    z0f = z0[:rhs, :] + mm_first(c0[24:48], z0[rhs:, :])
-    v1f = v1[:rhs, :] + mm_first(c0[16:56], v1[rhs:, :])
-    z1f = z1[:rhs, :] + mm_first(
-        jnp.concatenate([c0[8:64], c1[8:32]], axis=0),
-        jnp.concatenate([z1[rhs:, :], z0[rhs:, :]], axis=0),
-    )
-    v2f = vv2[...]
-    z0_o[...] = z0f
-    z1_o[...] = z1f
-    w0_o[...] = v1f + SHIFT * r[...]
-    w1_o[...] = v2f + SHIFT * v1f
-    vs = (r[...], v1f, v2f)
-    dots_o[...] = dot_rows(
-        [(0, (vs[0], z0f)), (1, (vs[0], z1f)), (2, (vs[1], z0f)), (3, (vs[1], z1f)), (4, (v2f, z1f))]
-    )
-
-
-def k_last_schur(
-    place, t, g0, g1, g2, g3, pbasis, c2, diag, couple, blocks, r, w0, vv2, dots,
-    z_o, q_o, pay_o, s0, s1, s2, s3,
-):
-    at = Place(place)
-    rhs = z_o.shape[0]
-    z = assembled(t[...], (g0, g1, g2, g3), at, rhs) + mm_first(c2[...], pbasis[rhs:, :])
-    z_o[...] = z
-    q = schur(z, diag[...], held(couple), held(blocks))
+    c0 = c0_s[pl.ds(pl.multiple_of(start, 8), 88), :]
+    c1 = c1_s[pl.ds(pl.multiple_of(start + 16, 8), 56), :]
+    c2 = c2_s[pl.ds(pl.multiple_of(start + 32, 8), 24), :]
+    r0 = r[...]
+    z2 = assembled(t[...], (g0, g1, g2, g3), at, rhs)
+    z2f = z2[:rhs] + lift(
+        jnp.concatenate([c0, c1, c2], axis=0),
+        jnp.concatenate([z2[rhs:], z1[rhs:, :], z0[rhs:, :]], axis=0),
+    )
+    q = schur(z2f, diag[...], held(couple), held(blocks))
     q_o[...] = q
     put_sends((s0, s1, s2, s3), q, at)
-    v1 = w0[...] - SHIFT * r[...]
-    pairs = [(5 + i, (v, z)) for i, v in enumerate((r[...], v1, vv2[...]))]
-    table = dots[...] + dot_rows(pairs + [(8, (z, q + q))])
+    z0f = z0[:rhs, :] + lift(c0[32:56], z0[rhs:, :])
+    v1f = v1[:rhs, :] + lift(c0[24:64], v1[rhs:, :])
+    z1f = z1[:rhs, :] + lift(
+        jnp.concatenate([c0[16:72], c1[16:40]], axis=0),
+        jnp.concatenate([z1[rhs:, :], z0[rhs:, :]], axis=0),
+    )
+    v2f = v2[:rhs, :] + lift(
+        jnp.concatenate([c0[8:80], c1[8:48]], axis=0),
+        jnp.concatenate([v2[rhs:, :], v1[rhs:, :]], axis=0),
+    )
+    kept = ((z0f, z0_o), (z1f, z1_o), (z2f, z2_o), (v1f + SHIFT * r0, w0_o), (v2f + SHIFT * v1f, w1_o))
+    copies = []
+    for n, (value, out) in enumerate(kept):
+        full_s[n] = value
+        copies.append(pltpu.make_async_copy(full_s.at[n], out, sem.at[n]))
+        copies[n].start()
+    table = dot_rows(
+        [(r0, z0f), (r0, z1f), (v1f, z0f), (v1f, z1f), (v2f, z1f)]
+        + [(r0, z2f), (v1f, z2f), (v2f, z2f), (z2f, q + q)]
+    )
     line = jnp.concatenate([table[i : i + 1] for i in range(9)], axis=1)
     for item in range(pay_o.shape[0]):
         pay_o[item] = line
+    for copy in copies:
+        copy.wait()
+
+
+def dot_rows(pairs):
+    parts = []
+    for a, b in pairs:
+        faces = faces_of(a * b)
+        parts.append((faces[0] + faces[1]) + (faces[2] + faces[3]))
+    wide = jnp.concatenate(parts, axis=1)
+    shape = (16, wide.shape[1])
+    pick = jnp.where(
+        lax.broadcasted_iota(jnp.int32, shape, 0) == lax.broadcasted_iota(jnp.int32, shape, 1) // LANES,
+        1.0,
+        0.0,
+    ).astype(BF16)
+    high, middle, low = [narrow(pick, piece, True) for piece in cut(wide, 3)]
+    return (low + middle) + high
 
 
 def k_final(place, got, q, g0, g1, g2, g3, order, r0, z0, z1, z2, w0, w1, x_o, r_o):
@@ -622,16 +648,20 @@
     )
     got = swap(sends)
     inner = interior_inverse.shape[2:]
-    diag, couple, blocks = call(
+    diag, couple, blocks, coefs = call(
         k_couple,
-        [(1, points), bf16(points, points), bf16(*inner)],
+        [(1, points), bf16(points, points), bf16(*inner), (32, LANES)],
         None, order, share, interface_diag[0], coupling[0, 0], interior_inverse[0, 0],
-        raw=(2, 3, 4),
+        row_coarse[0], lower_coef, upper_coef,
+        raw=(2, 3, 4, 5, 6, 7),
         scratch=[
             pltpu.VMEM((1, points), F32),
             pltpu.VMEM((points, points), F32),
             pltpu.VMEM(inner, F32),
-            dma((6,)),
+            pltpu.VMEM(row_coarse.shape[1:], F32),
+            pltpu.VMEM(lower_coef.shape, F32),
+            pltpu.VMEM(upper_coef.shape, F32),
+            dma((9,)),
         ],
         flops=2_000_000_000,
     )
@@ -656,30 +686,26 @@
     got = swap(sends)
     n = rhs + 72
     v2, pay = call(
-        k_third, [(n, points), (columns, 32, LANES)], place, q1, *got, v1, share, avg, prim0, prim1
-    )
-    coefs = jnp.concatenate(
-        [jnp.swapaxes(row_coarse[0], 0, 1), lower_coef[0][:, None], upper_coef[0][:, None]], axis=1
-    )
-    coefs = jnp.pad(coefs, ((24, 0), (112, LANES - 112 - coefs.shape[1])))
+        k_third, [(n, points), (columns, 32, LANES)], place, q1, *got, v1, share, avg, prim0, prim1,
+        raw_outs=(0,), scratch=[pltpu.VMEM((n, points), F32), dma((1,))],
+    )
     got = spread(pay, "circ")
     (pay,) = call(k_sum_halves, [(rows, 16, LANES)], None, got, coefs)
     mine = spread(pay, "axial")
+    t2, *sends = call(
+        k_fourth, [(n, points)] + face(n), place, v2, share, neumann, pay, flops=500_000_000
+    )
+    mine, *got = lax.optimization_barrier((mine, *swap(sends)))
     other = lax.ppermute(mine, "axial", [(i, i ^ 1) for i in range(rows)])
     width = max(LANES, 8 * rows)
-    vv2, t2, c0, c1, c2, *sends = call(
-        k_coarse,
-        [(rhs, points)] * 2 + [(72, rhs), (40, rhs), (24, rhs)] + face(rhs),
-        place, mine, other, v2, v1, share, neumann,
-        scratch=[pltpu.VMEM((width, width), F32)] * 3 + [pltpu.VMEM((width + 64, rhs), F32)] * 3,
-    )
-    got = swap(sends)
-    z0f, w0f, z1f, w1f, dots = call(
-        k_known, [(rhs, points)] * 4 + [(16, rhs)], None, r0, z0, v1, z1, v2, vv2, c0, c1
-    )
-    z2f, q2, pay, *sends = call(
-        k_last_schur, [(rhs, points)] * 2 + [(columns, 1, 9 * LANES)] + face(rhs),
-        place, t2, *got, z0, c2, diag, couple, blocks, r0, w0f, vv2, dots,
+    z0f, z1f, z2f, w0f, w1f, q2, pay, *sends = call(
+        k_core,
+        [(rhs, points)] * 6 + [(columns, 1, 9 * LANES)] + face(rhs),
+        place, mine, other, t2, *got, z0, v1, z1, v2, r0, diag, couple, blocks,
+        raw_outs=(0, 1, 2, 3, 4),
+        scratch=[pltpu.VMEM((width, width), F32)] * 3
+        + [pltpu.VMEM((width + 80, rhs), F32)] * 3
+        + [pltpu.VMEM((5, rhs, points), F32), dma((5,))],
     )
     dots = spread(pay, "circ")
     got = swap(sends)

time: 199 us -> 191 us (0.960)
  blocking collectives: 48.9 us -> 22 us
  starting transfers between devices: 100 us -> 115 us
  local copies, waits for them, and re-layouts: 4.42 us -> 7.61 us
    all_to_all x2, blocking collectives: 48.9 us -> 22 us  [spread(): return lax.all_to_all(value, axis, split_axis=0, concat_axis=0, tiled=True)]
    all_to_all x2, starting transfers between devices: 11.4 us -> 24.4 us  [spread(): return lax.all_to_all(value, axis, split_axis=0, concat_axis=0, tiled=True)]
    unnamed x24 -> x22, local copies, waits for them, and re-layouts: 4.19 us -> 7.61 us
    pallas_call x14 -> x13, Pallas kernels: 26.3 us -> 25.6 us  [call(): pl.pallas_call(body, out_shape=[out if isinstance(out, jax.ShapeDtypeStru...]
  transfers between devices with their start and end apart: 31 -> 31, of which waited for: 11 -> 13; matrix products, arithmetic and copies ran while one was open for 0% -> 0% of each run, Pallas kernels for 4% -> 4%
where the time goes in v4:
time: 191 us; the launch traced here: 190 us
  starting transfers between devices  115 us (60%)
  Pallas kernels  25.6 us (13%)
  blocking collectives  22 us (12%)
  waiting for transfers between devices  18.3 us (10%)
  local copies, waits for them, and re-layouts  7.61 us (4%)
    ppermute x7, starting transfers between devices, exchange(): lax.ppermute(sends[0], 'circ', far)  31.9 us
    ppermute x7, starting transfers between devices, exchange(): lax.ppermute(sends[2], 'axial', link)  28.7 us
    pallas_call x13, Pallas kernels, call(): pl.pallas_call(body, out_shape=[out if isinstance(out, jax.ShapeDtypeStru...  25.6 us
    all_to_all x2, starting transfers between devices, spread(): return lax.all_to_all(value, axis, split_axis=0, concat_axis=0, tiled=True)  24.4 us
    all_to_all x2, blocking collectives, spread(): return lax.all_to_all(value, axis, split_axis=0, concat_axis=0, tiled=True)  22 us
    ppermute x7, starting transfers between devices, exchange(): lax.ppermute(sends[1], 'circ', near)  13.4 us
    ppermute x7, starting transfers between devices, exchange(): lax.ppermute(sends[3], 'axial', core)  13.4 us
    all_to_all x2, waiting for transfers between devices, spread(): return lax.all_to_all(value, axis, split_axis=0, concat_axis=0, tiled=True)  11 us
  transfers between devices with their start and end apart: 31, of which 13 were waited for; matrix products, arithmetic and copies ran while one was open for 0% of the time, Pallas kernels for 4%

profile of v4, /device:TPU:1, one launch (start us, length us, event | category | flops | bytes accessed | tf_op | source)
XLA Modules:
  0.0 189.7 jit_solution(7424605854397478136)
XLA Ops:
  0.7 1.9 %shard_map.122 = (f32[136,512]{1,0:T(8,128)S(1)}, s32[1,512]{1,0:T(1,128)S(1)}, f32[136,128]{1,0:T(8,128)S(1)}, f32[136,128]{1,0:T(8,128)S(1)}, f32[136,128]{1,0:T(8,128)S(1)}, /*index=5*/f32[136,128]{1,0:T(8,128)S(1)}) custom-call(s32[3]{0:T(128)S(1)} %pad_add_fusion.place, f32[128,512]{1,0:T(8,128)} %bitcast.13, f32[1,512]{1,0:T(1,128)} %bitcast.14, ...), custom_call_target="tpu_custom_call" | custom-call | flops 1000000 | bytes 1000000 | tf_op jit(solution)/shard_map/pallas_call | solution.py:570
  2.6 7.7 %collective-permute-start = (f32[136,128]{1,0:T(8,128)S(1)}, f32[136,128]{1,0:T(8,128)S(1)}, u32[]{:S(2)}, u32[]{:S(2)}) collective-permute-start(f32[136,128]{1,0:T(8,128)S(1)} %get-tuple-element.67), channel_id=1, source_target_pairs={{0,15},{1,2},{2,1},{3,4},{4,3},{5,6},{6,5},{7,8},{8,7},{9,10},{10,... | collective-permute-start | bytes 208904 | tf_op jit(solution)/shard_map/ppermute | solution.py:595
  10.3 1.9 %collective-permute-start.1 = (f32[136,128]{1,0:T(8,128)S(1)}, f32[136,128]{1,0:T(8,128)S(1)}, u32[]{:S(2)}, u32[]{:S(2)}) collective-permute-start(f32[136,128]{1,0:T(8,128)S(1)} %get-tuple-element.68), channel_id=1, source_target_pairs={{0,1},{1,0},{2,3},{3,2},{4,5},{5,4},{6,7},{7,6},{8,9},{9,8},{10,11... | collective-permute-start | bytes 208904 | tf_op jit(solution)/shard_map/ppermute | solution.py:596
  12.2 4.4 %collective-permute-start.2 = (f32[136,128]{1,0:T(8,128)S(1)}, f32[136,128]{1,0:T(8,128)S(1)}, u32[]{:S(2)}, u32[]{:S(2)}) collective-permute-start(f32[136,128]{1,0:T(8,128)S(1)} %get-tuple-element.69), channel_id=1, source_target_pairs={{16,32},{32,16},{48,64},{64,48},{80,96},{96,80},{112,128},{128,112... | collective-permute-start | bytes 208904 | tf_op jit(solution)/shard_map/ppermute | solution.py:597
  16.6 1.9 %collective-permute-start.3 = (f32[136,128]{1,0:T(8,128)S(1)}, f32[136,128]{1,0:T(8,128)S(1)}, u32[]{:S(2)}, u32[]{:S(2)}) collective-permute-start(f32[136,128]{1,0:T(8,128)S(1)} %get-tuple-element.70), channel_id=1, source_target_pairs={{0,16},{16,0},{32,48},{48,32},{64,80},{80,64},{96,112},{112,96},{1... | collective-permute-start | bytes 208904 | tf_op jit(solution)/shard_map/ppermute | solution.py:598
  18.6 3.1 %shard_map.123 = (bf16[2,512,512]{2,1,0:T(8,128)(2,1)S(1)}, f32[8,512]{1,0:T(8,128)S(1)}) custom-call(s32[1,512]{1,0:T(1,128)S(1)} %get-tuple-element.71.order, f32[512,512]{1,0:T(8,128)} %bitcast.16, s32[8,64]{1,0:T(8,128)} %bitcast.21), custom_call_target="tpu_custom_call" | custom-call | flops 2000000000 | bytes 1000000 | tf_op jit(solution)/shard_map/pallas_call | solution.py:570
  21.7 1.1 shard_map.124
  22.8 4.4 %collective-permute-start.4 = (f32[136,128]{1,0:T(8,128)S(1)}, f32[136,128]{1,0:T(8,128)S(1)}, u32[]{:S(2)}, u32[]{:S(2)}) collective-permute-start(f32[136,128]{1,0:T(8,128)S(1)} %get-tuple-element.75), channel_id=1, source_target_pairs={{0,15},{1,2},{2,1},{3,4},{4,3},{5,6},{6,5},{7,8},{8,7},{9,10},{10,... | collective-permute-start | bytes 208904 | tf_op jit(solution)/shard_map/ppermute | solution.py:595
  27.2 1.9 %collective-permute-start.5 = (f32[136,128]{1,0:T(8,128)S(1)}, f32[136,128]{1,0:T(8,128)S(1)}, u32[]{:S(2)}, u32[]{:S(2)}) collective-permute-start(f32[136,128]{1,0:T(8,128)S(1)} %get-tuple-element.76), channel_id=1, source_target_pairs={{0,1},{1,0},{2,3},{3,2},{4,5},{5,4},{6,7},{7,6},{8,9},{9,8},{10,11... | collective-permute-start | bytes 208904 | tf_op jit(solution)/shard_map/ppermute | solution.py:596
  29.2 3.5 %collective-permute-start.6 = (f32[136,128]{1,0:T(8,128)S(1)}, f32[136,128]{1,0:T(8,128)S(1)}, u32[]{:S(2)}, u32[]{:S(2)}) collective-permute-start(f32[136,128]{1,0:T(8,128)S(1)} %get-tuple-element.77), channel_id=1, source_target_pairs={{16,32},{32,16},{48,64},{64,48},{80,96},{96,80},{112,128},{128,112... | collective-permute-start | bytes 208904 | tf_op jit(solution)/shard_map/ppermute | solution.py:597
  32.7 1.9 %collective-permute-start.7 = (f32[136,128]{1,0:T(8,128)S(1)}, f32[136,128]{1,0:T(8,128)S(1)}, u32[]{:S(2)}, u32[]{:S(2)}) collective-permute-start(f32[136,128]{1,0:T(8,128)S(1)} %get-tuple-element.78), channel_id=1, source_target_pairs={{0,16},{16,0},{32,48},{48,32},{64,80},{80,64},{96,112},{112,96},{1... | collective-permute-start | bytes 208904 | tf_op jit(solution)/shard_map/ppermute | solution.py:598
  34.6 2.4 %shard_map.125 = (f32[1,512]{1,0:T(1,128)S(1)}, bf16[2,512,512]{2,1,0:T(8,128)(2,1)S(1)}, bf16[2,4,128,128]{3,2,1,0:T(8,128)(2,1)S(1)}, f32[32,128]{1,0:T(8,128)S(1)}) custom-call(s32[1,512]{1,0:T(1,128)S(1)} %get-tuple-element.71.order, f32[1,512]{1,0:T(1,128)S(1)} %get-tuple-element.79.after.share, f32[1,512]{1,0:T(1,128)} %bitcast.23, ...), custom_call_target="tpu_custom_call" | custom-call | flops 2000000000 | bytes 1000000 | tf_op jit(solution)/shard_map/pallas_call | solution.py:570
  37.0 2.1 %shard_map.126 = (f32[152,512]{1,0:T(8,128)}, f32[152,512]{1,0:T(8,128)S(1)}, f32[152,128]{1,0:T(8,128)S(1)}, f32[152,128]{1,0:T(8,128)S(1)}, f32[152,128]{1,0:T(8,128)S(1)}, /*index=5*/f32[152,128]{1,0:T(8,128)S(1)}) custom-call(s32[3]{0:T(128)S(1)} %pad_add_fusion.place, f32[136,512]{1,0:T(8,128)S(1)} %get-tuple-element.74.t, ...), custom_call_target="tpu_custom_call" | custom-call | flops 1000000 | bytes 1000000 | tf_op jit(solution)/shard_map/pallas_call | solution.py:570
  39.2 5.0 %collective-permute-start.8 = (f32[152,128]{1,0:T(8,128)S(1)}, f32[152,128]{1,0:T(8,128)S(1)}, u32[]{:S(2)}, u32[]{:S(2)}) collective-permute-start(f32[152,128]{1,0:T(8,128)S(1)} %get-tuple-element.84), channel_id=1, source_target_pairs={{0,15},{1,2},{2,1},{3,4},{4,3},{5,6},{6,5},{7,8},{8,7},{9,10},{10,... | collective-permute-start | bytes 233480 | tf_op jit(solution)/shard_map/ppermute | solution.py:595
  44.1 1.9 %collective-permute-start.9 = (f32[152,128]{1,0:T(8,128)S(1)}, f32[152,128]{1,0:T(8,128)S(1)}, u32[]{:S(2)}, u32[]{:S(2)}) collective-permute-start(f32[152,128]{1,0:T(8,128)S(1)} %get-tuple-element.85), channel_id=1, source_target_pairs={{0,1},{1,0},{2,3},{3,2},{4,5},{5,4},{6,7},{7,6},{8,9},{9,8},{10,11... | collective-permute-start | bytes 233480 | tf_op jit(solution)/shard_map/ppermute | solution.py:596
  46.1 4.2 %collective-permute-start.10 = (f32[152,128]{1,0:T(8,128)S(1)}, f32[152,128]{1,0:T(8,128)S(1)}, u32[]{:S(2)}, u32[]{:S(2)}) collective-permute-start(f32[152,128]{1,0:T(8,128)S(1)} %get-tuple-element.86), channel_id=1, source_target_pairs={{16,32},{32,16},{48,64},{64,48},{80,96},{96,80},{112,128},{128,112... | collective-permute-start | bytes 233480 | tf_op jit(solution)/shard_map/ppermute | solution.py:597
  50.3 1.9 %collective-permute-start.11 = (f32[152,128]{1,0:T(8,128)S(1)}, f32[152,128]{1,0:T(8,128)S(1)}, u32[]{:S(2)}, u32[]{:S(2)}) collective-permute-start(f32[152,128]{1,0:T(8,128)S(1)} %get-tuple-element.87), channel_id=1, source_target_pairs={{0,16},{16,0},{32,48},{48,32},{64,80},{80,64},{96,112},{112,96},{1... | collective-permute-start | bytes 233480 | tf_op jit(solution)/shard_map/ppermute | solution.py:598
  52.3 1.1 collective-permute-done.11.g3
  53.4 1.3 shard_map.127
  54.7 3.6 %collective-permute-start.12 = (f32[168,128]{1,0:T(8,128)S(1)}, f32[168,128]{1,0:T(8,128)S(1)}, u32[]{:S(2)}, u32[]{:S(2)}) collective-permute-start(f32[168,128]{1,0:T(8,128)S(1)} %get-tuple-element.90), channel_id=1, source_target_pairs={{0,15},{1,2},{2,1},{3,4},{4,3},{5,6},{6,5},{7,8},{8,7},{9,10},{10,... | collective-permute-start | bytes 258056 | tf_op jit(solution)/shard_map/ppermute | solution.py:595
  58.4 1.9 %collective-permute-start.13 = (f32[168,128]{1,0:T(8,128)S(1)}, f32[168,128]{1,0:T(8,128)S(1)}, u32[]{:S(2)}, u32[]{:S(2)}) collective-permute-start(f32[168,128]{1,0:T(8,128)S(1)} %get-tuple-element.91), channel_id=1, source_target_pairs={{0,1},{1,0},{2,3},{3,2},{4,5},{5,4},{6,7},{7,6},{8,9},{9,8},{10,11... | collective-permute-start | bytes 258056 | tf_op jit(solution)/shard_map/ppermute | solution.py:596
  60.3 5.1 %collective-permute-start.14 = (f32[168,128]{1,0:T(8,128)S(1)}, f32[168,128]{1,0:T(8,128)S(1)}, u32[]{:S(2)}, u32[]{:S(2)}) collective-permute-start(f32[168,128]{1,0:T(8,128)S(1)} %get-tuple-element.92), channel_id=1, source_target_pairs={{16,32},{32,16},{48,64},{64,48},{80,96},{96,80},{112,128},{128,112... | collective-permute-start | bytes 258056 | tf_op jit(solution)/shard_map/ppermute | solution.py:597
  65.4 1.9 %collective-permute-start.15 = (f32[168,128]{1,0:T(8,128)S(1)}, f32[168,128]{1,0:T(8,128)S(1)}, u32[]{:S(2)}, u32[]{:S(2)}) collective-permute-start(f32[168,128]{1,0:T(8,128)S(1)} %get-tuple-element.93), channel_id=1, source_target_pairs={{0,16},{16,0},{32,48},{48,32},{64,80},{80,64},{96,112},{112,96},{1... | collective-permute-start | bytes 258056 | tf_op jit(solution)/shard_map/ppermute | solution.py:598
  68.6 2.2 %shard_map.128 = (f32[184,512]{1,0:T(8,128)}, f32[184,512]{1,0:T(8,128)S(1)}, f32[184,128]{1,0:T(8,128)S(1)}, f32[184,128]{1,0:T(8,128)S(1)}, f32[184,128]{1,0:T(8,128)S(1)}, /*index=5*/f32[184,128]{1,0:T(8,128)S(1)}) custom-call(s32[3]{0:T(128)S(1)} %pad_add_fusion.place, f32[168,512]{1,0:T(8,128)S(1)} %get-tuple-element.89.t, ...), custom_call_target="tpu_custom_call" | custom-call | flops 1000000 | bytes 1000000 | tf_op jit(solution)/shard_map/pallas_call | solution.py:570
  70.8 5.0 %collective-permute-start.16 = (f32[184,128]{1,0:T(8,128)S(1)}, f32[184,128]{1,0:T(8,128)S(1)}, u32[]{:S(2)}, u32[]{:S(2)}) collective-permute-start(f32[184,128]{1,0:T(8,128)S(1)} %get-tuple-element.95), channel_id=1, source_target_pairs={{0,15},{1,2},{2,1},{3,4},{4,3},{5,6},{6,5},{7,8},{8,7},{9,10},{10,... | collective-permute-start | bytes 282632 | tf_op jit(solution)/shard_map/ppermute | solution.py:595
  75.8 1.9 %collective-permute-start.17 = (f32[184,128]{1,0:T(8,128)S(1)}, f32[184,128]{1,0:T(8,128)S(1)}, u32[]{:S(2)}, u32[]{:S(2)}) collective-permute-start(f32[184,128]{1,0:T(8,128)S(1)} %get-tuple-element.96), channel_id=1, source_target_pairs={{0,1},{1,0},{2,3},{3,2},{4,5},{5,4},{6,7},{7,6},{8,9},{9,8},{10,11... | collective-permute-start | bytes 282632 | tf_op jit(solution)/shard_map/ppermute | solution.py:596
  77.7 3.9 %collective-permute-start.18 = (f32[184,128]{1,0:T(8,128)S(1)}, f32[184,128]{1,0:T(8,128)S(1)}, u32[]{:S(2)}, u32[]{:S(2)}) collective-permute-start(f32[184,128]{1,0:T(8,128)S(1)} %get-tuple-element.97), channel_id=1, source_target_pairs={{16,32},{32,16},{48,64},{64,48},{80,96},{96,80},{112,128},{128,112... | collective-permute-start | bytes 282632 | tf_op jit(solution)/shard_map/ppermute | solution.py:597
  81.6 1.9 %collective-permute-start.19 = (f32[184,128]{1,0:T(8,128)S(1)}, f32[184,128]{1,0:T(8,128)S(1)}, u32[]{:S(2)}, u32[]{:S(2)}) collective-permute-start(f32[184,128]{1,0:T(8,128)S(1)} %get-tuple-element.98), channel_id=1, source_target_pairs={{0,16},{16,0},{32,48},{48,32},{64,80},{80,64},{96,112},{112,96},{1... | collective-permute-start | bytes 282632 | tf_op jit(solution)/shard_map/ppermute | solution.py:598
  84.8 1.6 shard_map.129
  86.4 12.9 %all_to_all.20.got = f32[16,32,128]{2,1,0:T(8,128)S(1)} all-to-all(f32[16,32,128]{2,1,0:T(8,128)S(1)} %get-tuple-element.102), channel_id=1, replica_groups=mesh['axial'=32,'circ'=16] {'circ'}, dimensions={0} | all-to-all | bytes 524288 | tf_op jit(solution)/shard_map/all_to_all | solution.py:603
  100.0 14.2 %all-to-all-start.1 = ((f32[32,16,128]{2,1,0:T(8,128)}), f32[32,16,128]{2,1,0:T(8,128)S(1)}, u32[]{:S(2)}, u32[]{:S(2)}) async-start(f32[32,16,128]{2,1,0:T(8,128)} %shard_map.130.after), calls=%async_computation.1 | async-start | bytes 524288 | tf_op jit(solution)/shard_map/all_to_all | solution.py:603
  115.2 1.5 shard_map.131
  117.5 2.9 %collective-permute-start.20 = (f32[200,128]{1,0:T(8,128)S(1)}, f32[200,128]{1,0:T(8,128)S(1)}, u32[]{:S(2)}, u32[]{:S(2)}) collective-permute-start(f32[200,128]{1,0:T(8,128)S(1)} %get-tuple-element.105), channel_id=1, source_target_pairs={{0,15},{1,2},{2,1},{3,4},{4,3},{5,6},{6,5},{7,8},{8,7},{9,10},{10,... | collective-permute-start | bytes 307208 | tf_op jit(solution)/shard_map/ppermute | solution.py:595
  120.4 1.9 %collective-permute-start.21 = (f32[200,128]{1,0:T(8,128)S(1)}, f32[200,128]{1,0:T(8,128)S(1)}, u32[]{:S(2)}, u32[]{:S(2)}) collective-permute-start(f32[200,128]{1,0:T(8,128)S(1)} %get-tuple-element.106), channel_id=1, source_target_pairs={{0,1},{1,0},{2,3},{3,2},{4,5},{5,4},{6,7},{7,6},{8,9},{9,8},{10,11... | collective-permute-start | bytes 307208 | tf_op jit(solution)/shard_map/ppermute | solution.py:596
  122.3 3.8 %collective-permute-start.22 = (f32[200,128]{1,0:T(8,128)S(1)}, f32[200,128]{1,0:T(8,128)S(1)}, u32[]{:S(2)}, u32[]{:S(2)}) collective-permute-start(f32[200,128]{1,0:T(8,128)S(1)} %get-tuple-element.107), channel_id=1, source_target_pairs={{16,32},{32,16},{48,64},{64,48},{80,96},{96,80},{112,128},{128,112... | collective-permute-start | bytes 307208 | tf_op jit(solution)/shard_map/ppermute | solution.py:597
  126.2 1.9 %collective-permute-start.23 = (f32[200,128]{1,0:T(8,128)S(1)}, f32[200,128]{1,0:T(8,128)S(1)}, u32[]{:S(2)}, u32[]{:S(2)}) collective-permute-start(f32[200,128]{1,0:T(8,128)S(1)} %get-tuple-element.108), channel_id=1, source_target_pairs={{0,16},{16,0},{32,48},{48,32},{64,80},{80,64},{96,112},{112,96},{1... | collective-permute-start | bytes 307208 | tf_op jit(solution)/shard_map/ppermute | solution.py:598
  129.4 6.9 %all-to-all-done.1.mine = f32[32,16,128]{2,1,0:T(8,128)S(1)} async-done(((f32[32,16,128]{2,1,0:T(8,128)}), f32[32,16,128]{2,1,0:T(8,128)S(1)}, u32[]{:S(2)}, u32[]{:S(2)}) %all-to-all-start.1) | async-done | bytes 262176 | tf_op jit(solution)/shard_map/all_to_all | solution.py:603
  136.2 3.1 %collective-permute-start.24 = (f32[32,16,128]{2,1,0:T(8,128)S(1)}, f32[32,16,128]{2,1,0:T(8,128)S(1)}, u32[]{:S(2)}, u32[]{:S(2)}) collective-permute-start(f32[32,16,128]{2,1,0:T(8,128)S(1)} %all-to-all-done.1.mine), channel_id=1, source_target_pairs={{0,16},{16,0},{32,48},{48,32},{64,80},{80,64},{96,112},{112,96},{1... | collective-permute-start | bytes 786440 | tf_op jit(solution)/shard_map/ppermute | solution.py:699
  139.3 1.1 collective-permute-done.24.other
  143.4 4.6 %shard_map.132 = (f32[128,512]{1,0:T(8,128)}, f32[128,512]{1,0:T(8,128)}, f32[128,512]{1,0:T(8,128)}, f32[128,512]{1,0:T(8,128)}, f32[128,512]{1,0:T(8,128)}, /*...) custom-call(s32[3]{0:T(128)S(1)} %pad_add_fusion.place, ...), custom_call_target="tpu_custom_call" | custom-call | flops 1000000 | bytes 1000000 | tf_op jit(solution)/shard_map/pallas_call | solution.py:570
  148.1 9.1 %all_to_all.21.got = f32[16,1,1152]{2,1,0:T(1,128)S(1)} all-to-all(f32[16,1,1152]{2,1,0:T(1,128)S(1)} %get-tuple-element.117), channel_id=1, replica_groups=mesh['axial'=32,'circ'=16] {'circ'}, dimensions={0} | all-to-all | bytes 147456 | tf_op jit(solution)/shard_map/all_to_all | solution.py:603
  157.9 10.2 %all-to-all-start.3 = ((f32[32,1,1152]{2,1,0:T(1,128)}), f32[32,1,1152]{2,1,0:T(1,128)S(1)}, u32[]{:S(2)}, u32[]{:S(2)}) async-start(f32[32,1,1152]{2,1,0:T(1,128)} %shard_map.133), calls=%async_computation.3 | async-start | bytes 294912 | tf_op jit(solution)/shard_map/all_to_all | solution.py:603
  168.1 3.4 %collective-permute-start.25 = (f32[128,128]{1,0:T(8,128)S(1)}, f32[128,128]{1,0:T(8,128)S(1)}, u32[]{:S(2)}, u32[]{:S(2)}) collective-permute-start(f32[128,128]{1,0:T(8,128)S(1)} %get-tuple-element.119), channel_id=1, source_target_pairs={{0,15},{1,2},{2,1},{3,4},{4,3},{5,6},{6,5},{7,8},{8,7},{9,10},{10,... | collective-permute-start | bytes 196616 | tf_op jit(solution)/shard_map/ppermute | solution.py:595
  171.5 1.9 %collective-permute-start.26 = (f32[128,128]{1,0:T(8,128)S(1)}, f32[128,128]{1,0:T(8,128)S(1)}, u32[]{:S(2)}, u32[]{:S(2)}) collective-permute-start(f32[128,128]{1,0:T(8,128)S(1)} %get-tuple-element.120), channel_id=1, source_target_pairs={{0,1},{1,0},{2,3},{3,2},{4,5},{5,4},{6,7},{7,6},{8,9},{9,8},{10,11... | collective-permute-start | bytes 196616 | tf_op jit(solution)/shard_map/ppermute | solution.py:596
  173.4 3.8 %collective-permute-start.27 = (f32[128,128]{1,0:T(8,128)S(1)}, f32[128,128]{1,0:T(8,128)S(1)}, u32[]{:S(2)}, u32[]{:S(2)}) collective-permute-start(f32[128,128]{1,0:T(8,128)S(1)} %get-tuple-element.121), channel_id=1, source_target_pairs={{16,32},{32,16},{48,64},{64,48},{80,96},{96,80},{112,128},{128,112... | collective-permute-start | bytes 196616 | tf_op jit(solution)/shard_map/ppermute | solution.py:597
  177.3 1.9 %collective-permute-start.28 = (f32[128,128]{1,0:T(8,128)S(1)}, f32[128,128]{1,0:T(8,128)S(1)}, u32[]{:S(2)}, u32[]{:S(2)}) collective-permute-start(f32[128,128]{1,0:T(8,128)S(1)} %get-tuple-element.122), channel_id=1, source_target_pairs={{0,16},{16,0},{32,48},{48,32},{64,80},{80,64},{96,112},{112,96},{1... | collective-permute-start | bytes 196616 | tf_op jit(solution)/shard_map/ppermute | solution.py:598
  180.4 4.2 %all-to-all-done.3.got = f32[32,1,1152]{2,1,0:T(1,128)S(1)} async-done(((f32[32,1,1152]{2,1,0:T(1,128)}), f32[32,1,1152]{2,1,0:T(1,128)S(1)}, u32[]{:S(2)}, u32[]{:S(2)}) %all-to-all-start.3) | async-done | bytes 147488 | tf_op jit(solution)/shard_map/all_to_all | solution.py:603
  187.4 2.2 %shard_map.134 = (f32[128,512]{1,0:T(8,128)}, f32[128,512]{1,0:T(8,128)}) custom-call(s32[3]{0:T(128)S(1)} %pad_add_fusion.place, f32[32,1,1152]{2,1,0:T(1,128)S(1)} %all-to-all-done.3.got, f32[128,512]{1,0:T(8,128)S(1)} %get-tuple-element.118.q, f32[128,128]{1,0:T(8,128)S(1)} %collective-permute-done.25.g0, f32[128,128]{1,0:T(8,128)S(1)} %collective-permute-done.26.g1, ...), custom_call_target="tpu_custom_call" | custom-call | flops 1000000 | bytes 1000000 | tf_op jit(solution)/shard_map/pallas_call | solution.py:570
  (52 shorter events, 14.2 us)
Async XLA Ops:
  2.6 19.0 %collective-permute-start = (f32[136,128]{1,0:T(8,128)S(1)}, f32[136,128]{1,0:T(8,128)S(1)}, u32[]{:S(2)}, u32[]{:S(2)}) collective-permute-start(f32[136,128]{1,0:T(8,128)S(1)} %get-tuple-element.67), channel_id=1, source_target_pairs={{0,15},{1,2},{2,1},{3,4},{4,3},{5,6},{6,5},{7,8},{8,7},{9,10},{10,... | collective-permute-start | bytes 208904 | tf_op jit(solution)/shard_map/ppermute | solution.py:595
  10.3 11.4 %collective-permute-start.1 = (f32[136,128]{1,0:T(8,128)S(1)}, f32[136,128]{1,0:T(8,128)S(1)}, u32[]{:S(2)}, u32[]{:S(2)}) collective-permute-start(f32[136,128]{1,0:T(8,128)S(1)} %get-tuple-element.68), channel_id=1, source_target_pairs={{0,1},{1,0},{2,3},{3,2},{4,5},{5,4},{6,7},{7,6},{8,9},{9,8},{10,11... | collective-permute-start | bytes 208904 | tf_op jit(solution)/shard_map/ppermute | solution.py:596
  12.2 9.5 %collective-permute-start.2 = (f32[136,128]{1,0:T(8,128)S(1)}, f32[136,128]{1,0:T(8,128)S(1)}, u32[]{:S(2)}, u32[]{:S(2)}) collective-permute-start(f32[136,128]{1,0:T(8,128)S(1)} %get-tuple-element.69), channel_id=1, source_target_pairs={{16,32},{32,16},{48,64},{64,48},{80,96},{96,80},{112,128},{128,112... | collective-permute-start | bytes 208904 | tf_op jit(solution)/shard_map/ppermute | solution.py:597
  16.6 5.1 %collective-permute-start.3 = (f32[136,128]{1,0:T(8,128)S(1)}, f32[136,128]{1,0:T(8,128)S(1)}, u32[]{:S(2)}, u32[]{:S(2)}) collective-permute-start(f32[136,128]{1,0:T(8,128)S(1)} %get-tuple-element.70), channel_id=1, source_target_pairs={{0,16},{16,0},{32,48},{48,32},{64,80},{80,64},{96,112},{112,96},{1... | collective-permute-start | bytes 208904 | tf_op jit(solution)/shard_map/ppermute | solution.py:598
  22.8 14.1 %collective-permute-start.4 = (f32[136,128]{1,0:T(8,128)S(1)}, f32[136,128]{1,0:T(8,128)S(1)}, u32[]{:S(2)}, u32[]{:S(2)}) collective-permute-start(f32[136,128]{1,0:T(8,128)S(1)} %get-tuple-element.75), channel_id=1, source_target_pairs={{0,15},{1,2},{2,1},{3,4},{4,3},{5,6},{6,5},{7,8},{8,7},{9,10},{10,... | collective-permute-start | bytes 208904 | tf_op jit(solution)/shard_map/ppermute | solution.py:595
  27.2 9.8 %collective-permute-start.5 = (f32[136,128]{1,0:T(8,128)S(1)}, f32[136,128]{1,0:T(8,128)S(1)}, u32[]{:S(2)}, u32[]{:S(2)}) collective-permute-start(f32[136,128]{1,0:T(8,128)S(1)} %get-tuple-element.76), channel_id=1, source_target_pairs={{0,1},{1,0},{2,3},{3,2},{4,5},{5,4},{6,7},{7,6},{8,9},{9,8},{10,11... | collective-permute-start | bytes 208904 | tf_op jit(solution)/shard_map/ppermute | solution.py:596
  29.2 7.8 %collective-permute-start.6 = (f32[136,128]{1,0:T(8,128)S(1)}, f32[136,128]{1,0:T(8,128)S(1)}, u32[]{:S(2)}, u32[]{:S(2)}) collective-permute-start(f32[136,128]{1,0:T(8,128)S(1)} %get-tuple-element.77), channel_id=1, source_target_pairs={{16,32},{32,16},{48,64},{64,48},{80,96},{96,80},{112,128},{128,112... | collective-permute-start | bytes 208904 | tf_op jit(solution)/shard_map/ppermute | solution.py:597
  32.7 4.4 %collective-permute-start.7 = (f32[136,128]{1,0:T(8,128)S(1)}, f32[136,128]{1,0:T(8,128)S(1)}, u32[]{:S(2)}, u32[]{:S(2)}) collective-permute-start(f32[136,128]{1,0:T(8,128)S(1)} %get-tuple-element.78), channel_id=1, source_target_pairs={{0,16},{16,0},{32,48},{48,32},{64,80},{80,64},{96,112},{112,96},{1... | collective-permute-start | bytes 208904 | tf_op jit(solution)/shard_map/ppermute | solution.py:598
  39.2 13.0 %collective-permute-start.8 = (f32[152,128]{1,0:T(8,128)S(1)}, f32[152,128]{1,0:T(8,128)S(1)}, u32[]{:S(2)}, u32[]{:S(2)}) collective-permute-start(f32[152,128]{1,0:T(8,128)S(1)} %get-tuple-element.84), channel_id=1, source_target_pairs={{0,15},{1,2},{2,1},{3,4},{4,3},{5,6},{6,5},{7,8},{8,7},{9,10},{10,... | collective-permute-start | bytes 233480 | tf_op jit(solution)/shard_map/ppermute | solution.py:595
  44.1 8.1 %collective-permute-start.9 = (f32[152,128]{1,0:T(8,128)S(1)}, f32[152,128]{1,0:T(8,128)S(1)}, u32[]{:S(2)}, u32[]{:S(2)}) collective-permute-start(f32[152,128]{1,0:T(8,128)S(1)} %get-tuple-element.85), channel_id=1, source_target_pairs={{0,1},{1,0},{2,3},{3,2},{4,5},{5,4},{6,7},{7,6},{8,9},{9,8},{10,11... | collective-permute-start | bytes 233480 | tf_op jit(solution)/shard_map/ppermute | solution.py:596
  46.1 6.3 %collective-permute-start.10 = (f32[152,128]{1,0:T(8,128)S(1)}, f32[152,128]{1,0:T(8,128)S(1)}, u32[]{:S(2)}, u32[]{:S(2)}) collective-permute-start(f32[152,128]{1,0:T(8,128)S(1)} %get-tuple-element.86), channel_id=1, source_target_pairs={{16,32},{32,16},{48,64},{64,48},{80,96},{96,80},{112,128},{128,112... | collective-permute-start | bytes 233480 | tf_op jit(solution)/shard_map/ppermute | solution.py:597
  50.3 3.2 %collective-permute-start.11 = (f32[152,128]{1,0:T(8,128)S(1)}, f32[152,128]{1,0:T(8,128)S(1)}, u32[]{:S(2)}, u32[]{:S(2)}) collective-permute-start(f32[152,128]{1,0:T(8,128)S(1)} %get-tuple-element.87), channel_id=1, source_target_pairs={{0,16},{16,0},{32,48},{48,32},{64,80},{80,64},{96,112},{112,96},{1... | collective-permute-start | bytes 233480 | tf_op jit(solution)/shard_map/ppermute | solution.py:598
  54.7 12.6 %collective-permute-start.12 = (f32[168,128]{1,0:T(8,128)S(1)}, f32[168,128]{1,0:T(8,128)S(1)}, u32[]{:S(2)}, u32[]{:S(2)}) collective-permute-start(f32[168,128]{1,0:T(8,128)S(1)} %get-tuple-element.90), channel_id=1, source_target_pairs={{0,15},{1,2},{2,1},{3,4},{4,3},{5,6},{6,5},{7,8},{8,7},{9,10},{10,... | collective-permute-start | bytes 258056 | tf_op jit(solution)/shard_map/ppermute | solution.py:595
  58.4 8.9 %collective-permute-start.13 = (f32[168,128]{1,0:T(8,128)S(1)}, f32[168,128]{1,0:T(8,128)S(1)}, u32[]{:S(2)}, u32[]{:S(2)}) collective-permute-start(f32[168,128]{1,0:T(8,128)S(1)} %get-tuple-element.91), channel_id=1, source_target_pairs={{0,1},{1,0},{2,3},{3,2},{4,5},{5,4},{6,7},{7,6},{8,9},{9,8},{10,11... | collective-permute-start | bytes 258056 | tf_op jit(solution)/shard_map/ppermute | solution.py:596
  60.3 7.2 %collective-permute-start.14 = (f32[168,128]{1,0:T(8,128)S(1)}, f32[168,128]{1,0:T(8,128)S(1)}, u32[]{:S(2)}, u32[]{:S(2)}) collective-permute-start(f32[168,128]{1,0:T(8,128)S(1)} %get-tuple-element.92), channel_id=1, source_target_pairs={{16,32},{32,16},{48,64},{64,48},{80,96},{96,80},{112,128},{128,112... | collective-permute-start | bytes 258056 | tf_op jit(solution)/shard_map/ppermute | solution.py:597
  65.4 3.2 %collective-permute-start.15 = (f32[168,128]{1,0:T(8,128)S(1)}, f32[168,128]{1,0:T(8,128)S(1)}, u32[]{:S(2)}, u32[]{:S(2)}) collective-permute-start(f32[168,128]{1,0:T(8,128)S(1)} %get-tuple-element.93), channel_id=1, source_target_pairs={{0,16},{16,0},{32,48},{48,32},{64,80},{80,64},{96,112},{112,96},{1... | collective-permute-start | bytes 258056 | tf_op jit(solution)/shard_map/ppermute | solution.py:598
  70.8 12.7 %collective-permute-start.16 = (f32[184,128]{1,0:T(8,128)S(1)}, f32[184,128]{1,0:T(8,128)S(1)}, u32[]{:S(2)}, u32[]{:S(2)}) collective-permute-start(f32[184,128]{1,0:T(8,128)S(1)} %get-tuple-element.95), channel_id=1, source_target_pairs={{0,15},{1,2},{2,1},{3,4},{4,3},{5,6},{6,5},{7,8},{8,7},{9,10},{10,... | collective-permute-start | bytes 282632 | tf_op jit(solution)/shard_map/ppermute | solution.py:595
  75.8 7.8 %collective-permute-start.17 = (f32[184,128]{1,0:T(8,128)S(1)}, f32[184,128]{1,0:T(8,128)S(1)}, u32[]{:S(2)}, u32[]{:S(2)}) collective-permute-start(f32[184,128]{1,0:T(8,128)S(1)} %get-tuple-element.96), channel_id=1, source_target_pairs={{0,1},{1,0},{2,3},{3,2},{4,5},{5,4},{6,7},{7,6},{8,9},{9,8},{10,11... | collective-permute-start | bytes 282632 | tf_op jit(solution)/shard_map/ppermute | solution.py:596
  77.7 6.1 %collective-permute-start.18 = (f32[184,128]{1,0:T(8,128)S(1)}, f32[184,128]{1,0:T(8,128)S(1)}, u32[]{:S(2)}, u32[]{:S(2)}) collective-permute-start(f32[184,128]{1,0:T(8,128)S(1)} %get-tuple-element.97), channel_id=1, source_target_pairs={{16,32},{32,16},{48,64},{64,48},{80,96},{96,80},{112,128},{128,112... | collective-permute-start | bytes 282632 | tf_op jit(solution)/shard_map/ppermute | solution.py:597
  81.6 3.2 %collective-permute-start.19 = (f32[184,128]{1,0:T(8,128)S(1)}, f32[184,128]{1,0:T(8,128)S(1)}, u32[]{:S(2)}, u32[]{:S(2)}) collective-permute-start(f32[184,128]{1,0:T(8,128)S(1)} %get-tuple-element.98), channel_id=1, source_target_pairs={{0,16},{16,0},{32,48},{48,32},{64,80},{80,64},{96,112},{112,96},{1... | collective-permute-start | bytes 282632 | tf_op jit(solution)/shard_map/ppermute | solution.py:598
  100.0 36.2 %all-to-all-start.1 = ((f32[32,16,128]{2,1,0:T(8,128)}), f32[32,16,128]{2,1,0:T(8,128)S(1)}, u32[]{:S(2)}, u32[]{:S(2)}) async-start(f32[32,16,128]{2,1,0:T(8,128)} %shard_map.130.after), calls=%async_computation.1 | async-start | bytes 524288 | tf_op jit(solution)/shard_map/all_to_all | solution.py:603
  114.2 1.0 copy-start
  115.2 25.2 %copy-start.5 = (f32[152,512]{1,0:T(8,128)S(1)}, f32[152,512]{1,0:T(8,128)}, u32[]{:S(2)}) copy-start(f32[152,512]{1,0:T(8,128)} %get-tuple-element.115.z0) | copy-start | bytes 933892
  116.7 0.8 copy-start.2
  117.5 10.6 %collective-permute-start.20 = (f32[200,128]{1,0:T(8,128)S(1)}, f32[200,128]{1,0:T(8,128)S(1)}, u32[]{:S(2)}, u32[]{:S(2)}) collective-permute-start(f32[200,128]{1,0:T(8,128)S(1)} %get-tuple-element.105), channel_id=1, source_target_pairs={{0,15},{1,2},{2,1},{3,4},{4,3},{5,6},{6,5},{7,8},{8,7},{9,10},{10,... | collective-permute-start | bytes 307208 | tf_op jit(solution)/shard_map/ppermute | solution.py:595
  120.4 7.7 %collective-permute-start.21 = (f32[200,128]{1,0:T(8,128)S(1)}, f32[200,128]{1,0:T(8,128)S(1)}, u32[]{:S(2)}, u32[]{:S(2)}) collective-permute-start(f32[200,128]{1,0:T(8,128)S(1)} %get-tuple-element.106), channel_id=1, source_target_pairs={{0,1},{1,0},{2,3},{3,2},{4,5},{5,4},{6,7},{7,6},{8,9},{9,8},{10,11... | collective-permute-start | bytes 307208 | tf_op jit(solution)/shard_map/ppermute | solution.py:596
  122.3 6.8 %collective-permute-start.22 = (f32[200,128]{1,0:T(8,128)S(1)}, f32[200,128]{1,0:T(8,128)S(1)}, u32[]{:S(2)}, u32[]{:S(2)}) collective-permute-start(f32[200,128]{1,0:T(8,128)S(1)} %get-tuple-element.107), channel_id=1, source_target_pairs={{16,32},{32,16},{48,64},{64,48},{80,96},{96,80},{112,128},{128,112... | collective-permute-start | bytes 307208 | tf_op jit(solution)/shard_map/ppermute | solution.py:597
  126.2 3.2 %collective-permute-start.23 = (f32[200,128]{1,0:T(8,128)S(1)}, f32[200,128]{1,0:T(8,128)S(1)}, u32[]{:S(2)}, u32[]{:S(2)}) collective-permute-start(f32[200,128]{1,0:T(8,128)S(1)} %get-tuple-element.108), channel_id=1, source_target_pairs={{0,16},{16,0},{32,48},{48,32},{64,80},{80,64},{96,112},{112,96},{1... | collective-permute-start | bytes 307208 | tf_op jit(solution)/shard_map/ppermute | solution.py:598
  136.2 4.2 %collective-permute-start.24 = (f32[32,16,128]{2,1,0:T(8,128)S(1)}, f32[32,16,128]{2,1,0:T(8,128)S(1)}, u32[]{:S(2)}, u32[]{:S(2)}) collective-permute-start(f32[32,16,128]{2,1,0:T(8,128)S(1)} %all-to-all-done.1.mine), channel_id=1, source_target_pairs={{0,16},{16,0},{32,48},{48,32},{64,80},{80,64},{96,112},{112,96},{1... | collective-permute-start | bytes 786440 | tf_op jit(solution)/shard_map/ppermute | solution.py:699
  140.4 1.0 copy-start.1
  141.4 1.0 copy-start.3
  142.4 1.0 copy-start.4
  157.2 27.4 %copy-start.6 = (f32[128,512]{1,0:T(8,128)S(1)}, f32[128,512]{1,0:T(8,128)}, u32[]{:S(2)}) copy-start(f32[128,512]{1,0:T(8,128)} %get-tuple-element.123.z0) | copy-start | bytes 786436
  157.2 27.4 %copy-start.7 = (f32[128,512]{1,0:T(8,128)S(1)}, f32[128,512]{1,0:T(8,128)}, u32[]{:S(2)}) copy-start(f32[128,512]{1,0:T(8,128)} %get-tuple-element.124.z1) | copy-start | bytes 786436
  157.9 26.7 %all-to-all-start.3 = ((f32[32,1,1152]{2,1,0:T(1,128)}), f32[32,1,1152]{2,1,0:T(1,128)S(1)}, u32[]{:S(2)}, u32[]{:S(2)}) async-start(f32[32,1,1152]{2,1,0:T(1,128)} %shard_map.133), calls=%async_computation.3 | async-start | bytes 294912 | tf_op jit(solution)/shard_map/all_to_all | solution.py:603
  168.1 11.1 %collective-permute-start.25 = (f32[128,128]{1,0:T(8,128)S(1)}, f32[128,128]{1,0:T(8,128)S(1)}, u32[]{:S(2)}, u32[]{:S(2)}) collective-permute-start(f32[128,128]{1,0:T(8,128)S(1)} %get-tuple-element.119), channel_id=1, source_target_pairs={{0,15},{1,2},{2,1},{3,4},{4,3},{5,6},{6,5},{7,8},{8,7},{9,10},{10,... | collective-permute-start | bytes 196616 | tf_op jit(solution)/shard_map/ppermute | solution.py:595
  171.5 7.7 %collective-permute-start.26 = (f32[128,128]{1,0:T(8,128)S(1)}, f32[128,128]{1,0:T(8,128)S(1)}, u32[]{:S(2)}, u32[]{:S(2)}) collective-permute-start(f32[128,128]{1,0:T(8,128)S(1)} %get-tuple-element.120), channel_id=1, source_target_pairs={{0,1},{1,0},{2,3},{3,2},{4,5},{5,4},{6,7},{7,6},{8,9},{9,8},{10,11... | collective-permute-start | bytes 196616 | tf_op jit(solution)/shard_map/ppermute | solution.py:596
  173.4 6.5 %collective-permute-start.27 = (f32[128,128]{1,0:T(8,128)S(1)}, f32[128,128]{1,0:T(8,128)S(1)}, u32[]{:S(2)}, u32[]{:S(2)}) collective-permute-start(f32[128,128]{1,0:T(8,128)S(1)} %get-tuple-element.121), channel_id=1, source_target_pairs={{16,32},{32,16},{48,64},{64,48},{80,96},{96,80},{112,128},{128,112... | collective-permute-start | bytes 196616 | tf_op jit(solution)/shard_map/ppermute | solution.py:597
  177.3 3.1 %collective-permute-start.28 = (f32[128,128]{1,0:T(8,128)S(1)}, f32[128,128]{1,0:T(8,128)S(1)}, u32[]{:S(2)}, u32[]{:S(2)}) collective-permute-start(f32[128,128]{1,0:T(8,128)S(1)} %get-tuple-element.122), channel_id=1, source_target_pairs={{0,16},{16,0},{32,48},{48,32},{64,80},{80,64},{96,112},{112,96},{1... | collective-permute-start | bytes 196616 | tf_op jit(solution)/shard_map/ppermute | solution.py:598
  184.6 1.0 copy-start.8
  185.5 0.9 copy-start.9
  186.5 0.9 copy-start.10

commit v5 on v4

--- a/solution.py
+++ b/solution.py
@@ -360,11 +360,17 @@
     return tops[::-1]
 
 
-def k_fourth(place, v2, share, neumann, after, t_o, *sends):
+def k_fourth(place, v2, share, neumann, t_o, s0, s1, s2, s3, v2_s, t_s, sem):
     at = Place(place)
-    t = share[...] * product(share[...] * v2[...], held(neumann))
-    t_o[...] = t
-    put_sends(sends, t, at)
+    copy = pltpu.make_async_copy(v2, v2_s, sem.at[0])
+    copy.start()
+    copy.wait()
+    t = share[...] * product(share[...] * v2_s[...], held(neumann))
+    t_s[...] = t
+    copy = pltpu.make_async_copy(t_s, t_o, sem.at[1])
+    copy.start()
+    put_sends((s0, s1, s2, s3), t, at)
+    copy.wait()
 
 
 def lift(coefs, basis):
@@ -383,9 +389,16 @@
 def k_core(
     place, mine, other, t, g0, g1, g2, g3, z0, v1, z1, v2, r, diag, couple, blocks,
     z0_o, z1_o, z2_o, w0_o, w1_o, q_o, pay_o, s0, s1, s2, s3,
-    band0, band1, band2, c0_s, c1_s, c2_s, full_s, sem,
+    band0, band1, band2, c0_s, c1_s, c2_s, full_s, t_s, z0_s, z1_s, v2_s, sem, in_sem,
 ):
     at = Place(place)
+    loads = [
+        pltpu.make_async_copy(source, target, in_sem.at[n])
+        for n, (source, target) in enumerate(((t, t_s), (z1, z1_s), (z0, z0_s), (v2, v2_s)))
+    ]
+    for load in loads:
+        load.start()
+    t, z0, z1, v2 = t_s, z0_s, z1_s, v2_s
     rhs = r.shape[0]
     rows = mine.shape[0]
     width = band0.shape[1]
@@ -439,6 +452,8 @@
     c1 = c1_s[pl.ds(pl.multiple_of(start + 16, 8), 56), :]
     c2 = c2_s[pl.ds(pl.multiple_of(start + 32, 8), 24), :]
     r0 = r[...]
+    for load in loads:
+        load.wait()
     z2 = assembled(t[...], (g0, g1, g2, g3), at, rhs)
     z2f = z2[:rhs] + lift(
         jnp.concatenate([c0, c1, c2], axis=0),
@@ -490,7 +505,13 @@
     return (low + middle) + high
 
 
-def k_final(place, got, q, g0, g1, g2, g3, order, r0, z0, z1, z2, w0, w1, x_o, r_o):
+def k_final(
+    place, got, q, g0, g1, g2, g3, order, r0, z0, z1, z2, w0, w1, x_o, r_o, full_s, sem
+):
+    loads = []
+    for n, source in enumerate((z0, z1, z2, w0, w1)):
+        loads.append(pltpu.make_async_copy(source, full_s.at[n], sem.at[n]))
+        loads[n].start()
     w2 = assembled(q[...], (g0, g1, g2, g3), Place(place), q.shape[0])
     total = summed(got)
     v0z0, v0z1, v1z0, v1z1, v2z1, v0z2, v1z2, v2z2, z2w2 = [
@@ -549,8 +570,10 @@
     columns = mm_t(eye, table)
     col = [columns[:, i : i + 1] for i in range(6)]
     hots = one_hot_faces(order[...])
-    x = col[0] * z0[...] + col[1] * z1[...] + col[2] * z2[...]
-    r = r0[...] + col[3] * w0[...] + col[4] * w1[...] + col[5] * w2
+    for load in loads:
+        load.wait()
+    x = col[0] * full_s[0] + col[1] * full_s[1] + col[2] * full_s[2]
+    r = r0[...] + col[3] * full_s[3] + col[4] * full_s[4] + col[5] * w2
     both = to_points(jnp.concatenate([x, r], axis=0), hots)
     rhs = x.shape[0]
     x_o[...] = both[:rhs]
@@ -586,17 +609,20 @@
     )(*args)
 
 
-def exchange(sends, rows, columns):
+def exchange_columns(sends, columns):
+    near = [(i, i ^ 1) for i in range(columns)]
+    far = [(i, (i + 1 if i % 2 else i - 1) % columns) for i in range(columns)]
+    return [lax.ppermute(sends[0], "circ", far), lax.ppermute(sends[1], "circ", near)]
+
+
+def exchange_rows(sends, rows):
     core = [(i, i ^ 1) for i in range(rows)]
     link = [(i, i + 1 if i % 2 else i - 1) for i in range(1, rows - 1)]
-    near = [(i, i ^ 1) for i in range(columns)]
-    far = [(i, (i + 1 if i % 2 else i - 1) % columns) for i in range(columns)]
-    return [
-        lax.ppermute(sends[0], "circ", far),
-        lax.ppermute(sends[1], "circ", near),
-        lax.ppermute(sends[2], "axial", link),
-        lax.ppermute(sends[3], "axial", core),
-    ]
+    return [lax.ppermute(sends[2], "axial", link), lax.ppermute(sends[3], "axial", core)]
+
+
+def exchange(sends, rows, columns):
+    return exchange_columns(sends, columns) + exchange_rows(sends, rows)
 
 
 def spread(value, axis):
@@ -690,11 +716,16 @@
         raw_outs=(0,), scratch=[pltpu.VMEM((n, points), F32), dma((1,))],
     )
     got = spread(pay, "circ")
+    t2, *sends = call(
+        k_fourth, [(n, points)] + face(n), place, v2, share, neumann,
+        raw=(0,), raw_outs=(0,),
+        scratch=[pltpu.VMEM((n, points), F32)] * 2 + [dma((2,))],
+        flops=500_000_000,
+    )
+    got, t2 = lax.optimization_barrier((got, t2))
     (pay,) = call(k_sum_halves, [(rows, 16, LANES)], None, got, coefs)
+    pay, *sends = lax.optimization_barrier((pay, *sends))
     mine = spread(pay, "axial")
-    t2, *sends = call(
-        k_fourth, [(n, points)] + face(n), place, v2, share, neumann, pay, flops=500_000_000
-    )
     mine, *got = lax.optimization_barrier((mine, *swap(sends)))
     other = lax.ppermute(mine, "axial", [(i, i ^ 1) for i in range(rows)])
     width = max(LANES, 8 * rows)
@@ -702,18 +733,26 @@
         k_core,
         [(rhs, points)] * 6 + [(columns, 1, 9 * LANES)] + face(rhs),
         place, mine, other, t2, *got, z0, v1, z1, v2, r0, diag, couple, blocks,
+        raw=(2, 7, 9, 10),
         raw_outs=(0, 1, 2, 3, 4),
         scratch=[pltpu.VMEM((width, width), F32)] * 3
         + [pltpu.VMEM((width + 80, rhs), F32)] * 3
-        + [pltpu.VMEM((5, rhs, points), F32), dma((5,))],
+        + [pltpu.VMEM((5, rhs, points), F32)]
+        + [pltpu.VMEM((rhs + m, points), F32) for m in (72, 24, 56, 72)]
+        + [dma((5,)), dma((4,))],
     )
     dots = spread(pay, "circ")
-    got = swap(sends)
+    got = exchange_columns(sends, columns)
+    dots, *got = lax.optimization_barrier((dots, *got))
     (pay,) = call(k_sum_spread, [(rows, 1, 9 * LANES)], None, dots)
+    pay, *sends = lax.optimization_barrier((pay, *sends))
     dots = spread(pay, "axial")
+    got = got + exchange_rows(sends, rows)
     x, r = call(
         k_final, [(rhs, points)] * 2,
         place, dots, q2, *got, order, r0, z0f, z1f, z2f, w0f, w1f,
+        raw=(8, 9, 10, 11, 12),
+        scratch=[pltpu.VMEM((5, rhs, points), F32), dma((5,))],
     )
     return (x[None, None], r[None, None])
 

time: 191 us -> 191 us (level)
  blocking collectives: 22 us -> 0 us
  waiting for transfers between devices: 18.3 us -> 34.4 us
  starting transfers between devices: 115 us -> 123 us
  local copies, waits for them, and re-layouts: 7.61 us -> 1.28 us
  Pallas kernels: 25.6 us -> 30.2 us
    all_to_all x2 -> x0, blocking collectives: 22 us -> none  [spread(): return lax.all_to_all(value, axis, split_axis=0, concat_axis=0, tiled=True)]
    all_to_all x2 -> x4, waiting for transfers between devices: 11 us -> 20.2 us  [spread(): return lax.all_to_all(value, axis, split_axis=0, concat_axis=0, tiled=True)]
    ppermute x28, waiting for transfers between devices: 6.18 us -> 13 us  [the longest x7 6.82 us: exchange_rows(): lax.ppermute(sends[2], 'axial', link)]
    unnamed x22 -> x8, local copies, waits for them, and re-layouts: 7.61 us -> 1.28 us
    all_to_all x2 -> x4, starting transfers between devices: 24.4 us -> 29.5 us  [spread(): return lax.all_to_all(value, axis, split_axis=0, concat_axis=0, tiled=True)]
    pallas_call x13, Pallas kernels: 25.6 us -> 30.2 us  [call(): pl.pallas_call(body, out_shape=[out if isinstance(out, jax.ShapeDtypeStru...]
    ppermute x28, starting transfers between devices: 87.4 us -> 90.3 us  [the longest x7 35.1 us: exchange_columns(): lax.ppermute(sends[0], 'circ', far)]
  transfers between devices with their start and end apart: 31 -> 33, of which waited for: 13 -> 13; matrix products, arithmetic and copies ran while one was open for 0% -> 0% of each run, Pallas kernels for 4% -> 4%
where the time goes in v5:
time: 191 us; the launch traced here: 190 us
  starting transfers between devices  123 us (64%)
  waiting for transfers between devices  34.4 us (18%)
  Pallas kernels  30.2 us (16%)
    ppermute x7, starting transfers between devices, exchange_columns(): lax.ppermute(sends[0], 'circ', far)  35.1 us
    pallas_call x13, Pallas kernels, call(): pl.pallas_call(body, out_shape=[out if isinstance(out, jax.ShapeDtypeStru...  30.2 us
    all_to_all x4, starting transfers between devices, spread(): return lax.all_to_all(value, axis, split_axis=0, concat_axis=0, tiled=True)  29.5 us
    ppermute x7, starting transfers between devices, exchange_rows(): lax.ppermute(sends[2], 'axial', link)  28.4 us
    all_to_all x4, waiting for transfers between devices, spread(): return lax.all_to_all(value, axis, split_axis=0, concat_axis=0, tiled=True)  20.2 us
    ppermute x7, starting transfers between devices, exchange_columns(): lax.ppermute(sends[1], 'circ', near)  13.4 us
    ppermute x7, starting transfers between devices, exchange_rows(): lax.ppermute(sends[3], 'axial', core)  13.4 us
    ppermute x7, waiting for transfers between devices, exchange_rows(): lax.ppermute(sends[2], 'axial', link)  6.82 us
  transfers between devices with their start and end apart: 33, of which 13 were waited for; matrix products, arithmetic and copies ran while one was open for 0% of the time, Pallas kernels for 4%

profile of v5, /device:TPU:1, one launch (start us, length us, event | category | flops | bytes accessed | tf_op | source)
XLA Modules:
  0.0 190.1 jit_solution(7749320445043851776)
XLA Ops:
  0.7 1.9 %shard_map.122 = (f32[136,512]{1,0:T(8,128)S(1)}, s32[1,512]{1,0:T(1,128)S(1)}, f32[136,128]{1,0:T(8,128)S(1)}, f32[136,128]{1,0:T(8,128)S(1)}, f32[136,128]{1,0:T(8,128)S(1)}, /*index=5*/f32[136,128]{1,0:T(8,128)S(1)}) custom-call(s32[3]{0:T(128)S(1)} %pad_add_fusion.place, f32[128,512]{1,0:T(8,128)} %bitcast.13, f32[1,512]{1,0:T(1,128)} %bitcast.14, ...), custom_call_target="tpu_custom_call" | custom-call | flops 1000000 | bytes 1000000 | tf_op jit(solution)/shard_map/pallas_call | solution.py:593
  2.6 7.7 %collective-permute-start = (f32[136,128]{1,0:T(8,128)S(1)}, f32[136,128]{1,0:T(8,128)S(1)}, u32[]{:S(2)}, u32[]{:S(2)}) collective-permute-start(f32[136,128]{1,0:T(8,128)S(1)} %get-tuple-element.80), channel_id=1, source_target_pairs={{0,15},{1,2},{2,1},{3,4},{4,3},{5,6},{6,5},{7,8},{8,7},{9,10},{10,... | collective-permute-start | bytes 208904 | tf_op jit(solution)/shard_map/ppermute | solution.py:615
  10.3 1.9 %collective-permute-start.1 = (f32[136,128]{1,0:T(8,128)S(1)}, f32[136,128]{1,0:T(8,128)S(1)}, u32[]{:S(2)}, u32[]{:S(2)}) collective-permute-start(f32[136,128]{1,0:T(8,128)S(1)} %get-tuple-element.81), channel_id=1, source_target_pairs={{0,1},{1,0},{2,3},{3,2},{4,5},{5,4},{6,7},{7,6},{8,9},{9,8},{10,11... | collective-permute-start | bytes 208904 | tf_op jit(solution)/shard_map/ppermute | solution.py:615
  12.2 4.4 %collective-permute-start.2 = (f32[136,128]{1,0:T(8,128)S(1)}, f32[136,128]{1,0:T(8,128)S(1)}, u32[]{:S(2)}, u32[]{:S(2)}) collective-permute-start(f32[136,128]{1,0:T(8,128)S(1)} %get-tuple-element.82), channel_id=1, source_target_pairs={{16,32},{32,16},{48,64},{64,48},{80,96},{96,80},{112,128},{128,112... | collective-permute-start | bytes 208904 | tf_op jit(solution)/shard_map/ppermute | solution.py:621
  16.6 1.9 %collective-permute-start.3 = (f32[136,128]{1,0:T(8,128)S(1)}, f32[136,128]{1,0:T(8,128)S(1)}, u32[]{:S(2)}, u32[]{:S(2)}) collective-permute-start(f32[136,128]{1,0:T(8,128)S(1)} %get-tuple-element.83), channel_id=1, source_target_pairs={{0,16},{16,0},{32,48},{48,32},{64,80},{80,64},{96,112},{112,96},{1... | collective-permute-start | bytes 208904 | tf_op jit(solution)/shard_map/ppermute | solution.py:621
  18.6 3.1 %shard_map.123 = (bf16[2,512,512]{2,1,0:T(8,128)(2,1)S(1)}, f32[8,512]{1,0:T(8,128)S(1)}) custom-call(s32[1,512]{1,0:T(1,128)S(1)} %get-tuple-element.84.order, f32[512,512]{1,0:T(8,128)} %bitcast.16, s32[8,64]{1,0:T(8,128)} %bitcast.21), custom_call_target="tpu_custom_call" | custom-call | flops 2000000000 | bytes 1000000 | tf_op jit(solution)/shard_map/pallas_call | solution.py:593
  22.8 4.4 %collective-permute-start.4 = (f32[136,128]{1,0:T(8,128)S(1)}, f32[136,128]{1,0:T(8,128)S(1)}, u32[]{:S(2)}, u32[]{:S(2)}) collective-permute-start(f32[136,128]{1,0:T(8,128)S(1)} %get-tuple-element.88), channel_id=1, source_target_pairs={{0,15},{1,2},{2,1},{3,4},{4,3},{5,6},{6,5},{7,8},{8,7},{9,10},{10,... | collective-permute-start | bytes 208904 | tf_op jit(solution)/shard_map/ppermute | solution.py:615
  27.2 1.9 %collective-permute-start.5 = (f32[136,128]{1,0:T(8,128)S(1)}, f32[136,128]{1,0:T(8,128)S(1)}, u32[]{:S(2)}, u32[]{:S(2)}) collective-permute-start(f32[136,128]{1,0:T(8,128)S(1)} %get-tuple-element.89), channel_id=1, source_target_pairs={{0,1},{1,0},{2,3},{3,2},{4,5},{5,4},{6,7},{7,6},{8,9},{9,8},{10,11... | collective-permute-start | bytes 208904 | tf_op jit(solution)/shard_map/ppermute | solution.py:615
  29.2 3.5 %collective-permute-start.6 = (f32[136,128]{1,0:T(8,128)S(1)}, f32[136,128]{1,0:T(8,128)S(1)}, u32[]{:S(2)}, u32[]{:S(2)}) collective-permute-start(f32[136,128]{1,0:T(8,128)S(1)} %get-tuple-element.90), channel_id=1, source_target_pairs={{16,32},{32,16},{48,64},{64,48},{80,96},{96,80},{112,128},{128,112... | collective-permute-start | bytes 208904 | tf_op jit(solution)/shard_map/ppermute | solution.py:621
  32.7 1.9 %collective-permute-start.7 = (f32[136,128]{1,0:T(8,128)S(1)}, f32[136,128]{1,0:T(8,128)S(1)}, u32[]{:S(2)}, u32[]{:S(2)}) collective-permute-start(f32[136,128]{1,0:T(8,128)S(1)} %get-tuple-element.91), channel_id=1, source_target_pairs={{0,16},{16,0},{32,48},{48,32},{64,80},{80,64},{96,112},{112,96},{1... | collective-permute-start | bytes 208904 | tf_op jit(solution)/shard_map/ppermute | solution.py:621
  34.6 2.4 %shard_map.125 = (f32[1,512]{1,0:T(1,128)S(1)}, bf16[2,512,512]{2,1,0:T(8,128)(2,1)S(1)}, bf16[2,4,128,128]{3,2,1,0:T(8,128)(2,1)S(1)}, f32[32,128]{1,0:T(8,128)S(1)}) custom-call(s32[1,512]{1,0:T(1,128)S(1)} %get-tuple-element.84.order, f32[1,512]{1,0:T(1,128)S(1)} %get-tuple-element.92.after.share, f32[1,512]{1,0:T(1,128)} %bitcast.23, ...), custom_call_target="tpu_custom_call" | custom-call | flops 2000000000 | bytes 1000000 | tf_op jit(solution)/shard_map/pallas_call | solution.py:593
  37.0 2.1 %shard_map.126 = (f32[152,512]{1,0:T(8,128)}, f32[152,512]{1,0:T(8,128)S(1)}, f32[152,128]{1,0:T(8,128)S(1)}, f32[152,128]{1,0:T(8,128)S(1)}, f32[152,128]{1,0:T(8,128)S(1)}, /*index=5*/f32[152,128]{1,0:T(8,128)S(1)}) custom-call(s32[3]{0:T(128)S(1)} %pad_add_fusion.place, f32[136,512]{1,0:T(8,128)S(1)} %get-tuple-element.87.t, ...), custom_call_target="tpu_custom_call" | custom-call | flops 1000000 | bytes 1000000 | tf_op jit(solution)/shard_map/pallas_call | solution.py:593
  39.2 5.0 %collective-permute-start.8 = (f32[152,128]{1,0:T(8,128)S(1)}, f32[152,128]{1,0:T(8,128)S(1)}, u32[]{:S(2)}, u32[]{:S(2)}) collective-permute-start(f32[152,128]{1,0:T(8,128)S(1)} %get-tuple-element.97), channel_id=1, source_target_pairs={{0,15},{1,2},{2,1},{3,4},{4,3},{5,6},{6,5},{7,8},{8,7},{9,10},{10,... | collective-permute-start | bytes 233480 | tf_op jit(solution)/shard_map/ppermute | solution.py:615
  44.1 1.9 %collective-permute-start.9 = (f32[152,128]{1,0:T(8,128)S(1)}, f32[152,128]{1,0:T(8,128)S(1)}, u32[]{:S(2)}, u32[]{:S(2)}) collective-permute-start(f32[152,128]{1,0:T(8,128)S(1)} %get-tuple-element.98), channel_id=1, source_target_pairs={{0,1},{1,0},{2,3},{3,2},{4,5},{5,4},{6,7},{7,6},{8,9},{9,8},{10,11... | collective-permute-start | bytes 233480 | tf_op jit(solution)/shard_map/ppermute | solution.py:615
  46.1 4.2 %collective-permute-start.10 = (f32[152,128]{1,0:T(8,128)S(1)}, f32[152,128]{1,0:T(8,128)S(1)}, u32[]{:S(2)}, u32[]{:S(2)}) collective-permute-start(f32[152,128]{1,0:T(8,128)S(1)} %get-tuple-element.99), channel_id=1, source_target_pairs={{16,32},{32,16},{48,64},{64,48},{80,96},{96,80},{112,128},{128,112... | collective-permute-start | bytes 233480 | tf_op jit(solution)/shard_map/ppermute | solution.py:621
  50.3 1.9 %collective-permute-start.11 = (f32[152,128]{1,0:T(8,128)S(1)}, f32[152,128]{1,0:T(8,128)S(1)}, u32[]{:S(2)}, u32[]{:S(2)}) collective-permute-start(f32[152,128]{1,0:T(8,128)S(1)} %get-tuple-element.100), channel_id=1, source_target_pairs={{0,16},{16,0},{32,48},{48,32},{64,80},{80,64},{96,112},{112,96},{1... | collective-permute-start | bytes 233480 | tf_op jit(solution)/shard_map/ppermute | solution.py:621
  54.7 3.6 %collective-permute-start.12 = (f32[168,128]{1,0:T(8,128)S(1)}, f32[168,128]{1,0:T(8,128)S(1)}, u32[]{:S(2)}, u32[]{:S(2)}) collective-permute-start(f32[168,128]{1,0:T(8,128)S(1)} %get-tuple-element.103), channel_id=1, source_target_pairs={{0,15},{1,2},{2,1},{3,4},{4,3},{5,6},{6,5},{7,8},{8,7},{9,10},{10,... | collective-permute-start | bytes 258056 | tf_op jit(solution)/shard_map/ppermute | solution.py:615
  58.4 1.9 %collective-permute-start.13 = (f32[168,128]{1,0:T(8,128)S(1)}, f32[168,128]{1,0:T(8,128)S(1)}, u32[]{:S(2)}, u32[]{:S(2)}) collective-permute-start(f32[168,128]{1,0:T(8,128)S(1)} %get-tuple-element.104), channel_id=1, source_target_pairs={{0,1},{1,0},{2,3},{3,2},{4,5},{5,4},{6,7},{7,6},{8,9},{9,8},{10,11... | collective-permute-start | bytes 258056 | tf_op jit(solution)/shard_map/ppermute | solution.py:615
  60.3 5.1 %collective-permute-start.14 = (f32[168,128]{1,0:T(8,128)S(1)}, f32[168,128]{1,0:T(8,128)S(1)}, u32[]{:S(2)}, u32[]{:S(2)}) collective-permute-start(f32[168,128]{1,0:T(8,128)S(1)} %get-tuple-element.105), channel_id=1, source_target_pairs={{16,32},{32,16},{48,64},{64,48},{80,96},{96,80},{112,128},{128,112... | collective-permute-start | bytes 258056 | tf_op jit(solution)/shard_map/ppermute | solution.py:621
  65.4 1.9 %collective-permute-start.15 = (f32[168,128]{1,0:T(8,128)S(1)}, f32[168,128]{1,0:T(8,128)S(1)}, u32[]{:S(2)}, u32[]{:S(2)}) collective-permute-start(f32[168,128]{1,0:T(8,128)S(1)} %get-tuple-element.106), channel_id=1, source_target_pairs={{0,16},{16,0},{32,48},{48,32},{64,80},{80,64},{96,112},{112,96},{1... | collective-permute-start | bytes 258056 | tf_op jit(solution)/shard_map/ppermute | solution.py:621
  68.6 2.2 %shard_map.128 = (f32[184,512]{1,0:T(8,128)}, f32[184,512]{1,0:T(8,128)S(1)}, f32[184,128]{1,0:T(8,128)S(1)}, f32[184,128]{1,0:T(8,128)S(1)}, f32[184,128]{1,0:T(8,128)S(1)}, /*index=5*/f32[184,128]{1,0:T(8,128)S(1)}) custom-call(s32[3]{0:T(128)S(1)} %pad_add_fusion.place, f32[168,512]{1,0:T(8,128)S(1)} %get-tuple-element.102.t, ...), custom_call_target="tpu_custom_call" | custom-call | flops 1000000 | bytes 1000000 | tf_op jit(solution)/shard_map/pallas_call | solution.py:593
  70.8 5.0 %collective-permute-start.16 = (f32[184,128]{1,0:T(8,128)S(1)}, f32[184,128]{1,0:T(8,128)S(1)}, u32[]{:S(2)}, u32[]{:S(2)}) collective-permute-start(f32[184,128]{1,0:T(8,128)S(1)} %get-tuple-element.108), channel_id=1, source_target_pairs={{0,15},{1,2},{2,1},{3,4},{4,3},{5,6},{6,5},{7,8},{8,7},{9,10},{10,... | collective-permute-start | bytes 282632 | tf_op jit(solution)/shard_map/ppermute | solution.py:615
  75.8 1.9 %collective-permute-start.17 = (f32[184,128]{1,0:T(8,128)S(1)}, f32[184,128]{1,0:T(8,128)S(1)}, u32[]{:S(2)}, u32[]{:S(2)}) collective-permute-start(f32[184,128]{1,0:T(8,128)S(1)} %get-tuple-element.109), channel_id=1, source_target_pairs={{0,1},{1,0},{2,3},{3,2},{4,5},{5,4},{6,7},{7,6},{8,9},{9,8},{10,11... | collective-permute-start | bytes 282632 | tf_op jit(solution)/shard_map/ppermute | solution.py:615
  77.7 3.9 %collective-permute-start.18 = (f32[184,128]{1,0:T(8,128)S(1)}, f32[184,128]{1,0:T(8,128)S(1)}, u32[]{:S(2)}, u32[]{:S(2)}) collective-permute-start(f32[184,128]{1,0:T(8,128)S(1)} %get-tuple-element.110), channel_id=1, source_target_pairs={{16,32},{32,16},{48,64},{64,48},{80,96},{96,80},{112,128},{128,112... | collective-permute-start | bytes 282632 | tf_op jit(solution)/shard_map/ppermute | solution.py:621
  81.6 1.9 %collective-permute-start.19 = (f32[184,128]{1,0:T(8,128)S(1)}, f32[184,128]{1,0:T(8,128)S(1)}, u32[]{:S(2)}, u32[]{:S(2)}) collective-permute-start(f32[184,128]{1,0:T(8,128)S(1)} %get-tuple-element.111), channel_id=1, source_target_pairs={{0,16},{16,0},{32,48},{48,32},{64,80},{80,64},{96,112},{112,96},{1... | collective-permute-start | bytes 282632 | tf_op jit(solution)/shard_map/ppermute | solution.py:621
  84.8 2.3 %shard_map.129 = (f32[200,512]{1,0:T(8,128)}, f32[16,32,128]{2,1,0:T(8,128)}) custom-call(s32[3]{0:T(128)S(1)} %pad_add_fusion.place, f32[184,512]{1,0:T(8,128)S(1)} %get-tuple-element.107.q, f32[184,128]{1,0:T(8,128)S(1)} %collective-permute-done.16.g0, f32[184,128]{1,0:T(8,128)S(1)} %collective-permute-done.17.g1, ...), custom_call_target="tpu_custom_call" | custom-call | flops 1000000 | bytes 1000000 | tf_op jit(solution)/shard_map/pallas_call | solution.py:593
  87.1 4.8 %all-to-all-start = ((f32[16,32,128]{2,1,0:T(8,128)}), f32[16,32,128]{2,1,0:T(8,128)S(1)}, u32[]{:S(2)}, u32[]{:S(2)}) async-start(f32[16,32,128]{2,1,0:T(8,128)} %get-tuple-element.115), calls=%async_computation | async-start | bytes 524288 | tf_op jit(solution)/shard_map/all_to_all | solution.py:629
  91.9 2.8 %shard_map.130 = (f32[200,512]{1,0:T(8,128)}, f32[200,128]{1,0:T(8,128)S(1)}, f32[200,128]{1,0:T(8,128)S(1)}, f32[200,128]{1,0:T(8,128)S(1)}, f32[200,128]{1,0:T(8,128)S(1)}) custom-call(s32[3]{0:T(128)S(1)} %pad_add_fusion.place, f32[200,512]{1,0:T(8,128)} %get-tuple-element.116.v2, f32[1,512]{1,0:T(1,128)S(1)} %get-tuple-element.92.after.share, ...), custom_call_target="tpu_custom_call" | custom-call | flops 500000000 | bytes 1000000 | tf_op jit(solution)/shard_map/pallas_call | solution.py:593
  96.0 4.2 %all-to-all-done.got = f32[16,32,128]{2,1,0:T(8,128)S(1)} async-done(((f32[16,32,128]{2,1,0:T(8,128)}), f32[16,32,128]{2,1,0:T(8,128)S(1)}, u32[]{:S(2)}, u32[]{:S(2)}) %all-to-all-start) | async-done | bytes 262176 | tf_op jit(solution)/shard_map/all_to_all | solution.py:629
  101.0 14.3 %all-to-all-start.1 = ((f32[32,16,128]{2,1,0:T(8,128)}), f32[32,16,128]{2,1,0:T(8,128)S(1)}, u32[]{:S(2)}, u32[]{:S(2)}) async-start(f32[32,16,128]{2,1,0:T(8,128)} %shard_map.131), calls=%async_computation.1 | async-start | bytes 524288 | tf_op jit(solution)/shard_map/all_to_all | solution.py:629
  115.3 2.9 %collective-permute-start.20 = (f32[200,128]{1,0:T(8,128)S(1)}, f32[200,128]{1,0:T(8,128)S(1)}, u32[]{:S(2)}, u32[]{:S(2)}) collective-permute-start(f32[200,128]{1,0:T(8,128)S(1)} %copy-done.3), channel_id=1, source_target_pairs={{0,15},{1,2},{2,1},{3,4},{4,3},{5,6},{6,5},{7,8},{8,7},{9,10},{10,... | collective-permute-start | bytes 307208 | tf_op jit(solution)/shard_map/ppermute | solution.py:615
  118.2 1.9 %collective-permute-start.21 = (f32[200,128]{1,0:T(8,128)S(1)}, f32[200,128]{1,0:T(8,128)S(1)}, u32[]{:S(2)}, u32[]{:S(2)}) collective-permute-start(f32[200,128]{1,0:T(8,128)S(1)} %copy-done.1), channel_id=1, source_target_pairs={{0,1},{1,0},{2,3},{3,2},{4,5},{5,4},{6,7},{7,6},{8,9},{9,8},{10,11... | collective-permute-start | bytes 307208 | tf_op jit(solution)/shard_map/ppermute | solution.py:615
  120.1 3.8 %collective-permute-start.22 = (f32[200,128]{1,0:T(8,128)S(1)}, f32[200,128]{1,0:T(8,128)S(1)}, u32[]{:S(2)}, u32[]{:S(2)}) collective-permute-start(f32[200,128]{1,0:T(8,128)S(1)} %get-tuple-element.127), channel_id=1, source_target_pairs={{16,32},{32,16},{48,64},{64,48},{80,96},{96,80},{112,128},{128,112... | collective-permute-start | bytes 307208 | tf_op jit(solution)/shard_map/ppermute | solution.py:621
  124.0 1.9 %collective-permute-start.23 = (f32[200,128]{1,0:T(8,128)S(1)}, f32[200,128]{1,0:T(8,128)S(1)}, u32[]{:S(2)}, u32[]{:S(2)}) collective-permute-start(f32[200,128]{1,0:T(8,128)S(1)} %get-tuple-element.128), channel_id=1, source_target_pairs={{0,16},{16,0},{32,48},{48,32},{64,80},{80,64},{96,112},{112,96},{1... | collective-permute-start | bytes 307208 | tf_op jit(solution)/shard_map/ppermute | solution.py:621
  125.9 3.4 %collective-permute-done.22.g2 = f32[200,128]{1,0:T(8,128)S(1)} collective-permute-done((f32[200,128]{1,0:T(8,128)S(1)}, f32[200,128]{1,0:T(8,128)S(1)}, u32[]{:S(2)}, u32[]{:S(2)}) %collective-permute-start.22) | collective-permute-done | bytes 102432 | tf_op jit(solution)/shard_map/ppermute | solution.py:621
  129.4 7.7 %all-to-all-done.1.mine = f32[32,16,128]{2,1,0:T(8,128)S(1)} async-done(((f32[32,16,128]{2,1,0:T(8,128)}), f32[32,16,128]{2,1,0:T(8,128)S(1)}, u32[]{:S(2)}, u32[]{:S(2)}) %all-to-all-start.1) | async-done | bytes 262176 | tf_op jit(solution)/shard_map/all_to_all | solution.py:629
  137.1 3.3 %collective-permute-start.24 = (f32[32,16,128]{2,1,0:T(8,128)S(1)}, f32[32,16,128]{2,1,0:T(8,128)S(1)}, u32[]{:S(2)}, u32[]{:S(2)}) collective-permute-start(f32[32,16,128]{2,1,0:T(8,128)S(1)} %all-to-all-done.1.mine), channel_id=1, source_target_pairs={{0,16},{16,0},{32,48},{48,32},{64,80},{80,64},{96,112},{112,96},{1... | collective-permute-start | bytes 786440 | tf_op jit(solution)/shard_map/ppermute | solution.py:730
  141.5 6.1 %shard_map.132 = (f32[128,512]{1,0:T(8,128)}, f32[128,512]{1,0:T(8,128)}, f32[128,512]{1,0:T(8,128)}, f32[128,512]{1,0:T(8,128)}, f32[128,512]{1,0:T(8,128)}, /*...) custom-call(s32[3]{0:T(128)S(1)} %pad_add_fusion.place, ...), custom_call_target="tpu_custom_call" | custom-call | flops 1000000 | bytes 1000000 | tf_op jit(solution)/shard_map/pallas_call | solution.py:593
  147.6 3.5 %all-to-all-start.2 = ((f32[16,1,1152]{2,1,0:T(1,128)}), f32[16,1,1152]{2,1,0:T(1,128)S(1)}, u32[]{:S(2)}, u32[]{:S(2)}) async-start(f32[16,1,1152]{2,1,0:T(1,128)} %get-tuple-element.137), calls=%async_computation.2 | async-start | bytes 147456 | tf_op jit(solution)/shard_map/all_to_all | solution.py:629
  151.2 6.6 %collective-permute-start.25 = (f32[128,128]{1,0:T(8,128)S(1)}, f32[128,128]{1,0:T(8,128)S(1)}, u32[]{:S(2)}, u32[]{:S(2)}) collective-permute-start(f32[128,128]{1,0:T(8,128)S(1)} %get-tuple-element.138), channel_id=1, source_target_pairs={{0,15},{1,2},{2,1},{3,4},{4,3},{5,6},{6,5},{7,8},{8,7},{9,10},{10,... | collective-permute-start | bytes 196616 | tf_op jit(solution)/shard_map/ppermute | solution.py:615
  157.7 1.9 %collective-permute-start.26 = (f32[128,128]{1,0:T(8,128)S(1)}, f32[128,128]{1,0:T(8,128)S(1)}, u32[]{:S(2)}, u32[]{:S(2)}) collective-permute-start(f32[128,128]{1,0:T(8,128)S(1)} %get-tuple-element.139), channel_id=1, source_target_pairs={{0,1},{1,0},{2,3},{3,2},{4,5},{5,4},{6,7},{7,6},{8,9},{9,8},{10,11... | collective-permute-start | bytes 196616 | tf_op jit(solution)/shard_map/ppermute | solution.py:615
  159.7 3.1 %collective-permute-done.26.g1 = f32[128,128]{1,0:T(8,128)S(1)} collective-permute-done((f32[128,128]{1,0:T(8,128)S(1)}, f32[128,128]{1,0:T(8,128)S(1)}, u32[]{:S(2)}, u32[]{:S(2)}) %collective-permute-start.26) | collective-permute-done | bytes 65568 | tf_op jit(solution)/shard_map/ppermute | solution.py:615
  163.4 6.9 %all-to-all-start.3 = ((f32[32,1,1152]{2,1,0:T(1,128)}), f32[32,1,1152]{2,1,0:T(1,128)S(1)}, u32[]{:S(2)}, u32[]{:S(2)}) async-start(f32[32,1,1152]{2,1,0:T(1,128)} %shard_map.133), calls=%async_computation.3 | async-start | bytes 294912 | tf_op jit(solution)/shard_map/all_to_all | solution.py:629
  170.3 3.5 %collective-permute-start.27 = (f32[128,128]{1,0:T(8,128)S(1)}, f32[128,128]{1,0:T(8,128)S(1)}, u32[]{:S(2)}, u32[]{:S(2)}) collective-permute-start(f32[128,128]{1,0:T(8,128)S(1)} %get-tuple-element.147), channel_id=1, source_target_pairs={{16,32},{32,16},{48,64},{64,48},{80,96},{96,80},{112,128},{128,112... | collective-permute-start | bytes 196616 | tf_op jit(solution)/shard_map/ppermute | solution.py:621
  173.9 1.9 %collective-permute-start.28 = (f32[128,128]{1,0:T(8,128)S(1)}, f32[128,128]{1,0:T(8,128)S(1)}, u32[]{:S(2)}, u32[]{:S(2)}) collective-permute-start(f32[128,128]{1,0:T(8,128)S(1)} %get-tuple-element.148), channel_id=1, source_target_pairs={{0,16},{16,0},{32,48},{48,32},{64,80},{80,64},{96,112},{112,96},{1... | collective-permute-start | bytes 196616 | tf_op jit(solution)/shard_map/ppermute | solution.py:621
  175.8 2.8 %collective-permute-done.27.g2 = f32[128,128]{1,0:T(8,128)S(1)} collective-permute-done((f32[128,128]{1,0:T(8,128)S(1)}, f32[128,128]{1,0:T(8,128)S(1)}, u32[]{:S(2)}, u32[]{:S(2)}) %collective-permute-start.27) | collective-permute-done | bytes 65568 | tf_op jit(solution)/shard_map/ppermute | solution.py:621
  178.5 8.3 %all-to-all-done.3.got = f32[32,1,1152]{2,1,0:T(1,128)S(1)} async-done(((f32[32,1,1152]{2,1,0:T(1,128)}), f32[32,1,1152]{2,1,0:T(1,128)S(1)}, u32[]{:S(2)}, u32[]{:S(2)}) %all-to-all-start.3) | async-done | bytes 147488 | tf_op jit(solution)/shard_map/all_to_all | solution.py:629
  186.8 3.3 %shard_map.134 = (f32[128,512]{1,0:T(8,128)}, f32[128,512]{1,0:T(8,128)}) custom-call(s32[3]{0:T(128)S(1)} %pad_add_fusion.place, f32[32,1,1152]{2,1,0:T(1,128)S(1)} %all-to-all-done.3.got, f32[128,512]{1,0:T(8,128)S(1)} %get-tuple-element.144.q, f32[128,128]{1,0:T(8,128)S(1)} %collective-permute-done.25.g0, f32[128,128]{1,0:T(8,128)S(1)} %collective-permute-done.26.g1, ...), custom_call_target="tpu_custom_call" | custom-call | flops 1000000 | bytes 1000000 | tf_op jit(solution)/shard_map/pallas_call | solution.py:593
  (40 shorter events, 10.1 us)
Async XLA Ops:
  2.6 19.0 %collective-permute-start = (f32[136,128]{1,0:T(8,128)S(1)}, f32[136,128]{1,0:T(8,128)S(1)}, u32[]{:S(2)}, u32[]{:S(2)}) collective-permute-start(f32[136,128]{1,0:T(8,128)S(1)} %get-tuple-element.80), channel_id=1, source_target_pairs={{0,15},{1,2},{2,1},{3,4},{4,3},{5,6},{6,5},{7,8},{8,7},{9,10},{10,... | collective-permute-start | bytes 208904 | tf_op jit(solution)/shard_map/ppermute | solution.py:615
  10.3 11.4 %collective-permute-start.1 = (f32[136,128]{1,0:T(8,128)S(1)}, f32[136,128]{1,0:T(8,128)S(1)}, u32[]{:S(2)}, u32[]{:S(2)}) collective-permute-start(f32[136,128]{1,0:T(8,128)S(1)} %get-tuple-element.81), channel_id=1, source_target_pairs={{0,1},{1,0},{2,3},{3,2},{4,5},{5,4},{6,7},{7,6},{8,9},{9,8},{10,11... | collective-permute-start | bytes 208904 | tf_op jit(solution)/shard_map/ppermute | solution.py:615
  12.2 9.5 %collective-permute-start.2 = (f32[136,128]{1,0:T(8,128)S(1)}, f32[136,128]{1,0:T(8,128)S(1)}, u32[]{:S(2)}, u32[]{:S(2)}) collective-permute-start(f32[136,128]{1,0:T(8,128)S(1)} %get-tuple-element.82), channel_id=1, source_target_pairs={{16,32},{32,16},{48,64},{64,48},{80,96},{96,80},{112,128},{128,112... | collective-permute-start | bytes 208904 | tf_op jit(solution)/shard_map/ppermute | solution.py:621
  16.6 5.1 %collective-permute-start.3 = (f32[136,128]{1,0:T(8,128)S(1)}, f32[136,128]{1,0:T(8,128)S(1)}, u32[]{:S(2)}, u32[]{:S(2)}) collective-permute-start(f32[136,128]{1,0:T(8,128)S(1)} %get-tuple-element.83), channel_id=1, source_target_pairs={{0,16},{16,0},{32,48},{48,32},{64,80},{80,64},{96,112},{112,96},{1... | collective-permute-start | bytes 208904 | tf_op jit(solution)/shard_map/ppermute | solution.py:621
  22.8 14.1 %collective-permute-start.4 = (f32[136,128]{1,0:T(8,128)S(1)}, f32[136,128]{1,0:T(8,128)S(1)}, u32[]{:S(2)}, u32[]{:S(2)}) collective-permute-start(f32[136,128]{1,0:T(8,128)S(1)} %get-tuple-element.88), channel_id=1, source_target_pairs={{0,15},{1,2},{2,1},{3,4},{4,3},{5,6},{6,5},{7,8},{8,7},{9,10},{10,... | collective-permute-start | bytes 208904 | tf_op jit(solution)/shard_map/ppermute | solution.py:615
  27.2 9.8 %collective-permute-start.5 = (f32[136,128]{1,0:T(8,128)S(1)}, f32[136,128]{1,0:T(8,128)S(1)}, u32[]{:S(2)}, u32[]{:S(2)}) collective-permute-start(f32[136,128]{1,0:T(8,128)S(1)} %get-tuple-element.89), channel_id=1, source_target_pairs={{0,1},{1,0},{2,3},{3,2},{4,5},{5,4},{6,7},{7,6},{8,9},{9,8},{10,11... | collective-permute-start | bytes 208904 | tf_op jit(solution)/shard_map/ppermute | solution.py:615
  29.2 7.8 %collective-permute-start.6 = (f32[136,128]{1,0:T(8,128)S(1)}, f32[136,128]{1,0:T(8,128)S(1)}, u32[]{:S(2)}, u32[]{:S(2)}) collective-permute-start(f32[136,128]{1,0:T(8,128)S(1)} %get-tuple-element.90), channel_id=1, source_target_pairs={{16,32},{32,16},{48,64},{64,48},{80,96},{96,80},{112,128},{128,112... | collective-permute-start | bytes 208904 | tf_op jit(solution)/shard_map/ppermute | solution.py:621
  32.7 4.4 %collective-permute-start.7 = (f32[136,128]{1,0:T(8,128)S(1)}, f32[136,128]{1,0:T(8,128)S(1)}, u32[]{:S(2)}, u32[]{:S(2)}) collective-permute-start(f32[136,128]{1,0:T(8,128)S(1)} %get-tuple-element.91), channel_id=1, source_target_pairs={{0,16},{16,0},{32,48},{48,32},{64,80},{80,64},{96,112},{112,96},{1... | collective-permute-start | bytes 208904 | tf_op jit(solution)/shard_map/ppermute | solution.py:621
  39.2 13.0 %collective-permute-start.8 = (f32[152,128]{1,0:T(8,128)S(1)}, f32[152,128]{1,0:T(8,128)S(1)}, u32[]{:S(2)}, u32[]{:S(2)}) collective-permute-start(f32[152,128]{1,0:T(8,128)S(1)} %get-tuple-element.97), channel_id=1, source_target_pairs={{0,15},{1,2},{2,1},{3,4},{4,3},{5,6},{6,5},{7,8},{8,7},{9,10},{10,... | collective-permute-start | bytes 233480 | tf_op jit(solution)/shard_map/ppermute | solution.py:615
  44.1 8.1 %collective-permute-start.9 = (f32[152,128]{1,0:T(8,128)S(1)}, f32[152,128]{1,0:T(8,128)S(1)}, u32[]{:S(2)}, u32[]{:S(2)}) collective-permute-start(f32[152,128]{1,0:T(8,128)S(1)} %get-tuple-element.98), channel_id=1, source_target_pairs={{0,1},{1,0},{2,3},{3,2},{4,5},{5,4},{6,7},{7,6},{8,9},{9,8},{10,11... | collective-permute-start | bytes 233480 | tf_op jit(solution)/shard_map/ppermute | solution.py:615
  46.1 6.3 %collective-permute-start.10 = (f32[152,128]{1,0:T(8,128)S(1)}, f32[152,128]{1,0:T(8,128)S(1)}, u32[]{:S(2)}, u32[]{:S(2)}) collective-permute-start(f32[152,128]{1,0:T(8,128)S(1)} %get-tuple-element.99), channel_id=1, source_target_pairs={{16,32},{32,16},{48,64},{64,48},{80,96},{96,80},{112,128},{128,112... | collective-permute-start | bytes 233480 | tf_op jit(solution)/shard_map/ppermute | solution.py:621
  50.3 3.2 %collective-permute-start.11 = (f32[152,128]{1,0:T(8,128)S(1)}, f32[152,128]{1,0:T(8,128)S(1)}, u32[]{:S(2)}, u32[]{:S(2)}) collective-permute-start(f32[152,128]{1,0:T(8,128)S(1)} %get-tuple-element.100), channel_id=1, source_target_pairs={{0,16},{16,0},{32,48},{48,32},{64,80},{80,64},{96,112},{112,96},{1... | collective-permute-start | bytes 233480 | tf_op jit(solution)/shard_map/ppermute | solution.py:621
  54.7 12.6 %collective-permute-start.12 = (f32[168,128]{1,0:T(8,128)S(1)}, f32[168,128]{1,0:T(8,128)S(1)}, u32[]{:S(2)}, u32[]{:S(2)}) collective-permute-start(f32[168,128]{1,0:T(8,128)S(1)} %get-tuple-element.103), channel_id=1, source_target_pairs={{0,15},{1,2},{2,1},{3,4},{4,3},{5,6},{6,5},{7,8},{8,7},{9,10},{10,... | collective-permute-start | bytes 258056 | tf_op jit(solution)/shard_map/ppermute | solution.py:615
  58.4 8.9 %collective-permute-start.13 = (f32[168,128]{1,0:T(8,128)S(1)}, f32[168,128]{1,0:T(8,128)S(1)}, u32[]{:S(2)}, u32[]{:S(2)}) collective-permute-start(f32[168,128]{1,0:T(8,128)S(1)} %get-tuple-element.104), channel_id=1, source_target_pairs={{0,1},{1,0},{2,3},{3,2},{4,5},{5,4},{6,7},{7,6},{8,9},{9,8},{10,11... | collective-permute-start | bytes 258056 | tf_op jit(solution)/shard_map/ppermute | solution.py:615
  60.3 7.2 %collective-permute-start.14 = (f32[168,128]{1,0:T(8,128)S(1)}, f32[168,128]{1,0:T(8,128)S(1)}, u32[]{:S(2)}, u32[]{:S(2)}) collective-permute-start(f32[168,128]{1,0:T(8,128)S(1)} %get-tuple-element.105), channel_id=1, source_target_pairs={{16,32},{32,16},{48,64},{64,48},{80,96},{96,80},{112,128},{128,112... | collective-permute-start | bytes 258056 | tf_op jit(solution)/shard_map/ppermute | solution.py:621
  65.4 3.2 %collective-permute-start.15 = (f32[168,128]{1,0:T(8,128)S(1)}, f32[168,128]{1,0:T(8,128)S(1)}, u32[]{:S(2)}, u32[]{:S(2)}) collective-permute-start(f32[168,128]{1,0:T(8,128)S(1)} %get-tuple-element.106), channel_id=1, source_target_pairs={{0,16},{16,0},{32,48},{48,32},{64,80},{80,64},{96,112},{112,96},{1... | collective-permute-start | bytes 258056 | tf_op jit(solution)/shard_map/ppermute | solution.py:621
  70.8 12.7 %collective-permute-start.16 = (f32[184,128]{1,0:T(8,128)S(1)}, f32[184,128]{1,0:T(8,128)S(1)}, u32[]{:S(2)}, u32[]{:S(2)}) collective-permute-start(f32[184,128]{1,0:T(8,128)S(1)} %get-tuple-element.108), channel_id=1, source_target_pairs={{0,15},{1,2},{2,1},{3,4},{4,3},{5,6},{6,5},{7,8},{8,7},{9,10},{10,... | collective-permute-start | bytes 282632 | tf_op jit(solution)/shard_map/ppermute | solution.py:615
  75.8 7.8 %collective-permute-start.17 = (f32[184,128]{1,0:T(8,128)S(1)}, f32[184,128]{1,0:T(8,128)S(1)}, u32[]{:S(2)}, u32[]{:S(2)}) collective-permute-start(f32[184,128]{1,0:T(8,128)S(1)} %get-tuple-element.109), channel_id=1, source_target_pairs={{0,1},{1,0},{2,3},{3,2},{4,5},{5,4},{6,7},{7,6},{8,9},{9,8},{10,11... | collective-permute-start | bytes 282632 | tf_op jit(solution)/shard_map/ppermute | solution.py:615
  77.7 6.1 %collective-permute-start.18 = (f32[184,128]{1,0:T(8,128)S(1)}, f32[184,128]{1,0:T(8,128)S(1)}, u32[]{:S(2)}, u32[]{:S(2)}) collective-permute-start(f32[184,128]{1,0:T(8,128)S(1)} %get-tuple-element.110), channel_id=1, source_target_pairs={{16,32},{32,16},{48,64},{64,48},{80,96},{96,80},{112,128},{128,112... | collective-permute-start | bytes 282632 | tf_op jit(solution)/shard_map/ppermute | solution.py:621
  81.6 3.2 %collective-permute-start.19 = (f32[184,128]{1,0:T(8,128)S(1)}, f32[184,128]{1,0:T(8,128)S(1)}, u32[]{:S(2)}, u32[]{:S(2)}) collective-permute-start(f32[184,128]{1,0:T(8,128)S(1)} %get-tuple-element.111), channel_id=1, source_target_pairs={{0,16},{16,0},{32,48},{48,32},{64,80},{80,64},{96,112},{112,96},{1... | collective-permute-start | bytes 282632 | tf_op jit(solution)/shard_map/ppermute | solution.py:621
  87.1 13.1 %all-to-all-start = ((f32[16,32,128]{2,1,0:T(8,128)}), f32[16,32,128]{2,1,0:T(8,128)S(1)}, u32[]{:S(2)}, u32[]{:S(2)}) async-start(f32[16,32,128]{2,1,0:T(8,128)} %get-tuple-element.115), calls=%async_computation | async-start | bytes 524288 | tf_op jit(solution)/shard_map/all_to_all | solution.py:629
  94.7 0.6 copy-start
  95.3 0.6 copy-start.2
  100.9 14.3 %copy-start.3 = (f32[200,128]{1,0:T(8,128)S(1)}, f32[200,128]{1,0:T(8,128)}, u32[]{:S(2)}) copy-start(f32[200,128]{1,0:T(8,128)} %copy-done.2) | copy-start | bytes 307204
  101.0 17.2 %copy-start.1 = (f32[200,128]{1,0:T(8,128)S(1)}, f32[200,128]{1,0:T(8,128)}, u32[]{:S(2)}) copy-start(f32[200,128]{1,0:T(8,128)} %copy-done) | copy-start | bytes 307204
  101.0 36.1 %all-to-all-start.1 = ((f32[32,16,128]{2,1,0:T(8,128)}), f32[32,16,128]{2,1,0:T(8,128)S(1)}, u32[]{:S(2)}, u32[]{:S(2)}) async-start(f32[32,16,128]{2,1,0:T(8,128)} %shard_map.131), calls=%async_computation.1 | async-start | bytes 524288 | tf_op jit(solution)/shard_map/all_to_all | solution.py:629
  115.3 10.6 %collective-permute-start.20 = (f32[200,128]{1,0:T(8,128)S(1)}, f32[200,128]{1,0:T(8,128)S(1)}, u32[]{:S(2)}, u32[]{:S(2)}) collective-permute-start(f32[200,128]{1,0:T(8,128)S(1)} %copy-done.3), channel_id=1, source_target_pairs={{0,15},{1,2},{2,1},{3,4},{4,3},{5,6},{6,5},{7,8},{8,7},{9,10},{10,... | collective-permute-start | bytes 307208 | tf_op jit(solution)/shard_map/ppermute | solution.py:615
  118.2 7.7 %collective-permute-start.21 = (f32[200,128]{1,0:T(8,128)S(1)}, f32[200,128]{1,0:T(8,128)S(1)}, u32[]{:S(2)}, u32[]{:S(2)}) collective-permute-start(f32[200,128]{1,0:T(8,128)S(1)} %copy-done.1), channel_id=1, source_target_pairs={{0,1},{1,0},{2,3},{3,2},{4,5},{5,4},{6,7},{7,6},{8,9},{9,8},{10,11... | collective-permute-start | bytes 307208 | tf_op jit(solution)/shard_map/ppermute | solution.py:615
  120.1 9.2 %collective-permute-start.22 = (f32[200,128]{1,0:T(8,128)S(1)}, f32[200,128]{1,0:T(8,128)S(1)}, u32[]{:S(2)}, u32[]{:S(2)}) collective-permute-start(f32[200,128]{1,0:T(8,128)S(1)} %get-tuple-element.127), channel_id=1, source_target_pairs={{16,32},{32,16},{48,64},{64,48},{80,96},{96,80},{112,128},{128,112... | collective-permute-start | bytes 307208 | tf_op jit(solution)/shard_map/ppermute | solution.py:621
  124.0 5.4 %collective-permute-start.23 = (f32[200,128]{1,0:T(8,128)S(1)}, f32[200,128]{1,0:T(8,128)S(1)}, u32[]{:S(2)}, u32[]{:S(2)}) collective-permute-start(f32[200,128]{1,0:T(8,128)S(1)} %get-tuple-element.128), channel_id=1, source_target_pairs={{0,16},{16,0},{32,48},{48,32},{64,80},{80,64},{96,112},{112,96},{1... | collective-permute-start | bytes 307208 | tf_op jit(solution)/shard_map/ppermute | solution.py:621
  137.1 4.4 %collective-permute-start.24 = (f32[32,16,128]{2,1,0:T(8,128)S(1)}, f32[32,16,128]{2,1,0:T(8,128)S(1)}, u32[]{:S(2)}, u32[]{:S(2)}) collective-permute-start(f32[32,16,128]{2,1,0:T(8,128)S(1)} %all-to-all-done.1.mine), channel_id=1, source_target_pairs={{0,16},{16,0},{32,48},{48,32},{64,80},{80,64},{96,112},{112,96},{1... | collective-permute-start | bytes 786440 | tf_op jit(solution)/shard_map/ppermute | solution.py:730
  147.6 15.1 %all-to-all-start.2 = ((f32[16,1,1152]{2,1,0:T(1,128)}), f32[16,1,1152]{2,1,0:T(1,128)S(1)}, u32[]{:S(2)}, u32[]{:S(2)}) async-start(f32[16,1,1152]{2,1,0:T(1,128)} %get-tuple-element.137), calls=%async_computation.2 | async-start | bytes 147456 | tf_op jit(solution)/shard_map/all_to_all | solution.py:629
  151.2 8.5 %collective-permute-start.25 = (f32[128,128]{1,0:T(8,128)S(1)}, f32[128,128]{1,0:T(8,128)S(1)}, u32[]{:S(2)}, u32[]{:S(2)}) collective-permute-start(f32[128,128]{1,0:T(8,128)S(1)} %get-tuple-element.138), channel_id=1, source_target_pairs={{0,15},{1,2},{2,1},{3,4},{4,3},{5,6},{6,5},{7,8},{8,7},{9,10},{10,... | collective-permute-start | bytes 196616 | tf_op jit(solution)/shard_map/ppermute | solution.py:615
  157.7 5.0 %collective-permute-start.26 = (f32[128,128]{1,0:T(8,128)S(1)}, f32[128,128]{1,0:T(8,128)S(1)}, u32[]{:S(2)}, u32[]{:S(2)}) collective-permute-start(f32[128,128]{1,0:T(8,128)S(1)} %get-tuple-element.139), channel_id=1, source_target_pairs={{0,1},{1,0},{2,3},{3,2},{4,5},{5,4},{6,7},{7,6},{8,9},{9,8},{10,11... | collective-permute-start | bytes 196616 | tf_op jit(solution)/shard_map/ppermute | solution.py:615
  163.4 23.4 %all-to-all-start.3 = ((f32[32,1,1152]{2,1,0:T(1,128)}), f32[32,1,1152]{2,1,0:T(1,128)S(1)}, u32[]{:S(2)}, u32[]{:S(2)}) async-start(f32[32,1,1152]{2,1,0:T(1,128)} %shard_map.133), calls=%async_computation.3 | async-start | bytes 294912 | tf_op jit(solution)/shard_map/all_to_all | solution.py:629
  170.3 8.2 %collective-permute-start.27 = (f32[128,128]{1,0:T(8,128)S(1)}, f32[128,128]{1,0:T(8,128)S(1)}, u32[]{:S(2)}, u32[]{:S(2)}) collective-permute-start(f32[128,128]{1,0:T(8,128)S(1)} %get-tuple-element.147), channel_id=1, source_target_pairs={{16,32},{32,16},{48,64},{64,48},{80,96},{96,80},{112,128},{128,112... | collective-permute-start | bytes 196616 | tf_op jit(solution)/shard_map/ppermute | solution.py:621
  173.9 4.7 %collective-permute-start.28 = (f32[128,128]{1,0:T(8,128)S(1)}, f32[128,128]{1,0:T(8,128)S(1)}, u32[]{:S(2)}, u32[]{:S(2)}) collective-permute-start(f32[128,128]{1,0:T(8,128)S(1)} %get-tuple-element.148), channel_id=1, source_target_pairs={{0,16},{16,0},{32,48},{48,32},{64,80},{80,64},{96,112},{112,96},{1... | collective-permute-start | bytes 196616 | tf_op jit(solution)/shard_map/ppermute | solution.py:621

commit v6 on v5

--- a/solution.py
+++ b/solution.py
@@ -158,6 +158,22 @@
         axis=1,
     )
     return diag * z - product(solved, couple, True)
+
+
+def begin(source, target, sems, parts):
+    rows = source.shape[0] // 8
+    edges = [8 * (rows * n // parts) for n in range(parts)] + [source.shape[0]]
+    copies = []
+    for n in range(parts):
+        band = pl.ds(edges[n], edges[n + 1] - edges[n])
+        copies.append(pltpu.make_async_copy(source.at[band], target.at[band], sems.at[n]))
+        copies[n].start()
+    return copies
+
+
+def finish(copies):
+    for copy in copies:
+        copy.wait()
 
 
 def k_prepare(place, load, rho, order, shared_o, order_o, s0, s1, s2, s3, load_s, rho_s, sem):
@@ -306,8 +322,7 @@
     older = jnp.concatenate([v[...][:rhs], zero, v[...][rhs:], zero], axis=0)
     v2 = w - SHIFT * older
     v2_s[...] = v2
-    copy = pltpu.make_async_copy(v2_s, v2_o, sem.at[0])
-    copy.start()
+    copies = begin(v2_s, v2_o, sem, 4)
     weighted = share[...] * v2
     prim2 = mm_t(avg[...], weighted[:rhs])
     reach2 = mm_t(avg[...], weighted[rhs:])
@@ -317,7 +332,7 @@
     pay = jnp.concatenate([prim0[...], prim1[...][:, :rhs], prim2, tail], axis=0)
     for item in range(pay_o.shape[0]):
         pay_o[item] = pay
-    copy.wait()
+    finish(copies)
 
 
 def summed(got):
@@ -327,15 +342,8 @@
     return total
 
 
-def k_sum_halves(got, coefs, out):
+def k_sum_spread(got, coefs, out):
     total = summed(got) + coefs[...]
-    half = total.shape[0] // 2
-    for item in range(out.shape[0]):
-        out[item] = total[half * (item % 2) : half * (item % 2) + half]
-
-
-def k_sum_spread(got, out):
-    total = summed(got)
     for item in range(out.shape[0]):
         out[item] = total
 
@@ -362,15 +370,12 @@
 
 def k_fourth(place, v2, share, neumann, t_o, s0, s1, s2, s3, v2_s, t_s, sem):
     at = Place(place)
-    copy = pltpu.make_async_copy(v2, v2_s, sem.at[0])
-    copy.start()
-    copy.wait()
+    finish(begin(v2, v2_s, sem.at[0], 4))
     t = share[...] * product(share[...] * v2_s[...], held(neumann))
     t_s[...] = t
-    copy = pltpu.make_async_copy(t_s, t_o, sem.at[1])
-    copy.start()
+    copies = begin(t_s, t_o, sem.at[1], 4)
     put_sends((s0, s1, s2, s3), t, at)
-    copy.wait()
+    finish(copies)
 
 
 def lift(coefs, basis):
@@ -392,25 +397,24 @@
     band0, band1, band2, c0_s, c1_s, c2_s, full_s, t_s, z0_s, z1_s, v2_s, sem, in_sem,
 ):
     at = Place(place)
-    loads = [
-        pltpu.make_async_copy(source, target, in_sem.at[n])
-        for n, (source, target) in enumerate(((t, t_s), (z1, z1_s), (z0, z0_s), (v2, v2_s)))
-    ]
-    for load in loads:
-        load.start()
+    loads = []
+    for n, (source, target) in enumerate(((z0, z0_s), (z1, z1_s), (v2, v2_s), (t, t_s))):
+        loads += begin(source, target, in_sem.at[n], 2)
     t, z0, z1, v2 = t_s, z0_s, z1_s, v2_s
     rhs = r.shape[0]
-    rows = mine.shape[0]
+    rows = 2 * mine.shape[0]
     width = band0.shape[1]
     lane = lax.broadcasted_iota(jnp.int32, (8, width), 1)
     lowers, uppers = [], []
     for ref in (band0, band1, band2):
         if ref.shape[0] > rows * 8:
             ref[rows * 8 :, :] = jnp.zeros((ref.shape[0] - rows * 8, width), F32)
-    upper = [jnp.where(at.even_row, mine[k], other[k]) for k in range(rows)]
-    lower = [jnp.where(at.even_row, other[k], mine[k]) for k in range(rows)]
+    pays = []
+    for k in range(rows // 2):
+        pays.append(jnp.where(at.even_row, mine[k], other[k]))
+        pays.append(jnp.where(at.even_row, other[k], mine[k]))
     for k in range(rows):
-        tail = lower[k][8:16]
+        tail = pays[k][24:32]
         lowers.append(jnp.broadcast_to(tail[:, 120:121], (8, rhs)))
         uppers.append(jnp.broadcast_to(tail[:, 121:122], (8, rhs)))
         wide = tail
@@ -436,10 +440,10 @@
         return stacked(coarse_rows(tiles, lowers, uppers)) + banded_product(own, total)
 
     edge = jnp.zeros((40, rhs), F32)
-    c0 = solve(stacked([part[0:8] for part in upper]))
-    c1 = solve(stacked([part[8:16] for part in upper]) + banded_product(near, c0))
+    c0 = solve(stacked([part[0:8] for part in pays]))
+    c1 = solve(stacked([part[8:16] for part in pays]) + banded_product(near, c0))
     c2 = solve(
-        stacked([part[0:8] for part in lower])
+        stacked([part[16:24] for part in pays])
         + banded_product(wide, c0)
         + banded_product(near, c1)
     )
@@ -452,16 +456,7 @@
     c1 = c1_s[pl.ds(pl.multiple_of(start + 16, 8), 56), :]
     c2 = c2_s[pl.ds(pl.multiple_of(start + 32, 8), 24), :]
     r0 = r[...]
-    for load in loads:
-        load.wait()
-    z2 = assembled(t[...], (g0, g1, g2, g3), at, rhs)
-    z2f = z2[:rhs] + lift(
-        jnp.concatenate([c0, c1, c2], axis=0),
-        jnp.concatenate([z2[rhs:], z1[rhs:, :], z0[rhs:, :]], axis=0),
-    )
-    q = schur(z2f, diag[...], held(couple), held(blocks))
-    q_o[...] = q
-    put_sends((s0, s1, s2, s3), q, at)
+    finish(loads)
     z0f = z0[:rhs, :] + lift(c0[32:56], z0[rhs:, :])
     v1f = v1[:rhs, :] + lift(c0[24:64], v1[rhs:, :])
     z1f = z1[:rhs, :] + lift(
@@ -472,12 +467,25 @@
         jnp.concatenate([c0[8:80], c1[8:48]], axis=0),
         jnp.concatenate([v2[rhs:, :], v1[rhs:, :]], axis=0),
     )
-    kept = ((z0f, z0_o), (z1f, z1_o), (z2f, z2_o), (v1f + SHIFT * r0, w0_o), (v2f + SHIFT * v1f, w1_o))
     copies = []
-    for n, (value, out) in enumerate(kept):
+
+    def keep(n, value, out):
         full_s[n] = value
-        copies.append(pltpu.make_async_copy(full_s.at[n], out, sem.at[n]))
-        copies[n].start()
+        copies.extend(begin(full_s.at[n], out, sem.at[n], 2))
+
+    keep(0, z0f, z0_o)
+    keep(1, z1f, z1_o)
+    keep(2, v1f + SHIFT * r0, w0_o)
+    keep(3, v2f + SHIFT * v1f, w1_o)
+    z2 = assembled(t[...], (g0, g1, g2, g3), at, rhs)
+    z2f = z2[:rhs] + lift(
+        jnp.concatenate([c0, c1, c2], axis=0),
+        jnp.concatenate([z2[rhs:], z1[rhs:, :], z0[rhs:, :]], axis=0),
+    )
+    keep(4, z2f, z2_o)
+    q = schur(z2f, diag[...], held(couple), held(blocks))
+    q_o[...] = q
+    put_sends((s0, s1, s2, s3), q, at)
     table = dot_rows(
         [(r0, z0f), (r0, z1f), (v1f, z0f), (v1f, z1f), (v2f, z1f)]
         + [(r0, z2f), (v1f, z2f), (v2f, z2f), (z2f, q + q)]
@@ -485,8 +493,7 @@
     line = jnp.concatenate([table[i : i + 1] for i in range(9)], axis=1)
     for item in range(pay_o.shape[0]):
         pay_o[item] = line
-    for copy in copies:
-        copy.wait()
+    finish(copies)
 
 
 def dot_rows(pairs):
@@ -510,8 +517,7 @@
 ):
     loads = []
     for n, source in enumerate((z0, z1, z2, w0, w1)):
-        loads.append(pltpu.make_async_copy(source, full_s.at[n], sem.at[n]))
-        loads[n].start()
+        loads += begin(source, full_s.at[n], sem.at[n], 2)
     w2 = assembled(q[...], (g0, g1, g2, g3), Place(place), q.shape[0])
     total = summed(got)
     v0z0, v0z1, v1z0, v1z1, v2z1, v0z2, v1z2, v2z2, z2w2 = [
@@ -570,8 +576,7 @@
     columns = mm_t(eye, table)
     col = [columns[:, i : i + 1] for i in range(6)]
     hots = one_hot_faces(order[...])
-    for load in loads:
-        load.wait()
+    finish(loads)
     x = col[0] * full_s[0] + col[1] * full_s[1] + col[2] * full_s[2]
     r = r0[...] + col[3] * full_s[3] + col[4] * full_s[4] + col[5] * w2
     both = to_points(jnp.concatenate([x, r], axis=0), hots)
@@ -625,8 +630,10 @@
     return exchange_columns(sends, columns) + exchange_rows(sends, rows)
 
 
-def spread(value, axis):
-    return lax.all_to_all(value, axis, split_axis=0, concat_axis=0, tiled=True)
+def spread(value, axis, groups=None):
+    return lax.all_to_all(
+        value, axis, split_axis=0, concat_axis=0, tiled=True, axis_index_groups=groups
+    )
 
 
 def local(
@@ -713,25 +720,26 @@
     n = rhs + 72
     v2, pay = call(
         k_third, [(n, points), (columns, 32, LANES)], place, q1, *got, v1, share, avg, prim0, prim1,
-        raw_outs=(0,), scratch=[pltpu.VMEM((n, points), F32), dma((1,))],
+        raw_outs=(0,), scratch=[pltpu.VMEM((n, points), F32), dma((4,))],
     )
     got = spread(pay, "circ")
     t2, *sends = call(
         k_fourth, [(n, points)] + face(n), place, v2, share, neumann,
         raw=(0,), raw_outs=(0,),
-        scratch=[pltpu.VMEM((n, points), F32)] * 2 + [dma((2,))],
+        scratch=[pltpu.VMEM((n, points), F32)] * 2 + [dma((2, 4))],
         flops=500_000_000,
     )
     got, t2 = lax.optimization_barrier((got, t2))
-    (pay,) = call(k_sum_halves, [(rows, 16, LANES)], None, got, coefs)
+    (pay,) = call(k_sum_spread, [(rows // 2, 32, LANES)], None, got, coefs)
     pay, *sends = lax.optimization_barrier((pay, *sends))
-    mine = spread(pay, "axial")
+    along = [list(range(core, rows, 2)) for core in range(2)]
+    mine = spread(pay, "axial", along)
     mine, *got = lax.optimization_barrier((mine, *swap(sends)))
     other = lax.ppermute(mine, "axial", [(i, i ^ 1) for i in range(rows)])
     width = max(LANES, 8 * rows)
     z0f, z1f, z2f, w0f, w1f, q2, pay, *sends = call(
         k_core,
-        [(rhs, points)] * 6 + [(columns, 1, 9 * LANES)] + face(rhs),
+        [(rhs, points)] * 6 + [(2 * columns, 1, 9 * LANES)] + face(rhs),
         place, mine, other, t2, *got, z0, v1, z1, v2, r0, diag, couple, blocks,
         raw=(2, 7, 9, 10),
         raw_outs=(0, 1, 2, 3, 4),
@@ -739,20 +747,25 @@
         + [pltpu.VMEM((width + 80, rhs), F32)] * 3
         + [pltpu.VMEM((5, rhs, points), F32)]
         + [pltpu.VMEM((rhs + m, points), F32) for m in (72, 24, 56, 72)]
-        + [dma((5,)), dma((4,))],
-    )
-    dots = spread(pay, "circ")
+        + [dma((5, 2)), dma((4, 2))],
+    )
+    chips = [
+        [row * columns + column for row in (pair, pair + 1) for column in range(columns)]
+        for pair in range(0, rows, 2)
+    ]
+    dots = spread(pay, ("axial", "circ"), chips)
     got = exchange_columns(sends, columns)
     dots, *got = lax.optimization_barrier((dots, *got))
-    (pay,) = call(k_sum_spread, [(rows, 1, 9 * LANES)], None, dots)
+    blank = jnp.zeros((1, 9 * LANES), F32)
+    (pay,) = call(k_sum_spread, [(rows // 2, 1, 9 * LANES)], None, dots, blank)
     pay, *sends = lax.optimization_barrier((pay, *sends))
-    dots = spread(pay, "axial")
+    dots = spread(pay, "axial", along)
     got = got + exchange_rows(sends, rows)
     x, r = call(
         k_final, [(rhs, points)] * 2,
         place, dots, q2, *got, order, r0, z0f, z1f, z2f, w0f, w1f,
         raw=(8, 9, 10, 11, 12),
-        scratch=[pltpu.VMEM((5, rhs, points), F32), dma((5,))],
+        scratch=[pltpu.VMEM((5, rhs, points), F32), dma((5, 2))],
     )
     return (x[None, None], r[None, None])
 

time: 191 us -> 188 us (0.984)
  waiting for transfers between devices: 34.4 us -> 20.3 us
  starting transfers between devices: 123 us -> 133 us
    all_to_all x4, waiting for transfers between devices: 20.2 us -> 7.26 us  [spread(): lax.all_to_all(value, axis, split_axis=0, concat_axis=0, tiled=True, axis...]
    ppermute x7, starting transfers between devices: 28.4 us -> 34.2 us  [exchange_rows(): lax.ppermute(sends[2], 'axial', link)]
    ppermute x7, waiting for transfers between devices: 6.82 us -> 3.22 us  [exchange_rows(): lax.ppermute(sends[2], 'axial', link)]
    ppermute x1, starting transfers between devices: 3.26 us -> 6.55 us  [local(): other = lax.ppermute(mine, 'axial', [(i, i ^ 1) for i in range(rows)])]
  transfers between devices with their start and end apart: 33 -> 33, of which waited for: 13 -> 13; matrix products, arithmetic and copies ran while one was open for 0% -> 0% of each run, Pallas kernels for 4% -> 5%
where the time goes in v6:
time: 188 us; the launch traced here: 186 us
  starting transfers between devices  133 us (71%)
  Pallas kernels  30.5 us (16%)
  waiting for transfers between devices  20.3 us (11%)
    ppermute x7, starting transfers between devices, exchange_columns(): lax.ppermute(sends[0], 'circ', far)  35.4 us
    ppermute x7, starting transfers between devices, exchange_rows(): lax.ppermute(sends[2], 'axial', link)  34.2 us
    pallas_call x13, Pallas kernels, call(): pl.pallas_call(body, out_shape=[out if isinstance(out, jax.ShapeDtypeStru...  30.5 us
    all_to_all x4, starting transfers between devices, spread(): lax.all_to_all(value, axis, split_axis=0, concat_axis=0, tiled=True, axis...  29.7 us
    ppermute x7, starting transfers between devices, exchange_columns(): lax.ppermute(sends[1], 'circ', near)  13.4 us
    ppermute x7, starting transfers between devices, exchange_rows(): lax.ppermute(sends[3], 'axial', core)  13.4 us
    all_to_all x4, waiting for transfers between devices, spread(): lax.all_to_all(value, axis, split_axis=0, concat_axis=0, tiled=True, axis...  7.26 us
    ppermute x1, starting transfers between devices, local(): other = lax.ppermute(mine, 'axial', [(i, i ^ 1) for i in range(rows)])  6.55 us
  transfers between devices with their start and end apart: 33, of which 13 were waited for; matrix products, arithmetic and copies ran while one was open for 0% of the time, Pallas kernels for 5%

profile of v6, /device:TPU:1, one launch (start us, length us, event | category | flops | bytes accessed | tf_op | source)
XLA Modules:
  0.0 186.0 jit_solution(11701222868806169088)
XLA Ops:
  0.7 1.9 %shard_map.122 = (f32[136,512]{1,0:T(8,128)S(1)}, s32[1,512]{1,0:T(1,128)S(1)}, f32[136,128]{1,0:T(8,128)S(1)}, f32[136,128]{1,0:T(8,128)S(1)}, f32[136,128]{1,0:T(8,128)S(1)}, /*index=5*/f32[136,128]{1,0:T(8,128)S(1)}) custom-call(s32[3]{0:T(128)S(1)} %pad_add_fusion.place, f32[128,512]{1,0:T(8,128)} %bitcast.13, f32[1,512]{1,0:T(1,128)} %bitcast.14, ...), custom_call_target="tpu_custom_call" | custom-call | flops 1000000 | bytes 1000000 | tf_op jit(solution)/shard_map/pallas_call | solution.py:598
  2.6 7.7 %collective-permute-start = (f32[136,128]{1,0:T(8,128)S(1)}, f32[136,128]{1,0:T(8,128)S(1)}, u32[]{:S(2)}, u32[]{:S(2)}) collective-permute-start(f32[136,128]{1,0:T(8,128)S(1)} %get-tuple-element.80), channel_id=1, source_target_pairs={{0,15},{1,2},{2,1},{3,4},{4,3},{5,6},{6,5},{7,8},{8,7},{9,10},{10,... | collective-permute-start | bytes 208904 | tf_op jit(solution)/shard_map/ppermute | solution.py:620
  10.3 1.9 %collective-permute-start.1 = (f32[136,128]{1,0:T(8,128)S(1)}, f32[136,128]{1,0:T(8,128)S(1)}, u32[]{:S(2)}, u32[]{:S(2)}) collective-permute-start(f32[136,128]{1,0:T(8,128)S(1)} %get-tuple-element.81), channel_id=1, source_target_pairs={{0,1},{1,0},{2,3},{3,2},{4,5},{5,4},{6,7},{7,6},{8,9},{9,8},{10,11... | collective-permute-start | bytes 208904 | tf_op jit(solution)/shard_map/ppermute | solution.py:620
  12.2 4.4 %collective-permute-start.2 = (f32[136,128]{1,0:T(8,128)S(1)}, f32[136,128]{1,0:T(8,128)S(1)}, u32[]{:S(2)}, u32[]{:S(2)}) collective-permute-start(f32[136,128]{1,0:T(8,128)S(1)} %get-tuple-element.82), channel_id=1, source_target_pairs={{16,32},{32,16},{48,64},{64,48},{80,96},{96,80},{112,128},{128,112... | collective-permute-start | bytes 208904 | tf_op jit(solution)/shard_map/ppermute | solution.py:626
  16.6 1.9 %collective-permute-start.3 = (f32[136,128]{1,0:T(8,128)S(1)}, f32[136,128]{1,0:T(8,128)S(1)}, u32[]{:S(2)}, u32[]{:S(2)}) collective-permute-start(f32[136,128]{1,0:T(8,128)S(1)} %get-tuple-element.83), channel_id=1, source_target_pairs={{0,16},{16,0},{32,48},{48,32},{64,80},{80,64},{96,112},{112,96},{1... | collective-permute-start | bytes 208904 | tf_op jit(solution)/shard_map/ppermute | solution.py:626
  18.6 3.1 %shard_map.123 = (bf16[2,512,512]{2,1,0:T(8,128)(2,1)S(1)}, f32[8,512]{1,0:T(8,128)S(1)}) custom-call(s32[1,512]{1,0:T(1,128)S(1)} %get-tuple-element.84.order, f32[512,512]{1,0:T(8,128)} %bitcast.16, s32[8,64]{1,0:T(8,128)} %bitcast.21), custom_call_target="tpu_custom_call" | custom-call | flops 2000000000 | bytes 1000000 | tf_op jit(solution)/shard_map/pallas_call | solution.py:598
  22.8 4.4 %collective-permute-start.4 = (f32[136,128]{1,0:T(8,128)S(1)}, f32[136,128]{1,0:T(8,128)S(1)}, u32[]{:S(2)}, u32[]{:S(2)}) collective-permute-start(f32[136,128]{1,0:T(8,128)S(1)} %get-tuple-element.88), channel_id=1, source_target_pairs={{0,15},{1,2},{2,1},{3,4},{4,3},{5,6},{6,5},{7,8},{8,7},{9,10},{10,... | collective-permute-start | bytes 208904 | tf_op jit(solution)/shard_map/ppermute | solution.py:620
  27.2 1.9 %collective-permute-start.5 = (f32[136,128]{1,0:T(8,128)S(1)}, f32[136,128]{1,0:T(8,128)S(1)}, u32[]{:S(2)}, u32[]{:S(2)}) collective-permute-start(f32[136,128]{1,0:T(8,128)S(1)} %get-tuple-element.89), channel_id=1, source_target_pairs={{0,1},{1,0},{2,3},{3,2},{4,5},{5,4},{6,7},{7,6},{8,9},{9,8},{10,11... | collective-permute-start | bytes 208904 | tf_op jit(solution)/shard_map/ppermute | solution.py:620
  29.2 3.5 %collective-permute-start.6 = (f32[136,128]{1,0:T(8,128)S(1)}, f32[136,128]{1,0:T(8,128)S(1)}, u32[]{:S(2)}, u32[]{:S(2)}) collective-permute-start(f32[136,128]{1,0:T(8,128)S(1)} %get-tuple-element.90), channel_id=1, source_target_pairs={{16,32},{32,16},{48,64},{64,48},{80,96},{96,80},{112,128},{128,112... | collective-permute-start | bytes 208904 | tf_op jit(solution)/shard_map/ppermute | solution.py:626
  32.7 1.9 %collective-permute-start.7 = (f32[136,128]{1,0:T(8,128)S(1)}, f32[136,128]{1,0:T(8,128)S(1)}, u32[]{:S(2)}, u32[]{:S(2)}) collective-permute-start(f32[136,128]{1,0:T(8,128)S(1)} %get-tuple-element.91), channel_id=1, source_target_pairs={{0,16},{16,0},{32,48},{48,32},{64,80},{80,64},{96,112},{112,96},{1... | collective-permute-start | bytes 208904 | tf_op jit(solution)/shard_map/ppermute | solution.py:626
  34.6 2.4 %shard_map.125 = (f32[1,512]{1,0:T(1,128)S(1)}, bf16[2,512,512]{2,1,0:T(8,128)(2,1)S(1)}, bf16[2,4,128,128]{3,2,1,0:T(8,128)(2,1)S(1)}, f32[32,128]{1,0:T(8,128)S(1)}) custom-call(s32[1,512]{1,0:T(1,128)S(1)} %get-tuple-element.84.order, f32[1,512]{1,0:T(1,128)S(1)} %get-tuple-element.92.after.share, f32[1,512]{1,0:T(1,128)} %bitcast.23, ...), custom_call_target="tpu_custom_call" | custom-call | flops 2000000000 | bytes 1000000 | tf_op jit(solution)/shard_map/pallas_call | solution.py:598
  37.0 2.1 %shard_map.126 = (f32[152,512]{1,0:T(8,128)}, f32[152,512]{1,0:T(8,128)S(1)}, f32[152,128]{1,0:T(8,128)S(1)}, f32[152,128]{1,0:T(8,128)S(1)}, f32[152,128]{1,0:T(8,128)S(1)}, /*index=5*/f32[152,128]{1,0:T(8,128)S(1)}) custom-call(s32[3]{0:T(128)S(1)} %pad_add_fusion.place, f32[136,512]{1,0:T(8,128)S(1)} %get-tuple-element.87.t, ...), custom_call_target="tpu_custom_call" | custom-call | flops 1000000 | bytes 1000000 | tf_op jit(solution)/shard_map/pallas_call | solution.py:598
  39.2 3.9 %collective-permute-start.10 = (f32[152,128]{1,0:T(8,128)S(1)}, f32[152,128]{1,0:T(8,128)S(1)}, u32[]{:S(2)}, u32[]{:S(2)}) collective-permute-start(f32[152,128]{1,0:T(8,128)S(1)} %get-tuple-element.99), channel_id=1, source_target_pairs={{16,32},{32,16},{48,64},{64,48},{80,96},{96,80},{112,128},{128,112... | collective-permute-start | bytes 233480 | tf_op jit(solution)/shard_map/ppermute | solution.py:626
  43.1 1.9 %collective-permute-start.11 = (f32[152,128]{1,0:T(8,128)S(1)}, f32[152,128]{1,0:T(8,128)S(1)}, u32[]{:S(2)}, u32[]{:S(2)}) collective-permute-start(f32[152,128]{1,0:T(8,128)S(1)} %get-tuple-element.100), channel_id=1, source_target_pairs={{0,16},{16,0},{32,48},{48,32},{64,80},{80,64},{96,112},{112,96},{1... | collective-permute-start | bytes 233480 | tf_op jit(solution)/shard_map/ppermute | solution.py:626
  45.0 5.0 %collective-permute-start.8 = (f32[152,128]{1,0:T(8,128)S(1)}, f32[152,128]{1,0:T(8,128)S(1)}, u32[]{:S(2)}, u32[]{:S(2)}) collective-permute-start(f32[152,128]{1,0:T(8,128)S(1)} %get-tuple-element.97), channel_id=1, source_target_pairs={{0,15},{1,2},{2,1},{3,4},{4,3},{5,6},{6,5},{7,8},{8,7},{9,10},{10,... | collective-permute-start | bytes 233480 | tf_op jit(solution)/shard_map/ppermute | solution.py:620
  50.0 1.9 %collective-permute-start.9 = (f32[152,128]{1,0:T(8,128)S(1)}, f32[152,128]{1,0:T(8,128)S(1)}, u32[]{:S(2)}, u32[]{:S(2)}) collective-permute-start(f32[152,128]{1,0:T(8,128)S(1)} %get-tuple-element.98), channel_id=1, source_target_pairs={{0,1},{1,0},{2,3},{3,2},{4,5},{5,4},{6,7},{7,6},{8,9},{9,8},{10,11... | collective-permute-start | bytes 233480 | tf_op jit(solution)/shard_map/ppermute | solution.py:620
  51.9 1.5 collective-permute-done.8.g0
  53.5 1.6 collective-permute-done.9.g1
  56.4 3.9 %collective-permute-start.12 = (f32[168,128]{1,0:T(8,128)S(1)}, f32[168,128]{1,0:T(8,128)S(1)}, u32[]{:S(2)}, u32[]{:S(2)}) collective-permute-start(f32[168,128]{1,0:T(8,128)S(1)} %get-tuple-element.103), channel_id=1, source_target_pairs={{0,15},{1,2},{2,1},{3,4},{4,3},{5,6},{6,5},{7,8},{8,7},{9,10},{10,... | collective-permute-start | bytes 258056 | tf_op jit(solution)/shard_map/ppermute | solution.py:620
  60.4 1.9 %collective-permute-start.13 = (f32[168,128]{1,0:T(8,128)S(1)}, f32[168,128]{1,0:T(8,128)S(1)}, u32[]{:S(2)}, u32[]{:S(2)}) collective-permute-start(f32[168,128]{1,0:T(8,128)S(1)} %get-tuple-element.104), channel_id=1, source_target_pairs={{0,1},{1,0},{2,3},{3,2},{4,5},{5,4},{6,7},{7,6},{8,9},{9,8},{10,11... | collective-permute-start | bytes 258056 | tf_op jit(solution)/shard_map/ppermute | solution.py:620
  62.3 6.5 %collective-permute-start.14 = (f32[168,128]{1,0:T(8,128)S(1)}, f32[168,128]{1,0:T(8,128)S(1)}, u32[]{:S(2)}, u32[]{:S(2)}) collective-permute-start(f32[168,128]{1,0:T(8,128)S(1)} %get-tuple-element.105), channel_id=1, source_target_pairs={{16,32},{32,16},{48,64},{64,48},{80,96},{96,80},{112,128},{128,112... | collective-permute-start | bytes 258056 | tf_op jit(solution)/shard_map/ppermute | solution.py:626
  68.8 1.9 %collective-permute-start.15 = (f32[168,128]{1,0:T(8,128)S(1)}, f32[168,128]{1,0:T(8,128)S(1)}, u32[]{:S(2)}, u32[]{:S(2)}) collective-permute-start(f32[168,128]{1,0:T(8,128)S(1)} %get-tuple-element.106), channel_id=1, source_target_pairs={{0,16},{16,0},{32,48},{48,32},{64,80},{80,64},{96,112},{112,96},{1... | collective-permute-start | bytes 258056 | tf_op jit(solution)/shard_map/ppermute | solution.py:626
  72.0 2.2 %shard_map.128 = (f32[184,512]{1,0:T(8,128)}, f32[184,512]{1,0:T(8,128)S(1)}, f32[184,128]{1,0:T(8,128)S(1)}, f32[184,128]{1,0:T(8,128)S(1)}, f32[184,128]{1,0:T(8,128)S(1)}, /*index=5*/f32[184,128]{1,0:T(8,128)S(1)}) custom-call(s32[3]{0:T(128)S(1)} %pad_add_fusion.place, f32[168,512]{1,0:T(8,128)S(1)} %get-tuple-element.102.t, ...), custom_call_target="tpu_custom_call" | custom-call | flops 1000000 | bytes 1000000 | tf_op jit(solution)/shard_map/pallas_call | solution.py:598
  74.3 5.0 %collective-permute-start.16 = (f32[184,128]{1,0:T(8,128)S(1)}, f32[184,128]{1,0:T(8,128)S(1)}, u32[]{:S(2)}, u32[]{:S(2)}) collective-permute-start(f32[184,128]{1,0:T(8,128)S(1)} %get-tuple-element.108), channel_id=1, source_target_pairs={{0,15},{1,2},{2,1},{3,4},{4,3},{5,6},{6,5},{7,8},{8,7},{9,10},{10,... | collective-permute-start | bytes 282632 | tf_op jit(solution)/shard_map/ppermute | solution.py:620
  79.2 1.9 %collective-permute-start.17 = (f32[184,128]{1,0:T(8,128)S(1)}, f32[184,128]{1,0:T(8,128)S(1)}, u32[]{:S(2)}, u32[]{:S(2)}) collective-permute-start(f32[184,128]{1,0:T(8,128)S(1)} %get-tuple-element.109), channel_id=1, source_target_pairs={{0,1},{1,0},{2,3},{3,2},{4,5},{5,4},{6,7},{7,6},{8,9},{9,8},{10,11... | collective-permute-start | bytes 282632 | tf_op jit(solution)/shard_map/ppermute | solution.py:620
  81.2 3.9 %collective-permute-start.18 = (f32[184,128]{1,0:T(8,128)S(1)}, f32[184,128]{1,0:T(8,128)S(1)}, u32[]{:S(2)}, u32[]{:S(2)}) collective-permute-start(f32[184,128]{1,0:T(8,128)S(1)} %get-tuple-element.110), channel_id=1, source_target_pairs={{16,32},{32,16},{48,64},{64,48},{80,96},{96,80},{112,128},{128,112... | collective-permute-start | bytes 282632 | tf_op jit(solution)/shard_map/ppermute | solution.py:626
  85.1 1.9 %collective-permute-start.19 = (f32[184,128]{1,0:T(8,128)S(1)}, f32[184,128]{1,0:T(8,128)S(1)}, u32[]{:S(2)}, u32[]{:S(2)}) collective-permute-start(f32[184,128]{1,0:T(8,128)S(1)} %get-tuple-element.111), channel_id=1, source_target_pairs={{0,16},{16,0},{32,48},{48,32},{64,80},{80,64},{96,112},{112,96},{1... | collective-permute-start | bytes 282632 | tf_op jit(solution)/shard_map/ppermute | solution.py:626
  88.2 2.4 %shard_map.129 = (f32[200,512]{1,0:T(8,128)}, f32[16,32,128]{2,1,0:T(8,128)}) custom-call(s32[3]{0:T(128)S(1)} %pad_add_fusion.place, f32[184,512]{1,0:T(8,128)S(1)} %get-tuple-element.107.q, f32[184,128]{1,0:T(8,128)S(1)} %collective-permute-done.16.g0, f32[184,128]{1,0:T(8,128)S(1)} %collective-permute-done.17.g1, ...), custom_call_target="tpu_custom_call" | custom-call | flops 1000000 | bytes 1000000 | tf_op jit(solution)/shard_map/pallas_call | solution.py:598
  90.6 4.6 %all-to-all-start = ((f32[16,32,128]{2,1,0:T(8,128)}), f32[16,32,128]{2,1,0:T(8,128)S(1)}, u32[]{:S(2)}, u32[]{:S(2)}) async-start(f32[16,32,128]{2,1,0:T(8,128)} %get-tuple-element.115), calls=%async_computation | async-start | bytes 524288 | tf_op jit(solution)/shard_map/all_to_all | solution.py:634
  95.2 2.9 %shard_map.130 = (f32[200,512]{1,0:T(8,128)}, f32[200,128]{1,0:T(8,128)S(1)}, f32[200,128]{1,0:T(8,128)S(1)}, f32[200,128]{1,0:T(8,128)S(1)}, f32[200,128]{1,0:T(8,128)S(1)}) custom-call(s32[3]{0:T(128)S(1)} %pad_add_fusion.place, f32[200,512]{1,0:T(8,128)} %get-tuple-element.116.v2, f32[1,512]{1,0:T(1,128)S(1)} %get-tuple-element.92.after.share, ...), custom_call_target="tpu_custom_call" | custom-call | flops 500000000 | bytes 1000000 | tf_op jit(solution)/shard_map/pallas_call | solution.py:598
  99.4 4.1 %all-to-all-done.got = f32[16,32,128]{2,1,0:T(8,128)S(1)} async-done(((f32[16,32,128]{2,1,0:T(8,128)}), f32[16,32,128]{2,1,0:T(8,128)S(1)}, u32[]{:S(2)}, u32[]{:S(2)}) %all-to-all-start) | async-done | bytes 262176 | tf_op jit(solution)/shard_map/all_to_all | solution.py:634
  104.3 10.8 %all-to-all-start.1 = ((f32[16,32,128]{2,1,0:T(8,128)}), f32[16,32,128]{2,1,0:T(8,128)S(1)}, u32[]{:S(2)}, u32[]{:S(2)}) async-start(f32[16,32,128]{2,1,0:T(8,128)} %shard_map.131), calls=%async_computation.1 | async-start | bytes 524288 | tf_op jit(solution)/shard_map/all_to_all | solution.py:634
  115.2 2.8 %collective-permute-start.20 = (f32[200,128]{1,0:T(8,128)S(1)}, f32[200,128]{1,0:T(8,128)S(1)}, u32[]{:S(2)}, u32[]{:S(2)}) collective-permute-start(f32[200,128]{1,0:T(8,128)S(1)} %copy-done.3), channel_id=1, source_target_pairs={{0,15},{1,2},{2,1},{3,4},{4,3},{5,6},{6,5},{7,8},{8,7},{9,10},{10,... | collective-permute-start | bytes 307208 | tf_op jit(solution)/shard_map/ppermute | solution.py:620
  118.0 1.9 %collective-permute-start.21 = (f32[200,128]{1,0:T(8,128)S(1)}, f32[200,128]{1,0:T(8,128)S(1)}, u32[]{:S(2)}, u32[]{:S(2)}) collective-permute-start(f32[200,128]{1,0:T(8,128)S(1)} %copy-done.1), channel_id=1, source_target_pairs={{0,1},{1,0},{2,3},{3,2},{4,5},{5,4},{6,7},{7,6},{8,9},{9,8},{10,11... | collective-permute-start | bytes 307208 | tf_op jit(solution)/shard_map/ppermute | solution.py:620
  119.9 6.6 %collective-permute-start.22 = (f32[200,128]{1,0:T(8,128)S(1)}, f32[200,128]{1,0:T(8,128)S(1)}, u32[]{:S(2)}, u32[]{:S(2)}) collective-permute-start(f32[200,128]{1,0:T(8,128)S(1)} %get-tuple-element.127), channel_id=1, source_target_pairs={{16,32},{32,16},{48,64},{64,48},{80,96},{96,80},{112,128},{128,112... | collective-permute-start | bytes 307208 | tf_op jit(solution)/shard_map/ppermute | solution.py:626
  126.5 1.9 %collective-permute-start.23 = (f32[200,128]{1,0:T(8,128)S(1)}, f32[200,128]{1,0:T(8,128)S(1)}, u32[]{:S(2)}, u32[]{:S(2)}) collective-permute-start(f32[200,128]{1,0:T(8,128)S(1)} %get-tuple-element.128), channel_id=1, source_target_pairs={{0,16},{16,0},{32,48},{48,32},{64,80},{80,64},{96,112},{112,96},{1... | collective-permute-start | bytes 307208 | tf_op jit(solution)/shard_map/ppermute | solution.py:626
  128.4 1.9 %collective-permute-done.22.g2 = f32[200,128]{1,0:T(8,128)S(1)} collective-permute-done((f32[200,128]{1,0:T(8,128)S(1)}, f32[200,128]{1,0:T(8,128)S(1)}, u32[]{:S(2)}, u32[]{:S(2)}) %collective-permute-start.22) | collective-permute-done | bytes 102432 | tf_op jit(solution)/shard_map/ppermute | solution.py:626
  130.4 6.5 %collective-permute-start.24 = (f32[16,32,128]{2,1,0:T(8,128)S(1)}, f32[16,32,128]{2,1,0:T(8,128)S(1)}, u32[]{:S(2)}, u32[]{:S(2)}) collective-permute-start(f32[16,32,128]{2,1,0:T(8,128)S(1)} %all-to-all-done.1.mine), channel_id=1, source_target_pairs={{0,16},{16,0},{32,48},{48,32},{64,80},{80,64},{96,112},{112,96},{1... | collective-permute-start | bytes 786440 | tf_op jit(solution)/shard_map/ppermute | solution.py:738
  138.1 6.1 %shard_map.132 = (f32[128,512]{1,0:T(8,128)}, f32[128,512]{1,0:T(8,128)}, f32[128,512]{1,0:T(8,128)}, f32[128,512]{1,0:T(8,128)}, f32[128,512]{1,0:T(8,128)}, /*...) custom-call(s32[3]{0:T(128)S(1)} %pad_add_fusion.place, ...), custom_call_target="tpu_custom_call" | custom-call | flops 1000000 | bytes 1000000 | tf_op jit(solution)/shard_map/pallas_call | solution.py:598
  144.2 4.0 %all-to-all-start.2 = ((f32[32,1,1152]{2,1,0:T(1,128)}), f32[32,1,1152]{2,1,0:T(1,128)S(1)}, u32[]{:S(2)}, u32[]{:S(2)}) async-start(f32[32,1,1152]{2,1,0:T(1,128)} %get-tuple-element.137), calls=%async_computation.2 | async-start | bytes 294912 | tf_op jit(solution)/shard_map/all_to_all | solution.py:634
  148.2 6.7 %collective-permute-start.25 = (f32[128,128]{1,0:T(8,128)S(1)}, f32[128,128]{1,0:T(8,128)S(1)}, u32[]{:S(2)}, u32[]{:S(2)}) collective-permute-start(f32[128,128]{1,0:T(8,128)S(1)} %get-tuple-element.138), channel_id=1, source_target_pairs={{0,15},{1,2},{2,1},{3,4},{4,3},{5,6},{6,5},{7,8},{8,7},{9,10},{10,... | collective-permute-start | bytes 196616 | tf_op jit(solution)/shard_map/ppermute | solution.py:620
  154.9 1.9 %collective-permute-start.26 = (f32[128,128]{1,0:T(8,128)S(1)}, f32[128,128]{1,0:T(8,128)S(1)}, u32[]{:S(2)}, u32[]{:S(2)}) collective-permute-start(f32[128,128]{1,0:T(8,128)S(1)} %get-tuple-element.139), channel_id=1, source_target_pairs={{0,1},{1,0},{2,3},{3,2},{4,5},{5,4},{6,7},{7,6},{8,9},{9,8},{10,11... | collective-permute-start | bytes 196616 | tf_op jit(solution)/shard_map/ppermute | solution.py:620
  156.8 3.1 %collective-permute-done.26.g1 = f32[128,128]{1,0:T(8,128)S(1)} collective-permute-done((f32[128,128]{1,0:T(8,128)S(1)}, f32[128,128]{1,0:T(8,128)S(1)}, u32[]{:S(2)}, u32[]{:S(2)}) %collective-permute-start.26) | collective-permute-done | bytes 65568 | tf_op jit(solution)/shard_map/ppermute | solution.py:620
  160.6 10.3 %all-to-all-start.3 = ((f32[16,1,1152]{2,1,0:T(1,128)}), f32[16,1,1152]{2,1,0:T(1,128)S(1)}, u32[]{:S(2)}, u32[]{:S(2)}) async-start(f32[16,1,1152]{2,1,0:T(1,128)} %shard_map.133), calls=%async_computation.3 | async-start | bytes 147456 | tf_op jit(solution)/shard_map/all_to_all | solution.py:634
  170.9 5.4 %collective-permute-start.27 = (f32[128,128]{1,0:T(8,128)S(1)}, f32[128,128]{1,0:T(8,128)S(1)}, u32[]{:S(2)}, u32[]{:S(2)}) collective-permute-start(f32[128,128]{1,0:T(8,128)S(1)} %get-tuple-element.147), channel_id=1, source_target_pairs={{16,32},{32,16},{48,64},{64,48},{80,96},{96,80},{112,128},{128,112... | collective-permute-start | bytes 196616 | tf_op jit(solution)/shard_map/ppermute | solution.py:626
  176.3 1.9 %collective-permute-start.28 = (f32[128,128]{1,0:T(8,128)S(1)}, f32[128,128]{1,0:T(8,128)S(1)}, u32[]{:S(2)}, u32[]{:S(2)}) collective-permute-start(f32[128,128]{1,0:T(8,128)S(1)} %get-tuple-element.148), channel_id=1, source_target_pairs={{0,16},{16,0},{32,48},{48,32},{64,80},{80,64},{96,112},{112,96},{1... | collective-permute-start | bytes 196616 | tf_op jit(solution)/shard_map/ppermute | solution.py:626
  179.5 3.1 %all-to-all-done.3.got = f32[16,1,1152]{2,1,0:T(1,128)S(1)} async-done(((f32[16,1,1152]{2,1,0:T(1,128)}), f32[16,1,1152]{2,1,0:T(1,128)S(1)}, u32[]{:S(2)}, u32[]{:S(2)}) %all-to-all-start.3) | async-done | bytes 73760 | tf_op jit(solution)/shard_map/all_to_all | solution.py:634
  182.6 3.4 %shard_map.134 = (f32[128,512]{1,0:T(8,128)}, f32[128,512]{1,0:T(8,128)}) custom-call(s32[3]{0:T(128)S(1)} %pad_add_fusion.place, f32[16,1,1152]{2,1,0:T(1,128)S(1)} %all-to-all-done.3.got, f32[128,512]{1,0:T(8,128)S(1)} %get-tuple-element.144.q, f32[128,128]{1,0:T(8,128)S(1)} %collective-permute-done.25.g0, f32[128,128]{1,0:T(8,128)S(1)} %collective-permute-done.26.g1, ...), custom_call_target="tpu_custom_call" | custom-call | flops 1000000 | bytes 1000000 | tf_op jit(solution)/shard_map/pallas_call | solution.py:598
  (41 shorter events, 10.0 us)
Async XLA Ops:
  2.6 19.0 %collective-permute-start = (f32[136,128]{1,0:T(8,128)S(1)}, f32[136,128]{1,0:T(8,128)S(1)}, u32[]{:S(2)}, u32[]{:S(2)}) collective-permute-start(f32[136,128]{1,0:T(8,128)S(1)} %get-tuple-element.80), channel_id=1, source_target_pairs={{0,15},{1,2},{2,1},{3,4},{4,3},{5,6},{6,5},{7,8},{8,7},{9,10},{10,... | collective-permute-start | bytes 208904 | tf_op jit(solution)/shard_map/ppermute | solution.py:620
  10.3 11.4 %collective-permute-start.1 = (f32[136,128]{1,0:T(8,128)S(1)}, f32[136,128]{1,0:T(8,128)S(1)}, u32[]{:S(2)}, u32[]{:S(2)}) collective-permute-start(f32[136,128]{1,0:T(8,128)S(1)} %get-tuple-element.81), channel_id=1, source_target_pairs={{0,1},{1,0},{2,3},{3,2},{4,5},{5,4},{6,7},{7,6},{8,9},{9,8},{10,11... | collective-permute-start | bytes 208904 | tf_op jit(solution)/shard_map/ppermute | solution.py:620
  12.2 9.5 %collective-permute-start.2 = (f32[136,128]{1,0:T(8,128)S(1)}, f32[136,128]{1,0:T(8,128)S(1)}, u32[]{:S(2)}, u32[]{:S(2)}) collective-permute-start(f32[136,128]{1,0:T(8,128)S(1)} %get-tuple-element.82), channel_id=1, source_target_pairs={{16,32},{32,16},{48,64},{64,48},{80,96},{96,80},{112,128},{128,112... | collective-permute-start | bytes 208904 | tf_op jit(solution)/shard_map/ppermute | solution.py:626
  16.6 5.1 %collective-permute-start.3 = (f32[136,128]{1,0:T(8,128)S(1)}, f32[136,128]{1,0:T(8,128)S(1)}, u32[]{:S(2)}, u32[]{:S(2)}) collective-permute-start(f32[136,128]{1,0:T(8,128)S(1)} %get-tuple-element.83), channel_id=1, source_target_pairs={{0,16},{16,0},{32,48},{48,32},{64,80},{80,64},{96,112},{112,96},{1... | collective-permute-start | bytes 208904 | tf_op jit(solution)/shard_map/ppermute | solution.py:626
  22.8 14.1 %collective-permute-start.4 = (f32[136,128]{1,0:T(8,128)S(1)}, f32[136,128]{1,0:T(8,128)S(1)}, u32[]{:S(2)}, u32[]{:S(2)}) collective-permute-start(f32[136,128]{1,0:T(8,128)S(1)} %get-tuple-element.88), channel_id=1, source_target_pairs={{0,15},{1,2},{2,1},{3,4},{4,3},{5,6},{6,5},{7,8},{8,7},{9,10},{10,... | collective-permute-start | bytes 208904 | tf_op jit(solution)/shard_map/ppermute | solution.py:620
  27.2 9.8 %collective-permute-start.5 = (f32[136,128]{1,0:T(8,128)S(1)}, f32[136,128]{1,0:T(8,128)S(1)}, u32[]{:S(2)}, u32[]{:S(2)}) collective-permute-start(f32[136,128]{1,0:T(8,128)S(1)} %get-tuple-element.89), channel_id=1, source_target_pairs={{0,1},{1,0},{2,3},{3,2},{4,5},{5,4},{6,7},{7,6},{8,9},{9,8},{10,11... | collective-permute-start | bytes 208904 | tf_op jit(solution)/shard_map/ppermute | solution.py:620
  29.2 7.8 %collective-permute-start.6 = (f32[136,128]{1,0:T(8,128)S(1)}, f32[136,128]{1,0:T(8,128)S(1)}, u32[]{:S(2)}, u32[]{:S(2)}) collective-permute-start(f32[136,128]{1,0:T(8,128)S(1)} %get-tuple-element.90), channel_id=1, source_target_pairs={{16,32},{32,16},{48,64},{64,48},{80,96},{96,80},{112,128},{128,112... | collective-permute-start | bytes 208904 | tf_op jit(solution)/shard_map/ppermute | solution.py:626
  32.7 4.4 %collective-permute-start.7 = (f32[136,128]{1,0:T(8,128)S(1)}, f32[136,128]{1,0:T(8,128)S(1)}, u32[]{:S(2)}, u32[]{:S(2)}) collective-permute-start(f32[136,128]{1,0:T(8,128)S(1)} %get-tuple-element.91), channel_id=1, source_target_pairs={{0,16},{16,0},{32,48},{48,32},{64,80},{80,64},{96,112},{112,96},{1... | collective-permute-start | bytes 208904 | tf_op jit(solution)/shard_map/ppermute | solution.py:626
  39.2 12.8 %collective-permute-start.10 = (f32[152,128]{1,0:T(8,128)S(1)}, f32[152,128]{1,0:T(8,128)S(1)}, u32[]{:S(2)}, u32[]{:S(2)}) collective-permute-start(f32[152,128]{1,0:T(8,128)S(1)} %get-tuple-element.99), channel_id=1, source_target_pairs={{16,32},{32,16},{48,64},{64,48},{80,96},{96,80},{112,128},{128,112... | collective-permute-start | bytes 233480 | tf_op jit(solution)/shard_map/ppermute | solution.py:626
  43.1 8.8 %collective-permute-start.11 = (f32[152,128]{1,0:T(8,128)S(1)}, f32[152,128]{1,0:T(8,128)S(1)}, u32[]{:S(2)}, u32[]{:S(2)}) collective-permute-start(f32[152,128]{1,0:T(8,128)S(1)} %get-tuple-element.100), channel_id=1, source_target_pairs={{0,16},{16,0},{32,48},{48,32},{64,80},{80,64},{96,112},{112,96},{1... | collective-permute-start | bytes 233480 | tf_op jit(solution)/shard_map/ppermute | solution.py:626
  45.0 8.5 %collective-permute-start.8 = (f32[152,128]{1,0:T(8,128)S(1)}, f32[152,128]{1,0:T(8,128)S(1)}, u32[]{:S(2)}, u32[]{:S(2)}) collective-permute-start(f32[152,128]{1,0:T(8,128)S(1)} %get-tuple-element.97), channel_id=1, source_target_pairs={{0,15},{1,2},{2,1},{3,4},{4,3},{5,6},{6,5},{7,8},{8,7},{9,10},{10,... | collective-permute-start | bytes 233480 | tf_op jit(solution)/shard_map/ppermute | solution.py:620
  50.0 5.1 %collective-permute-start.9 = (f32[152,128]{1,0:T(8,128)S(1)}, f32[152,128]{1,0:T(8,128)S(1)}, u32[]{:S(2)}, u32[]{:S(2)}) collective-permute-start(f32[152,128]{1,0:T(8,128)S(1)} %get-tuple-element.98), channel_id=1, source_target_pairs={{0,1},{1,0},{2,3},{3,2},{4,5},{5,4},{6,7},{7,6},{8,9},{9,8},{10,11... | collective-permute-start | bytes 233480 | tf_op jit(solution)/shard_map/ppermute | solution.py:620
  56.4 14.4 %collective-permute-start.12 = (f32[168,128]{1,0:T(8,128)S(1)}, f32[168,128]{1,0:T(8,128)S(1)}, u32[]{:S(2)}, u32[]{:S(2)}) collective-permute-start(f32[168,128]{1,0:T(8,128)S(1)} %get-tuple-element.103), channel_id=1, source_target_pairs={{0,15},{1,2},{2,1},{3,4},{4,3},{5,6},{6,5},{7,8},{8,7},{9,10},{10,... | collective-permute-start | bytes 258056 | tf_op jit(solution)/shard_map/ppermute | solution.py:620
  60.4 10.4 %collective-permute-start.13 = (f32[168,128]{1,0:T(8,128)S(1)}, f32[168,128]{1,0:T(8,128)S(1)}, u32[]{:S(2)}, u32[]{:S(2)}) collective-permute-start(f32[168,128]{1,0:T(8,128)S(1)} %get-tuple-element.104), channel_id=1, source_target_pairs={{0,1},{1,0},{2,3},{3,2},{4,5},{5,4},{6,7},{7,6},{8,9},{9,8},{10,11... | collective-permute-start | bytes 258056 | tf_op jit(solution)/shard_map/ppermute | solution.py:620
  62.3 8.7 %collective-permute-start.14 = (f32[168,128]{1,0:T(8,128)S(1)}, f32[168,128]{1,0:T(8,128)S(1)}, u32[]{:S(2)}, u32[]{:S(2)}) collective-permute-start(f32[168,128]{1,0:T(8,128)S(1)} %get-tuple-element.105), channel_id=1, source_target_pairs={{16,32},{32,16},{48,64},{64,48},{80,96},{96,80},{112,128},{128,112... | collective-permute-start | bytes 258056 | tf_op jit(solution)/shard_map/ppermute | solution.py:626
  68.8 3.2 %collective-permute-start.15 = (f32[168,128]{1,0:T(8,128)S(1)}, f32[168,128]{1,0:T(8,128)S(1)}, u32[]{:S(2)}, u32[]{:S(2)}) collective-permute-start(f32[168,128]{1,0:T(8,128)S(1)} %get-tuple-element.106), channel_id=1, source_target_pairs={{0,16},{16,0},{32,48},{48,32},{64,80},{80,64},{96,112},{112,96},{1... | collective-permute-start | bytes 258056 | tf_op jit(solution)/shard_map/ppermute | solution.py:626
  74.3 12.7 %collective-permute-start.16 = (f32[184,128]{1,0:T(8,128)S(1)}, f32[184,128]{1,0:T(8,128)S(1)}, u32[]{:S(2)}, u32[]{:S(2)}) collective-permute-start(f32[184,128]{1,0:T(8,128)S(1)} %get-tuple-element.108), channel_id=1, source_target_pairs={{0,15},{1,2},{2,1},{3,4},{4,3},{5,6},{6,5},{7,8},{8,7},{9,10},{10,... | collective-permute-start | bytes 282632 | tf_op jit(solution)/shard_map/ppermute | solution.py:620
  79.2 7.8 %collective-permute-start.17 = (f32[184,128]{1,0:T(8,128)S(1)}, f32[184,128]{1,0:T(8,128)S(1)}, u32[]{:S(2)}, u32[]{:S(2)}) collective-permute-start(f32[184,128]{1,0:T(8,128)S(1)} %get-tuple-element.109), channel_id=1, source_target_pairs={{0,1},{1,0},{2,3},{3,2},{4,5},{5,4},{6,7},{7,6},{8,9},{9,8},{10,11... | collective-permute-start | bytes 282632 | tf_op jit(solution)/shard_map/ppermute | solution.py:620
  81.2 6.1 %collective-permute-start.18 = (f32[184,128]{1,0:T(8,128)S(1)}, f32[184,128]{1,0:T(8,128)S(1)}, u32[]{:S(2)}, u32[]{:S(2)}) collective-permute-start(f32[184,128]{1,0:T(8,128)S(1)} %get-tuple-element.110), channel_id=1, source_target_pairs={{16,32},{32,16},{48,64},{64,48},{80,96},{96,80},{112,128},{128,112... | collective-permute-start | bytes 282632 | tf_op jit(solution)/shard_map/ppermute | solution.py:626
  85.1 3.2 %collective-permute-start.19 = (f32[184,128]{1,0:T(8,128)S(1)}, f32[184,128]{1,0:T(8,128)S(1)}, u32[]{:S(2)}, u32[]{:S(2)}) collective-permute-start(f32[184,128]{1,0:T(8,128)S(1)} %get-tuple-element.111), channel_id=1, source_target_pairs={{0,16},{16,0},{32,48},{48,32},{64,80},{80,64},{96,112},{112,96},{1... | collective-permute-start | bytes 282632 | tf_op jit(solution)/shard_map/ppermute | solution.py:626
  90.6 12.9 %all-to-all-start = ((f32[16,32,128]{2,1,0:T(8,128)}), f32[16,32,128]{2,1,0:T(8,128)S(1)}, u32[]{:S(2)}, u32[]{:S(2)}) async-start(f32[16,32,128]{2,1,0:T(8,128)} %get-tuple-element.115), calls=%async_computation | async-start | bytes 524288 | tf_op jit(solution)/shard_map/all_to_all | solution.py:634
  98.1 0.6 copy-start
  98.8 0.6 copy-start.2
  104.3 10.8 %copy-start.3 = (f32[200,128]{1,0:T(8,128)S(1)}, f32[200,128]{1,0:T(8,128)}, u32[]{:S(2)}) copy-start(f32[200,128]{1,0:T(8,128)} %copy-done.2) | copy-start | bytes 307204
  104.3 13.7 %copy-start.1 = (f32[200,128]{1,0:T(8,128)S(1)}, f32[200,128]{1,0:T(8,128)}, u32[]{:S(2)}) copy-start(f32[200,128]{1,0:T(8,128)} %copy-done) | copy-start | bytes 307204
  104.3 26.0 %all-to-all-start.1 = ((f32[16,32,128]{2,1,0:T(8,128)}), f32[16,32,128]{2,1,0:T(8,128)S(1)}, u32[]{:S(2)}, u32[]{:S(2)}) async-start(f32[16,32,128]{2,1,0:T(8,128)} %shard_map.131), calls=%async_computation.1 | async-start | bytes 524288 | tf_op jit(solution)/shard_map/all_to_all | solution.py:634
  115.2 13.2 %collective-permute-start.20 = (f32[200,128]{1,0:T(8,128)S(1)}, f32[200,128]{1,0:T(8,128)S(1)}, u32[]{:S(2)}, u32[]{:S(2)}) collective-permute-start(f32[200,128]{1,0:T(8,128)S(1)} %copy-done.3), channel_id=1, source_target_pairs={{0,15},{1,2},{2,1},{3,4},{4,3},{5,6},{6,5},{7,8},{8,7},{9,10},{10,... | collective-permute-start | bytes 307208 | tf_op jit(solution)/shard_map/ppermute | solution.py:620
  118.0 10.4 %collective-permute-start.21 = (f32[200,128]{1,0:T(8,128)S(1)}, f32[200,128]{1,0:T(8,128)S(1)}, u32[]{:S(2)}, u32[]{:S(2)}) collective-permute-start(f32[200,128]{1,0:T(8,128)S(1)} %copy-done.1), channel_id=1, source_target_pairs={{0,1},{1,0},{2,3},{3,2},{4,5},{5,4},{6,7},{7,6},{8,9},{9,8},{10,11... | collective-permute-start | bytes 307208 | tf_op jit(solution)/shard_map/ppermute | solution.py:620
  119.9 10.4 %collective-permute-start.22 = (f32[200,128]{1,0:T(8,128)S(1)}, f32[200,128]{1,0:T(8,128)S(1)}, u32[]{:S(2)}, u32[]{:S(2)}) collective-permute-start(f32[200,128]{1,0:T(8,128)S(1)} %get-tuple-element.127), channel_id=1, source_target_pairs={{16,32},{32,16},{48,64},{64,48},{80,96},{96,80},{112,128},{128,112... | collective-permute-start | bytes 307208 | tf_op jit(solution)/shard_map/ppermute | solution.py:626
  126.5 3.9 %collective-permute-start.23 = (f32[200,128]{1,0:T(8,128)S(1)}, f32[200,128]{1,0:T(8,128)S(1)}, u32[]{:S(2)}, u32[]{:S(2)}) collective-permute-start(f32[200,128]{1,0:T(8,128)S(1)} %get-tuple-element.128), channel_id=1, source_target_pairs={{0,16},{16,0},{32,48},{48,32},{64,80},{80,64},{96,112},{112,96},{1... | collective-permute-start | bytes 307208 | tf_op jit(solution)/shard_map/ppermute | solution.py:626
  130.4 7.7 %collective-permute-start.24 = (f32[16,32,128]{2,1,0:T(8,128)S(1)}, f32[16,32,128]{2,1,0:T(8,128)S(1)}, u32[]{:S(2)}, u32[]{:S(2)}) collective-permute-start(f32[16,32,128]{2,1,0:T(8,128)S(1)} %all-to-all-done.1.mine), channel_id=1, source_target_pairs={{0,16},{16,0},{32,48},{48,32},{64,80},{80,64},{96,112},{112,96},{1... | collective-permute-start | bytes 786440 | tf_op jit(solution)/shard_map/ppermute | solution.py:738
  144.2 15.7 %all-to-all-start.2 = ((f32[32,1,1152]{2,1,0:T(1,128)}), f32[32,1,1152]{2,1,0:T(1,128)S(1)}, u32[]{:S(2)}, u32[]{:S(2)}) async-start(f32[32,1,1152]{2,1,0:T(1,128)} %get-tuple-element.137), calls=%async_computation.2 | async-start | bytes 294912 | tf_op jit(solution)/shard_map/all_to_all | solution.py:634
  148.2 8.6 %collective-permute-start.25 = (f32[128,128]{1,0:T(8,128)S(1)}, f32[128,128]{1,0:T(8,128)S(1)}, u32[]{:S(2)}, u32[]{:S(2)}) collective-permute-start(f32[128,128]{1,0:T(8,128)S(1)} %get-tuple-element.138), channel_id=1, source_target_pairs={{0,15},{1,2},{2,1},{3,4},{4,3},{5,6},{6,5},{7,8},{8,7},{9,10},{10,... | collective-permute-start | bytes 196616 | tf_op jit(solution)/shard_map/ppermute | solution.py:620
  154.9 5.0 %collective-permute-start.26 = (f32[128,128]{1,0:T(8,128)S(1)}, f32[128,128]{1,0:T(8,128)S(1)}, u32[]{:S(2)}, u32[]{:S(2)}) collective-permute-start(f32[128,128]{1,0:T(8,128)S(1)} %get-tuple-element.139), channel_id=1, source_target_pairs={{0,1},{1,0},{2,3},{3,2},{4,5},{5,4},{6,7},{7,6},{8,9},{9,8},{10,11... | collective-permute-start | bytes 196616 | tf_op jit(solution)/shard_map/ppermute | solution.py:620
  160.6 22.0 %all-to-all-start.3 = ((f32[16,1,1152]{2,1,0:T(1,128)}), f32[16,1,1152]{2,1,0:T(1,128)S(1)}, u32[]{:S(2)}, u32[]{:S(2)}) async-start(f32[16,1,1152]{2,1,0:T(1,128)} %shard_map.133), calls=%async_computation.3 | async-start | bytes 147456 | tf_op jit(solution)/shard_map/all_to_all | solution.py:634
  170.9 8.2 %collective-permute-start.27 = (f32[128,128]{1,0:T(8,128)S(1)}, f32[128,128]{1,0:T(8,128)S(1)}, u32[]{:S(2)}, u32[]{:S(2)}) collective-permute-start(f32[128,128]{1,0:T(8,128)S(1)} %get-tuple-element.147), channel_id=1, source_target_pairs={{16,32},{32,16},{48,64},{64,48},{80,96},{96,80},{112,128},{128,112... | collective-permute-start | bytes 196616 | tf_op jit(solution)/shard_map/ppermute | solution.py:626
  176.3 3.1 %collective-permute-start.28 = (f32[128,128]{1,0:T(8,128)S(1)}, f32[128,128]{1,0:T(8,128)S(1)}, u32[]{:S(2)}, u32[]{:S(2)}) collective-permute-start(f32[128,128]{1,0:T(8,128)S(1)} %get-tuple-element.148), channel_id=1, source_target_pairs={{0,16},{16,0},{32,48},{48,32},{64,80},{80,64},{96,112},{112,96},{1... | collective-permute-start | bytes 196616 | tf_op jit(solution)/shard_map/ppermute | solution.py:626

commit v7 on v6

--- a/solution.py
+++ b/solution.py
@@ -176,7 +176,9 @@
         copy.wait()
 
 
-def k_prepare(place, load, rho, order, shared_o, order_o, s0, s1, s2, s3, load_s, rho_s, sem):
+def k_prepare(
+    place, load, rho, order, neumann, shared_o, order_o, s0, s1, s2, s3, neumann_o, load_s, rho_s, sem, far_sem
+):
     at = Place(place)
     copies = [
         pltpu.make_async_copy(source, target, sem.at[n])
@@ -184,6 +186,7 @@
     ]
     for copy in copies:
         copy.start()
+    ahead = begin(neumann, neumann_o, far_sem, 4)
     copies[0].wait()
     hots = one_hot_faces(order_o[...])
     copies[1].wait()
@@ -192,16 +195,13 @@
     full = to_shared(jnp.concatenate([load_s[...], rho_s[...], pad], axis=0), hots)
     shared_o[...] = full
     put_sends((s0, s1, s2, s3), full, at)
-
-
-def k_neumann(order, neumann, lists, neumann_o, avg_o, neumann_s, lists_s, sem):
+    finish(ahead)
+
+
+def k_neumann(order, neumann_s, lists, couple, neumann_o, avg_o, couple_o, lists_s, sem):
     listed = pltpu.make_async_copy(lists, lists_s, sem.at[4])
     listed.start()
-    copies = []
-    for f in range(4):
-        rows = pl.ds(f * LANES, LANES)
-        copies.append(pltpu.make_async_copy(neumann.at[rows], neumann_s.at[rows], sem.at[f]))
-        copies[f].start()
+    ahead = begin(couple, couple_o, sem, 4)
     hots = one_hot_faces(order[...])
     points = order.shape[1]
     listed.wait()
@@ -214,36 +214,32 @@
     avg_o[...] = to_shared(total * (1.0 / length), hots)
     for f in range(4):
         rows = slice(f * LANES, (f + 1) * LANES)
-        copies[f].wait()
         for n, piece in enumerate(cut(neumann_s[rows, :], PIECES)):
             half = narrow(hots[f], piece).astype(BF16)
             neumann_o[n, rows, :] = jnp.concatenate(
                 [narrow(part, hot, True) for part, hot in zip(faces_of(half), hots)], axis=1
             ).astype(BF16)
+    finish(ahead)
 
 
 def k_couple(
-    order, after, diag, couple, blocks, row_coarse, lower, upper,
+    order, after, couple_s, diag, blocks, row_coarse, lower, upper,
     diag_o, couple_o, blocks_o, coefs_o,
-    diag_s, couple_s, blocks_s, rows_s, lower_s, upper_s, sem,
+    diag_s, blocks_s, rows_s, lower_s, upper_s, sem,
 ):
-    copies = []
-    for f in range(4):
-        rows = pl.ds(f * LANES, LANES)
-        copies.append(pltpu.make_async_copy(couple.at[rows], couple_s.at[rows], sem.at[f]))
+    copies = [None] * 4
     copies.append(pltpu.make_async_copy(blocks, blocks_s, sem.at[4]))
     copies.append(pltpu.make_async_copy(diag, diag_s, sem.at[5]))
     copies.append(pltpu.make_async_copy(row_coarse, rows_s, sem.at[6]))
     copies.append(pltpu.make_async_copy(lower, lower_s, sem.at[7]))
     copies.append(pltpu.make_async_copy(upper, upper_s, sem.at[8]))
-    for copy in copies:
+    for copy in copies[4:]:
         copy.start()
     hots = one_hot_faces(order[...])
     copies[5].wait()
     diag_o[...] = to_shared(jnp.broadcast_to(diag_s[...], (8, diag_s.shape[1])), hots)[:1]
     for f in range(4):
         rows = slice(f * LANES, (f + 1) * LANES)
-        copies[f].wait()
         for n, piece in enumerate(cut(couple_s[rows, :], PIECES)):
             couple_o[n, rows, :] = narrow(hots[f], piece).astype(BF16)
     copies[4].wait()
@@ -456,13 +452,15 @@
     c1 = c1_s[pl.ds(pl.multiple_of(start + 16, 8), 56), :]
     c2 = c2_s[pl.ds(pl.multiple_of(start + 32, 8), 24), :]
     r0 = r[...]
-    finish(loads)
+    finish(loads[0:2])
     z0f = z0[:rhs, :] + lift(c0[32:56], z0[rhs:, :])
     v1f = v1[:rhs, :] + lift(c0[24:64], v1[rhs:, :])
+    finish(loads[2:4])
     z1f = z1[:rhs, :] + lift(
         jnp.concatenate([c0[16:72], c1[16:40]], axis=0),
         jnp.concatenate([z1[rhs:, :], z0[rhs:, :]], axis=0),
     )
+    finish(loads[4:6])
     v2f = v2[:rhs, :] + lift(
         jnp.concatenate([c0[8:80], c1[8:48]], axis=0),
         jnp.concatenate([v2[rhs:, :], v1[rhs:, :]], axis=0),
@@ -477,6 +475,7 @@
     keep(1, z1f, z1_o)
     keep(2, v1f + SHIFT * r0, w0_o)
     keep(3, v2f + SHIFT * v1f, w1_o)
+    finish(loads[6:8])
     z2 = assembled(t[...], (g0, g1, g2, g3), at, rhs)
     z2f = z2[:rhs] + lift(
         jnp.concatenate([c0, c1, c2], axis=0),
@@ -576,13 +575,12 @@
     columns = mm_t(eye, table)
     col = [columns[:, i : i + 1] for i in range(6)]
     hots = one_hot_faces(order[...])
-    finish(loads)
+    finish(loads[:6])
     x = col[0] * full_s[0] + col[1] * full_s[1] + col[2] * full_s[2]
+    x_o[...] = to_points(x, hots)
+    finish(loads[6:])
     r = r0[...] + col[3] * full_s[3] + col[4] * full_s[4] + col[5] * w2
-    both = to_points(jnp.concatenate([x, r], axis=0), hots)
-    rhs = x.shape[0]
-    x_o[...] = both[:rhs]
-    r_o[...] = both[rhs:]
+    r_o[...] = to_points(r, hots)
 
 
 def call(body, outs, place, *args, scratch=(), raw=(), raw_outs=(), flops=1_000_000):
@@ -654,21 +652,27 @@
     def bf16(*shape):
         return jax.ShapeDtypeStruct((PIECES,) + shape, BF16)
 
-    shared, order, *sends = call(
+    shared, order, *sends, neumann = call(
         k_prepare,
-        [(rhs + 8, points), jax.ShapeDtypeStruct((1, points), jnp.int32)] + face(rhs + 8),
-        place, load_terms[0, 0], diffusivity[0], face_order[0],
-        raw=(0, 1, 2),
-        scratch=[pltpu.VMEM((rhs, points), F32), pltpu.VMEM((1, points), F32), dma((3,))],
+        [(rhs + 8, points), jax.ShapeDtypeStruct((1, points), jnp.int32)]
+        + face(rhs + 8)
+        + [(points, points)],
+        place, load_terms[0, 0], diffusivity[0], face_order[0], neumann_solve[0, 0],
+        raw=(0, 1, 2, 3),
+        scratch=[
+            pltpu.VMEM((rhs, points), F32),
+            pltpu.VMEM((1, points), F32),
+            dma((3,)),
+            dma((4,)),
+        ],
     )
     got = swap(sends)
-    neumann, avg = call(
+    neumann, avg, couple = call(
         k_neumann,
-        [bf16(points, points), (8, points)],
-        None, order, neumann_solve[0, 0], primal_lists[0, 0],
-        raw=(1, 2),
+        [bf16(points, points), (8, points), (points, points)],
+        None, order, neumann, primal_lists[0, 0], coupling[0, 0],
+        raw=(2, 3),
         scratch=[
-            pltpu.VMEM((points, points), F32),
             pltpu.VMEM(primal_lists.shape[2:], jnp.int32),
             dma((5,)),
         ],
@@ -684,12 +688,11 @@
     diag, couple, blocks, coefs = call(
         k_couple,
         [(1, points), bf16(points, points), bf16(*inner), (32, LANES)],
-        None, order, share, interface_diag[0], coupling[0, 0], interior_inverse[0, 0],
+        None, order, share, couple, interface_diag[0], interior_inverse[0, 0],
         row_coarse[0], lower_coef, upper_coef,
-        raw=(2, 3, 4, 5, 6, 7),
+        raw=(3, 4, 5, 6, 7),
         scratch=[
             pltpu.VMEM((1, points), F32),
-            pltpu.VMEM((points, points), F32),
             pltpu.VMEM(inner, F32),
             pltpu.VMEM(row_coarse.shape[1:], F32),
             pltpu.VMEM(lower_coef.shape, F32),

time: 188 us -> 186 us (0.989)
  transfers between devices with their start and end apart: 33 -> 33, of which waited for: 13 -> 13; matrix products, arithmetic and copies ran while one was open for 0% -> 0% of each run, Pallas kernels for 5% -> 4%
where the time goes in v7:
time: 186 us; the launch traced here: 185 us
  starting transfers between devices  133 us (72%)
  Pallas kernels  29 us (16%)
  waiting for transfers between devices  20.3 us (11%)
    ppermute x7, starting transfers between devices, exchange_columns(): lax.ppermute(sends[0], 'circ', far)  35.4 us
    ppermute x7, starting transfers between devices, exchange_rows(): lax.ppermute(sends[2], 'axial', link)  34.2 us
    all_to_all x4, starting transfers between devices, spread(): lax.all_to_all(value, axis, split_axis=0, concat_axis=0, tiled=True, axis...  29.8 us
    pallas_call x13, Pallas kernels, call(): pl.pallas_call(body, out_shape=[out if isinstance(out, jax.ShapeDtypeStru...  29 us
    ppermute x7, starting transfers between devices, exchange_columns(): lax.ppermute(sends[1], 'circ', near)  13.4 us
    ppermute x7, starting transfers between devices, exchange_rows(): lax.ppermute(sends[3], 'axial', core)  13.4 us
    all_to_all x4, waiting for transfers between devices, spread(): lax.all_to_all(value, axis, split_axis=0, concat_axis=0, tiled=True, axis...  7.26 us
    ppermute x1, starting transfers between devices, local(): other = lax.ppermute(mine, 'axial', [(i, i ^ 1) for i in range(rows)])  6.55 us
  transfers between devices with their start and end apart: 33, of which 13 were waited for; matrix products, arithmetic and copies ran while one was open for 0% of the time, Pallas kernels for 4%

profile of v7, /device:TPU:1, one launch (start us, length us, event | category | flops | bytes accessed | tf_op | source)
XLA Modules:
  0.0 184.6 jit_solution(12012318801657389700)
XLA Ops:
  0.7 2.1 %shard_map.122 = (f32[136,512]{1,0:T(8,128)S(1)}, s32[1,512]{1,0:T(1,128)S(1)}, f32[136,128]{1,0:T(8,128)S(1)}, f32[136,128]{1,0:T(8,128)S(1)}, f32[136,128]{1,0...) custom-call(s32[3]{0:T(128)S(1)} %pad_add_fusion.place, f32[128,512]{1,0:T(8,128)} %bitcast.14, ...), custom_call_target="tpu_custom_call" | custom-call | flops 1000000 | bytes 1000000 | tf_op jit(solution)/shard_map/pallas_call | solution.py:596
  2.8 7.7 %collective-permute-start = (f32[136,128]{1,0:T(8,128)S(1)}, f32[136,128]{1,0:T(8,128)S(1)}, u32[]{:S(2)}, u32[]{:S(2)}) collective-permute-start(f32[136,128]{1,0:T(8,128)S(1)} %get-tuple-element.82), channel_id=1, source_target_pairs={{0,15},{1,2},{2,1},{3,4},{4,3},{5,6},{6,5},{7,8},{8,7},{9,10},{10,... | collective-permute-start | bytes 208904 | tf_op jit(solution)/shard_map/ppermute | solution.py:618
  10.5 1.9 %collective-permute-start.1 = (f32[136,128]{1,0:T(8,128)S(1)}, f32[136,128]{1,0:T(8,128)S(1)}, u32[]{:S(2)}, u32[]{:S(2)}) collective-permute-start(f32[136,128]{1,0:T(8,128)S(1)} %get-tuple-element.83), channel_id=1, source_target_pairs={{0,1},{1,0},{2,3},{3,2},{4,5},{5,4},{6,7},{7,6},{8,9},{9,8},{10,11... | collective-permute-start | bytes 208904 | tf_op jit(solution)/shard_map/ppermute | solution.py:618
  12.4 4.4 %collective-permute-start.2 = (f32[136,128]{1,0:T(8,128)S(1)}, f32[136,128]{1,0:T(8,128)S(1)}, u32[]{:S(2)}, u32[]{:S(2)}) collective-permute-start(f32[136,128]{1,0:T(8,128)S(1)} %get-tuple-element.84), channel_id=1, source_target_pairs={{16,32},{32,16},{48,64},{64,48},{80,96},{96,80},{112,128},{128,112... | collective-permute-start | bytes 208904 | tf_op jit(solution)/shard_map/ppermute | solution.py:624
  16.8 1.9 %collective-permute-start.3 = (f32[136,128]{1,0:T(8,128)S(1)}, f32[136,128]{1,0:T(8,128)S(1)}, u32[]{:S(2)}, u32[]{:S(2)}) collective-permute-start(f32[136,128]{1,0:T(8,128)S(1)} %get-tuple-element.85), channel_id=1, source_target_pairs={{0,16},{16,0},{32,48},{48,32},{64,80},{80,64},{96,112},{112,96},{1... | collective-permute-start | bytes 208904 | tf_op jit(solution)/shard_map/ppermute | solution.py:624
  18.8 2.6 %shard_map.123 = (bf16[2,512,512]{2,1,0:T(8,128)(2,1)S(1)}, f32[8,512]{1,0:T(8,128)S(1)}, f32[512,512]{1,0:T(8,128)S(1)}) custom-call(s32[1,512]{1,0:T(1,128)S(1)} %get-tuple-element.86.order, f32[512,512]{1,0:T(8,128)S(1)} %get-tuple-element.87.neumann_s, s32[8,64]{1,0:T(8,128)} %bitcast.21, f32[512,512]{1,0:T(8,128)} %bitcast.17), custom_call_target="tpu_custom_call" | custom-call | flops 2000000000 | bytes 1000000 | tf_op jit(solution)/shard_map/pallas_call | solution.py:596
  22.5 4.4 %collective-permute-start.4 = (f32[136,128]{1,0:T(8,128)S(1)}, f32[136,128]{1,0:T(8,128)S(1)}, u32[]{:S(2)}, u32[]{:S(2)}) collective-permute-start(f32[136,128]{1,0:T(8,128)S(1)} %get-tuple-element.91), channel_id=1, source_target_pairs={{0,15},{1,2},{2,1},{3,4},{4,3},{5,6},{6,5},{7,8},{8,7},{9,10},{10,... | collective-permute-start | bytes 208904 | tf_op jit(solution)/shard_map/ppermute | solution.py:618
  26.9 1.9 %collective-permute-start.5 = (f32[136,128]{1,0:T(8,128)S(1)}, f32[136,128]{1,0:T(8,128)S(1)}, u32[]{:S(2)}, u32[]{:S(2)}) collective-permute-start(f32[136,128]{1,0:T(8,128)S(1)} %get-tuple-element.92), channel_id=1, source_target_pairs={{0,1},{1,0},{2,3},{3,2},{4,5},{5,4},{6,7},{7,6},{8,9},{9,8},{10,11... | collective-permute-start | bytes 208904 | tf_op jit(solution)/shard_map/ppermute | solution.py:618
  28.8 3.5 %collective-permute-start.6 = (f32[136,128]{1,0:T(8,128)S(1)}, f32[136,128]{1,0:T(8,128)S(1)}, u32[]{:S(2)}, u32[]{:S(2)}) collective-permute-start(f32[136,128]{1,0:T(8,128)S(1)} %get-tuple-element.93), channel_id=1, source_target_pairs={{16,32},{32,16},{48,64},{64,48},{80,96},{96,80},{112,128},{128,112... | collective-permute-start | bytes 208904 | tf_op jit(solution)/shard_map/ppermute | solution.py:624
  32.3 1.9 %collective-permute-start.7 = (f32[136,128]{1,0:T(8,128)S(1)}, f32[136,128]{1,0:T(8,128)S(1)}, u32[]{:S(2)}, u32[]{:S(2)}) collective-permute-start(f32[136,128]{1,0:T(8,128)S(1)} %get-tuple-element.94), channel_id=1, source_target_pairs={{0,16},{16,0},{32,48},{48,32},{64,80},{80,64},{96,112},{112,96},{1... | collective-permute-start | bytes 208904 | tf_op jit(solution)/shard_map/ppermute | solution.py:624
  34.2 1.5 shard_map.125
  35.8 2.1 %shard_map.126 = (f32[152,512]{1,0:T(8,128)}, f32[152,512]{1,0:T(8,128)S(1)}, f32[152,128]{1,0:T(8,128)S(1)}, f32[152,128]{1,0:T(8,128)S(1)}, f32[152,128]{1,0:T(8,128)S(1)}, /*index=5*/f32[152,128]{1,0:T(8,128)S(1)}) custom-call(s32[3]{0:T(128)S(1)} %pad_add_fusion.place, f32[136,512]{1,0:T(8,128)S(1)} %get-tuple-element.90.t, ...), custom_call_target="tpu_custom_call" | custom-call | flops 1000000 | bytes 1000000 | tf_op jit(solution)/shard_map/pallas_call | solution.py:596
  37.9 3.9 %collective-permute-start.10 = (f32[152,128]{1,0:T(8,128)S(1)}, f32[152,128]{1,0:T(8,128)S(1)}, u32[]{:S(2)}, u32[]{:S(2)}) collective-permute-start(f32[152,128]{1,0:T(8,128)S(1)} %get-tuple-element.103), channel_id=1, source_target_pairs={{16,32},{32,16},{48,64},{64,48},{80,96},{96,80},{112,128},{128,112... | collective-permute-start | bytes 233480 | tf_op jit(solution)/shard_map/ppermute | solution.py:624
  41.8 1.9 %collective-permute-start.11 = (f32[152,128]{1,0:T(8,128)S(1)}, f32[152,128]{1,0:T(8,128)S(1)}, u32[]{:S(2)}, u32[]{:S(2)}) collective-permute-start(f32[152,128]{1,0:T(8,128)S(1)} %get-tuple-element.104), channel_id=1, source_target_pairs={{0,16},{16,0},{32,48},{48,32},{64,80},{80,64},{96,112},{112,96},{1... | collective-permute-start | bytes 233480 | tf_op jit(solution)/shard_map/ppermute | solution.py:624
  43.8 5.0 %collective-permute-start.8 = (f32[152,128]{1,0:T(8,128)S(1)}, f32[152,128]{1,0:T(8,128)S(1)}, u32[]{:S(2)}, u32[]{:S(2)}) collective-permute-start(f32[152,128]{1,0:T(8,128)S(1)} %get-tuple-element.101), channel_id=1, source_target_pairs={{0,15},{1,2},{2,1},{3,4},{4,3},{5,6},{6,5},{7,8},{8,7},{9,10},{10,... | collective-permute-start | bytes 233480 | tf_op jit(solution)/shard_map/ppermute | solution.py:618
  48.7 1.9 %collective-permute-start.9 = (f32[152,128]{1,0:T(8,128)S(1)}, f32[152,128]{1,0:T(8,128)S(1)}, u32[]{:S(2)}, u32[]{:S(2)}) collective-permute-start(f32[152,128]{1,0:T(8,128)S(1)} %get-tuple-element.102), channel_id=1, source_target_pairs={{0,1},{1,0},{2,3},{3,2},{4,5},{5,4},{6,7},{7,6},{8,9},{9,8},{10,11... | collective-permute-start | bytes 233480 | tf_op jit(solution)/shard_map/ppermute | solution.py:618
  50.7 1.5 collective-permute-done.8.g0
  52.2 1.7 collective-permute-done.9.g1
  55.2 3.9 %collective-permute-start.12 = (f32[168,128]{1,0:T(8,128)S(1)}, f32[168,128]{1,0:T(8,128)S(1)}, u32[]{:S(2)}, u32[]{:S(2)}) collective-permute-start(f32[168,128]{1,0:T(8,128)S(1)} %get-tuple-element.107), channel_id=1, source_target_pairs={{0,15},{1,2},{2,1},{3,4},{4,3},{5,6},{6,5},{7,8},{8,7},{9,10},{10,... | collective-permute-start | bytes 258056 | tf_op jit(solution)/shard_map/ppermute | solution.py:618
  59.1 1.9 %collective-permute-start.13 = (f32[168,128]{1,0:T(8,128)S(1)}, f32[168,128]{1,0:T(8,128)S(1)}, u32[]{:S(2)}, u32[]{:S(2)}) collective-permute-start(f32[168,128]{1,0:T(8,128)S(1)} %get-tuple-element.108), channel_id=1, source_target_pairs={{0,1},{1,0},{2,3},{3,2},{4,5},{5,4},{6,7},{7,6},{8,9},{9,8},{10,11... | collective-permute-start | bytes 258056 | tf_op jit(solution)/shard_map/ppermute | solution.py:618
  61.0 6.6 %collective-permute-start.14 = (f32[168,128]{1,0:T(8,128)S(1)}, f32[168,128]{1,0:T(8,128)S(1)}, u32[]{:S(2)}, u32[]{:S(2)}) collective-permute-start(f32[168,128]{1,0:T(8,128)S(1)} %get-tuple-element.109), channel_id=1, source_target_pairs={{16,32},{32,16},{48,64},{64,48},{80,96},{96,80},{112,128},{128,112... | collective-permute-start | bytes 258056 | tf_op jit(solution)/shard_map/ppermute | solution.py:624
  67.6 1.9 %collective-permute-start.15 = (f32[168,128]{1,0:T(8,128)S(1)}, f32[168,128]{1,0:T(8,128)S(1)}, u32[]{:S(2)}, u32[]{:S(2)}) collective-permute-start(f32[168,128]{1,0:T(8,128)S(1)} %get-tuple-element.110), channel_id=1, source_target_pairs={{0,16},{16,0},{32,48},{48,32},{64,80},{80,64},{96,112},{112,96},{1... | collective-permute-start | bytes 258056 | tf_op jit(solution)/shard_map/ppermute | solution.py:624
  70.8 2.2 %shard_map.128 = (f32[184,512]{1,0:T(8,128)}, f32[184,512]{1,0:T(8,128)S(1)}, f32[184,128]{1,0:T(8,128)S(1)}, f32[184,128]{1,0:T(8,128)S(1)}, f32[184,128]{1,0:T(8,128)S(1)}, /*index=5*/f32[184,128]{1,0:T(8,128)S(1)}) custom-call(s32[3]{0:T(128)S(1)} %pad_add_fusion.place, f32[168,512]{1,0:T(8,128)S(1)} %get-tuple-element.106.t, ...), custom_call_target="tpu_custom_call" | custom-call | flops 1000000 | bytes 1000000 | tf_op jit(solution)/shard_map/pallas_call | solution.py:596
  73.0 5.0 %collective-permute-start.16 = (f32[184,128]{1,0:T(8,128)S(1)}, f32[184,128]{1,0:T(8,128)S(1)}, u32[]{:S(2)}, u32[]{:S(2)}) collective-permute-start(f32[184,128]{1,0:T(8,128)S(1)} %get-tuple-element.112), channel_id=1, source_target_pairs={{0,15},{1,2},{2,1},{3,4},{4,3},{5,6},{6,5},{7,8},{8,7},{9,10},{10,... | collective-permute-start | bytes 282632 | tf_op jit(solution)/shard_map/ppermute | solution.py:618
  78.0 1.9 %collective-permute-start.17 = (f32[184,128]{1,0:T(8,128)S(1)}, f32[184,128]{1,0:T(8,128)S(1)}, u32[]{:S(2)}, u32[]{:S(2)}) collective-permute-start(f32[184,128]{1,0:T(8,128)S(1)} %get-tuple-element.113), channel_id=1, source_target_pairs={{0,1},{1,0},{2,3},{3,2},{4,5},{5,4},{6,7},{7,6},{8,9},{9,8},{10,11... | collective-permute-start | bytes 282632 | tf_op jit(solution)/shard_map/ppermute | solution.py:618
  79.9 3.9 %collective-permute-start.18 = (f32[184,128]{1,0:T(8,128)S(1)}, f32[184,128]{1,0:T(8,128)S(1)}, u32[]{:S(2)}, u32[]{:S(2)}) collective-permute-start(f32[184,128]{1,0:T(8,128)S(1)} %get-tuple-element.114), channel_id=1, source_target_pairs={{16,32},{32,16},{48,64},{64,48},{80,96},{96,80},{112,128},{128,112... | collective-permute-start | bytes 282632 | tf_op jit(solution)/shard_map/ppermute | solution.py:624
  83.8 1.9 %collective-permute-start.19 = (f32[184,128]{1,0:T(8,128)S(1)}, f32[184,128]{1,0:T(8,128)S(1)}, u32[]{:S(2)}, u32[]{:S(2)}) collective-permute-start(f32[184,128]{1,0:T(8,128)S(1)} %get-tuple-element.115), channel_id=1, source_target_pairs={{0,16},{16,0},{32,48},{48,32},{64,80},{80,64},{96,112},{112,96},{1... | collective-permute-start | bytes 282632 | tf_op jit(solution)/shard_map/ppermute | solution.py:624
  87.0 2.4 %shard_map.129 = (f32[200,512]{1,0:T(8,128)}, f32[16,32,128]{2,1,0:T(8,128)}) custom-call(s32[3]{0:T(128)S(1)} %pad_add_fusion.place, f32[184,512]{1,0:T(8,128)S(1)} %get-tuple-element.111.q, f32[184,128]{1,0:T(8,128)S(1)} %collective-permute-done.16.g0, f32[184,128]{1,0:T(8,128)S(1)} %collective-permute-done.17.g1, ...), custom_call_target="tpu_custom_call" | custom-call | flops 1000000 | bytes 1000000 | tf_op jit(solution)/shard_map/pallas_call | solution.py:596
  89.4 4.6 %all-to-all-start = ((f32[16,32,128]{2,1,0:T(8,128)}), f32[16,32,128]{2,1,0:T(8,128)S(1)}, u32[]{:S(2)}, u32[]{:S(2)}) async-start(f32[16,32,128]{2,1,0:T(8,128)} %get-tuple-element.119), calls=%async_computation | async-start | bytes 524288 | tf_op jit(solution)/shard_map/all_to_all | solution.py:632
  94.0 2.9 %shard_map.130 = (f32[200,512]{1,0:T(8,128)}, f32[200,128]{1,0:T(8,128)S(1)}, f32[200,128]{1,0:T(8,128)S(1)}, f32[200,128]{1,0:T(8,128)S(1)}, f32[200,128]{1,0:T(8,128)S(1)}) custom-call(s32[3]{0:T(128)S(1)} %pad_add_fusion.place, f32[200,512]{1,0:T(8,128)} %get-tuple-element.120.v2, f32[1,512]{1,0:T(1,128)S(1)} %get-tuple-element.95.after.share, ...), custom_call_target="tpu_custom_call" | custom-call | flops 500000000 | bytes 1000000 | tf_op jit(solution)/shard_map/pallas_call | solution.py:596
  98.2 4.1 %all-to-all-done.got = f32[16,32,128]{2,1,0:T(8,128)S(1)} async-done(((f32[16,32,128]{2,1,0:T(8,128)}), f32[16,32,128]{2,1,0:T(8,128)S(1)}, u32[]{:S(2)}, u32[]{:S(2)}) %all-to-all-start) | async-done | bytes 262176 | tf_op jit(solution)/shard_map/all_to_all | solution.py:632
  103.1 10.9 %all-to-all-start.1 = ((f32[16,32,128]{2,1,0:T(8,128)}), f32[16,32,128]{2,1,0:T(8,128)S(1)}, u32[]{:S(2)}, u32[]{:S(2)}) async-start(f32[16,32,128]{2,1,0:T(8,128)} %shard_map.131), calls=%async_computation.1 | async-start | bytes 524288 | tf_op jit(solution)/shard_map/all_to_all | solution.py:632
  114.0 2.8 %collective-permute-start.20 = (f32[200,128]{1,0:T(8,128)S(1)}, f32[200,128]{1,0:T(8,128)S(1)}, u32[]{:S(2)}, u32[]{:S(2)}) collective-permute-start(f32[200,128]{1,0:T(8,128)S(1)} %copy-done.3), channel_id=1, source_target_pairs={{0,15},{1,2},{2,1},{3,4},{4,3},{5,6},{6,5},{7,8},{8,7},{9,10},{10,... | collective-permute-start | bytes 307208 | tf_op jit(solution)/shard_map/ppermute | solution.py:618
  116.8 1.9 %collective-permute-start.21 = (f32[200,128]{1,0:T(8,128)S(1)}, f32[200,128]{1,0:T(8,128)S(1)}, u32[]{:S(2)}, u32[]{:S(2)}) collective-permute-start(f32[200,128]{1,0:T(8,128)S(1)} %copy-done.1), channel_id=1, source_target_pairs={{0,1},{1,0},{2,3},{3,2},{4,5},{5,4},{6,7},{7,6},{8,9},{9,8},{10,11... | collective-permute-start | bytes 307208 | tf_op jit(solution)/shard_map/ppermute | solution.py:618
  118.7 6.6 %collective-permute-start.22 = (f32[200,128]{1,0:T(8,128)S(1)}, f32[200,128]{1,0:T(8,128)S(1)}, u32[]{:S(2)}, u32[]{:S(2)}) collective-permute-start(f32[200,128]{1,0:T(8,128)S(1)} %get-tuple-element.131), channel_id=1, source_target_pairs={{16,32},{32,16},{48,64},{64,48},{80,96},{96,80},{112,128},{128,112... | collective-permute-start | bytes 307208 | tf_op jit(solution)/shard_map/ppermute | solution.py:624
  125.3 1.9 %collective-permute-start.23 = (f32[200,128]{1,0:T(8,128)S(1)}, f32[200,128]{1,0:T(8,128)S(1)}, u32[]{:S(2)}, u32[]{:S(2)}) collective-permute-start(f32[200,128]{1,0:T(8,128)S(1)} %get-tuple-element.132), channel_id=1, source_target_pairs={{0,16},{16,0},{32,48},{48,32},{64,80},{80,64},{96,112},{112,96},{1... | collective-permute-start | bytes 307208 | tf_op jit(solution)/shard_map/ppermute | solution.py:624
  127.2 1.9 %collective-permute-done.22.g2 = f32[200,128]{1,0:T(8,128)S(1)} collective-permute-done((f32[200,128]{1,0:T(8,128)S(1)}, f32[200,128]{1,0:T(8,128)S(1)}, u32[]{:S(2)}, u32[]{:S(2)}) %collective-permute-start.22) | collective-permute-done | bytes 102432 | tf_op jit(solution)/shard_map/ppermute | solution.py:624
  129.2 6.5 %collective-permute-start.24 = (f32[16,32,128]{2,1,0:T(8,128)S(1)}, f32[16,32,128]{2,1,0:T(8,128)S(1)}, u32[]{:S(2)}, u32[]{:S(2)}) collective-permute-start(f32[16,32,128]{2,1,0:T(8,128)S(1)} %all-to-all-done.1.mine), channel_id=1, source_target_pairs={{0,16},{16,0},{32,48},{48,32},{64,80},{80,64},{96,112},{112,96},{1... | collective-permute-start | bytes 786440 | tf_op jit(solution)/shard_map/ppermute | solution.py:741
  136.9 5.8 %shard_map.132 = (f32[128,512]{1,0:T(8,128)}, f32[128,512]{1,0:T(8,128)}, f32[128,512]{1,0:T(8,128)}, f32[128,512]{1,0:T(8,128)}, f32[128,512]{1,0:T(8,128)}, /*...) custom-call(s32[3]{0:T(128)S(1)} %pad_add_fusion.place, ...), custom_call_target="tpu_custom_call" | custom-call | flops 1000000 | bytes 1000000 | tf_op jit(solution)/shard_map/pallas_call | solution.py:596
  142.7 4.0 %all-to-all-start.2 = ((f32[32,1,1152]{2,1,0:T(1,128)}), f32[32,1,1152]{2,1,0:T(1,128)S(1)}, u32[]{:S(2)}, u32[]{:S(2)}) async-start(f32[32,1,1152]{2,1,0:T(1,128)} %get-tuple-element.141), calls=%async_computation.2 | async-start | bytes 294912 | tf_op jit(solution)/shard_map/all_to_all | solution.py:632
  146.7 6.7 %collective-permute-start.25 = (f32[128,128]{1,0:T(8,128)S(1)}, f32[128,128]{1,0:T(8,128)S(1)}, u32[]{:S(2)}, u32[]{:S(2)}) collective-permute-start(f32[128,128]{1,0:T(8,128)S(1)} %get-tuple-element.142), channel_id=1, source_target_pairs={{0,15},{1,2},{2,1},{3,4},{4,3},{5,6},{6,5},{7,8},{8,7},{9,10},{10,... | collective-permute-start | bytes 196616 | tf_op jit(solution)/shard_map/ppermute | solution.py:618
  153.4 1.9 %collective-permute-start.26 = (f32[128,128]{1,0:T(8,128)S(1)}, f32[128,128]{1,0:T(8,128)S(1)}, u32[]{:S(2)}, u32[]{:S(2)}) collective-permute-start(f32[128,128]{1,0:T(8,128)S(1)} %get-tuple-element.143), channel_id=1, source_target_pairs={{0,1},{1,0},{2,3},{3,2},{4,5},{5,4},{6,7},{7,6},{8,9},{9,8},{10,11... | collective-permute-start | bytes 196616 | tf_op jit(solution)/shard_map/ppermute | solution.py:618
  155.3 3.1 %collective-permute-done.26.g1 = f32[128,128]{1,0:T(8,128)S(1)} collective-permute-done((f32[128,128]{1,0:T(8,128)S(1)}, f32[128,128]{1,0:T(8,128)S(1)}, u32[]{:S(2)}, u32[]{:S(2)}) %collective-permute-start.26) | collective-permute-done | bytes 65568 | tf_op jit(solution)/shard_map/ppermute | solution.py:618
  159.1 10.3 %all-to-all-start.3 = ((f32[16,1,1152]{2,1,0:T(1,128)}), f32[16,1,1152]{2,1,0:T(1,128)S(1)}, u32[]{:S(2)}, u32[]{:S(2)}) async-start(f32[16,1,1152]{2,1,0:T(1,128)} %shard_map.133), calls=%async_computation.3 | async-start | bytes 147456 | tf_op jit(solution)/shard_map/all_to_all | solution.py:632
  169.4 5.4 %collective-permute-start.27 = (f32[128,128]{1,0:T(8,128)S(1)}, f32[128,128]{1,0:T(8,128)S(1)}, u32[]{:S(2)}, u32[]{:S(2)}) collective-permute-start(f32[128,128]{1,0:T(8,128)S(1)} %get-tuple-element.151), channel_id=1, source_target_pairs={{16,32},{32,16},{48,64},{64,48},{80,96},{96,80},{112,128},{128,112... | collective-permute-start | bytes 196616 | tf_op jit(solution)/shard_map/ppermute | solution.py:624
  174.9 1.9 %collective-permute-start.28 = (f32[128,128]{1,0:T(8,128)S(1)}, f32[128,128]{1,0:T(8,128)S(1)}, u32[]{:S(2)}, u32[]{:S(2)}) collective-permute-start(f32[128,128]{1,0:T(8,128)S(1)} %get-tuple-element.152), channel_id=1, source_target_pairs={{0,16},{16,0},{32,48},{48,32},{64,80},{80,64},{96,112},{112,96},{1... | collective-permute-start | bytes 196616 | tf_op jit(solution)/shard_map/ppermute | solution.py:624
  178.0 3.1 %all-to-all-done.3.got = f32[16,1,1152]{2,1,0:T(1,128)S(1)} async-done(((f32[16,1,1152]{2,1,0:T(1,128)}), f32[16,1,1152]{2,1,0:T(1,128)S(1)}, u32[]{:S(2)}, u32[]{:S(2)}) %all-to-all-start.3) | async-done | bytes 73760 | tf_op jit(solution)/shard_map/all_to_all | solution.py:632
  181.1 3.4 %shard_map.134 = (f32[128,512]{1,0:T(8,128)}, f32[128,512]{1,0:T(8,128)}) custom-call(s32[3]{0:T(128)S(1)} %pad_add_fusion.place, f32[16,1,1152]{2,1,0:T(1,128)S(1)} %all-to-all-done.3.got, f32[128,512]{1,0:T(8,128)S(1)} %get-tuple-element.148.q, f32[128,128]{1,0:T(8,128)S(1)} %collective-permute-done.25.g0, f32[128,128]{1,0:T(8,128)S(1)} %collective-permute-done.26.g1, ...), custom_call_target="tpu_custom_call" | custom-call | flops 1000000 | bytes 1000000 | tf_op jit(solution)/shard_map/pallas_call | solution.py:596
  (41 shorter events, 10.0 us)
Async XLA Ops:
  2.8 18.5 %collective-permute-start = (f32[136,128]{1,0:T(8,128)S(1)}, f32[136,128]{1,0:T(8,128)S(1)}, u32[]{:S(2)}, u32[]{:S(2)}) collective-permute-start(f32[136,128]{1,0:T(8,128)S(1)} %get-tuple-element.82), channel_id=1, source_target_pairs={{0,15},{1,2},{2,1},{3,4},{4,3},{5,6},{6,5},{7,8},{8,7},{9,10},{10,... | collective-permute-start | bytes 208904 | tf_op jit(solution)/shard_map/ppermute | solution.py:618
  10.5 10.9 %collective-permute-start.1 = (f32[136,128]{1,0:T(8,128)S(1)}, f32[136,128]{1,0:T(8,128)S(1)}, u32[]{:S(2)}, u32[]{:S(2)}) collective-permute-start(f32[136,128]{1,0:T(8,128)S(1)} %get-tuple-element.83), channel_id=1, source_target_pairs={{0,1},{1,0},{2,3},{3,2},{4,5},{5,4},{6,7},{7,6},{8,9},{9,8},{10,11... | collective-permute-start | bytes 208904 | tf_op jit(solution)/shard_map/ppermute | solution.py:618
  12.4 8.9 %collective-permute-start.2 = (f32[136,128]{1,0:T(8,128)S(1)}, f32[136,128]{1,0:T(8,128)S(1)}, u32[]{:S(2)}, u32[]{:S(2)}) collective-permute-start(f32[136,128]{1,0:T(8,128)S(1)} %get-tuple-element.84), channel_id=1, source_target_pairs={{16,32},{32,16},{48,64},{64,48},{80,96},{96,80},{112,128},{128,112... | collective-permute-start | bytes 208904 | tf_op jit(solution)/shard_map/ppermute | solution.py:624
  16.8 4.6 %collective-permute-start.3 = (f32[136,128]{1,0:T(8,128)S(1)}, f32[136,128]{1,0:T(8,128)S(1)}, u32[]{:S(2)}, u32[]{:S(2)}) collective-permute-start(f32[136,128]{1,0:T(8,128)S(1)} %get-tuple-element.85), channel_id=1, source_target_pairs={{0,16},{16,0},{32,48},{48,32},{64,80},{80,64},{96,112},{112,96},{1... | collective-permute-start | bytes 208904 | tf_op jit(solution)/shard_map/ppermute | solution.py:624
  22.5 13.2 %collective-permute-start.4 = (f32[136,128]{1,0:T(8,128)S(1)}, f32[136,128]{1,0:T(8,128)S(1)}, u32[]{:S(2)}, u32[]{:S(2)}) collective-permute-start(f32[136,128]{1,0:T(8,128)S(1)} %get-tuple-element.91), channel_id=1, source_target_pairs={{0,15},{1,2},{2,1},{3,4},{4,3},{5,6},{6,5},{7,8},{8,7},{9,10},{10,... | collective-permute-start | bytes 208904 | tf_op jit(solution)/shard_map/ppermute | solution.py:618
  26.9 8.9 %collective-permute-start.5 = (f32[136,128]{1,0:T(8,128)S(1)}, f32[136,128]{1,0:T(8,128)S(1)}, u32[]{:S(2)}, u32[]{:S(2)}) collective-permute-start(f32[136,128]{1,0:T(8,128)S(1)} %get-tuple-element.92), channel_id=1, source_target_pairs={{0,1},{1,0},{2,3},{3,2},{4,5},{5,4},{6,7},{7,6},{8,9},{9,8},{10,11... | collective-permute-start | bytes 208904 | tf_op jit(solution)/shard_map/ppermute | solution.py:618
  28.8 6.9 %collective-permute-start.6 = (f32[136,128]{1,0:T(8,128)S(1)}, f32[136,128]{1,0:T(8,128)S(1)}, u32[]{:S(2)}, u32[]{:S(2)}) collective-permute-start(f32[136,128]{1,0:T(8,128)S(1)} %get-tuple-element.93), channel_id=1, source_target_pairs={{16,32},{32,16},{48,64},{64,48},{80,96},{96,80},{112,128},{128,112... | collective-permute-start | bytes 208904 | tf_op jit(solution)/shard_map/ppermute | solution.py:624
  32.3 3.5 %collective-permute-start.7 = (f32[136,128]{1,0:T(8,128)S(1)}, f32[136,128]{1,0:T(8,128)S(1)}, u32[]{:S(2)}, u32[]{:S(2)}) collective-permute-start(f32[136,128]{1,0:T(8,128)S(1)} %get-tuple-element.94), channel_id=1, source_target_pairs={{0,16},{16,0},{32,48},{48,32},{64,80},{80,64},{96,112},{112,96},{1... | collective-permute-start | bytes 208904 | tf_op jit(solution)/shard_map/ppermute | solution.py:624
  37.9 12.8 %collective-permute-start.10 = (f32[152,128]{1,0:T(8,128)S(1)}, f32[152,128]{1,0:T(8,128)S(1)}, u32[]{:S(2)}, u32[]{:S(2)}) collective-permute-start(f32[152,128]{1,0:T(8,128)S(1)} %get-tuple-element.103), channel_id=1, source_target_pairs={{16,32},{32,16},{48,64},{64,48},{80,96},{96,80},{112,128},{128,112... | collective-permute-start | bytes 233480 | tf_op jit(solution)/shard_map/ppermute | solution.py:624
  41.8 8.8 %collective-permute-start.11 = (f32[152,128]{1,0:T(8,128)S(1)}, f32[152,128]{1,0:T(8,128)S(1)}, u32[]{:S(2)}, u32[]{:S(2)}) collective-permute-start(f32[152,128]{1,0:T(8,128)S(1)} %get-tuple-element.104), channel_id=1, source_target_pairs={{0,16},{16,0},{32,48},{48,32},{64,80},{80,64},{96,112},{112,96},{1... | collective-permute-start | bytes 233480 | tf_op jit(solution)/shard_map/ppermute | solution.py:624
  43.8 8.5 %collective-permute-start.8 = (f32[152,128]{1,0:T(8,128)S(1)}, f32[152,128]{1,0:T(8,128)S(1)}, u32[]{:S(2)}, u32[]{:S(2)}) collective-permute-start(f32[152,128]{1,0:T(8,128)S(1)} %get-tuple-element.101), channel_id=1, source_target_pairs={{0,15},{1,2},{2,1},{3,4},{4,3},{5,6},{6,5},{7,8},{8,7},{9,10},{10,... | collective-permute-start | bytes 233480 | tf_op jit(solution)/shard_map/ppermute | solution.py:618
  48.7 5.1 %collective-permute-start.9 = (f32[152,128]{1,0:T(8,128)S(1)}, f32[152,128]{1,0:T(8,128)S(1)}, u32[]{:S(2)}, u32[]{:S(2)}) collective-permute-start(f32[152,128]{1,0:T(8,128)S(1)} %get-tuple-element.102), channel_id=1, source_target_pairs={{0,1},{1,0},{2,3},{3,2},{4,5},{5,4},{6,7},{7,6},{8,9},{9,8},{10,11... | collective-permute-start | bytes 233480 | tf_op jit(solution)/shard_map/ppermute | solution.py:618
  55.2 14.4 %collective-permute-start.12 = (f32[168,128]{1,0:T(8,128)S(1)}, f32[168,128]{1,0:T(8,128)S(1)}, u32[]{:S(2)}, u32[]{:S(2)}) collective-permute-start(f32[168,128]{1,0:T(8,128)S(1)} %get-tuple-element.107), channel_id=1, source_target_pairs={{0,15},{1,2},{2,1},{3,4},{4,3},{5,6},{6,5},{7,8},{8,7},{9,10},{10,... | collective-permute-start | bytes 258056 | tf_op jit(solution)/shard_map/ppermute | solution.py:618
  59.1 10.4 %collective-permute-start.13 = (f32[168,128]{1,0:T(8,128)S(1)}, f32[168,128]{1,0:T(8,128)S(1)}, u32[]{:S(2)}, u32[]{:S(2)}) collective-permute-start(f32[168,128]{1,0:T(8,128)S(1)} %get-tuple-element.108), channel_id=1, source_target_pairs={{0,1},{1,0},{2,3},{3,2},{4,5},{5,4},{6,7},{7,6},{8,9},{9,8},{10,11... | collective-permute-start | bytes 258056 | tf_op jit(solution)/shard_map/ppermute | solution.py:618
  61.0 8.7 %collective-permute-start.14 = (f32[168,128]{1,0:T(8,128)S(1)}, f32[168,128]{1,0:T(8,128)S(1)}, u32[]{:S(2)}, u32[]{:S(2)}) collective-permute-start(f32[168,128]{1,0:T(8,128)S(1)} %get-tuple-element.109), channel_id=1, source_target_pairs={{16,32},{32,16},{48,64},{64,48},{80,96},{96,80},{112,128},{128,112... | collective-permute-start | bytes 258056 | tf_op jit(solution)/shard_map/ppermute | solution.py:624
  67.6 3.2 %collective-permute-start.15 = (f32[168,128]{1,0:T(8,128)S(1)}, f32[168,128]{1,0:T(8,128)S(1)}, u32[]{:S(2)}, u32[]{:S(2)}) collective-permute-start(f32[168,128]{1,0:T(8,128)S(1)} %get-tuple-element.110), channel_id=1, source_target_pairs={{0,16},{16,0},{32,48},{48,32},{64,80},{80,64},{96,112},{112,96},{1... | collective-permute-start | bytes 258056 | tf_op jit(solution)/shard_map/ppermute | solution.py:624
  73.0 12.7 %collective-permute-start.16 = (f32[184,128]{1,0:T(8,128)S(1)}, f32[184,128]{1,0:T(8,128)S(1)}, u32[]{:S(2)}, u32[]{:S(2)}) collective-permute-start(f32[184,128]{1,0:T(8,128)S(1)} %get-tuple-element.112), channel_id=1, source_target_pairs={{0,15},{1,2},{2,1},{3,4},{4,3},{5,6},{6,5},{7,8},{8,7},{9,10},{10,... | collective-permute-start | bytes 282632 | tf_op jit(solution)/shard_map/ppermute | solution.py:618
  78.0 7.7 %collective-permute-start.17 = (f32[184,128]{1,0:T(8,128)S(1)}, f32[184,128]{1,0:T(8,128)S(1)}, u32[]{:S(2)}, u32[]{:S(2)}) collective-permute-start(f32[184,128]{1,0:T(8,128)S(1)} %get-tuple-element.113), channel_id=1, source_target_pairs={{0,1},{1,0},{2,3},{3,2},{4,5},{5,4},{6,7},{7,6},{8,9},{9,8},{10,11... | collective-permute-start | bytes 282632 | tf_op jit(solution)/shard_map/ppermute | solution.py:618
  79.9 6.1 %collective-permute-start.18 = (f32[184,128]{1,0:T(8,128)S(1)}, f32[184,128]{1,0:T(8,128)S(1)}, u32[]{:S(2)}, u32[]{:S(2)}) collective-permute-start(f32[184,128]{1,0:T(8,128)S(1)} %get-tuple-element.114), channel_id=1, source_target_pairs={{16,32},{32,16},{48,64},{64,48},{80,96},{96,80},{112,128},{128,112... | collective-permute-start | bytes 282632 | tf_op jit(solution)/shard_map/ppermute | solution.py:624
  83.8 3.2 %collective-permute-start.19 = (f32[184,128]{1,0:T(8,128)S(1)}, f32[184,128]{1,0:T(8,128)S(1)}, u32[]{:S(2)}, u32[]{:S(2)}) collective-permute-start(f32[184,128]{1,0:T(8,128)S(1)} %get-tuple-element.115), channel_id=1, source_target_pairs={{0,16},{16,0},{32,48},{48,32},{64,80},{80,64},{96,112},{112,96},{1... | collective-permute-start | bytes 282632 | tf_op jit(solution)/shard_map/ppermute | solution.py:624
  89.4 12.9 %all-to-all-start = ((f32[16,32,128]{2,1,0:T(8,128)}), f32[16,32,128]{2,1,0:T(8,128)S(1)}, u32[]{:S(2)}, u32[]{:S(2)}) async-start(f32[16,32,128]{2,1,0:T(8,128)} %get-tuple-element.119), calls=%async_computation | async-start | bytes 524288 | tf_op jit(solution)/shard_map/all_to_all | solution.py:632
  96.9 0.6 copy-start
  97.5 0.6 copy-start.2
  103.1 10.9 %copy-start.3 = (f32[200,128]{1,0:T(8,128)S(1)}, f32[200,128]{1,0:T(8,128)}, u32[]{:S(2)}) copy-start(f32[200,128]{1,0:T(8,128)} %copy-done.2) | copy-start | bytes 307204
  103.1 13.7 %copy-start.1 = (f32[200,128]{1,0:T(8,128)S(1)}, f32[200,128]{1,0:T(8,128)}, u32[]{:S(2)}) copy-start(f32[200,128]{1,0:T(8,128)} %copy-done) | copy-start | bytes 307204
  103.1 26.1 %all-to-all-start.1 = ((f32[16,32,128]{2,1,0:T(8,128)}), f32[16,32,128]{2,1,0:T(8,128)S(1)}, u32[]{:S(2)}, u32[]{:S(2)}) async-start(f32[16,32,128]{2,1,0:T(8,128)} %shard_map.131), calls=%async_computation.1 | async-start | bytes 524288 | tf_op jit(solution)/shard_map/all_to_all | solution.py:632
  114.0 13.2 %collective-permute-start.20 = (f32[200,128]{1,0:T(8,128)S(1)}, f32[200,128]{1,0:T(8,128)S(1)}, u32[]{:S(2)}, u32[]{:S(2)}) collective-permute-start(f32[200,128]{1,0:T(8,128)S(1)} %copy-done.3), channel_id=1, source_target_pairs={{0,15},{1,2},{2,1},{3,4},{4,3},{5,6},{6,5},{7,8},{8,7},{9,10},{10,... | collective-permute-start | bytes 307208 | tf_op jit(solution)/shard_map/ppermute | solution.py:618
  116.8 10.4 %collective-permute-start.21 = (f32[200,128]{1,0:T(8,128)S(1)}, f32[200,128]{1,0:T(8,128)S(1)}, u32[]{:S(2)}, u32[]{:S(2)}) collective-permute-start(f32[200,128]{1,0:T(8,128)S(1)} %copy-done.1), channel_id=1, source_target_pairs={{0,1},{1,0},{2,3},{3,2},{4,5},{5,4},{6,7},{7,6},{8,9},{9,8},{10,11... | collective-permute-start | bytes 307208 | tf_op jit(solution)/shard_map/ppermute | solution.py:618
  118.7 10.4 %collective-permute-start.22 = (f32[200,128]{1,0:T(8,128)S(1)}, f32[200,128]{1,0:T(8,128)S(1)}, u32[]{:S(2)}, u32[]{:S(2)}) collective-permute-start(f32[200,128]{1,0:T(8,128)S(1)} %get-tuple-element.131), channel_id=1, source_target_pairs={{16,32},{32,16},{48,64},{64,48},{80,96},{96,80},{112,128},{128,112... | collective-permute-start | bytes 307208 | tf_op jit(solution)/shard_map/ppermute | solution.py:624
  125.3 3.9 %collective-permute-start.23 = (f32[200,128]{1,0:T(8,128)S(1)}, f32[200,128]{1,0:T(8,128)S(1)}, u32[]{:S(2)}, u32[]{:S(2)}) collective-permute-start(f32[200,128]{1,0:T(8,128)S(1)} %get-tuple-element.132), channel_id=1, source_target_pairs={{0,16},{16,0},{32,48},{48,32},{64,80},{80,64},{96,112},{112,96},{1... | collective-permute-start | bytes 307208 | tf_op jit(solution)/shard_map/ppermute | solution.py:624
  129.2 7.7 %collective-permute-start.24 = (f32[16,32,128]{2,1,0:T(8,128)S(1)}, f32[16,32,128]{2,1,0:T(8,128)S(1)}, u32[]{:S(2)}, u32[]{:S(2)}) collective-permute-start(f32[16,32,128]{2,1,0:T(8,128)S(1)} %all-to-all-done.1.mine), channel_id=1, source_target_pairs={{0,16},{16,0},{32,48},{48,32},{64,80},{80,64},{96,112},{112,96},{1... | collective-permute-start | bytes 786440 | tf_op jit(solution)/shard_map/ppermute | solution.py:741
  142.7 15.7 %all-to-all-start.2 = ((f32[32,1,1152]{2,1,0:T(1,128)}), f32[32,1,1152]{2,1,0:T(1,128)S(1)}, u32[]{:S(2)}, u32[]{:S(2)}) async-start(f32[32,1,1152]{2,1,0:T(1,128)} %get-tuple-element.141), calls=%async_computation.2 | async-start | bytes 294912 | tf_op jit(solution)/shard_map/all_to_all | solution.py:632
  146.7 8.6 %collective-permute-start.25 = (f32[128,128]{1,0:T(8,128)S(1)}, f32[128,128]{1,0:T(8,128)S(1)}, u32[]{:S(2)}, u32[]{:S(2)}) collective-permute-start(f32[128,128]{1,0:T(8,128)S(1)} %get-tuple-element.142), channel_id=1, source_target_pairs={{0,15},{1,2},{2,1},{3,4},{4,3},{5,6},{6,5},{7,8},{8,7},{9,10},{10,... | collective-permute-start | bytes 196616 | tf_op jit(solution)/shard_map/ppermute | solution.py:618
  153.4 5.0 %collective-permute-start.26 = (f32[128,128]{1,0:T(8,128)S(1)}, f32[128,128]{1,0:T(8,128)S(1)}, u32[]{:S(2)}, u32[]{:S(2)}) collective-permute-start(f32[128,128]{1,0:T(8,128)S(1)} %get-tuple-element.143), channel_id=1, source_target_pairs={{0,1},{1,0},{2,3},{3,2},{4,5},{5,4},{6,7},{7,6},{8,9},{9,8},{10,11... | collective-permute-start | bytes 196616 | tf_op jit(solution)/shard_map/ppermute | solution.py:618
  159.1 22.0 %all-to-all-start.3 = ((f32[16,1,1152]{2,1,0:T(1,128)}), f32[16,1,1152]{2,1,0:T(1,128)S(1)}, u32[]{:S(2)}, u32[]{:S(2)}) async-start(f32[16,1,1152]{2,1,0:T(1,128)} %shard_map.133), calls=%async_computation.3 | async-start | bytes 147456 | tf_op jit(solution)/shard_map/all_to_all | solution.py:632
  169.4 8.2 %collective-permute-start.27 = (f32[128,128]{1,0:T(8,128)S(1)}, f32[128,128]{1,0:T(8,128)S(1)}, u32[]{:S(2)}, u32[]{:S(2)}) collective-permute-start(f32[128,128]{1,0:T(8,128)S(1)} %get-tuple-element.151), channel_id=1, source_target_pairs={{16,32},{32,16},{48,64},{64,48},{80,96},{96,80},{112,128},{128,112... | collective-permute-start | bytes 196616 | tf_op jit(solution)/shard_map/ppermute | solution.py:624
  174.9 3.1 %collective-permute-start.28 = (f32[128,128]{1,0:T(8,128)S(1)}, f32[128,128]{1,0:T(8,128)S(1)}, u32[]{:S(2)}, u32[]{:S(2)}) collective-permute-start(f32[128,128]{1,0:T(8,128)S(1)} %get-tuple-element.152), channel_id=1, source_target_pairs={{0,16},{16,0},{32,48},{48,32},{64,80},{80,64},{96,112},{112,96},{1... | collective-permute-start | bytes 196616 | tf_op jit(solution)/shard_map/ppermute | solution.py:624

commit v8 on v7

--- a/solution.py
+++ b/solution.py
@@ -295,7 +295,7 @@
     copy.wait()
 
 
-def k_second(place, q, g0, g1, g2, g3, r, share, neumann, avg, v_o, t_o, pr_o, *sends):
+def k_second(place, q, g2, g3, g0, g1, r, share, neumann, avg, v_o, t_o, pr_o, *sends):
     at = Place(place)
     rhs = r.shape[0]
     w = assembled(q[...], (g0, g1, g2, g3), at, rhs)
@@ -390,13 +390,13 @@
 def k_core(
     place, mine, other, t, g0, g1, g2, g3, z0, v1, z1, v2, r, diag, couple, blocks,
     z0_o, z1_o, z2_o, w0_o, w1_o, q_o, pay_o, s0, s1, s2, s3,
-    band0, band1, band2, c0_s, c1_s, c2_s, full_s, t_s, z0_s, z1_s, v2_s, sem, in_sem,
+    band0, band1, band2, c0_s, c1_s, c2_s, full_s, t_s, z1_s, v2_s, sem, in_sem,
 ):
     at = Place(place)
     loads = []
-    for n, (source, target) in enumerate(((z0, z0_s), (z1, z1_s), (v2, v2_s), (t, t_s))):
+    for n, (source, target) in enumerate(((z1, z1_s), (v2, v2_s), (t, t_s))):
         loads += begin(source, target, in_sem.at[n], 2)
-    t, z0, z1, v2 = t_s, z0_s, z1_s, v2_s
+    t, z1, v2 = t_s, z1_s, v2_s
     rhs = r.shape[0]
     rows = 2 * mine.shape[0]
     width = band0.shape[1]
@@ -452,15 +452,14 @@
     c1 = c1_s[pl.ds(pl.multiple_of(start + 16, 8), 56), :]
     c2 = c2_s[pl.ds(pl.multiple_of(start + 32, 8), 24), :]
     r0 = r[...]
-    finish(loads[0:2])
     z0f = z0[:rhs, :] + lift(c0[32:56], z0[rhs:, :])
     v1f = v1[:rhs, :] + lift(c0[24:64], v1[rhs:, :])
-    finish(loads[2:4])
+    finish(loads[0:2])
     z1f = z1[:rhs, :] + lift(
         jnp.concatenate([c0[16:72], c1[16:40]], axis=0),
         jnp.concatenate([z1[rhs:, :], z0[rhs:, :]], axis=0),
     )
-    finish(loads[4:6])
+    finish(loads[2:4])
     v2f = v2[:rhs, :] + lift(
         jnp.concatenate([c0[8:80], c1[8:48]], axis=0),
         jnp.concatenate([v2[rhs:, :], v1[rhs:, :]], axis=0),
@@ -475,7 +474,7 @@
     keep(1, z1f, z1_o)
     keep(2, v1f + SHIFT * r0, w0_o)
     keep(3, v2f + SHIFT * v1f, w1_o)
-    finish(loads[6:8])
+    finish(loads[4:6])
     z2 = assembled(t[...], (g0, g1, g2, g3), at, rhs)
     z2f = z2[:rhs] + lift(
         jnp.concatenate([c0, c1, c2], axis=0),
@@ -515,7 +514,7 @@
     place, got, q, g0, g1, g2, g3, order, r0, z0, z1, z2, w0, w1, x_o, r_o, full_s, sem
 ):
     loads = []
-    for n, source in enumerate((z0, z1, z2, w0, w1)):
+    for n, source in enumerate((z2, w0, w1)):
         loads += begin(source, full_s.at[n], sem.at[n], 2)
     w2 = assembled(q[...], (g0, g1, g2, g3), Place(place), q.shape[0])
     total = summed(got)
@@ -575,12 +574,13 @@
     columns = mm_t(eye, table)
     col = [columns[:, i : i + 1] for i in range(6)]
     hots = one_hot_faces(order[...])
-    finish(loads[:6])
-    x = col[0] * full_s[0] + col[1] * full_s[1] + col[2] * full_s[2]
-    x_o[...] = to_points(x, hots)
-    finish(loads[6:])
-    r = r0[...] + col[3] * full_s[3] + col[4] * full_s[4] + col[5] * w2
-    r_o[...] = to_points(r, hots)
+    finish(loads)
+    x = col[0] * z0[...] + col[1] * z1[...] + col[2] * full_s[0]
+    r = r0[...] + col[3] * full_s[1] + col[4] * full_s[2] + col[5] * w2
+    both = to_points(jnp.concatenate([x, r], axis=0), hots)
+    rhs = x.shape[0]
+    x_o[...] = both[:rhs]
+    r_o[...] = both[rhs:]
 
 
 def call(body, outs, place, *args, scratch=(), raw=(), raw_outs=(), flops=1_000_000):
@@ -710,7 +710,7 @@
     got = swap(sends)
     n = rhs + 40
     v1, t1, prim1, *sends = call(
-        k_second, [(n, points)] * 2 + [(8, n)] + face(n), place, q0, *got, r0, share, neumann, avg
+        k_second, [(n, points)] * 2 + [(8, n)] + face(n), place, q0, *got[2:], *got[:2], r0, share, neumann, avg
     )
     got = swap(sends)
     n = rhs + 56
@@ -744,13 +744,13 @@
         k_core,
         [(rhs, points)] * 6 + [(2 * columns, 1, 9 * LANES)] + face(rhs),
         place, mine, other, t2, *got, z0, v1, z1, v2, r0, diag, couple, blocks,
-        raw=(2, 7, 9, 10),
+        raw=(2, 9, 10),
         raw_outs=(0, 1, 2, 3, 4),
         scratch=[pltpu.VMEM((width, width), F32)] * 3
         + [pltpu.VMEM((width + 80, rhs), F32)] * 3
         + [pltpu.VMEM((5, rhs, points), F32)]
-        + [pltpu.VMEM((rhs + m, points), F32) for m in (72, 24, 56, 72)]
-        + [dma((5, 2)), dma((4, 2))],
+        + [pltpu.VMEM((rhs + m, points), F32) for m in (72, 56, 72)]
+        + [dma((5, 2)), dma((3, 2))],
     )
     chips = [
         [row * columns + column for row in (pair, pair + 1) for column in range(columns)]
@@ -767,8 +767,8 @@
     x, r = call(
         k_final, [(rhs, points)] * 2,
         place, dots, q2, *got, order, r0, z0f, z1f, z2f, w0f, w1f,
-        raw=(8, 9, 10, 11, 12),
-        scratch=[pltpu.VMEM((5, rhs, points), F32), dma((5, 2))],
+        raw=(10, 11, 12),
+        scratch=[pltpu.VMEM((3, rhs, points), F32), dma((3, 2))],
     )
     return (x[None, None], r[None, None])
 

time: 186 us -> 184 us (0.989)
  waiting for transfers between devices: 20.3 us -> 18.3 us
where the time goes in v8:
time: 184 us; the launch traced here: 182 us
  starting transfers between devices  132 us (72%)
  Pallas kernels  28.9 us (16%)
  waiting for transfers between devices  18.3 us (10%)
    ppermute x7, starting transfers between devices, exchange_columns(): lax.ppermute(sends[0], 'circ', far)  35.2 us
    ppermute x7, starting transfers between devices, exchange_rows(): lax.ppermute(sends[2], 'axial', link)  33 us
    all_to_all x4, starting transfers between devices, spread(): lax.all_to_all(value, axis, split_axis=0, concat_axis=0, tiled=True, axis...  30.7 us
    pallas_call x13, Pallas kernels, call(): pl.pallas_call(body, out_shape=[out if isinstance(out, jax.ShapeDtypeStru...  28.9 us
    ppermute x7, starting transfers between devices, exchange_columns(): lax.ppermute(sends[1], 'circ', near)  13.4 us
    ppermute x7, starting transfers between devices, exchange_rows(): lax.ppermute(sends[3], 'axial', core)  13.4 us
    all_to_all x4, waiting for transfers between devices, spread(): lax.all_to_all(value, axis, split_axis=0, concat_axis=0, tiled=True, axis...  7.25 us
    ppermute x1, starting transfers between devices, local(): other = lax.ppermute(mine, 'axial', [(i, i ^ 1) for i in range(rows)])  6.55 us
  transfers between devices with their start and end apart: 33, of which 13 were waited for; matrix products, arithmetic and copies ran while one was open for 0% of the time, Pallas kernels for 4%

profile of v8, /device:TPU:1, one launch (start us, length us, event | category | flops | bytes accessed | tf_op | source)
XLA Modules:
  0.0 182.2 jit_solution(13974743263581058280)
XLA Ops:
  0.7 2.1 %shard_map.122 = (f32[136,512]{1,0:T(8,128)S(1)}, s32[1,512]{1,0:T(1,128)S(1)}, f32[136,128]{1,0:T(8,128)S(1)}, f32[136,128]{1,0:T(8,128)S(1)}, f32[136,128]{1,0...) custom-call(s32[3]{0:T(128)S(1)} %pad_add_fusion.place, f32[128,512]{1,0:T(8,128)} %bitcast.14, ...), custom_call_target="tpu_custom_call" | custom-call | flops 1000000 | bytes 1000000 | tf_op jit(solution)/shard_map/pallas_call | solution.py:596
  2.8 7.7 %collective-permute-start = (f32[136,128]{1,0:T(8,128)S(1)}, f32[136,128]{1,0:T(8,128)S(1)}, u32[]{:S(2)}, u32[]{:S(2)}) collective-permute-start(f32[136,128]{1,0:T(8,128)S(1)} %get-tuple-element.82), channel_id=1, source_target_pairs={{0,15},{1,2},{2,1},{3,4},{4,3},{5,6},{6,5},{7,8},{8,7},{9,10},{10,... | collective-permute-start | bytes 208904 | tf_op jit(solution)/shard_map/ppermute | solution.py:618
  10.5 1.9 %collective-permute-start.1 = (f32[136,128]{1,0:T(8,128)S(1)}, f32[136,128]{1,0:T(8,128)S(1)}, u32[]{:S(2)}, u32[]{:S(2)}) collective-permute-start(f32[136,128]{1,0:T(8,128)S(1)} %get-tuple-element.83), channel_id=1, source_target_pairs={{0,1},{1,0},{2,3},{3,2},{4,5},{5,4},{6,7},{7,6},{8,9},{9,8},{10,11... | collective-permute-start | bytes 208904 | tf_op jit(solution)/shard_map/ppermute | solution.py:618
  12.4 4.4 %collective-permute-start.2 = (f32[136,128]{1,0:T(8,128)S(1)}, f32[136,128]{1,0:T(8,128)S(1)}, u32[]{:S(2)}, u32[]{:S(2)}) collective-permute-start(f32[136,128]{1,0:T(8,128)S(1)} %get-tuple-element.84), channel_id=1, source_target_pairs={{16,32},{32,16},{48,64},{64,48},{80,96},{96,80},{112,128},{128,112... | collective-permute-start | bytes 208904 | tf_op jit(solution)/shard_map/ppermute | solution.py:624
  16.8 1.9 %collective-permute-start.3 = (f32[136,128]{1,0:T(8,128)S(1)}, f32[136,128]{1,0:T(8,128)S(1)}, u32[]{:S(2)}, u32[]{:S(2)}) collective-permute-start(f32[136,128]{1,0:T(8,128)S(1)} %get-tuple-element.85), channel_id=1, source_target_pairs={{0,16},{16,0},{32,48},{48,32},{64,80},{80,64},{96,112},{112,96},{1... | collective-permute-start | bytes 208904 | tf_op jit(solution)/shard_map/ppermute | solution.py:624
  18.8 2.6 %shard_map.123 = (bf16[2,512,512]{2,1,0:T(8,128)(2,1)S(1)}, f32[8,512]{1,0:T(8,128)S(1)}, f32[512,512]{1,0:T(8,128)S(1)}) custom-call(s32[1,512]{1,0:T(1,128)S(1)} %get-tuple-element.86.order, f32[512,512]{1,0:T(8,128)S(1)} %get-tuple-element.87.neumann_s, s32[8,64]{1,0:T(8,128)} %bitcast.21, f32[512,512]{1,0:T(8,128)} %bitcast.17), custom_call_target="tpu_custom_call" | custom-call | flops 2000000000 | bytes 1000000 | tf_op jit(solution)/shard_map/pallas_call | solution.py:596
  22.5 4.4 %collective-permute-start.4 = (f32[136,128]{1,0:T(8,128)S(1)}, f32[136,128]{1,0:T(8,128)S(1)}, u32[]{:S(2)}, u32[]{:S(2)}) collective-permute-start(f32[136,128]{1,0:T(8,128)S(1)} %get-tuple-element.91), channel_id=1, source_target_pairs={{0,15},{1,2},{2,1},{3,4},{4,3},{5,6},{6,5},{7,8},{8,7},{9,10},{10,... | collective-permute-start | bytes 208904 | tf_op jit(solution)/shard_map/ppermute | solution.py:618
  26.9 1.9 %collective-permute-start.5 = (f32[136,128]{1,0:T(8,128)S(1)}, f32[136,128]{1,0:T(8,128)S(1)}, u32[]{:S(2)}, u32[]{:S(2)}) collective-permute-start(f32[136,128]{1,0:T(8,128)S(1)} %get-tuple-element.92), channel_id=1, source_target_pairs={{0,1},{1,0},{2,3},{3,2},{4,5},{5,4},{6,7},{7,6},{8,9},{9,8},{10,11... | collective-permute-start | bytes 208904 | tf_op jit(solution)/shard_map/ppermute | solution.py:618
  28.8 3.5 %collective-permute-start.6 = (f32[136,128]{1,0:T(8,128)S(1)}, f32[136,128]{1,0:T(8,128)S(1)}, u32[]{:S(2)}, u32[]{:S(2)}) collective-permute-start(f32[136,128]{1,0:T(8,128)S(1)} %get-tuple-element.93), channel_id=1, source_target_pairs={{16,32},{32,16},{48,64},{64,48},{80,96},{96,80},{112,128},{128,112... | collective-permute-start | bytes 208904 | tf_op jit(solution)/shard_map/ppermute | solution.py:624
  32.3 1.9 %collective-permute-start.7 = (f32[136,128]{1,0:T(8,128)S(1)}, f32[136,128]{1,0:T(8,128)S(1)}, u32[]{:S(2)}, u32[]{:S(2)}) collective-permute-start(f32[136,128]{1,0:T(8,128)S(1)} %get-tuple-element.94), channel_id=1, source_target_pairs={{0,16},{16,0},{32,48},{48,32},{64,80},{80,64},{96,112},{112,96},{1... | collective-permute-start | bytes 208904 | tf_op jit(solution)/shard_map/ppermute | solution.py:624
  34.2 1.5 shard_map.125
  35.8 2.1 %shard_map.126 = (f32[152,512]{1,0:T(8,128)}, f32[152,512]{1,0:T(8,128)S(1)}, f32[152,128]{1,0:T(8,128)S(1)}, f32[152,128]{1,0:T(8,128)S(1)}, f32[152,128]{1,0:T(8,128)S(1)}, /*index=5*/f32[152,128]{1,0:T(8,128)S(1)}) custom-call(s32[3]{0:T(128)S(1)} %pad_add_fusion.place, f32[136,512]{1,0:T(8,128)S(1)} %get-tuple-element.90.t, ...), custom_call_target="tpu_custom_call" | custom-call | flops 1000000 | bytes 1000000 | tf_op jit(solution)/shard_map/pallas_call | solution.py:596
  37.9 5.0 %collective-permute-start.10 = (f32[152,128]{1,0:T(8,128)S(1)}, f32[152,128]{1,0:T(8,128)S(1)}, u32[]{:S(2)}, u32[]{:S(2)}) collective-permute-start(f32[152,128]{1,0:T(8,128)S(1)} %get-tuple-element.103), channel_id=1, source_target_pairs={{0,15},{1,2},{2,1},{3,4},{4,3},{5,6},{6,5},{7,8},{8,7},{9,10},{10,... | collective-permute-start | bytes 233480 | tf_op jit(solution)/shard_map/ppermute | solution.py:618
  42.9 1.9 %collective-permute-start.11 = (f32[152,128]{1,0:T(8,128)S(1)}, f32[152,128]{1,0:T(8,128)S(1)}, u32[]{:S(2)}, u32[]{:S(2)}) collective-permute-start(f32[152,128]{1,0:T(8,128)S(1)} %get-tuple-element.104), channel_id=1, source_target_pairs={{0,1},{1,0},{2,3},{3,2},{4,5},{5,4},{6,7},{7,6},{8,9},{9,8},{10,11... | collective-permute-start | bytes 233480 | tf_op jit(solution)/shard_map/ppermute | solution.py:618
  44.8 4.2 %collective-permute-start.8 = (f32[152,128]{1,0:T(8,128)S(1)}, f32[152,128]{1,0:T(8,128)S(1)}, u32[]{:S(2)}, u32[]{:S(2)}) collective-permute-start(f32[152,128]{1,0:T(8,128)S(1)} %get-tuple-element.101), channel_id=1, source_target_pairs={{16,32},{32,16},{48,64},{64,48},{80,96},{96,80},{112,128},{128,112... | collective-permute-start | bytes 233480 | tf_op jit(solution)/shard_map/ppermute | solution.py:624
  49.0 1.9 %collective-permute-start.9 = (f32[152,128]{1,0:T(8,128)S(1)}, f32[152,128]{1,0:T(8,128)S(1)}, u32[]{:S(2)}, u32[]{:S(2)}) collective-permute-start(f32[152,128]{1,0:T(8,128)S(1)} %get-tuple-element.102), channel_id=1, source_target_pairs={{0,16},{16,0},{32,48},{48,32},{64,80},{80,64},{96,112},{112,96},{1... | collective-permute-start | bytes 233480 | tf_op jit(solution)/shard_map/ppermute | solution.py:624
  52.2 1.3 shard_map.127
  53.5 3.7 %collective-permute-start.12 = (f32[168,128]{1,0:T(8,128)S(1)}, f32[168,128]{1,0:T(8,128)S(1)}, u32[]{:S(2)}, u32[]{:S(2)}) collective-permute-start(f32[168,128]{1,0:T(8,128)S(1)} %get-tuple-element.107), channel_id=1, source_target_pairs={{0,15},{1,2},{2,1},{3,4},{4,3},{5,6},{6,5},{7,8},{8,7},{9,10},{10,... | collective-permute-start | bytes 258056 | tf_op jit(solution)/shard_map/ppermute | solution.py:618
  57.1 1.9 %collective-permute-start.13 = (f32[168,128]{1,0:T(8,128)S(1)}, f32[168,128]{1,0:T(8,128)S(1)}, u32[]{:S(2)}, u32[]{:S(2)}) collective-permute-start(f32[168,128]{1,0:T(8,128)S(1)} %get-tuple-element.108), channel_id=1, source_target_pairs={{0,1},{1,0},{2,3},{3,2},{4,5},{5,4},{6,7},{7,6},{8,9},{9,8},{10,11... | collective-permute-start | bytes 258056 | tf_op jit(solution)/shard_map/ppermute | solution.py:618
  59.1 5.1 %collective-permute-start.14 = (f32[168,128]{1,0:T(8,128)S(1)}, f32[168,128]{1,0:T(8,128)S(1)}, u32[]{:S(2)}, u32[]{:S(2)}) collective-permute-start(f32[168,128]{1,0:T(8,128)S(1)} %get-tuple-element.109), channel_id=1, source_target_pairs={{16,32},{32,16},{48,64},{64,48},{80,96},{96,80},{112,128},{128,112... | collective-permute-start | bytes 258056 | tf_op jit(solution)/shard_map/ppermute | solution.py:624
  64.1 1.9 %collective-permute-start.15 = (f32[168,128]{1,0:T(8,128)S(1)}, f32[168,128]{1,0:T(8,128)S(1)}, u32[]{:S(2)}, u32[]{:S(2)}) collective-permute-start(f32[168,128]{1,0:T(8,128)S(1)} %get-tuple-element.110), channel_id=1, source_target_pairs={{0,16},{16,0},{32,48},{48,32},{64,80},{80,64},{96,112},{112,96},{1... | collective-permute-start | bytes 258056 | tf_op jit(solution)/shard_map/ppermute | solution.py:624
  67.3 2.3 %shard_map.128 = (f32[184,512]{1,0:T(8,128)}, f32[184,512]{1,0:T(8,128)S(1)}, f32[184,128]{1,0:T(8,128)S(1)}, f32[184,128]{1,0:T(8,128)S(1)}, f32[184,128]{1,0:T(8,128)S(1)}, /*index=5*/f32[184,128]{1,0:T(8,128)S(1)}) custom-call(s32[3]{0:T(128)S(1)} %pad_add_fusion.place, f32[168,512]{1,0:T(8,128)S(1)} %get-tuple-element.106.t, ...), custom_call_target="tpu_custom_call" | custom-call | flops 1000000 | bytes 1000000 | tf_op jit(solution)/shard_map/pallas_call | solution.py:596
  69.6 4.9 %collective-permute-start.16 = (f32[184,128]{1,0:T(8,128)S(1)}, f32[184,128]{1,0:T(8,128)S(1)}, u32[]{:S(2)}, u32[]{:S(2)}) collective-permute-start(f32[184,128]{1,0:T(8,128)S(1)} %get-tuple-element.112), channel_id=1, source_target_pairs={{0,15},{1,2},{2,1},{3,4},{4,3},{5,6},{6,5},{7,8},{8,7},{9,10},{10,... | collective-permute-start | bytes 282632 | tf_op jit(solution)/shard_map/ppermute | solution.py:618
  74.5 1.9 %collective-permute-start.17 = (f32[184,128]{1,0:T(8,128)S(1)}, f32[184,128]{1,0:T(8,128)S(1)}, u32[]{:S(2)}, u32[]{:S(2)}) collective-permute-start(f32[184,128]{1,0:T(8,128)S(1)} %get-tuple-element.113), channel_id=1, source_target_pairs={{0,1},{1,0},{2,3},{3,2},{4,5},{5,4},{6,7},{7,6},{8,9},{9,8},{10,11... | collective-permute-start | bytes 282632 | tf_op jit(solution)/shard_map/ppermute | solution.py:618
  76.5 3.9 %collective-permute-start.18 = (f32[184,128]{1,0:T(8,128)S(1)}, f32[184,128]{1,0:T(8,128)S(1)}, u32[]{:S(2)}, u32[]{:S(2)}) collective-permute-start(f32[184,128]{1,0:T(8,128)S(1)} %get-tuple-element.114), channel_id=1, source_target_pairs={{16,32},{32,16},{48,64},{64,48},{80,96},{96,80},{112,128},{128,112... | collective-permute-start | bytes 282632 | tf_op jit(solution)/shard_map/ppermute | solution.py:624
  80.3 1.9 %collective-permute-start.19 = (f32[184,128]{1,0:T(8,128)S(1)}, f32[184,128]{1,0:T(8,128)S(1)}, u32[]{:S(2)}, u32[]{:S(2)}) collective-permute-start(f32[184,128]{1,0:T(8,128)S(1)} %get-tuple-element.115), channel_id=1, source_target_pairs={{0,16},{16,0},{32,48},{48,32},{64,80},{80,64},{96,112},{112,96},{1... | collective-permute-start | bytes 282632 | tf_op jit(solution)/shard_map/ppermute | solution.py:624
  83.5 2.4 %shard_map.129 = (f32[200,512]{1,0:T(8,128)}, f32[16,32,128]{2,1,0:T(8,128)}) custom-call(s32[3]{0:T(128)S(1)} %pad_add_fusion.place, f32[184,512]{1,0:T(8,128)S(1)} %get-tuple-element.111.q, f32[184,128]{1,0:T(8,128)S(1)} %collective-permute-done.16.g0, f32[184,128]{1,0:T(8,128)S(1)} %collective-permute-done.17.g1, ...), custom_call_target="tpu_custom_call" | custom-call | flops 1000000 | bytes 1000000 | tf_op jit(solution)/shard_map/pallas_call | solution.py:596
  85.9 4.8 %all-to-all-start = ((f32[16,32,128]{2,1,0:T(8,128)}), f32[16,32,128]{2,1,0:T(8,128)S(1)}, u32[]{:S(2)}, u32[]{:S(2)}) async-start(f32[16,32,128]{2,1,0:T(8,128)} %get-tuple-element.119), calls=%async_computation | async-start | bytes 524288 | tf_op jit(solution)/shard_map/all_to_all | solution.py:632
  90.7 2.9 %shard_map.130 = (f32[200,512]{1,0:T(8,128)}, f32[200,128]{1,0:T(8,128)S(1)}, f32[200,128]{1,0:T(8,128)S(1)}, f32[200,128]{1,0:T(8,128)S(1)}, f32[200,128]{1,0:T(8,128)S(1)}) custom-call(s32[3]{0:T(128)S(1)} %pad_add_fusion.place, f32[200,512]{1,0:T(8,128)} %get-tuple-element.120.v2, f32[1,512]{1,0:T(1,128)S(1)} %get-tuple-element.95.after.share, ...), custom_call_target="tpu_custom_call" | custom-call | flops 500000000 | bytes 1000000 | tf_op jit(solution)/shard_map/pallas_call | solution.py:596
  94.9 4.1 %all-to-all-done.got = f32[16,32,128]{2,1,0:T(8,128)S(1)} async-done(((f32[16,32,128]{2,1,0:T(8,128)}), f32[16,32,128]{2,1,0:T(8,128)S(1)}, u32[]{:S(2)}, u32[]{:S(2)}) %all-to-all-start) | async-done | bytes 262176 | tf_op jit(solution)/shard_map/all_to_all | solution.py:632
  99.8 11.5 %all-to-all-start.1 = ((f32[16,32,128]{2,1,0:T(8,128)}), f32[16,32,128]{2,1,0:T(8,128)S(1)}, u32[]{:S(2)}, u32[]{:S(2)}) async-start(f32[16,32,128]{2,1,0:T(8,128)} %shard_map.131), calls=%async_computation.1 | async-start | bytes 524288 | tf_op jit(solution)/shard_map/all_to_all | solution.py:632
  111.3 2.8 %collective-permute-start.20 = (f32[200,128]{1,0:T(8,128)S(1)}, f32[200,128]{1,0:T(8,128)S(1)}, u32[]{:S(2)}, u32[]{:S(2)}) collective-permute-start(f32[200,128]{1,0:T(8,128)S(1)} %copy-done.6), channel_id=1, source_target_pairs={{0,15},{1,2},{2,1},{3,4},{4,3},{5,6},{6,5},{7,8},{8,7},{9,10},{10,... | collective-permute-start | bytes 307208 | tf_op jit(solution)/shard_map/ppermute | solution.py:618
  114.2 1.9 %collective-permute-start.21 = (f32[200,128]{1,0:T(8,128)S(1)}, f32[200,128]{1,0:T(8,128)S(1)}, u32[]{:S(2)}, u32[]{:S(2)}) collective-permute-start(f32[200,128]{1,0:T(8,128)S(1)} %copy-done.4), channel_id=1, source_target_pairs={{0,1},{1,0},{2,3},{3,2},{4,5},{5,4},{6,7},{7,6},{8,9},{9,8},{10,11... | collective-permute-start | bytes 307208 | tf_op jit(solution)/shard_map/ppermute | solution.py:618
  116.1 6.6 %collective-permute-start.22 = (f32[200,128]{1,0:T(8,128)S(1)}, f32[200,128]{1,0:T(8,128)S(1)}, u32[]{:S(2)}, u32[]{:S(2)}) collective-permute-start(f32[200,128]{1,0:T(8,128)S(1)} %get-tuple-element.131), channel_id=1, source_target_pairs={{16,32},{32,16},{48,64},{64,48},{80,96},{96,80},{112,128},{128,112... | collective-permute-start | bytes 307208 | tf_op jit(solution)/shard_map/ppermute | solution.py:624
  122.7 1.9 %collective-permute-start.23 = (f32[200,128]{1,0:T(8,128)S(1)}, f32[200,128]{1,0:T(8,128)S(1)}, u32[]{:S(2)}, u32[]{:S(2)}) collective-permute-start(f32[200,128]{1,0:T(8,128)S(1)} %get-tuple-element.132), channel_id=1, source_target_pairs={{0,16},{16,0},{32,48},{48,32},{64,80},{80,64},{96,112},{112,96},{1... | collective-permute-start | bytes 307208 | tf_op jit(solution)/shard_map/ppermute | solution.py:624
  124.6 1.9 %collective-permute-done.22.g2 = f32[200,128]{1,0:T(8,128)S(1)} collective-permute-done((f32[200,128]{1,0:T(8,128)S(1)}, f32[200,128]{1,0:T(8,128)S(1)}, u32[]{:S(2)}, u32[]{:S(2)}) %collective-permute-start.22) | collective-permute-done | bytes 102432 | tf_op jit(solution)/shard_map/ppermute | solution.py:624
  126.5 6.5 %collective-permute-start.24 = (f32[16,32,128]{2,1,0:T(8,128)S(1)}, f32[16,32,128]{2,1,0:T(8,128)S(1)}, u32[]{:S(2)}, u32[]{:S(2)}) collective-permute-start(f32[16,32,128]{2,1,0:T(8,128)S(1)} %all-to-all-done.1.mine), channel_id=1, source_target_pairs={{0,16},{16,0},{32,48},{48,32},{64,80},{80,64},{96,112},{112,96},{1... | collective-permute-start | bytes 786440 | tf_op jit(solution)/shard_map/ppermute | solution.py:741
  133.1 1.1 collective-permute-done.24.other
  134.2 6.0 %shard_map.132 = (f32[128,512]{1,0:T(8,128)}, f32[128,512]{1,0:T(8,128)}, f32[128,512]{1,0:T(8,128)}, f32[128,512]{1,0:T(8,128)}, f32[128,512]{1,0:T(8,128)}, /*...) custom-call(s32[3]{0:T(128)S(1)} %pad_add_fusion.place, ...), custom_call_target="tpu_custom_call" | custom-call | flops 1000000 | bytes 1000000 | tf_op jit(solution)/shard_map/pallas_call | solution.py:596
  140.2 4.1 %all-to-all-start.2 = ((f32[32,1,1152]{2,1,0:T(1,128)}), f32[32,1,1152]{2,1,0:T(1,128)S(1)}, u32[]{:S(2)}, u32[]{:S(2)}) async-start(f32[32,1,1152]{2,1,0:T(1,128)} %get-tuple-element.141), calls=%async_computation.2 | async-start | bytes 294912 | tf_op jit(solution)/shard_map/all_to_all | solution.py:632
  144.4 6.8 %collective-permute-start.25 = (f32[128,128]{1,0:T(8,128)S(1)}, f32[128,128]{1,0:T(8,128)S(1)}, u32[]{:S(2)}, u32[]{:S(2)}) collective-permute-start(f32[128,128]{1,0:T(8,128)S(1)} %get-tuple-element.142), channel_id=1, source_target_pairs={{0,15},{1,2},{2,1},{3,4},{4,3},{5,6},{6,5},{7,8},{8,7},{9,10},{10,... | collective-permute-start | bytes 196616 | tf_op jit(solution)/shard_map/ppermute | solution.py:618
  151.2 1.9 %collective-permute-start.26 = (f32[128,128]{1,0:T(8,128)S(1)}, f32[128,128]{1,0:T(8,128)S(1)}, u32[]{:S(2)}, u32[]{:S(2)}) collective-permute-start(f32[128,128]{1,0:T(8,128)S(1)} %get-tuple-element.143), channel_id=1, source_target_pairs={{0,1},{1,0},{2,3},{3,2},{4,5},{5,4},{6,7},{7,6},{8,9},{9,8},{10,11... | collective-permute-start | bytes 196616 | tf_op jit(solution)/shard_map/ppermute | solution.py:618
  153.1 3.1 %collective-permute-done.26.g1 = f32[128,128]{1,0:T(8,128)S(1)} collective-permute-done((f32[128,128]{1,0:T(8,128)S(1)}, f32[128,128]{1,0:T(8,128)S(1)}, u32[]{:S(2)}, u32[]{:S(2)}) %collective-permute-start.26) | collective-permute-done | bytes 65568 | tf_op jit(solution)/shard_map/ppermute | solution.py:618
  156.9 10.3 %all-to-all-start.3 = ((f32[16,1,1152]{2,1,0:T(1,128)}), f32[16,1,1152]{2,1,0:T(1,128)S(1)}, u32[]{:S(2)}, u32[]{:S(2)}) async-start(f32[16,1,1152]{2,1,0:T(1,128)} %shard_map.133), calls=%async_computation.3 | async-start | bytes 147456 | tf_op jit(solution)/shard_map/all_to_all | solution.py:632
  167.2 5.4 %collective-permute-start.27 = (f32[128,128]{1,0:T(8,128)S(1)}, f32[128,128]{1,0:T(8,128)S(1)}, u32[]{:S(2)}, u32[]{:S(2)}) collective-permute-start(f32[128,128]{1,0:T(8,128)S(1)} %get-tuple-element.151), channel_id=1, source_target_pairs={{16,32},{32,16},{48,64},{64,48},{80,96},{96,80},{112,128},{128,112... | collective-permute-start | bytes 196616 | tf_op jit(solution)/shard_map/ppermute | solution.py:624
  172.6 1.9 %collective-permute-start.28 = (f32[128,128]{1,0:T(8,128)S(1)}, f32[128,128]{1,0:T(8,128)S(1)}, u32[]{:S(2)}, u32[]{:S(2)}) collective-permute-start(f32[128,128]{1,0:T(8,128)S(1)} %get-tuple-element.152), channel_id=1, source_target_pairs={{0,16},{16,0},{32,48},{48,32},{64,80},{80,64},{96,112},{112,96},{1... | collective-permute-start | bytes 196616 | tf_op jit(solution)/shard_map/ppermute | solution.py:624
  175.8 3.1 %all-to-all-done.3.got = f32[16,1,1152]{2,1,0:T(1,128)S(1)} async-done(((f32[16,1,1152]{2,1,0:T(1,128)}), f32[16,1,1152]{2,1,0:T(1,128)S(1)}, u32[]{:S(2)}, u32[]{:S(2)}) %all-to-all-start.3) | async-done | bytes 73760 | tf_op jit(solution)/shard_map/all_to_all | solution.py:632
  178.9 3.3 %shard_map.134 = (f32[128,512]{1,0:T(8,128)}, f32[128,512]{1,0:T(8,128)}) custom-call(s32[3]{0:T(128)S(1)} %pad_add_fusion.place, f32[16,1,1152]{2,1,0:T(1,128)S(1)} %all-to-all-done.3.got, f32[128,512]{1,0:T(8,128)S(1)} %get-tuple-element.148.q, f32[128,128]{1,0:T(8,128)S(1)} %collective-permute-done.25.g0, f32[128,128]{1,0:T(8,128)S(1)} %collective-permute-done.26.g1, ...), custom_call_target="tpu_custom_call" | custom-call | flops 1000000 | bytes 1000000 | tf_op jit(solution)/shard_map/pallas_call | solution.py:596
  (47 shorter events, 8.9 us)
Async XLA Ops:
  2.8 18.5 %collective-permute-start = (f32[136,128]{1,0:T(8,128)S(1)}, f32[136,128]{1,0:T(8,128)S(1)}, u32[]{:S(2)}, u32[]{:S(2)}) collective-permute-start(f32[136,128]{1,0:T(8,128)S(1)} %get-tuple-element.82), channel_id=1, source_target_pairs={{0,15},{1,2},{2,1},{3,4},{4,3},{5,6},{6,5},{7,8},{8,7},{9,10},{10,... | collective-permute-start | bytes 208904 | tf_op jit(solution)/shard_map/ppermute | solution.py:618
  10.5 10.9 %collective-permute-start.1 = (f32[136,128]{1,0:T(8,128)S(1)}, f32[136,128]{1,0:T(8,128)S(1)}, u32[]{:S(2)}, u32[]{:S(2)}) collective-permute-start(f32[136,128]{1,0:T(8,128)S(1)} %get-tuple-element.83), channel_id=1, source_target_pairs={{0,1},{1,0},{2,3},{3,2},{4,5},{5,4},{6,7},{7,6},{8,9},{9,8},{10,11... | collective-permute-start | bytes 208904 | tf_op jit(solution)/shard_map/ppermute | solution.py:618
  12.4 8.9 %collective-permute-start.2 = (f32[136,128]{1,0:T(8,128)S(1)}, f32[136,128]{1,0:T(8,128)S(1)}, u32[]{:S(2)}, u32[]{:S(2)}) collective-permute-start(f32[136,128]{1,0:T(8,128)S(1)} %get-tuple-element.84), channel_id=1, source_target_pairs={{16,32},{32,16},{48,64},{64,48},{80,96},{96,80},{112,128},{128,112... | collective-permute-start | bytes 208904 | tf_op jit(solution)/shard_map/ppermute | solution.py:624
  16.8 4.6 %collective-permute-start.3 = (f32[136,128]{1,0:T(8,128)S(1)}, f32[136,128]{1,0:T(8,128)S(1)}, u32[]{:S(2)}, u32[]{:S(2)}) collective-permute-start(f32[136,128]{1,0:T(8,128)S(1)} %get-tuple-element.85), channel_id=1, source_target_pairs={{0,16},{16,0},{32,48},{48,32},{64,80},{80,64},{96,112},{112,96},{1... | collective-permute-start | bytes 208904 | tf_op jit(solution)/shard_map/ppermute | solution.py:624
  22.5 13.2 %collective-permute-start.4 = (f32[136,128]{1,0:T(8,128)S(1)}, f32[136,128]{1,0:T(8,128)S(1)}, u32[]{:S(2)}, u32[]{:S(2)}) collective-permute-start(f32[136,128]{1,0:T(8,128)S(1)} %get-tuple-element.91), channel_id=1, source_target_pairs={{0,15},{1,2},{2,1},{3,4},{4,3},{5,6},{6,5},{7,8},{8,7},{9,10},{10,... | collective-permute-start | bytes 208904 | tf_op jit(solution)/shard_map/ppermute | solution.py:618
  26.9 8.9 %collective-permute-start.5 = (f32[136,128]{1,0:T(8,128)S(1)}, f32[136,128]{1,0:T(8,128)S(1)}, u32[]{:S(2)}, u32[]{:S(2)}) collective-permute-start(f32[136,128]{1,0:T(8,128)S(1)} %get-tuple-element.92), channel_id=1, source_target_pairs={{0,1},{1,0},{2,3},{3,2},{4,5},{5,4},{6,7},{7,6},{8,9},{9,8},{10,11... | collective-permute-start | bytes 208904 | tf_op jit(solution)/shard_map/ppermute | solution.py:618
  28.8 6.9 %collective-permute-start.6 = (f32[136,128]{1,0:T(8,128)S(1)}, f32[136,128]{1,0:T(8,128)S(1)}, u32[]{:S(2)}, u32[]{:S(2)}) collective-permute-start(f32[136,128]{1,0:T(8,128)S(1)} %get-tuple-element.93), channel_id=1, source_target_pairs={{16,32},{32,16},{48,64},{64,48},{80,96},{96,80},{112,128},{128,112... | collective-permute-start | bytes 208904 | tf_op jit(solution)/shard_map/ppermute | solution.py:624
  32.3 3.5 %collective-permute-start.7 = (f32[136,128]{1,0:T(8,128)S(1)}, f32[136,128]{1,0:T(8,128)S(1)}, u32[]{:S(2)}, u32[]{:S(2)}) collective-permute-start(f32[136,128]{1,0:T(8,128)S(1)} %get-tuple-element.94), channel_id=1, source_target_pairs={{0,16},{16,0},{32,48},{48,32},{64,80},{80,64},{96,112},{112,96},{1... | collective-permute-start | bytes 208904 | tf_op jit(solution)/shard_map/ppermute | solution.py:624
  37.9 13.0 %collective-permute-start.10 = (f32[152,128]{1,0:T(8,128)S(1)}, f32[152,128]{1,0:T(8,128)S(1)}, u32[]{:S(2)}, u32[]{:S(2)}) collective-permute-start(f32[152,128]{1,0:T(8,128)S(1)} %get-tuple-element.103), channel_id=1, source_target_pairs={{0,15},{1,2},{2,1},{3,4},{4,3},{5,6},{6,5},{7,8},{8,7},{9,10},{10,... | collective-permute-start | bytes 233480 | tf_op jit(solution)/shard_map/ppermute | solution.py:618
  42.9 8.1 %collective-permute-start.11 = (f32[152,128]{1,0:T(8,128)S(1)}, f32[152,128]{1,0:T(8,128)S(1)}, u32[]{:S(2)}, u32[]{:S(2)}) collective-permute-start(f32[152,128]{1,0:T(8,128)S(1)} %get-tuple-element.104), channel_id=1, source_target_pairs={{0,1},{1,0},{2,3},{3,2},{4,5},{5,4},{6,7},{7,6},{8,9},{9,8},{10,11... | collective-permute-start | bytes 233480 | tf_op jit(solution)/shard_map/ppermute | solution.py:618
  44.8 6.3 %collective-permute-start.8 = (f32[152,128]{1,0:T(8,128)S(1)}, f32[152,128]{1,0:T(8,128)S(1)}, u32[]{:S(2)}, u32[]{:S(2)}) collective-permute-start(f32[152,128]{1,0:T(8,128)S(1)} %get-tuple-element.101), channel_id=1, source_target_pairs={{16,32},{32,16},{48,64},{64,48},{80,96},{96,80},{112,128},{128,112... | collective-permute-start | bytes 233480 | tf_op jit(solution)/shard_map/ppermute | solution.py:624
  49.0 3.2 %collective-permute-start.9 = (f32[152,128]{1,0:T(8,128)S(1)}, f32[152,128]{1,0:T(8,128)S(1)}, u32[]{:S(2)}, u32[]{:S(2)}) collective-permute-start(f32[152,128]{1,0:T(8,128)S(1)} %get-tuple-element.102), channel_id=1, source_target_pairs={{0,16},{16,0},{32,48},{48,32},{64,80},{80,64},{96,112},{112,96},{1... | collective-permute-start | bytes 233480 | tf_op jit(solution)/shard_map/ppermute | solution.py:624
  53.5 12.6 %collective-permute-start.12 = (f32[168,128]{1,0:T(8,128)S(1)}, f32[168,128]{1,0:T(8,128)S(1)}, u32[]{:S(2)}, u32[]{:S(2)}) collective-permute-start(f32[168,128]{1,0:T(8,128)S(1)} %get-tuple-element.107), channel_id=1, source_target_pairs={{0,15},{1,2},{2,1},{3,4},{4,3},{5,6},{6,5},{7,8},{8,7},{9,10},{10,... | collective-permute-start | bytes 258056 | tf_op jit(solution)/shard_map/ppermute | solution.py:618
  57.1 9.0 %collective-permute-start.13 = (f32[168,128]{1,0:T(8,128)S(1)}, f32[168,128]{1,0:T(8,128)S(1)}, u32[]{:S(2)}, u32[]{:S(2)}) collective-permute-start(f32[168,128]{1,0:T(8,128)S(1)} %get-tuple-element.108), channel_id=1, source_target_pairs={{0,1},{1,0},{2,3},{3,2},{4,5},{5,4},{6,7},{7,6},{8,9},{9,8},{10,11... | collective-permute-start | bytes 258056 | tf_op jit(solution)/shard_map/ppermute | solution.py:618
  59.1 7.2 %collective-permute-start.14 = (f32[168,128]{1,0:T(8,128)S(1)}, f32[168,128]{1,0:T(8,128)S(1)}, u32[]{:S(2)}, u32[]{:S(2)}) collective-permute-start(f32[168,128]{1,0:T(8,128)S(1)} %get-tuple-element.109), channel_id=1, source_target_pairs={{16,32},{32,16},{48,64},{64,48},{80,96},{96,80},{112,128},{128,112... | collective-permute-start | bytes 258056 | tf_op jit(solution)/shard_map/ppermute | solution.py:624
  64.1 3.2 %collective-permute-start.15 = (f32[168,128]{1,0:T(8,128)S(1)}, f32[168,128]{1,0:T(8,128)S(1)}, u32[]{:S(2)}, u32[]{:S(2)}) collective-permute-start(f32[168,128]{1,0:T(8,128)S(1)} %get-tuple-element.110), channel_id=1, source_target_pairs={{0,16},{16,0},{32,48},{48,32},{64,80},{80,64},{96,112},{112,96},{1... | collective-permute-start | bytes 258056 | tf_op jit(solution)/shard_map/ppermute | solution.py:624
  69.6 12.7 %collective-permute-start.16 = (f32[184,128]{1,0:T(8,128)S(1)}, f32[184,128]{1,0:T(8,128)S(1)}, u32[]{:S(2)}, u32[]{:S(2)}) collective-permute-start(f32[184,128]{1,0:T(8,128)S(1)} %get-tuple-element.112), channel_id=1, source_target_pairs={{0,15},{1,2},{2,1},{3,4},{4,3},{5,6},{6,5},{7,8},{8,7},{9,10},{10,... | collective-permute-start | bytes 282632 | tf_op jit(solution)/shard_map/ppermute | solution.py:618
  74.5 7.7 %collective-permute-start.17 = (f32[184,128]{1,0:T(8,128)S(1)}, f32[184,128]{1,0:T(8,128)S(1)}, u32[]{:S(2)}, u32[]{:S(2)}) collective-permute-start(f32[184,128]{1,0:T(8,128)S(1)} %get-tuple-element.113), channel_id=1, source_target_pairs={{0,1},{1,0},{2,3},{3,2},{4,5},{5,4},{6,7},{7,6},{8,9},{9,8},{10,11... | collective-permute-start | bytes 282632 | tf_op jit(solution)/shard_map/ppermute | solution.py:618
  76.5 6.1 %collective-permute-start.18 = (f32[184,128]{1,0:T(8,128)S(1)}, f32[184,128]{1,0:T(8,128)S(1)}, u32[]{:S(2)}, u32[]{:S(2)}) collective-permute-start(f32[184,128]{1,0:T(8,128)S(1)} %get-tuple-element.114), channel_id=1, source_target_pairs={{16,32},{32,16},{48,64},{64,48},{80,96},{96,80},{112,128},{128,112... | collective-permute-start | bytes 282632 | tf_op jit(solution)/shard_map/ppermute | solution.py:624
  80.3 3.2 %collective-permute-start.19 = (f32[184,128]{1,0:T(8,128)S(1)}, f32[184,128]{1,0:T(8,128)S(1)}, u32[]{:S(2)}, u32[]{:S(2)}) collective-permute-start(f32[184,128]{1,0:T(8,128)S(1)} %get-tuple-element.115), channel_id=1, source_target_pairs={{0,16},{16,0},{32,48},{48,32},{64,80},{80,64},{96,112},{112,96},{1... | collective-permute-start | bytes 282632 | tf_op jit(solution)/shard_map/ppermute | solution.py:624
  85.9 13.1 %all-to-all-start = ((f32[16,32,128]{2,1,0:T(8,128)}), f32[16,32,128]{2,1,0:T(8,128)S(1)}, u32[]{:S(2)}, u32[]{:S(2)}) async-start(f32[16,32,128]{2,1,0:T(8,128)} %get-tuple-element.119), calls=%async_computation | async-start | bytes 524288 | tf_op jit(solution)/shard_map/all_to_all | solution.py:632
  93.6 0.6 copy-start.3
  94.3 0.6 copy-start.5
  99.8 34.4 %copy-start = (f32[152,512]{1,0:T(8,128)S(1)}, f32[152,512]{1,0:T(8,128)}, u32[]{:S(2)}) copy-start(f32[152,512]{1,0:T(8,128)} %get-tuple-element.139.z0) | copy-start | bytes 933892
  99.8 11.5 %copy-start.6 = (f32[200,128]{1,0:T(8,128)S(1)}, f32[200,128]{1,0:T(8,128)}, u32[]{:S(2)}) copy-start(f32[200,128]{1,0:T(8,128)} %copy-done.5) | copy-start | bytes 307204
  99.8 14.4 %copy-start.4 = (f32[200,128]{1,0:T(8,128)S(1)}, f32[200,128]{1,0:T(8,128)}, u32[]{:S(2)}) copy-start(f32[200,128]{1,0:T(8,128)} %copy-done.3) | copy-start | bytes 307204
  99.8 26.7 %all-to-all-start.1 = ((f32[16,32,128]{2,1,0:T(8,128)}), f32[16,32,128]{2,1,0:T(8,128)S(1)}, u32[]{:S(2)}, u32[]{:S(2)}) async-start(f32[16,32,128]{2,1,0:T(8,128)} %shard_map.131), calls=%async_computation.1 | async-start | bytes 524288 | tf_op jit(solution)/shard_map/all_to_all | solution.py:632
  111.3 13.2 %collective-permute-start.20 = (f32[200,128]{1,0:T(8,128)S(1)}, f32[200,128]{1,0:T(8,128)S(1)}, u32[]{:S(2)}, u32[]{:S(2)}) collective-permute-start(f32[200,128]{1,0:T(8,128)S(1)} %copy-done.6), channel_id=1, source_target_pairs={{0,15},{1,2},{2,1},{3,4},{4,3},{5,6},{6,5},{7,8},{8,7},{9,10},{10,... | collective-permute-start | bytes 307208 | tf_op jit(solution)/shard_map/ppermute | solution.py:618
  114.2 10.4 %collective-permute-start.21 = (f32[200,128]{1,0:T(8,128)S(1)}, f32[200,128]{1,0:T(8,128)S(1)}, u32[]{:S(2)}, u32[]{:S(2)}) collective-permute-start(f32[200,128]{1,0:T(8,128)S(1)} %copy-done.4), channel_id=1, source_target_pairs={{0,1},{1,0},{2,3},{3,2},{4,5},{5,4},{6,7},{7,6},{8,9},{9,8},{10,11... | collective-permute-start | bytes 307208 | tf_op jit(solution)/shard_map/ppermute | solution.py:618
  116.1 10.4 %collective-permute-start.22 = (f32[200,128]{1,0:T(8,128)S(1)}, f32[200,128]{1,0:T(8,128)S(1)}, u32[]{:S(2)}, u32[]{:S(2)}) collective-permute-start(f32[200,128]{1,0:T(8,128)S(1)} %get-tuple-element.131), channel_id=1, source_target_pairs={{16,32},{32,16},{48,64},{64,48},{80,96},{96,80},{112,128},{128,112... | collective-permute-start | bytes 307208 | tf_op jit(solution)/shard_map/ppermute | solution.py:624
  122.7 3.9 %collective-permute-start.23 = (f32[200,128]{1,0:T(8,128)S(1)}, f32[200,128]{1,0:T(8,128)S(1)}, u32[]{:S(2)}, u32[]{:S(2)}) collective-permute-start(f32[200,128]{1,0:T(8,128)S(1)} %get-tuple-element.132), channel_id=1, source_target_pairs={{0,16},{16,0},{32,48},{48,32},{64,80},{80,64},{96,112},{112,96},{1... | collective-permute-start | bytes 307208 | tf_op jit(solution)/shard_map/ppermute | solution.py:624
  126.5 7.7 %collective-permute-start.24 = (f32[16,32,128]{2,1,0:T(8,128)S(1)}, f32[16,32,128]{2,1,0:T(8,128)S(1)}, u32[]{:S(2)}, u32[]{:S(2)}) collective-permute-start(f32[16,32,128]{2,1,0:T(8,128)S(1)} %all-to-all-done.1.mine), channel_id=1, source_target_pairs={{0,16},{16,0},{32,48},{48,32},{64,80},{80,64},{96,112},{112,96},{1... | collective-permute-start | bytes 786440 | tf_op jit(solution)/shard_map/ppermute | solution.py:741
  140.2 38.7 %copy-start.2 = (f32[128,512]{1,0:T(8,128)S(1)}, f32[128,512]{1,0:T(8,128)}, u32[]{:S(2)}) copy-start(f32[128,512]{1,0:T(8,128)} %get-tuple-element.154.z1) | copy-start | bytes 786436
  140.2 16.0 %all-to-all-start.2 = ((f32[32,1,1152]{2,1,0:T(1,128)}), f32[32,1,1152]{2,1,0:T(1,128)S(1)}, u32[]{:S(2)}, u32[]{:S(2)}) async-start(f32[32,1,1152]{2,1,0:T(1,128)} %get-tuple-element.141), calls=%async_computation.2 | async-start | bytes 294912 | tf_op jit(solution)/shard_map/all_to_all | solution.py:632
  144.4 34.5 %copy-start.1 = (f32[128,512]{1,0:T(8,128)S(1)}, f32[128,512]{1,0:T(8,128)}, u32[]{:S(2)}) copy-start(f32[128,512]{1,0:T(8,128)} %get-tuple-element.153.z0) | copy-start | bytes 786436
  144.4 8.8 %collective-permute-start.25 = (f32[128,128]{1,0:T(8,128)S(1)}, f32[128,128]{1,0:T(8,128)S(1)}, u32[]{:S(2)}, u32[]{:S(2)}) collective-permute-start(f32[128,128]{1,0:T(8,128)S(1)} %get-tuple-element.142), channel_id=1, source_target_pairs={{0,15},{1,2},{2,1},{3,4},{4,3},{5,6},{6,5},{7,8},{8,7},{9,10},{10,... | collective-permute-start | bytes 196616 | tf_op jit(solution)/shard_map/ppermute | solution.py:618
  151.2 5.0 %collective-permute-start.26 = (f32[128,128]{1,0:T(8,128)S(1)}, f32[128,128]{1,0:T(8,128)S(1)}, u32[]{:S(2)}, u32[]{:S(2)}) collective-permute-start(f32[128,128]{1,0:T(8,128)S(1)} %get-tuple-element.143), channel_id=1, source_target_pairs={{0,1},{1,0},{2,3},{3,2},{4,5},{5,4},{6,7},{7,6},{8,9},{9,8},{10,11... | collective-permute-start | bytes 196616 | tf_op jit(solution)/shard_map/ppermute | solution.py:618
  156.9 22.0 %all-to-all-start.3 = ((f32[16,1,1152]{2,1,0:T(1,128)}), f32[16,1,1152]{2,1,0:T(1,128)S(1)}, u32[]{:S(2)}, u32[]{:S(2)}) async-start(f32[16,1,1152]{2,1,0:T(1,128)} %shard_map.133), calls=%async_computation.3 | async-start | bytes 147456 | tf_op jit(solution)/shard_map/all_to_all | solution.py:632
  167.2 8.2 %collective-permute-start.27 = (f32[128,128]{1,0:T(8,128)S(1)}, f32[128,128]{1,0:T(8,128)S(1)}, u32[]{:S(2)}, u32[]{:S(2)}) collective-permute-start(f32[128,128]{1,0:T(8,128)S(1)} %get-tuple-element.151), channel_id=1, source_target_pairs={{16,32},{32,16},{48,64},{64,48},{80,96},{96,80},{112,128},{128,112... | collective-permute-start | bytes 196616 | tf_op jit(solution)/shard_map/ppermute | solution.py:624
  172.6 3.1 %collective-permute-start.28 = (f32[128,128]{1,0:T(8,128)S(1)}, f32[128,128]{1,0:T(8,128)S(1)}, u32[]{:S(2)}, u32[]{:S(2)}) collective-permute-start(f32[128,128]{1,0:T(8,128)S(1)} %get-tuple-element.152), channel_id=1, source_target_pairs={{0,16},{16,0},{32,48},{48,32},{64,80},{80,64},{96,112},{112,96},{1... | collective-permute-start | bytes 196616 | tf_op jit(solution)/shard_map/ppermute | solution.py:624

commit v9 on v8

--- a/solution.py
+++ b/solution.py
@@ -212,12 +212,15 @@
     for item in range(length):
         total = total + jnp.where(named[:, item : item + 1] == position, 1.0, 0.0)
     avg_o[...] = to_shared(total * (1.0 / length), hots)
-    for f in range(4):
-        rows = slice(f * LANES, (f + 1) * LANES)
-        for n, piece in enumerate(cut(neumann_s[rows, :], PIECES)):
-            half = narrow(hots[f], piece).astype(BF16)
-            neumann_o[n, rows, :] = jnp.concatenate(
-                [narrow(part, hot, True) for part, hot in zip(faces_of(half), hots)], axis=1
+    tall = jnp.concatenate(cut(neumann_s[...], PIECES), axis=0)
+    half = jnp.concatenate(
+        [narrow(part, hot, True).astype(BF16) for part, hot in zip(faces_of(tall), hots)], axis=1
+    )
+    for n in range(PIECES):
+        for f in range(4):
+            first = n * points + f * LANES
+            neumann_o[n, f * LANES : (f + 1) * LANES, :] = narrow(
+                hots[f], half[first : first + LANES]
             ).astype(BF16)
     finish(ahead)
 
@@ -511,7 +514,7 @@
 
 
 def k_final(
-    place, got, q, g0, g1, g2, g3, order, r0, z0, z1, z2, w0, w1, x_o, r_o, full_s, sem
+    place, got, q, g0, g1, g2, g3, order, r0, z0, z1, z2, w0, w1, x_o, r_o, full_s, both_s, sem, out_sem
 ):
     loads = []
     for n, source in enumerate((z2, w0, w1)):
@@ -576,11 +579,12 @@
     hots = one_hot_faces(order[...])
     finish(loads)
     x = col[0] * z0[...] + col[1] * z1[...] + col[2] * full_s[0]
+    both_s[0] = to_points(x, hots)
+    copies = begin(both_s.at[0], x_o, out_sem.at[0], 2)
     r = r0[...] + col[3] * full_s[1] + col[4] * full_s[2] + col[5] * w2
-    both = to_points(jnp.concatenate([x, r], axis=0), hots)
-    rhs = x.shape[0]
-    x_o[...] = both[:rhs]
-    r_o[...] = both[rhs:]
+    both_s[1] = to_points(r, hots)
+    copies += begin(both_s.at[1], r_o, out_sem.at[1], 2)
+    finish(copies)
 
 
 def call(body, outs, place, *args, scratch=(), raw=(), raw_outs=(), flops=1_000_000):
@@ -768,7 +772,13 @@
         k_final, [(rhs, points)] * 2,
         place, dots, q2, *got, order, r0, z0f, z1f, z2f, w0f, w1f,
         raw=(10, 11, 12),
-        scratch=[pltpu.VMEM((3, rhs, points), F32), dma((3, 2))],
+        raw_outs=(0, 1),
+        scratch=[
+            pltpu.VMEM((3, rhs, points), F32),
+            pltpu.VMEM((2, rhs, points), F32),
+            dma((3, 2)),
+            dma((2, 2)),
+        ],
     )
     return (x[None, None], r[None, None])
 

time: 184 us -> 183 us (level)
  transfers between devices with their start and end apart: 33 -> 33, of which waited for: 13 -> 13; matrix products, arithmetic and copies ran while one was open for 0% -> 0% of each run, Pallas kernels for 4% -> 3%
where the time goes in v9:
time: 183 us; the launch traced here: 181 us
  starting transfers between devices  132 us (72%)
  Pallas kernels  27.9 us (15%)
  waiting for transfers between devices  18.3 us (10%)
    ppermute x7, starting transfers between devices, exchange_columns(): lax.ppermute(sends[0], 'circ', far)  35.2 us
    ppermute x7, starting transfers between devices, exchange_rows(): lax.ppermute(sends[2], 'axial', link)  33 us
    all_to_all x4, starting transfers between devices, spread(): lax.all_to_all(value, axis, split_axis=0, concat_axis=0, tiled=True, axis...  30.7 us
    pallas_call x13, Pallas kernels, call(): pl.pallas_call(body, out_shape=[out if isinstance(out, jax.ShapeDtypeStru...  27.9 us
    ppermute x7, starting transfers between devices, exchange_columns(): lax.ppermute(sends[1], 'circ', near)  13.4 us
    ppermute x7, starting transfers between devices, exchange_rows(): lax.ppermute(sends[3], 'axial', core)  13.4 us
    all_to_all x4, waiting for transfers between devices, spread(): lax.all_to_all(value, axis, split_axis=0, concat_axis=0, tiled=True, axis...  7.25 us
    ppermute x1, starting transfers between devices, local(): other = lax.ppermute(mine, 'axial', [(i, i ^ 1) for i in range(rows)])  6.55 us
  transfers between devices with their start and end apart: 33, of which 13 were waited for; matrix products, arithmetic and copies ran while one was open for 0% of the time, Pallas kernels for 3%

profile of v9, /device:TPU:1, one launch (start us, length us, event | category | flops | bytes accessed | tf_op | source)
XLA Modules:
  0.0 181.2 jit_solution(7276655130326694978)
XLA Ops:
  0.7 2.1 %shard_map.122 = (f32[136,512]{1,0:T(8,128)S(1)}, s32[1,512]{1,0:T(1,128)S(1)}, f32[136,128]{1,0:T(8,128)S(1)}, f32[136,128]{1,0:T(8,128)S(1)}, f32[136,128]{1,0...) custom-call(s32[3]{0:T(128)S(1)} %pad_add_fusion.place, f32[128,512]{1,0:T(8,128)} %bitcast.14, ...), custom_call_target="tpu_custom_call" | custom-call | flops 1000000 | bytes 1000000 | tf_op jit(solution)/shard_map/pallas_call | solution.py:600
  2.8 7.7 %collective-permute-start = (f32[136,128]{1,0:T(8,128)S(1)}, f32[136,128]{1,0:T(8,128)S(1)}, u32[]{:S(2)}, u32[]{:S(2)}) collective-permute-start(f32[136,128]{1,0:T(8,128)S(1)} %get-tuple-element.82), channel_id=1, source_target_pairs={{0,15},{1,2},{2,1},{3,4},{4,3},{5,6},{6,5},{7,8},{8,7},{9,10},{10,... | collective-permute-start | bytes 208904 | tf_op jit(solution)/shard_map/ppermute | solution.py:622
  10.5 1.9 %collective-permute-start.1 = (f32[136,128]{1,0:T(8,128)S(1)}, f32[136,128]{1,0:T(8,128)S(1)}, u32[]{:S(2)}, u32[]{:S(2)}) collective-permute-start(f32[136,128]{1,0:T(8,128)S(1)} %get-tuple-element.83), channel_id=1, source_target_pairs={{0,1},{1,0},{2,3},{3,2},{4,5},{5,4},{6,7},{7,6},{8,9},{9,8},{10,11... | collective-permute-start | bytes 208904 | tf_op jit(solution)/shard_map/ppermute | solution.py:622
  12.4 4.4 %collective-permute-start.2 = (f32[136,128]{1,0:T(8,128)S(1)}, f32[136,128]{1,0:T(8,128)S(1)}, u32[]{:S(2)}, u32[]{:S(2)}) collective-permute-start(f32[136,128]{1,0:T(8,128)S(1)} %get-tuple-element.84), channel_id=1, source_target_pairs={{16,32},{32,16},{48,64},{64,48},{80,96},{96,80},{112,128},{128,112... | collective-permute-start | bytes 208904 | tf_op jit(solution)/shard_map/ppermute | solution.py:628
  16.8 1.9 %collective-permute-start.3 = (f32[136,128]{1,0:T(8,128)S(1)}, f32[136,128]{1,0:T(8,128)S(1)}, u32[]{:S(2)}, u32[]{:S(2)}) collective-permute-start(f32[136,128]{1,0:T(8,128)S(1)} %get-tuple-element.85), channel_id=1, source_target_pairs={{0,16},{16,0},{32,48},{48,32},{64,80},{80,64},{96,112},{112,96},{1... | collective-permute-start | bytes 208904 | tf_op jit(solution)/shard_map/ppermute | solution.py:628
  18.8 1.7 shard_map.123
  21.7 4.4 %collective-permute-start.4 = (f32[136,128]{1,0:T(8,128)S(1)}, f32[136,128]{1,0:T(8,128)S(1)}, u32[]{:S(2)}, u32[]{:S(2)}) collective-permute-start(f32[136,128]{1,0:T(8,128)S(1)} %get-tuple-element.91), channel_id=1, source_target_pairs={{0,15},{1,2},{2,1},{3,4},{4,3},{5,6},{6,5},{7,8},{8,7},{9,10},{10,... | collective-permute-start | bytes 208904 | tf_op jit(solution)/shard_map/ppermute | solution.py:622
  26.0 1.9 %collective-permute-start.5 = (f32[136,128]{1,0:T(8,128)S(1)}, f32[136,128]{1,0:T(8,128)S(1)}, u32[]{:S(2)}, u32[]{:S(2)}) collective-permute-start(f32[136,128]{1,0:T(8,128)S(1)} %get-tuple-element.92), channel_id=1, source_target_pairs={{0,1},{1,0},{2,3},{3,2},{4,5},{5,4},{6,7},{7,6},{8,9},{9,8},{10,11... | collective-permute-start | bytes 208904 | tf_op jit(solution)/shard_map/ppermute | solution.py:622
  27.9 3.5 %collective-permute-start.6 = (f32[136,128]{1,0:T(8,128)S(1)}, f32[136,128]{1,0:T(8,128)S(1)}, u32[]{:S(2)}, u32[]{:S(2)}) collective-permute-start(f32[136,128]{1,0:T(8,128)S(1)} %get-tuple-element.93), channel_id=1, source_target_pairs={{16,32},{32,16},{48,64},{64,48},{80,96},{96,80},{112,128},{128,112... | collective-permute-start | bytes 208904 | tf_op jit(solution)/shard_map/ppermute | solution.py:628
  31.4 1.9 %collective-permute-start.7 = (f32[136,128]{1,0:T(8,128)S(1)}, f32[136,128]{1,0:T(8,128)S(1)}, u32[]{:S(2)}, u32[]{:S(2)}) collective-permute-start(f32[136,128]{1,0:T(8,128)S(1)} %get-tuple-element.94), channel_id=1, source_target_pairs={{0,16},{16,0},{32,48},{48,32},{64,80},{80,64},{96,112},{112,96},{1... | collective-permute-start | bytes 208904 | tf_op jit(solution)/shard_map/ppermute | solution.py:628
  33.4 1.5 shard_map.125
  34.9 2.1 %shard_map.126 = (f32[152,512]{1,0:T(8,128)}, f32[152,512]{1,0:T(8,128)S(1)}, f32[152,128]{1,0:T(8,128)S(1)}, f32[152,128]{1,0:T(8,128)S(1)}, f32[152,128]{1,0:T(8,128)S(1)}, /*index=5*/f32[152,128]{1,0:T(8,128)S(1)}) custom-call(s32[3]{0:T(128)S(1)} %pad_add_fusion.place, f32[136,512]{1,0:T(8,128)S(1)} %get-tuple-element.90.t, ...), custom_call_target="tpu_custom_call" | custom-call | flops 1000000 | bytes 1000000 | tf_op jit(solution)/shard_map/pallas_call | solution.py:600
  37.0 5.0 %collective-permute-start.10 = (f32[152,128]{1,0:T(8,128)S(1)}, f32[152,128]{1,0:T(8,128)S(1)}, u32[]{:S(2)}, u32[]{:S(2)}) collective-permute-start(f32[152,128]{1,0:T(8,128)S(1)} %get-tuple-element.103), channel_id=1, source_target_pairs={{0,15},{1,2},{2,1},{3,4},{4,3},{5,6},{6,5},{7,8},{8,7},{9,10},{10,... | collective-permute-start | bytes 233480 | tf_op jit(solution)/shard_map/ppermute | solution.py:622
  42.0 1.9 %collective-permute-start.11 = (f32[152,128]{1,0:T(8,128)S(1)}, f32[152,128]{1,0:T(8,128)S(1)}, u32[]{:S(2)}, u32[]{:S(2)}) collective-permute-start(f32[152,128]{1,0:T(8,128)S(1)} %get-tuple-element.104), channel_id=1, source_target_pairs={{0,1},{1,0},{2,3},{3,2},{4,5},{5,4},{6,7},{7,6},{8,9},{9,8},{10,11... | collective-permute-start | bytes 233480 | tf_op jit(solution)/shard_map/ppermute | solution.py:622
  44.0 4.2 %collective-permute-start.8 = (f32[152,128]{1,0:T(8,128)S(1)}, f32[152,128]{1,0:T(8,128)S(1)}, u32[]{:S(2)}, u32[]{:S(2)}) collective-permute-start(f32[152,128]{1,0:T(8,128)S(1)} %get-tuple-element.101), channel_id=1, source_target_pairs={{16,32},{32,16},{48,64},{64,48},{80,96},{96,80},{112,128},{128,112... | collective-permute-start | bytes 233480 | tf_op jit(solution)/shard_map/ppermute | solution.py:628
  48.2 1.9 %collective-permute-start.9 = (f32[152,128]{1,0:T(8,128)S(1)}, f32[152,128]{1,0:T(8,128)S(1)}, u32[]{:S(2)}, u32[]{:S(2)}) collective-permute-start(f32[152,128]{1,0:T(8,128)S(1)} %get-tuple-element.102), channel_id=1, source_target_pairs={{0,16},{16,0},{32,48},{48,32},{64,80},{80,64},{96,112},{112,96},{1... | collective-permute-start | bytes 233480 | tf_op jit(solution)/shard_map/ppermute | solution.py:628
  51.3 1.3 shard_map.127
  52.6 3.6 %collective-permute-start.12 = (f32[168,128]{1,0:T(8,128)S(1)}, f32[168,128]{1,0:T(8,128)S(1)}, u32[]{:S(2)}, u32[]{:S(2)}) collective-permute-start(f32[168,128]{1,0:T(8,128)S(1)} %get-tuple-element.107), channel_id=1, source_target_pairs={{0,15},{1,2},{2,1},{3,4},{4,3},{5,6},{6,5},{7,8},{8,7},{9,10},{10,... | collective-permute-start | bytes 258056 | tf_op jit(solution)/shard_map/ppermute | solution.py:622
  56.3 1.9 %collective-permute-start.13 = (f32[168,128]{1,0:T(8,128)S(1)}, f32[168,128]{1,0:T(8,128)S(1)}, u32[]{:S(2)}, u32[]{:S(2)}) collective-permute-start(f32[168,128]{1,0:T(8,128)S(1)} %get-tuple-element.108), channel_id=1, source_target_pairs={{0,1},{1,0},{2,3},{3,2},{4,5},{5,4},{6,7},{7,6},{8,9},{9,8},{10,11... | collective-permute-start | bytes 258056 | tf_op jit(solution)/shard_map/ppermute | solution.py:622
  58.2 5.1 %collective-permute-start.14 = (f32[168,128]{1,0:T(8,128)S(1)}, f32[168,128]{1,0:T(8,128)S(1)}, u32[]{:S(2)}, u32[]{:S(2)}) collective-permute-start(f32[168,128]{1,0:T(8,128)S(1)} %get-tuple-element.109), channel_id=1, source_target_pairs={{16,32},{32,16},{48,64},{64,48},{80,96},{96,80},{112,128},{128,112... | collective-permute-start | bytes 258056 | tf_op jit(solution)/shard_map/ppermute | solution.py:628
  63.3 1.9 %collective-permute-start.15 = (f32[168,128]{1,0:T(8,128)S(1)}, f32[168,128]{1,0:T(8,128)S(1)}, u32[]{:S(2)}, u32[]{:S(2)}) collective-permute-start(f32[168,128]{1,0:T(8,128)S(1)} %get-tuple-element.110), channel_id=1, source_target_pairs={{0,16},{16,0},{32,48},{48,32},{64,80},{80,64},{96,112},{112,96},{1... | collective-permute-start | bytes 258056 | tf_op jit(solution)/shard_map/ppermute | solution.py:628
  66.4 2.2 %shard_map.128 = (f32[184,512]{1,0:T(8,128)}, f32[184,512]{1,0:T(8,128)S(1)}, f32[184,128]{1,0:T(8,128)S(1)}, f32[184,128]{1,0:T(8,128)S(1)}, f32[184,128]{1,0:T(8,128)S(1)}, /*index=5*/f32[184,128]{1,0:T(8,128)S(1)}) custom-call(s32[3]{0:T(128)S(1)} %pad_add_fusion.place, f32[168,512]{1,0:T(8,128)S(1)} %get-tuple-element.106.t, ...), custom_call_target="tpu_custom_call" | custom-call | flops 1000000 | bytes 1000000 | tf_op jit(solution)/shard_map/pallas_call | solution.py:600
  68.7 5.0 %collective-permute-start.16 = (f32[184,128]{1,0:T(8,128)S(1)}, f32[184,128]{1,0:T(8,128)S(1)}, u32[]{:S(2)}, u32[]{:S(2)}) collective-permute-start(f32[184,128]{1,0:T(8,128)S(1)} %get-tuple-element.112), channel_id=1, source_target_pairs={{0,15},{1,2},{2,1},{3,4},{4,3},{5,6},{6,5},{7,8},{8,7},{9,10},{10,... | collective-permute-start | bytes 282632 | tf_op jit(solution)/shard_map/ppermute | solution.py:622
  73.7 1.9 %collective-permute-start.17 = (f32[184,128]{1,0:T(8,128)S(1)}, f32[184,128]{1,0:T(8,128)S(1)}, u32[]{:S(2)}, u32[]{:S(2)}) collective-permute-start(f32[184,128]{1,0:T(8,128)S(1)} %get-tuple-element.113), channel_id=1, source_target_pairs={{0,1},{1,0},{2,3},{3,2},{4,5},{5,4},{6,7},{7,6},{8,9},{9,8},{10,11... | collective-permute-start | bytes 282632 | tf_op jit(solution)/shard_map/ppermute | solution.py:622
  75.6 3.9 %collective-permute-start.18 = (f32[184,128]{1,0:T(8,128)S(1)}, f32[184,128]{1,0:T(8,128)S(1)}, u32[]{:S(2)}, u32[]{:S(2)}) collective-permute-start(f32[184,128]{1,0:T(8,128)S(1)} %get-tuple-element.114), channel_id=1, source_target_pairs={{16,32},{32,16},{48,64},{64,48},{80,96},{96,80},{112,128},{128,112... | collective-permute-start | bytes 282632 | tf_op jit(solution)/shard_map/ppermute | solution.py:628
  79.5 1.9 %collective-permute-start.19 = (f32[184,128]{1,0:T(8,128)S(1)}, f32[184,128]{1,0:T(8,128)S(1)}, u32[]{:S(2)}, u32[]{:S(2)}) collective-permute-start(f32[184,128]{1,0:T(8,128)S(1)} %get-tuple-element.115), channel_id=1, source_target_pairs={{0,16},{16,0},{32,48},{48,32},{64,80},{80,64},{96,112},{112,96},{1... | collective-permute-start | bytes 282632 | tf_op jit(solution)/shard_map/ppermute | solution.py:628
  82.7 2.4 %shard_map.129 = (f32[200,512]{1,0:T(8,128)}, f32[16,32,128]{2,1,0:T(8,128)}) custom-call(s32[3]{0:T(128)S(1)} %pad_add_fusion.place, f32[184,512]{1,0:T(8,128)S(1)} %get-tuple-element.111.q, f32[184,128]{1,0:T(8,128)S(1)} %collective-permute-done.16.g0, f32[184,128]{1,0:T(8,128)S(1)} %collective-permute-done.17.g1, ...), custom_call_target="tpu_custom_call" | custom-call | flops 1000000 | bytes 1000000 | tf_op jit(solution)/shard_map/pallas_call | solution.py:600
  85.1 4.8 %all-to-all-start = ((f32[16,32,128]{2,1,0:T(8,128)}), f32[16,32,128]{2,1,0:T(8,128)S(1)}, u32[]{:S(2)}, u32[]{:S(2)}) async-start(f32[16,32,128]{2,1,0:T(8,128)} %get-tuple-element.119), calls=%async_computation | async-start | bytes 524288 | tf_op jit(solution)/shard_map/all_to_all | solution.py:636
  89.8 2.9 %shard_map.130 = (f32[200,512]{1,0:T(8,128)}, f32[200,128]{1,0:T(8,128)S(1)}, f32[200,128]{1,0:T(8,128)S(1)}, f32[200,128]{1,0:T(8,128)S(1)}, f32[200,128]{1,0:T(8,128)S(1)}) custom-call(s32[3]{0:T(128)S(1)} %pad_add_fusion.place, f32[200,512]{1,0:T(8,128)} %get-tuple-element.120.v2, f32[1,512]{1,0:T(1,128)S(1)} %get-tuple-element.95.after.share, ...), custom_call_target="tpu_custom_call" | custom-call | flops 500000000 | bytes 1000000 | tf_op jit(solution)/shard_map/pallas_call | solution.py:600
  94.0 4.1 %all-to-all-done.got = f32[16,32,128]{2,1,0:T(8,128)S(1)} async-done(((f32[16,32,128]{2,1,0:T(8,128)}), f32[16,32,128]{2,1,0:T(8,128)S(1)}, u32[]{:S(2)}, u32[]{:S(2)}) %all-to-all-start) | async-done | bytes 262176 | tf_op jit(solution)/shard_map/all_to_all | solution.py:636
  98.9 11.6 %all-to-all-start.1 = ((f32[16,32,128]{2,1,0:T(8,128)}), f32[16,32,128]{2,1,0:T(8,128)S(1)}, u32[]{:S(2)}, u32[]{:S(2)}) async-start(f32[16,32,128]{2,1,0:T(8,128)} %shard_map.131), calls=%async_computation.1 | async-start | bytes 524288 | tf_op jit(solution)/shard_map/all_to_all | solution.py:636
  110.5 2.8 %collective-permute-start.20 = (f32[200,128]{1,0:T(8,128)S(1)}, f32[200,128]{1,0:T(8,128)S(1)}, u32[]{:S(2)}, u32[]{:S(2)}) collective-permute-start(f32[200,128]{1,0:T(8,128)S(1)} %copy-done.6), channel_id=1, source_target_pairs={{0,15},{1,2},{2,1},{3,4},{4,3},{5,6},{6,5},{7,8},{8,7},{9,10},{10,... | collective-permute-start | bytes 307208 | tf_op jit(solution)/shard_map/ppermute | solution.py:622
  113.3 1.9 %collective-permute-start.21 = (f32[200,128]{1,0:T(8,128)S(1)}, f32[200,128]{1,0:T(8,128)S(1)}, u32[]{:S(2)}, u32[]{:S(2)}) collective-permute-start(f32[200,128]{1,0:T(8,128)S(1)} %copy-done.4), channel_id=1, source_target_pairs={{0,1},{1,0},{2,3},{3,2},{4,5},{5,4},{6,7},{7,6},{8,9},{9,8},{10,11... | collective-permute-start | bytes 307208 | tf_op jit(solution)/shard_map/ppermute | solution.py:622
  115.2 6.6 %collective-permute-start.22 = (f32[200,128]{1,0:T(8,128)S(1)}, f32[200,128]{1,0:T(8,128)S(1)}, u32[]{:S(2)}, u32[]{:S(2)}) collective-permute-start(f32[200,128]{1,0:T(8,128)S(1)} %get-tuple-element.131), channel_id=1, source_target_pairs={{16,32},{32,16},{48,64},{64,48},{80,96},{96,80},{112,128},{128,112... | collective-permute-start | bytes 307208 | tf_op jit(solution)/shard_map/ppermute | solution.py:628
  121.8 1.9 %collective-permute-start.23 = (f32[200,128]{1,0:T(8,128)S(1)}, f32[200,128]{1,0:T(8,128)S(1)}, u32[]{:S(2)}, u32[]{:S(2)}) collective-permute-start(f32[200,128]{1,0:T(8,128)S(1)} %get-tuple-element.132), channel_id=1, source_target_pairs={{0,16},{16,0},{32,48},{48,32},{64,80},{80,64},{96,112},{112,96},{1... | collective-permute-start | bytes 307208 | tf_op jit(solution)/shard_map/ppermute | solution.py:628
  123.8 1.9 %collective-permute-done.22.g2 = f32[200,128]{1,0:T(8,128)S(1)} collective-permute-done((f32[200,128]{1,0:T(8,128)S(1)}, f32[200,128]{1,0:T(8,128)S(1)}, u32[]{:S(2)}, u32[]{:S(2)}) %collective-permute-start.22) | collective-permute-done | bytes 102432 | tf_op jit(solution)/shard_map/ppermute | solution.py:628
  125.7 6.5 %collective-permute-start.24 = (f32[16,32,128]{2,1,0:T(8,128)S(1)}, f32[16,32,128]{2,1,0:T(8,128)S(1)}, u32[]{:S(2)}, u32[]{:S(2)}) collective-permute-start(f32[16,32,128]{2,1,0:T(8,128)S(1)} %all-to-all-done.1.mine), channel_id=1, source_target_pairs={{0,16},{16,0},{32,48},{48,32},{64,80},{80,64},{96,112},{112,96},{1... | collective-permute-start | bytes 786440 | tf_op jit(solution)/shard_map/ppermute | solution.py:745
  132.3 1.1 collective-permute-done.24.other
  133.4 6.0 %shard_map.132 = (f32[128,512]{1,0:T(8,128)}, f32[128,512]{1,0:T(8,128)}, f32[128,512]{1,0:T(8,128)}, f32[128,512]{1,0:T(8,128)}, f32[128,512]{1,0:T(8,128)}, /*...) custom-call(s32[3]{0:T(128)S(1)} %pad_add_fusion.place, ...), custom_call_target="tpu_custom_call" | custom-call | flops 1000000 | bytes 1000000 | tf_op jit(solution)/shard_map/pallas_call | solution.py:600
  139.4 4.1 %all-to-all-start.2 = ((f32[32,1,1152]{2,1,0:T(1,128)}), f32[32,1,1152]{2,1,0:T(1,128)S(1)}, u32[]{:S(2)}, u32[]{:S(2)}) async-start(f32[32,1,1152]{2,1,0:T(1,128)} %get-tuple-element.141), calls=%async_computation.2 | async-start | bytes 294912 | tf_op jit(solution)/shard_map/all_to_all | solution.py:636
  143.5 6.8 %collective-permute-start.25 = (f32[128,128]{1,0:T(8,128)S(1)}, f32[128,128]{1,0:T(8,128)S(1)}, u32[]{:S(2)}, u32[]{:S(2)}) collective-permute-start(f32[128,128]{1,0:T(8,128)S(1)} %get-tuple-element.142), channel_id=1, source_target_pairs={{0,15},{1,2},{2,1},{3,4},{4,3},{5,6},{6,5},{7,8},{8,7},{9,10},{10,... | collective-permute-start | bytes 196616 | tf_op jit(solution)/shard_map/ppermute | solution.py:622
  150.3 1.9 %collective-permute-start.26 = (f32[128,128]{1,0:T(8,128)S(1)}, f32[128,128]{1,0:T(8,128)S(1)}, u32[]{:S(2)}, u32[]{:S(2)}) collective-permute-start(f32[128,128]{1,0:T(8,128)S(1)} %get-tuple-element.143), channel_id=1, source_target_pairs={{0,1},{1,0},{2,3},{3,2},{4,5},{5,4},{6,7},{7,6},{8,9},{9,8},{10,11... | collective-permute-start | bytes 196616 | tf_op jit(solution)/shard_map/ppermute | solution.py:622
  152.3 3.1 %collective-permute-done.26.g1 = f32[128,128]{1,0:T(8,128)S(1)} collective-permute-done((f32[128,128]{1,0:T(8,128)S(1)}, f32[128,128]{1,0:T(8,128)S(1)}, u32[]{:S(2)}, u32[]{:S(2)}) %collective-permute-start.26) | collective-permute-done | bytes 65568 | tf_op jit(solution)/shard_map/ppermute | solution.py:622
  156.0 10.3 %all-to-all-start.3 = ((f32[16,1,1152]{2,1,0:T(1,128)}), f32[16,1,1152]{2,1,0:T(1,128)S(1)}, u32[]{:S(2)}, u32[]{:S(2)}) async-start(f32[16,1,1152]{2,1,0:T(1,128)} %shard_map.133), calls=%async_computation.3 | async-start | bytes 147456 | tf_op jit(solution)/shard_map/all_to_all | solution.py:636
  166.3 5.4 %collective-permute-start.27 = (f32[128,128]{1,0:T(8,128)S(1)}, f32[128,128]{1,0:T(8,128)S(1)}, u32[]{:S(2)}, u32[]{:S(2)}) collective-permute-start(f32[128,128]{1,0:T(8,128)S(1)} %get-tuple-element.151), channel_id=1, source_target_pairs={{16,32},{32,16},{48,64},{64,48},{80,96},{96,80},{112,128},{128,112... | collective-permute-start | bytes 196616 | tf_op jit(solution)/shard_map/ppermute | solution.py:628
  171.8 1.9 %collective-permute-start.28 = (f32[128,128]{1,0:T(8,128)S(1)}, f32[128,128]{1,0:T(8,128)S(1)}, u32[]{:S(2)}, u32[]{:S(2)}) collective-permute-start(f32[128,128]{1,0:T(8,128)S(1)} %get-tuple-element.152), channel_id=1, source_target_pairs={{0,16},{16,0},{32,48},{48,32},{64,80},{80,64},{96,112},{112,96},{1... | collective-permute-start | bytes 196616 | tf_op jit(solution)/shard_map/ppermute | solution.py:628
  174.9 3.1 %all-to-all-done.3.got = f32[16,1,1152]{2,1,0:T(1,128)S(1)} async-done(((f32[16,1,1152]{2,1,0:T(1,128)}), f32[16,1,1152]{2,1,0:T(1,128)S(1)}, u32[]{:S(2)}, u32[]{:S(2)}) %all-to-all-start.3) | async-done | bytes 73760 | tf_op jit(solution)/shard_map/all_to_all | solution.py:636
  178.0 3.2 %shard_map.134 = (f32[128,512]{1,0:T(8,128)}, f32[128,512]{1,0:T(8,128)}) custom-call(s32[3]{0:T(128)S(1)} %pad_add_fusion.place, f32[16,1,1152]{2,1,0:T(1,128)S(1)} %all-to-all-done.3.got, f32[128,512]{1,0:T(8,128)S(1)} %get-tuple-element.148.q, f32[128,128]{1,0:T(8,128)S(1)} %collective-permute-done.25.g0, f32[128,128]{1,0:T(8,128)S(1)} %collective-permute-done.26.g1, ...), custom_call_target="tpu_custom_call" | custom-call | flops 1000000 | bytes 1000000 | tf_op jit(solution)/shard_map/pallas_call | solution.py:600
  (47 shorter events, 8.9 us)
Async XLA Ops:
  2.8 17.7 %collective-permute-start = (f32[136,128]{1,0:T(8,128)S(1)}, f32[136,128]{1,0:T(8,128)S(1)}, u32[]{:S(2)}, u32[]{:S(2)}) collective-permute-start(f32[136,128]{1,0:T(8,128)S(1)} %get-tuple-element.82), channel_id=1, source_target_pairs={{0,15},{1,2},{2,1},{3,4},{4,3},{5,6},{6,5},{7,8},{8,7},{9,10},{10,... | collective-permute-start | bytes 208904 | tf_op jit(solution)/shard_map/ppermute | solution.py:622
  10.5 10.0 %collective-permute-start.1 = (f32[136,128]{1,0:T(8,128)S(1)}, f32[136,128]{1,0:T(8,128)S(1)}, u32[]{:S(2)}, u32[]{:S(2)}) collective-permute-start(f32[136,128]{1,0:T(8,128)S(1)} %get-tuple-element.83), channel_id=1, source_target_pairs={{0,1},{1,0},{2,3},{3,2},{4,5},{5,4},{6,7},{7,6},{8,9},{9,8},{10,11... | collective-permute-start | bytes 208904 | tf_op jit(solution)/shard_map/ppermute | solution.py:622
  12.4 8.1 %collective-permute-start.2 = (f32[136,128]{1,0:T(8,128)S(1)}, f32[136,128]{1,0:T(8,128)S(1)}, u32[]{:S(2)}, u32[]{:S(2)}) collective-permute-start(f32[136,128]{1,0:T(8,128)S(1)} %get-tuple-element.84), channel_id=1, source_target_pairs={{16,32},{32,16},{48,64},{64,48},{80,96},{96,80},{112,128},{128,112... | collective-permute-start | bytes 208904 | tf_op jit(solution)/shard_map/ppermute | solution.py:628
  16.8 3.7 %collective-permute-start.3 = (f32[136,128]{1,0:T(8,128)S(1)}, f32[136,128]{1,0:T(8,128)S(1)}, u32[]{:S(2)}, u32[]{:S(2)}) collective-permute-start(f32[136,128]{1,0:T(8,128)S(1)} %get-tuple-element.85), channel_id=1, source_target_pairs={{0,16},{16,0},{32,48},{48,32},{64,80},{80,64},{96,112},{112,96},{1... | collective-permute-start | bytes 208904 | tf_op jit(solution)/shard_map/ppermute | solution.py:628
  21.7 13.2 %collective-permute-start.4 = (f32[136,128]{1,0:T(8,128)S(1)}, f32[136,128]{1,0:T(8,128)S(1)}, u32[]{:S(2)}, u32[]{:S(2)}) collective-permute-start(f32[136,128]{1,0:T(8,128)S(1)} %get-tuple-element.91), channel_id=1, source_target_pairs={{0,15},{1,2},{2,1},{3,4},{4,3},{5,6},{6,5},{7,8},{8,7},{9,10},{10,... | collective-permute-start | bytes 208904 | tf_op jit(solution)/shard_map/ppermute | solution.py:622
  26.0 8.8 %collective-permute-start.5 = (f32[136,128]{1,0:T(8,128)S(1)}, f32[136,128]{1,0:T(8,128)S(1)}, u32[]{:S(2)}, u32[]{:S(2)}) collective-permute-start(f32[136,128]{1,0:T(8,128)S(1)} %get-tuple-element.92), channel_id=1, source_target_pairs={{0,1},{1,0},{2,3},{3,2},{4,5},{5,4},{6,7},{7,6},{8,9},{9,8},{10,11... | collective-permute-start | bytes 208904 | tf_op jit(solution)/shard_map/ppermute | solution.py:622
  27.9 6.9 %collective-permute-start.6 = (f32[136,128]{1,0:T(8,128)S(1)}, f32[136,128]{1,0:T(8,128)S(1)}, u32[]{:S(2)}, u32[]{:S(2)}) collective-permute-start(f32[136,128]{1,0:T(8,128)S(1)} %get-tuple-element.93), channel_id=1, source_target_pairs={{16,32},{32,16},{48,64},{64,48},{80,96},{96,80},{112,128},{128,112... | collective-permute-start | bytes 208904 | tf_op jit(solution)/shard_map/ppermute | solution.py:628
  31.4 3.4 %collective-permute-start.7 = (f32[136,128]{1,0:T(8,128)S(1)}, f32[136,128]{1,0:T(8,128)S(1)}, u32[]{:S(2)}, u32[]{:S(2)}) collective-permute-start(f32[136,128]{1,0:T(8,128)S(1)} %get-tuple-element.94), channel_id=1, source_target_pairs={{0,16},{16,0},{32,48},{48,32},{64,80},{80,64},{96,112},{112,96},{1... | collective-permute-start | bytes 208904 | tf_op jit(solution)/shard_map/ppermute | solution.py:628
  37.0 13.1 %collective-permute-start.10 = (f32[152,128]{1,0:T(8,128)S(1)}, f32[152,128]{1,0:T(8,128)S(1)}, u32[]{:S(2)}, u32[]{:S(2)}) collective-permute-start(f32[152,128]{1,0:T(8,128)S(1)} %get-tuple-element.103), channel_id=1, source_target_pairs={{0,15},{1,2},{2,1},{3,4},{4,3},{5,6},{6,5},{7,8},{8,7},{9,10},{10,... | collective-permute-start | bytes 233480 | tf_op jit(solution)/shard_map/ppermute | solution.py:622
  42.0 8.1 %collective-permute-start.11 = (f32[152,128]{1,0:T(8,128)S(1)}, f32[152,128]{1,0:T(8,128)S(1)}, u32[]{:S(2)}, u32[]{:S(2)}) collective-permute-start(f32[152,128]{1,0:T(8,128)S(1)} %get-tuple-element.104), channel_id=1, source_target_pairs={{0,1},{1,0},{2,3},{3,2},{4,5},{5,4},{6,7},{7,6},{8,9},{9,8},{10,11... | collective-permute-start | bytes 233480 | tf_op jit(solution)/shard_map/ppermute | solution.py:622
  44.0 6.3 %collective-permute-start.8 = (f32[152,128]{1,0:T(8,128)S(1)}, f32[152,128]{1,0:T(8,128)S(1)}, u32[]{:S(2)}, u32[]{:S(2)}) collective-permute-start(f32[152,128]{1,0:T(8,128)S(1)} %get-tuple-element.101), channel_id=1, source_target_pairs={{16,32},{32,16},{48,64},{64,48},{80,96},{96,80},{112,128},{128,112... | collective-permute-start | bytes 233480 | tf_op jit(solution)/shard_map/ppermute | solution.py:628
  48.2 3.2 %collective-permute-start.9 = (f32[152,128]{1,0:T(8,128)S(1)}, f32[152,128]{1,0:T(8,128)S(1)}, u32[]{:S(2)}, u32[]{:S(2)}) collective-permute-start(f32[152,128]{1,0:T(8,128)S(1)} %get-tuple-element.102), channel_id=1, source_target_pairs={{0,16},{16,0},{32,48},{48,32},{64,80},{80,64},{96,112},{112,96},{1... | collective-permute-start | bytes 233480 | tf_op jit(solution)/shard_map/ppermute | solution.py:628
  52.6 12.6 %collective-permute-start.12 = (f32[168,128]{1,0:T(8,128)S(1)}, f32[168,128]{1,0:T(8,128)S(1)}, u32[]{:S(2)}, u32[]{:S(2)}) collective-permute-start(f32[168,128]{1,0:T(8,128)S(1)} %get-tuple-element.107), channel_id=1, source_target_pairs={{0,15},{1,2},{2,1},{3,4},{4,3},{5,6},{6,5},{7,8},{8,7},{9,10},{10,... | collective-permute-start | bytes 258056 | tf_op jit(solution)/shard_map/ppermute | solution.py:622
  56.3 8.9 %collective-permute-start.13 = (f32[168,128]{1,0:T(8,128)S(1)}, f32[168,128]{1,0:T(8,128)S(1)}, u32[]{:S(2)}, u32[]{:S(2)}) collective-permute-start(f32[168,128]{1,0:T(8,128)S(1)} %get-tuple-element.108), channel_id=1, source_target_pairs={{0,1},{1,0},{2,3},{3,2},{4,5},{5,4},{6,7},{7,6},{8,9},{9,8},{10,11... | collective-permute-start | bytes 258056 | tf_op jit(solution)/shard_map/ppermute | solution.py:622
  58.2 7.2 %collective-permute-start.14 = (f32[168,128]{1,0:T(8,128)S(1)}, f32[168,128]{1,0:T(8,128)S(1)}, u32[]{:S(2)}, u32[]{:S(2)}) collective-permute-start(f32[168,128]{1,0:T(8,128)S(1)} %get-tuple-element.109), channel_id=1, source_target_pairs={{16,32},{32,16},{48,64},{64,48},{80,96},{96,80},{112,128},{128,112... | collective-permute-start | bytes 258056 | tf_op jit(solution)/shard_map/ppermute | solution.py:628
  63.3 3.2 %collective-permute-start.15 = (f32[168,128]{1,0:T(8,128)S(1)}, f32[168,128]{1,0:T(8,128)S(1)}, u32[]{:S(2)}, u32[]{:S(2)}) collective-permute-start(f32[168,128]{1,0:T(8,128)S(1)} %get-tuple-element.110), channel_id=1, source_target_pairs={{0,16},{16,0},{32,48},{48,32},{64,80},{80,64},{96,112},{112,96},{1... | collective-permute-start | bytes 258056 | tf_op jit(solution)/shard_map/ppermute | solution.py:628
  68.7 12.7 %collective-permute-start.16 = (f32[184,128]{1,0:T(8,128)S(1)}, f32[184,128]{1,0:T(8,128)S(1)}, u32[]{:S(2)}, u32[]{:S(2)}) collective-permute-start(f32[184,128]{1,0:T(8,128)S(1)} %get-tuple-element.112), channel_id=1, source_target_pairs={{0,15},{1,2},{2,1},{3,4},{4,3},{5,6},{6,5},{7,8},{8,7},{9,10},{10,... | collective-permute-start | bytes 282632 | tf_op jit(solution)/shard_map/ppermute | solution.py:622
  73.7 7.8 %collective-permute-start.17 = (f32[184,128]{1,0:T(8,128)S(1)}, f32[184,128]{1,0:T(8,128)S(1)}, u32[]{:S(2)}, u32[]{:S(2)}) collective-permute-start(f32[184,128]{1,0:T(8,128)S(1)} %get-tuple-element.113), channel_id=1, source_target_pairs={{0,1},{1,0},{2,3},{3,2},{4,5},{5,4},{6,7},{7,6},{8,9},{9,8},{10,11... | collective-permute-start | bytes 282632 | tf_op jit(solution)/shard_map/ppermute | solution.py:622
  75.6 6.1 %collective-permute-start.18 = (f32[184,128]{1,0:T(8,128)S(1)}, f32[184,128]{1,0:T(8,128)S(1)}, u32[]{:S(2)}, u32[]{:S(2)}) collective-permute-start(f32[184,128]{1,0:T(8,128)S(1)} %get-tuple-element.114), channel_id=1, source_target_pairs={{16,32},{32,16},{48,64},{64,48},{80,96},{96,80},{112,128},{128,112... | collective-permute-start | bytes 282632 | tf_op jit(solution)/shard_map/ppermute | solution.py:628
  79.5 3.2 %collective-permute-start.19 = (f32[184,128]{1,0:T(8,128)S(1)}, f32[184,128]{1,0:T(8,128)S(1)}, u32[]{:S(2)}, u32[]{:S(2)}) collective-permute-start(f32[184,128]{1,0:T(8,128)S(1)} %get-tuple-element.115), channel_id=1, source_target_pairs={{0,16},{16,0},{32,48},{48,32},{64,80},{80,64},{96,112},{112,96},{1... | collective-permute-start | bytes 282632 | tf_op jit(solution)/shard_map/ppermute | solution.py:628
  85.1 13.1 %all-to-all-start = ((f32[16,32,128]{2,1,0:T(8,128)}), f32[16,32,128]{2,1,0:T(8,128)S(1)}, u32[]{:S(2)}, u32[]{:S(2)}) async-start(f32[16,32,128]{2,1,0:T(8,128)} %get-tuple-element.119), calls=%async_computation | async-start | bytes 524288 | tf_op jit(solution)/shard_map/all_to_all | solution.py:636
  92.8 0.6 copy-start.3
  93.4 0.6 copy-start.5
  98.9 34.5 %copy-start = (f32[152,512]{1,0:T(8,128)S(1)}, f32[152,512]{1,0:T(8,128)}, u32[]{:S(2)}) copy-start(f32[152,512]{1,0:T(8,128)} %get-tuple-element.139.z0) | copy-start | bytes 933892
  98.9 11.6 %copy-start.6 = (f32[200,128]{1,0:T(8,128)S(1)}, f32[200,128]{1,0:T(8,128)}, u32[]{:S(2)}) copy-start(f32[200,128]{1,0:T(8,128)} %copy-done.5) | copy-start | bytes 307204
  98.9 14.4 %copy-start.4 = (f32[200,128]{1,0:T(8,128)S(1)}, f32[200,128]{1,0:T(8,128)}, u32[]{:S(2)}) copy-start(f32[200,128]{1,0:T(8,128)} %copy-done.3) | copy-start | bytes 307204
  98.9 26.8 %all-to-all-start.1 = ((f32[16,32,128]{2,1,0:T(8,128)}), f32[16,32,128]{2,1,0:T(8,128)S(1)}, u32[]{:S(2)}, u32[]{:S(2)}) async-start(f32[16,32,128]{2,1,0:T(8,128)} %shard_map.131), calls=%async_computation.1 | async-start | bytes 524288 | tf_op jit(solution)/shard_map/all_to_all | solution.py:636
  110.5 13.2 %collective-permute-start.20 = (f32[200,128]{1,0:T(8,128)S(1)}, f32[200,128]{1,0:T(8,128)S(1)}, u32[]{:S(2)}, u32[]{:S(2)}) collective-permute-start(f32[200,128]{1,0:T(8,128)S(1)} %copy-done.6), channel_id=1, source_target_pairs={{0,15},{1,2},{2,1},{3,4},{4,3},{5,6},{6,5},{7,8},{8,7},{9,10},{10,... | collective-permute-start | bytes 307208 | tf_op jit(solution)/shard_map/ppermute | solution.py:622
  113.3 10.4 %collective-permute-start.21 = (f32[200,128]{1,0:T(8,128)S(1)}, f32[200,128]{1,0:T(8,128)S(1)}, u32[]{:S(2)}, u32[]{:S(2)}) collective-permute-start(f32[200,128]{1,0:T(8,128)S(1)} %copy-done.4), channel_id=1, source_target_pairs={{0,1},{1,0},{2,3},{3,2},{4,5},{5,4},{6,7},{7,6},{8,9},{9,8},{10,11... | collective-permute-start | bytes 307208 | tf_op jit(solution)/shard_map/ppermute | solution.py:622
  115.2 10.4 %collective-permute-start.22 = (f32[200,128]{1,0:T(8,128)S(1)}, f32[200,128]{1,0:T(8,128)S(1)}, u32[]{:S(2)}, u32[]{:S(2)}) collective-permute-start(f32[200,128]{1,0:T(8,128)S(1)} %get-tuple-element.131), channel_id=1, source_target_pairs={{16,32},{32,16},{48,64},{64,48},{80,96},{96,80},{112,128},{128,112... | collective-permute-start | bytes 307208 | tf_op jit(solution)/shard_map/ppermute | solution.py:628
  121.8 3.9 %collective-permute-start.23 = (f32[200,128]{1,0:T(8,128)S(1)}, f32[200,128]{1,0:T(8,128)S(1)}, u32[]{:S(2)}, u32[]{:S(2)}) collective-permute-start(f32[200,128]{1,0:T(8,128)S(1)} %get-tuple-element.132), channel_id=1, source_target_pairs={{0,16},{16,0},{32,48},{48,32},{64,80},{80,64},{96,112},{112,96},{1... | collective-permute-start | bytes 307208 | tf_op jit(solution)/shard_map/ppermute | solution.py:628
  125.7 7.7 %collective-permute-start.24 = (f32[16,32,128]{2,1,0:T(8,128)S(1)}, f32[16,32,128]{2,1,0:T(8,128)S(1)}, u32[]{:S(2)}, u32[]{:S(2)}) collective-permute-start(f32[16,32,128]{2,1,0:T(8,128)S(1)} %all-to-all-done.1.mine), channel_id=1, source_target_pairs={{0,16},{16,0},{32,48},{48,32},{64,80},{80,64},{96,112},{112,96},{1... | collective-permute-start | bytes 786440 | tf_op jit(solution)/shard_map/ppermute | solution.py:745
  139.4 38.7 %copy-start.2 = (f32[128,512]{1,0:T(8,128)S(1)}, f32[128,512]{1,0:T(8,128)}, u32[]{:S(2)}) copy-start(f32[128,512]{1,0:T(8,128)} %get-tuple-element.154.z1) | copy-start | bytes 786436
  139.4 16.0 %all-to-all-start.2 = ((f32[32,1,1152]{2,1,0:T(1,128)}), f32[32,1,1152]{2,1,0:T(1,128)S(1)}, u32[]{:S(2)}, u32[]{:S(2)}) async-start(f32[32,1,1152]{2,1,0:T(1,128)} %get-tuple-element.141), calls=%async_computation.2 | async-start | bytes 294912 | tf_op jit(solution)/shard_map/all_to_all | solution.py:636
  143.5 34.5 %copy-start.1 = (f32[128,512]{1,0:T(8,128)S(1)}, f32[128,512]{1,0:T(8,128)}, u32[]{:S(2)}) copy-start(f32[128,512]{1,0:T(8,128)} %get-tuple-element.153.z0) | copy-start | bytes 786436
  143.5 8.8 %collective-permute-start.25 = (f32[128,128]{1,0:T(8,128)S(1)}, f32[128,128]{1,0:T(8,128)S(1)}, u32[]{:S(2)}, u32[]{:S(2)}) collective-permute-start(f32[128,128]{1,0:T(8,128)S(1)} %get-tuple-element.142), channel_id=1, source_target_pairs={{0,15},{1,2},{2,1},{3,4},{4,3},{5,6},{6,5},{7,8},{8,7},{9,10},{10,... | collective-permute-start | bytes 196616 | tf_op jit(solution)/shard_map/ppermute | solution.py:622
  150.3 5.0 %collective-permute-start.26 = (f32[128,128]{1,0:T(8,128)S(1)}, f32[128,128]{1,0:T(8,128)S(1)}, u32[]{:S(2)}, u32[]{:S(2)}) collective-permute-start(f32[128,128]{1,0:T(8,128)S(1)} %get-tuple-element.143), channel_id=1, source_target_pairs={{0,1},{1,0},{2,3},{3,2},{4,5},{5,4},{6,7},{7,6},{8,9},{9,8},{10,11... | collective-permute-start | bytes 196616 | tf_op jit(solution)/shard_map/ppermute | solution.py:622
  156.0 22.0 %all-to-all-start.3 = ((f32[16,1,1152]{2,1,0:T(1,128)}), f32[16,1,1152]{2,1,0:T(1,128)S(1)}, u32[]{:S(2)}, u32[]{:S(2)}) async-start(f32[16,1,1152]{2,1,0:T(1,128)} %shard_map.133), calls=%async_computation.3 | async-start | bytes 147456 | tf_op jit(solution)/shard_map/all_to_all | solution.py:636
  166.3 8.2 %collective-permute-start.27 = (f32[128,128]{1,0:T(8,128)S(1)}, f32[128,128]{1,0:T(8,128)S(1)}, u32[]{:S(2)}, u32[]{:S(2)}) collective-permute-start(f32[128,128]{1,0:T(8,128)S(1)} %get-tuple-element.151), channel_id=1, source_target_pairs={{16,32},{32,16},{48,64},{64,48},{80,96},{96,80},{112,128},{128,112... | collective-permute-start | bytes 196616 | tf_op jit(solution)/shard_map/ppermute | solution.py:628
  171.8 3.1 %collective-permute-start.28 = (f32[128,128]{1,0:T(8,128)S(1)}, f32[128,128]{1,0:T(8,128)S(1)}, u32[]{:S(2)}, u32[]{:S(2)}) collective-permute-start(f32[128,128]{1,0:T(8,128)S(1)} %get-tuple-element.152), channel_id=1, source_target_pairs={{0,16},{16,0},{32,48},{48,32},{64,80},{80,64},{96,112},{112,96},{1... | collective-permute-start | bytes 196616 | tf_op jit(solution)/shard_map/ppermute | solution.py:628

commit v10 on v9

--- a/solution.py
+++ b/solution.py
@@ -412,20 +412,26 @@
     for k in range(rows // 2):
         pays.append(jnp.where(at.even_row, mine[k], other[k]))
         pays.append(jnp.where(at.even_row, other[k], mine[k]))
+    point = lax.broadcasted_iota(jnp.int32, (8, width), 0)
+    units = []
     for k in range(rows):
         tail = pays[k][24:32]
-        lowers.append(jnp.broadcast_to(tail[:, 120:121], (8, rhs)))
-        uppers.append(jnp.broadcast_to(tail[:, 121:122], (8, rhs)))
-        wide = tail
+        lowers.append(jnp.broadcast_to(tail[:, 120:121], (8, width)))
+        uppers.append(jnp.broadcast_to(tail[:, 121:122], (8, width)))
+        units.append(jnp.where(lane == point + 8 * k, 1.0, 0.0).astype(F32))
+    tops = coarse_rows(units, lowers, uppers)
+    for k in range(rows):
+        wide = pays[k][24:32]
         if width > LANES:
-            wide = jnp.concatenate([tail, jnp.zeros((8, width - LANES), F32)], axis=1)
+            wide = jnp.concatenate([wide, jnp.zeros((8, width - LANES), F32)], axis=1)
         for ref, first, last, to in (
             (band1, 0, 40, 8 * (k - 2)),
             (band2, 40, 112, 8 * (k - 4)),
             (band0, 112, 120, 8 * k),
         ):
             picked = jnp.where((lane >= first) & (lane < last), wide, 0.0)
-            ref[8 * k : 8 * k + 8, :] = pltpu.roll(picked, (to - first) % width, 1)
+            placed = pltpu.roll(picked, (to - first) % width, 1)
+            ref[8 * k : 8 * k + 8, :] = placed + tops[k] if ref is band0 else placed
 
     def stacked(tiles):
         if width > rows * 8:
@@ -435,8 +441,7 @@
     own, near, wide = [cut(ref[...], 2) for ref in (band0, band1, band2)]
 
     def solve(total):
-        tiles = [total[8 * k : 8 * k + 8] for k in range(rows)]
-        return stacked(coarse_rows(tiles, lowers, uppers)) + banded_product(own, total)
+        return banded_product(own, total)
 
     edge = jnp.zeros((40, rhs), F32)
     c0 = solve(stacked([part[0:8] for part in pays]))

time: 183 us -> 183 us (level)
  no operation moved by 1% of the time
where the time goes in v10:
time: 183 us; the launch traced here: 182 us
  starting transfers between devices  132 us (72%)
  Pallas kernels  28.2 us (15%)
  waiting for transfers between devices  18.3 us (10%)
    ppermute x7, starting transfers between devices, exchange_columns(): lax.ppermute(sends[0], 'circ', far)  35.2 us
    ppermute x7, starting transfers between devices, exchange_rows(): lax.ppermute(sends[2], 'axial', link)  33 us
    all_to_all x4, starting transfers between devices, spread(): lax.all_to_all(value, axis, split_axis=0, concat_axis=0, tiled=True, axis...  30.7 us
    pallas_call x13, Pallas kernels, call(): pl.pallas_call(body, out_shape=[out if isinstance(out, jax.ShapeDtypeStru...  28.2 us
    ppermute x7, starting transfers between devices, exchange_columns(): lax.ppermute(sends[1], 'circ', near)  13.4 us
    ppermute x7, starting transfers between devices, exchange_rows(): lax.ppermute(sends[3], 'axial', core)  13.4 us
    all_to_all x4, waiting for transfers between devices, spread(): lax.all_to_all(value, axis, split_axis=0, concat_axis=0, tiled=True, axis...  7.25 us
    ppermute x1, starting transfers between devices, local(): other = lax.ppermute(mine, 'axial', [(i, i ^ 1) for i in range(rows)])  6.55 us
  transfers between devices with their start and end apart: 33, of which 13 were waited for; matrix products, arithmetic and copies ran while one was open for 0% of the time, Pallas kernels for 3%

profile of v10, /device:TPU:1, one launch (start us, length us, event | category | flops | bytes accessed | tf_op | source)
XLA Modules:
  0.0 181.5 jit_solution(13136621593367988975)
XLA Ops:
  0.7 2.1 %shard_map.122 = (f32[136,512]{1,0:T(8,128)S(1)}, s32[1,512]{1,0:T(1,128)S(1)}, f32[136,128]{1,0:T(8,128)S(1)}, f32[136,128]{1,0:T(8,128)S(1)}, f32[136,128]{1,0...) custom-call(s32[3]{0:T(128)S(1)} %pad_add_fusion.place, f32[128,512]{1,0:T(8,128)} %bitcast.14, ...), custom_call_target="tpu_custom_call" | custom-call | flops 1000000 | bytes 1000000 | tf_op jit(solution)/shard_map/pallas_call | solution.py:605
  2.8 7.7 %collective-permute-start = (f32[136,128]{1,0:T(8,128)S(1)}, f32[136,128]{1,0:T(8,128)S(1)}, u32[]{:S(2)}, u32[]{:S(2)}) collective-permute-start(f32[136,128]{1,0:T(8,128)S(1)} %get-tuple-element.82), channel_id=1, source_target_pairs={{0,15},{1,2},{2,1},{3,4},{4,3},{5,6},{6,5},{7,8},{8,7},{9,10},{10,... | collective-permute-start | bytes 208904 | tf_op jit(solution)/shard_map/ppermute | solution.py:627
  10.5 1.9 %collective-permute-start.1 = (f32[136,128]{1,0:T(8,128)S(1)}, f32[136,128]{1,0:T(8,128)S(1)}, u32[]{:S(2)}, u32[]{:S(2)}) collective-permute-start(f32[136,128]{1,0:T(8,128)S(1)} %get-tuple-element.83), channel_id=1, source_target_pairs={{0,1},{1,0},{2,3},{3,2},{4,5},{5,4},{6,7},{7,6},{8,9},{9,8},{10,11... | collective-permute-start | bytes 208904 | tf_op jit(solution)/shard_map/ppermute | solution.py:627
  12.4 4.4 %collective-permute-start.2 = (f32[136,128]{1,0:T(8,128)S(1)}, f32[136,128]{1,0:T(8,128)S(1)}, u32[]{:S(2)}, u32[]{:S(2)}) collective-permute-start(f32[136,128]{1,0:T(8,128)S(1)} %get-tuple-element.84), channel_id=1, source_target_pairs={{16,32},{32,16},{48,64},{64,48},{80,96},{96,80},{112,128},{128,112... | collective-permute-start | bytes 208904 | tf_op jit(solution)/shard_map/ppermute | solution.py:633
  16.8 1.9 %collective-permute-start.3 = (f32[136,128]{1,0:T(8,128)S(1)}, f32[136,128]{1,0:T(8,128)S(1)}, u32[]{:S(2)}, u32[]{:S(2)}) collective-permute-start(f32[136,128]{1,0:T(8,128)S(1)} %get-tuple-element.85), channel_id=1, source_target_pairs={{0,16},{16,0},{32,48},{48,32},{64,80},{80,64},{96,112},{112,96},{1... | collective-permute-start | bytes 208904 | tf_op jit(solution)/shard_map/ppermute | solution.py:633
  18.8 1.7 shard_map.123
  21.7 4.4 %collective-permute-start.4 = (f32[136,128]{1,0:T(8,128)S(1)}, f32[136,128]{1,0:T(8,128)S(1)}, u32[]{:S(2)}, u32[]{:S(2)}) collective-permute-start(f32[136,128]{1,0:T(8,128)S(1)} %get-tuple-element.91), channel_id=1, source_target_pairs={{0,15},{1,2},{2,1},{3,4},{4,3},{5,6},{6,5},{7,8},{8,7},{9,10},{10,... | collective-permute-start | bytes 208904 | tf_op jit(solution)/shard_map/ppermute | solution.py:627
  26.0 1.9 %collective-permute-start.5 = (f32[136,128]{1,0:T(8,128)S(1)}, f32[136,128]{1,0:T(8,128)S(1)}, u32[]{:S(2)}, u32[]{:S(2)}) collective-permute-start(f32[136,128]{1,0:T(8,128)S(1)} %get-tuple-element.92), channel_id=1, source_target_pairs={{0,1},{1,0},{2,3},{3,2},{4,5},{5,4},{6,7},{7,6},{8,9},{9,8},{10,11... | collective-permute-start | bytes 208904 | tf_op jit(solution)/shard_map/ppermute | solution.py:627
  27.9 3.5 %collective-permute-start.6 = (f32[136,128]{1,0:T(8,128)S(1)}, f32[136,128]{1,0:T(8,128)S(1)}, u32[]{:S(2)}, u32[]{:S(2)}) collective-permute-start(f32[136,128]{1,0:T(8,128)S(1)} %get-tuple-element.93), channel_id=1, source_target_pairs={{16,32},{32,16},{48,64},{64,48},{80,96},{96,80},{112,128},{128,112... | collective-permute-start | bytes 208904 | tf_op jit(solution)/shard_map/ppermute | solution.py:633
  31.4 1.9 %collective-permute-start.7 = (f32[136,128]{1,0:T(8,128)S(1)}, f32[136,128]{1,0:T(8,128)S(1)}, u32[]{:S(2)}, u32[]{:S(2)}) collective-permute-start(f32[136,128]{1,0:T(8,128)S(1)} %get-tuple-element.94), channel_id=1, source_target_pairs={{0,16},{16,0},{32,48},{48,32},{64,80},{80,64},{96,112},{112,96},{1... | collective-permute-start | bytes 208904 | tf_op jit(solution)/shard_map/ppermute | solution.py:633
  33.4 1.5 shard_map.125
  34.9 2.1 %shard_map.126 = (f32[152,512]{1,0:T(8,128)}, f32[152,512]{1,0:T(8,128)S(1)}, f32[152,128]{1,0:T(8,128)S(1)}, f32[152,128]{1,0:T(8,128)S(1)}, f32[152,128]{1,0:T(8,128)S(1)}, /*index=5*/f32[152,128]{1,0:T(8,128)S(1)}) custom-call(s32[3]{0:T(128)S(1)} %pad_add_fusion.place, f32[136,512]{1,0:T(8,128)S(1)} %get-tuple-element.90.t, ...), custom_call_target="tpu_custom_call" | custom-call | flops 1000000 | bytes 1000000 | tf_op jit(solution)/shard_map/pallas_call | solution.py:605
  37.0 5.0 %collective-permute-start.10 = (f32[152,128]{1,0:T(8,128)S(1)}, f32[152,128]{1,0:T(8,128)S(1)}, u32[]{:S(2)}, u32[]{:S(2)}) collective-permute-start(f32[152,128]{1,0:T(8,128)S(1)} %get-tuple-element.103), channel_id=1, source_target_pairs={{0,15},{1,2},{2,1},{3,4},{4,3},{5,6},{6,5},{7,8},{8,7},{9,10},{10,... | collective-permute-start | bytes 233480 | tf_op jit(solution)/shard_map/ppermute | solution.py:627
  42.0 1.9 %collective-permute-start.11 = (f32[152,128]{1,0:T(8,128)S(1)}, f32[152,128]{1,0:T(8,128)S(1)}, u32[]{:S(2)}, u32[]{:S(2)}) collective-permute-start(f32[152,128]{1,0:T(8,128)S(1)} %get-tuple-element.104), channel_id=1, source_target_pairs={{0,1},{1,0},{2,3},{3,2},{4,5},{5,4},{6,7},{7,6},{8,9},{9,8},{10,11... | collective-permute-start | bytes 233480 | tf_op jit(solution)/shard_map/ppermute | solution.py:627
  44.0 4.2 %collective-permute-start.8 = (f32[152,128]{1,0:T(8,128)S(1)}, f32[152,128]{1,0:T(8,128)S(1)}, u32[]{:S(2)}, u32[]{:S(2)}) collective-permute-start(f32[152,128]{1,0:T(8,128)S(1)} %get-tuple-element.101), channel_id=1, source_target_pairs={{16,32},{32,16},{48,64},{64,48},{80,96},{96,80},{112,128},{128,112... | collective-permute-start | bytes 233480 | tf_op jit(solution)/shard_map/ppermute | solution.py:633
  48.2 1.9 %collective-permute-start.9 = (f32[152,128]{1,0:T(8,128)S(1)}, f32[152,128]{1,0:T(8,128)S(1)}, u32[]{:S(2)}, u32[]{:S(2)}) collective-permute-start(f32[152,128]{1,0:T(8,128)S(1)} %get-tuple-element.102), channel_id=1, source_target_pairs={{0,16},{16,0},{32,48},{48,32},{64,80},{80,64},{96,112},{112,96},{1... | collective-permute-start | bytes 233480 | tf_op jit(solution)/shard_map/ppermute | solution.py:633
  51.3 1.3 shard_map.127
  52.6 3.6 %collective-permute-start.12 = (f32[168,128]{1,0:T(8,128)S(1)}, f32[168,128]{1,0:T(8,128)S(1)}, u32[]{:S(2)}, u32[]{:S(2)}) collective-permute-start(f32[168,128]{1,0:T(8,128)S(1)} %get-tuple-element.107), channel_id=1, source_target_pairs={{0,15},{1,2},{2,1},{3,4},{4,3},{5,6},{6,5},{7,8},{8,7},{9,10},{10,... | collective-permute-start | bytes 258056 | tf_op jit(solution)/shard_map/ppermute | solution.py:627
  56.3 1.9 %collective-permute-start.13 = (f32[168,128]{1,0:T(8,128)S(1)}, f32[168,128]{1,0:T(8,128)S(1)}, u32[]{:S(2)}, u32[]{:S(2)}) collective-permute-start(f32[168,128]{1,0:T(8,128)S(1)} %get-tuple-element.108), channel_id=1, source_target_pairs={{0,1},{1,0},{2,3},{3,2},{4,5},{5,4},{6,7},{7,6},{8,9},{9,8},{10,11... | collective-permute-start | bytes 258056 | tf_op jit(solution)/shard_map/ppermute | solution.py:627
  58.2 5.1 %collective-permute-start.14 = (f32[168,128]{1,0:T(8,128)S(1)}, f32[168,128]{1,0:T(8,128)S(1)}, u32[]{:S(2)}, u32[]{:S(2)}) collective-permute-start(f32[168,128]{1,0:T(8,128)S(1)} %get-tuple-element.109), channel_id=1, source_target_pairs={{16,32},{32,16},{48,64},{64,48},{80,96},{96,80},{112,128},{128,112... | collective-permute-start | bytes 258056 | tf_op jit(solution)/shard_map/ppermute | solution.py:633
  63.3 1.9 %collective-permute-start.15 = (f32[168,128]{1,0:T(8,128)S(1)}, f32[168,128]{1,0:T(8,128)S(1)}, u32[]{:S(2)}, u32[]{:S(2)}) collective-permute-start(f32[168,128]{1,0:T(8,128)S(1)} %get-tuple-element.110), channel_id=1, source_target_pairs={{0,16},{16,0},{32,48},{48,32},{64,80},{80,64},{96,112},{112,96},{1... | collective-permute-start | bytes 258056 | tf_op jit(solution)/shard_map/ppermute | solution.py:633
  66.4 2.2 %shard_map.128 = (f32[184,512]{1,0:T(8,128)}, f32[184,512]{1,0:T(8,128)S(1)}, f32[184,128]{1,0:T(8,128)S(1)}, f32[184,128]{1,0:T(8,128)S(1)}, f32[184,128]{1,0:T(8,128)S(1)}, /*index=5*/f32[184,128]{1,0:T(8,128)S(1)}) custom-call(s32[3]{0:T(128)S(1)} %pad_add_fusion.place, f32[168,512]{1,0:T(8,128)S(1)} %get-tuple-element.106.t, ...), custom_call_target="tpu_custom_call" | custom-call | flops 1000000 | bytes 1000000 | tf_op jit(solution)/shard_map/pallas_call | solution.py:605
  68.7 5.0 %collective-permute-start.16 = (f32[184,128]{1,0:T(8,128)S(1)}, f32[184,128]{1,0:T(8,128)S(1)}, u32[]{:S(2)}, u32[]{:S(2)}) collective-permute-start(f32[184,128]{1,0:T(8,128)S(1)} %get-tuple-element.112), channel_id=1, source_target_pairs={{0,15},{1,2},{2,1},{3,4},{4,3},{5,6},{6,5},{7,8},{8,7},{9,10},{10,... | collective-permute-start | bytes 282632 | tf_op jit(solution)/shard_map/ppermute | solution.py:627
  73.7 1.9 %collective-permute-start.17 = (f32[184,128]{1,0:T(8,128)S(1)}, f32[184,128]{1,0:T(8,128)S(1)}, u32[]{:S(2)}, u32[]{:S(2)}) collective-permute-start(f32[184,128]{1,0:T(8,128)S(1)} %get-tuple-element.113), channel_id=1, source_target_pairs={{0,1},{1,0},{2,3},{3,2},{4,5},{5,4},{6,7},{7,6},{8,9},{9,8},{10,11... | collective-permute-start | bytes 282632 | tf_op jit(solution)/shard_map/ppermute | solution.py:627
  75.6 3.9 %collective-permute-start.18 = (f32[184,128]{1,0:T(8,128)S(1)}, f32[184,128]{1,0:T(8,128)S(1)}, u32[]{:S(2)}, u32[]{:S(2)}) collective-permute-start(f32[184,128]{1,0:T(8,128)S(1)} %get-tuple-element.114), channel_id=1, source_target_pairs={{16,32},{32,16},{48,64},{64,48},{80,96},{96,80},{112,128},{128,112... | collective-permute-start | bytes 282632 | tf_op jit(solution)/shard_map/ppermute | solution.py:633
  79.5 1.9 %collective-permute-start.19 = (f32[184,128]{1,0:T(8,128)S(1)}, f32[184,128]{1,0:T(8,128)S(1)}, u32[]{:S(2)}, u32[]{:S(2)}) collective-permute-start(f32[184,128]{1,0:T(8,128)S(1)} %get-tuple-element.115), channel_id=1, source_target_pairs={{0,16},{16,0},{32,48},{48,32},{64,80},{80,64},{96,112},{112,96},{1... | collective-permute-start | bytes 282632 | tf_op jit(solution)/shard_map/ppermute | solution.py:633
  82.7 2.4 %shard_map.129 = (f32[200,512]{1,0:T(8,128)}, f32[16,32,128]{2,1,0:T(8,128)}) custom-call(s32[3]{0:T(128)S(1)} %pad_add_fusion.place, f32[184,512]{1,0:T(8,128)S(1)} %get-tuple-element.111.q, f32[184,128]{1,0:T(8,128)S(1)} %collective-permute-done.16.g0, f32[184,128]{1,0:T(8,128)S(1)} %collective-permute-done.17.g1, ...), custom_call_target="tpu_custom_call" | custom-call | flops 1000000 | bytes 1000000 | tf_op jit(solution)/shard_map/pallas_call | solution.py:605
  85.1 4.8 %all-to-all-start = ((f32[16,32,128]{2,1,0:T(8,128)}), f32[16,32,128]{2,1,0:T(8,128)S(1)}, u32[]{:S(2)}, u32[]{:S(2)}) async-start(f32[16,32,128]{2,1,0:T(8,128)} %get-tuple-element.119), calls=%async_computation | async-start | bytes 524288 | tf_op jit(solution)/shard_map/all_to_all | solution.py:641
  89.8 2.9 %shard_map.130 = (f32[200,512]{1,0:T(8,128)}, f32[200,128]{1,0:T(8,128)S(1)}, f32[200,128]{1,0:T(8,128)S(1)}, f32[200,128]{1,0:T(8,128)S(1)}, f32[200,128]{1,0:T(8,128)S(1)}) custom-call(s32[3]{0:T(128)S(1)} %pad_add_fusion.place, f32[200,512]{1,0:T(8,128)} %get-tuple-element.120.v2, f32[1,512]{1,0:T(1,128)S(1)} %get-tuple-element.95.after.share, ...), custom_call_target="tpu_custom_call" | custom-call | flops 500000000 | bytes 1000000 | tf_op jit(solution)/shard_map/pallas_call | solution.py:605
  94.0 4.1 %all-to-all-done.got = f32[16,32,128]{2,1,0:T(8,128)S(1)} async-done(((f32[16,32,128]{2,1,0:T(8,128)}), f32[16,32,128]{2,1,0:T(8,128)S(1)}, u32[]{:S(2)}, u32[]{:S(2)}) %all-to-all-start) | async-done | bytes 262176 | tf_op jit(solution)/shard_map/all_to_all | solution.py:641
  98.9 11.6 %all-to-all-start.1 = ((f32[16,32,128]{2,1,0:T(8,128)}), f32[16,32,128]{2,1,0:T(8,128)S(1)}, u32[]{:S(2)}, u32[]{:S(2)}) async-start(f32[16,32,128]{2,1,0:T(8,128)} %shard_map.131), calls=%async_computation.1 | async-start | bytes 524288 | tf_op jit(solution)/shard_map/all_to_all | solution.py:641
  110.5 2.8 %collective-permute-start.20 = (f32[200,128]{1,0:T(8,128)S(1)}, f32[200,128]{1,0:T(8,128)S(1)}, u32[]{:S(2)}, u32[]{:S(2)}) collective-permute-start(f32[200,128]{1,0:T(8,128)S(1)} %copy-done.6), channel_id=1, source_target_pairs={{0,15},{1,2},{2,1},{3,4},{4,3},{5,6},{6,5},{7,8},{8,7},{9,10},{10,... | collective-permute-start | bytes 307208 | tf_op jit(solution)/shard_map/ppermute | solution.py:627
  113.3 1.9 %collective-permute-start.21 = (f32[200,128]{1,0:T(8,128)S(1)}, f32[200,128]{1,0:T(8,128)S(1)}, u32[]{:S(2)}, u32[]{:S(2)}) collective-permute-start(f32[200,128]{1,0:T(8,128)S(1)} %copy-done.4), channel_id=1, source_target_pairs={{0,1},{1,0},{2,3},{3,2},{4,5},{5,4},{6,7},{7,6},{8,9},{9,8},{10,11... | collective-permute-start | bytes 307208 | tf_op jit(solution)/shard_map/ppermute | solution.py:627
  115.2 6.6 %collective-permute-start.22 = (f32[200,128]{1,0:T(8,128)S(1)}, f32[200,128]{1,0:T(8,128)S(1)}, u32[]{:S(2)}, u32[]{:S(2)}) collective-permute-start(f32[200,128]{1,0:T(8,128)S(1)} %get-tuple-element.131), channel_id=1, source_target_pairs={{16,32},{32,16},{48,64},{64,48},{80,96},{96,80},{112,128},{128,112... | collective-permute-start | bytes 307208 | tf_op jit(solution)/shard_map/ppermute | solution.py:633
  121.8 1.9 %collective-permute-start.23 = (f32[200,128]{1,0:T(8,128)S(1)}, f32[200,128]{1,0:T(8,128)S(1)}, u32[]{:S(2)}, u32[]{:S(2)}) collective-permute-start(f32[200,128]{1,0:T(8,128)S(1)} %get-tuple-element.132), channel_id=1, source_target_pairs={{0,16},{16,0},{32,48},{48,32},{64,80},{80,64},{96,112},{112,96},{1... | collective-permute-start | bytes 307208 | tf_op jit(solution)/shard_map/ppermute | solution.py:633
  123.8 1.9 %collective-permute-done.22.g2 = f32[200,128]{1,0:T(8,128)S(1)} collective-permute-done((f32[200,128]{1,0:T(8,128)S(1)}, f32[200,128]{1,0:T(8,128)S(1)}, u32[]{:S(2)}, u32[]{:S(2)}) %collective-permute-start.22) | collective-permute-done | bytes 102432 | tf_op jit(solution)/shard_map/ppermute | solution.py:633
  125.7 6.5 %collective-permute-start.24 = (f32[16,32,128]{2,1,0:T(8,128)S(1)}, f32[16,32,128]{2,1,0:T(8,128)S(1)}, u32[]{:S(2)}, u32[]{:S(2)}) collective-permute-start(f32[16,32,128]{2,1,0:T(8,128)S(1)} %all-to-all-done.1.mine), channel_id=1, source_target_pairs={{0,16},{16,0},{32,48},{48,32},{64,80},{80,64},{96,112},{112,96},{1... | collective-permute-start | bytes 786440 | tf_op jit(solution)/shard_map/ppermute | solution.py:750
  132.3 1.1 collective-permute-done.24.other
  133.4 6.2 %shard_map.132 = (f32[128,512]{1,0:T(8,128)}, f32[128,512]{1,0:T(8,128)}, f32[128,512]{1,0:T(8,128)}, f32[128,512]{1,0:T(8,128)}, f32[128,512]{1,0:T(8,128)}, /*...) custom-call(s32[3]{0:T(128)S(1)} %pad_add_fusion.place, ...), custom_call_target="tpu_custom_call" | custom-call | flops 1000000 | bytes 1000000 | tf_op jit(solution)/shard_map/pallas_call | solution.py:605
  139.7 4.1 %all-to-all-start.2 = ((f32[32,1,1152]{2,1,0:T(1,128)}), f32[32,1,1152]{2,1,0:T(1,128)S(1)}, u32[]{:S(2)}, u32[]{:S(2)}) async-start(f32[32,1,1152]{2,1,0:T(1,128)} %get-tuple-element.141), calls=%async_computation.2 | async-start | bytes 294912 | tf_op jit(solution)/shard_map/all_to_all | solution.py:641
  143.8 6.8 %collective-permute-start.25 = (f32[128,128]{1,0:T(8,128)S(1)}, f32[128,128]{1,0:T(8,128)S(1)}, u32[]{:S(2)}, u32[]{:S(2)}) collective-permute-start(f32[128,128]{1,0:T(8,128)S(1)} %get-tuple-element.142), channel_id=1, source_target_pairs={{0,15},{1,2},{2,1},{3,4},{4,3},{5,6},{6,5},{7,8},{8,7},{9,10},{10,... | collective-permute-start | bytes 196616 | tf_op jit(solution)/shard_map/ppermute | solution.py:627
  150.6 1.9 %collective-permute-start.26 = (f32[128,128]{1,0:T(8,128)S(1)}, f32[128,128]{1,0:T(8,128)S(1)}, u32[]{:S(2)}, u32[]{:S(2)}) collective-permute-start(f32[128,128]{1,0:T(8,128)S(1)} %get-tuple-element.143), channel_id=1, source_target_pairs={{0,1},{1,0},{2,3},{3,2},{4,5},{5,4},{6,7},{7,6},{8,9},{9,8},{10,11... | collective-permute-start | bytes 196616 | tf_op jit(solution)/shard_map/ppermute | solution.py:627
  152.6 3.1 %collective-permute-done.26.g1 = f32[128,128]{1,0:T(8,128)S(1)} collective-permute-done((f32[128,128]{1,0:T(8,128)S(1)}, f32[128,128]{1,0:T(8,128)S(1)}, u32[]{:S(2)}, u32[]{:S(2)}) %collective-permute-start.26) | collective-permute-done | bytes 65568 | tf_op jit(solution)/shard_map/ppermute | solution.py:627
  156.3 10.3 %all-to-all-start.3 = ((f32[16,1,1152]{2,1,0:T(1,128)}), f32[16,1,1152]{2,1,0:T(1,128)S(1)}, u32[]{:S(2)}, u32[]{:S(2)}) async-start(f32[16,1,1152]{2,1,0:T(1,128)} %shard_map.133), calls=%async_computation.3 | async-start | bytes 147456 | tf_op jit(solution)/shard_map/all_to_all | solution.py:641
  166.6 5.4 %collective-permute-start.27 = (f32[128,128]{1,0:T(8,128)S(1)}, f32[128,128]{1,0:T(8,128)S(1)}, u32[]{:S(2)}, u32[]{:S(2)}) collective-permute-start(f32[128,128]{1,0:T(8,128)S(1)} %get-tuple-element.151), channel_id=1, source_target_pairs={{16,32},{32,16},{48,64},{64,48},{80,96},{96,80},{112,128},{128,112... | collective-permute-start | bytes 196616 | tf_op jit(solution)/shard_map/ppermute | solution.py:633
  172.1 1.9 %collective-permute-start.28 = (f32[128,128]{1,0:T(8,128)S(1)}, f32[128,128]{1,0:T(8,128)S(1)}, u32[]{:S(2)}, u32[]{:S(2)}) collective-permute-start(f32[128,128]{1,0:T(8,128)S(1)} %get-tuple-element.152), channel_id=1, source_target_pairs={{0,16},{16,0},{32,48},{48,32},{64,80},{80,64},{96,112},{112,96},{1... | collective-permute-start | bytes 196616 | tf_op jit(solution)/shard_map/ppermute | solution.py:633
  175.2 3.1 %all-to-all-done.3.got = f32[16,1,1152]{2,1,0:T(1,128)S(1)} async-done(((f32[16,1,1152]{2,1,0:T(1,128)}), f32[16,1,1152]{2,1,0:T(1,128)S(1)}, u32[]{:S(2)}, u32[]{:S(2)}) %all-to-all-start.3) | async-done | bytes 73760 | tf_op jit(solution)/shard_map/all_to_all | solution.py:641
  178.3 3.2 %shard_map.134 = (f32[128,512]{1,0:T(8,128)}, f32[128,512]{1,0:T(8,128)}) custom-call(s32[3]{0:T(128)S(1)} %pad_add_fusion.place, f32[16,1,1152]{2,1,0:T(1,128)S(1)} %all-to-all-done.3.got, f32[128,512]{1,0:T(8,128)S(1)} %get-tuple-element.148.q, f32[128,128]{1,0:T(8,128)S(1)} %collective-permute-done.25.g0, f32[128,128]{1,0:T(8,128)S(1)} %collective-permute-done.26.g1, ...), custom_call_target="tpu_custom_call" | custom-call | flops 1000000 | bytes 1000000 | tf_op jit(solution)/shard_map/pallas_call | solution.py:605
  (47 shorter events, 8.9 us)
Async XLA Ops:
  2.8 17.7 %collective-permute-start = (f32[136,128]{1,0:T(8,128)S(1)}, f32[136,128]{1,0:T(8,128)S(1)}, u32[]{:S(2)}, u32[]{:S(2)}) collective-permute-start(f32[136,128]{1,0:T(8,128)S(1)} %get-tuple-element.82), channel_id=1, source_target_pairs={{0,15},{1,2},{2,1},{3,4},{4,3},{5,6},{6,5},{7,8},{8,7},{9,10},{10,... | collective-permute-start | bytes 208904 | tf_op jit(solution)/shard_map/ppermute | solution.py:627
  10.5 10.0 %collective-permute-start.1 = (f32[136,128]{1,0:T(8,128)S(1)}, f32[136,128]{1,0:T(8,128)S(1)}, u32[]{:S(2)}, u32[]{:S(2)}) collective-permute-start(f32[136,128]{1,0:T(8,128)S(1)} %get-tuple-element.83), channel_id=1, source_target_pairs={{0,1},{1,0},{2,3},{3,2},{4,5},{5,4},{6,7},{7,6},{8,9},{9,8},{10,11... | collective-permute-start | bytes 208904 | tf_op jit(solution)/shard_map/ppermute | solution.py:627
  12.4 8.1 %collective-permute-start.2 = (f32[136,128]{1,0:T(8,128)S(1)}, f32[136,128]{1,0:T(8,128)S(1)}, u32[]{:S(2)}, u32[]{:S(2)}) collective-permute-start(f32[136,128]{1,0:T(8,128)S(1)} %get-tuple-element.84), channel_id=1, source_target_pairs={{16,32},{32,16},{48,64},{64,48},{80,96},{96,80},{112,128},{128,112... | collective-permute-start | bytes 208904 | tf_op jit(solution)/shard_map/ppermute | solution.py:633
  16.8 3.7 %collective-permute-start.3 = (f32[136,128]{1,0:T(8,128)S(1)}, f32[136,128]{1,0:T(8,128)S(1)}, u32[]{:S(2)}, u32[]{:S(2)}) collective-permute-start(f32[136,128]{1,0:T(8,128)S(1)} %get-tuple-element.85), channel_id=1, source_target_pairs={{0,16},{16,0},{32,48},{48,32},{64,80},{80,64},{96,112},{112,96},{1... | collective-permute-start | bytes 208904 | tf_op jit(solution)/shard_map/ppermute | solution.py:633
  21.7 13.2 %collective-permute-start.4 = (f32[136,128]{1,0:T(8,128)S(1)}, f32[136,128]{1,0:T(8,128)S(1)}, u32[]{:S(2)}, u32[]{:S(2)}) collective-permute-start(f32[136,128]{1,0:T(8,128)S(1)} %get-tuple-element.91), channel_id=1, source_target_pairs={{0,15},{1,2},{2,1},{3,4},{4,3},{5,6},{6,5},{7,8},{8,7},{9,10},{10,... | collective-permute-start | bytes 208904 | tf_op jit(solution)/shard_map/ppermute | solution.py:627
  26.0 8.8 %collective-permute-start.5 = (f32[136,128]{1,0:T(8,128)S(1)}, f32[136,128]{1,0:T(8,128)S(1)}, u32[]{:S(2)}, u32[]{:S(2)}) collective-permute-start(f32[136,128]{1,0:T(8,128)S(1)} %get-tuple-element.92), channel_id=1, source_target_pairs={{0,1},{1,0},{2,3},{3,2},{4,5},{5,4},{6,7},{7,6},{8,9},{9,8},{10,11... | collective-permute-start | bytes 208904 | tf_op jit(solution)/shard_map/ppermute | solution.py:627
  27.9 6.9 %collective-permute-start.6 = (f32[136,128]{1,0:T(8,128)S(1)}, f32[136,128]{1,0:T(8,128)S(1)}, u32[]{:S(2)}, u32[]{:S(2)}) collective-permute-start(f32[136,128]{1,0:T(8,128)S(1)} %get-tuple-element.93), channel_id=1, source_target_pairs={{16,32},{32,16},{48,64},{64,48},{80,96},{96,80},{112,128},{128,112... | collective-permute-start | bytes 208904 | tf_op jit(solution)/shard_map/ppermute | solution.py:633
  31.4 3.4 %collective-permute-start.7 = (f32[136,128]{1,0:T(8,128)S(1)}, f32[136,128]{1,0:T(8,128)S(1)}, u32[]{:S(2)}, u32[]{:S(2)}) collective-permute-start(f32[136,128]{1,0:T(8,128)S(1)} %get-tuple-element.94), channel_id=1, source_target_pairs={{0,16},{16,0},{32,48},{48,32},{64,80},{80,64},{96,112},{112,96},{1... | collective-permute-start | bytes 208904 | tf_op jit(solution)/shard_map/ppermute | solution.py:633
  37.0 13.1 %collective-permute-start.10 = (f32[152,128]{1,0:T(8,128)S(1)}, f32[152,128]{1,0:T(8,128)S(1)}, u32[]{:S(2)}, u32[]{:S(2)}) collective-permute-start(f32[152,128]{1,0:T(8,128)S(1)} %get-tuple-element.103), channel_id=1, source_target_pairs={{0,15},{1,2},{2,1},{3,4},{4,3},{5,6},{6,5},{7,8},{8,7},{9,10},{10,... | collective-permute-start | bytes 233480 | tf_op jit(solution)/shard_map/ppermute | solution.py:627
  42.0 8.1 %collective-permute-start.11 = (f32[152,128]{1,0:T(8,128)S(1)}, f32[152,128]{1,0:T(8,128)S(1)}, u32[]{:S(2)}, u32[]{:S(2)}) collective-permute-start(f32[152,128]{1,0:T(8,128)S(1)} %get-tuple-element.104), channel_id=1, source_target_pairs={{0,1},{1,0},{2,3},{3,2},{4,5},{5,4},{6,7},{7,6},{8,9},{9,8},{10,11... | collective-permute-start | bytes 233480 | tf_op jit(solution)/shard_map/ppermute | solution.py:627
  44.0 6.3 %collective-permute-start.8 = (f32[152,128]{1,0:T(8,128)S(1)}, f32[152,128]{1,0:T(8,128)S(1)}, u32[]{:S(2)}, u32[]{:S(2)}) collective-permute-start(f32[152,128]{1,0:T(8,128)S(1)} %get-tuple-element.101), channel_id=1, source_target_pairs={{16,32},{32,16},{48,64},{64,48},{80,96},{96,80},{112,128},{128,112... | collective-permute-start | bytes 233480 | tf_op jit(solution)/shard_map/ppermute | solution.py:633
  48.2 3.2 %collective-permute-start.9 = (f32[152,128]{1,0:T(8,128)S(1)}, f32[152,128]{1,0:T(8,128)S(1)}, u32[]{:S(2)}, u32[]{:S(2)}) collective-permute-start(f32[152,128]{1,0:T(8,128)S(1)} %get-tuple-element.102), channel_id=1, source_target_pairs={{0,16},{16,0},{32,48},{48,32},{64,80},{80,64},{96,112},{112,96},{1... | collective-permute-start | bytes 233480 | tf_op jit(solution)/shard_map/ppermute | solution.py:633
  52.6 12.6 %collective-permute-start.12 = (f32[168,128]{1,0:T(8,128)S(1)}, f32[168,128]{1,0:T(8,128)S(1)}, u32[]{:S(2)}, u32[]{:S(2)}) collective-permute-start(f32[168,128]{1,0:T(8,128)S(1)} %get-tuple-element.107), channel_id=1, source_target_pairs={{0,15},{1,2},{2,1},{3,4},{4,3},{5,6},{6,5},{7,8},{8,7},{9,10},{10,... | collective-permute-start | bytes 258056 | tf_op jit(solution)/shard_map/ppermute | solution.py:627
  56.3 8.9 %collective-permute-start.13 = (f32[168,128]{1,0:T(8,128)S(1)}, f32[168,128]{1,0:T(8,128)S(1)}, u32[]{:S(2)}, u32[]{:S(2)}) collective-permute-start(f32[168,128]{1,0:T(8,128)S(1)} %get-tuple-element.108), channel_id=1, source_target_pairs={{0,1},{1,0},{2,3},{3,2},{4,5},{5,4},{6,7},{7,6},{8,9},{9,8},{10,11... | collective-permute-start | bytes 258056 | tf_op jit(solution)/shard_map/ppermute | solution.py:627
  58.2 7.2 %collective-permute-start.14 = (f32[168,128]{1,0:T(8,128)S(1)}, f32[168,128]{1,0:T(8,128)S(1)}, u32[]{:S(2)}, u32[]{:S(2)}) collective-permute-start(f32[168,128]{1,0:T(8,128)S(1)} %get-tuple-element.109), channel_id=1, source_target_pairs={{16,32},{32,16},{48,64},{64,48},{80,96},{96,80},{112,128},{128,112... | collective-permute-start | bytes 258056 | tf_op jit(solution)/shard_map/ppermute | solution.py:633
  63.3 3.2 %collective-permute-start.15 = (f32[168,128]{1,0:T(8,128)S(1)}, f32[168,128]{1,0:T(8,128)S(1)}, u32[]{:S(2)}, u32[]{:S(2)}) collective-permute-start(f32[168,128]{1,0:T(8,128)S(1)} %get-tuple-element.110), channel_id=1, source_target_pairs={{0,16},{16,0},{32,48},{48,32},{64,80},{80,64},{96,112},{112,96},{1... | collective-permute-start | bytes 258056 | tf_op jit(solution)/shard_map/ppermute | solution.py:633
  68.7 12.7 %collective-permute-start.16 = (f32[184,128]{1,0:T(8,128)S(1)}, f32[184,128]{1,0:T(8,128)S(1)}, u32[]{:S(2)}, u32[]{:S(2)}) collective-permute-start(f32[184,128]{1,0:T(8,128)S(1)} %get-tuple-element.112), channel_id=1, source_target_pairs={{0,15},{1,2},{2,1},{3,4},{4,3},{5,6},{6,5},{7,8},{8,7},{9,10},{10,... | collective-permute-start | bytes 282632 | tf_op jit(solution)/shard_map/ppermute | solution.py:627
  73.7 7.8 %collective-permute-start.17 = (f32[184,128]{1,0:T(8,128)S(1)}, f32[184,128]{1,0:T(8,128)S(1)}, u32[]{:S(2)}, u32[]{:S(2)}) collective-permute-start(f32[184,128]{1,0:T(8,128)S(1)} %get-tuple-element.113), channel_id=1, source_target_pairs={{0,1},{1,0},{2,3},{3,2},{4,5},{5,4},{6,7},{7,6},{8,9},{9,8},{10,11... | collective-permute-start | bytes 282632 | tf_op jit(solution)/shard_map/ppermute | solution.py:627
  75.6 6.1 %collective-permute-start.18 = (f32[184,128]{1,0:T(8,128)S(1)}, f32[184,128]{1,0:T(8,128)S(1)}, u32[]{:S(2)}, u32[]{:S(2)}) collective-permute-start(f32[184,128]{1,0:T(8,128)S(1)} %get-tuple-element.114), channel_id=1, source_target_pairs={{16,32},{32,16},{48,64},{64,48},{80,96},{96,80},{112,128},{128,112... | collective-permute-start | bytes 282632 | tf_op jit(solution)/shard_map/ppermute | solution.py:633
  79.5 3.2 %collective-permute-start.19 = (f32[184,128]{1,0:T(8,128)S(1)}, f32[184,128]{1,0:T(8,128)S(1)}, u32[]{:S(2)}, u32[]{:S(2)}) collective-permute-start(f32[184,128]{1,0:T(8,128)S(1)} %get-tuple-element.115), channel_id=1, source_target_pairs={{0,16},{16,0},{32,48},{48,32},{64,80},{80,64},{96,112},{112,96},{1... | collective-permute-start | bytes 282632 | tf_op jit(solution)/shard_map/ppermute | solution.py:633
  85.1 13.1 %all-to-all-start = ((f32[16,32,128]{2,1,0:T(8,128)}), f32[16,32,128]{2,1,0:T(8,128)S(1)}, u32[]{:S(2)}, u32[]{:S(2)}) async-start(f32[16,32,128]{2,1,0:T(8,128)} %get-tuple-element.119), calls=%async_computation | async-start | bytes 524288 | tf_op jit(solution)/shard_map/all_to_all | solution.py:641
  92.8 0.6 copy-start.3
  93.4 0.6 copy-start.5
  98.9 34.5 %copy-start = (f32[152,512]{1,0:T(8,128)S(1)}, f32[152,512]{1,0:T(8,128)}, u32[]{:S(2)}) copy-start(f32[152,512]{1,0:T(8,128)} %get-tuple-element.139.z0) | copy-start | bytes 933892
  98.9 11.6 %copy-start.6 = (f32[200,128]{1,0:T(8,128)S(1)}, f32[200,128]{1,0:T(8,128)}, u32[]{:S(2)}) copy-start(f32[200,128]{1,0:T(8,128)} %copy-done.5) | copy-start | bytes 307204
  98.9 14.4 %copy-start.4 = (f32[200,128]{1,0:T(8,128)S(1)}, f32[200,128]{1,0:T(8,128)}, u32[]{:S(2)}) copy-start(f32[200,128]{1,0:T(8,128)} %copy-done.3) | copy-start | bytes 307204
  98.9 26.8 %all-to-all-start.1 = ((f32[16,32,128]{2,1,0:T(8,128)}), f32[16,32,128]{2,1,0:T(8,128)S(1)}, u32[]{:S(2)}, u32[]{:S(2)}) async-start(f32[16,32,128]{2,1,0:T(8,128)} %shard_map.131), calls=%async_computation.1 | async-start | bytes 524288 | tf_op jit(solution)/shard_map/all_to_all | solution.py:641
  110.5 13.2 %collective-permute-start.20 = (f32[200,128]{1,0:T(8,128)S(1)}, f32[200,128]{1,0:T(8,128)S(1)}, u32[]{:S(2)}, u32[]{:S(2)}) collective-permute-start(f32[200,128]{1,0:T(8,128)S(1)} %copy-done.6), channel_id=1, source_target_pairs={{0,15},{1,2},{2,1},{3,4},{4,3},{5,6},{6,5},{7,8},{8,7},{9,10},{10,... | collective-permute-start | bytes 307208 | tf_op jit(solution)/shard_map/ppermute | solution.py:627
  113.3 10.4 %collective-permute-start.21 = (f32[200,128]{1,0:T(8,128)S(1)}, f32[200,128]{1,0:T(8,128)S(1)}, u32[]{:S(2)}, u32[]{:S(2)}) collective-permute-start(f32[200,128]{1,0:T(8,128)S(1)} %copy-done.4), channel_id=1, source_target_pairs={{0,1},{1,0},{2,3},{3,2},{4,5},{5,4},{6,7},{7,6},{8,9},{9,8},{10,11... | collective-permute-start | bytes 307208 | tf_op jit(solution)/shard_map/ppermute | solution.py:627
  115.2 10.4 %collective-permute-start.22 = (f32[200,128]{1,0:T(8,128)S(1)}, f32[200,128]{1,0:T(8,128)S(1)}, u32[]{:S(2)}, u32[]{:S(2)}) collective-permute-start(f32[200,128]{1,0:T(8,128)S(1)} %get-tuple-element.131), channel_id=1, source_target_pairs={{16,32},{32,16},{48,64},{64,48},{80,96},{96,80},{112,128},{128,112... | collective-permute-start | bytes 307208 | tf_op jit(solution)/shard_map/ppermute | solution.py:633
  121.8 3.9 %collective-permute-start.23 = (f32[200,128]{1,0:T(8,128)S(1)}, f32[200,128]{1,0:T(8,128)S(1)}, u32[]{:S(2)}, u32[]{:S(2)}) collective-permute-start(f32[200,128]{1,0:T(8,128)S(1)} %get-tuple-element.132), channel_id=1, source_target_pairs={{0,16},{16,0},{32,48},{48,32},{64,80},{80,64},{96,112},{112,96},{1... | collective-permute-start | bytes 307208 | tf_op jit(solution)/shard_map/ppermute | solution.py:633
  125.7 7.7 %collective-permute-start.24 = (f32[16,32,128]{2,1,0:T(8,128)S(1)}, f32[16,32,128]{2,1,0:T(8,128)S(1)}, u32[]{:S(2)}, u32[]{:S(2)}) collective-permute-start(f32[16,32,128]{2,1,0:T(8,128)S(1)} %all-to-all-done.1.mine), channel_id=1, source_target_pairs={{0,16},{16,0},{32,48},{48,32},{64,80},{80,64},{96,112},{112,96},{1... | collective-permute-start | bytes 786440 | tf_op jit(solution)/shard_map/ppermute | solution.py:750
  139.6 38.7 %copy-start.2 = (f32[128,512]{1,0:T(8,128)S(1)}, f32[128,512]{1,0:T(8,128)}, u32[]{:S(2)}) copy-start(f32[128,512]{1,0:T(8,128)} %get-tuple-element.154.z1) | copy-start | bytes 786436
  139.7 16.0 %all-to-all-start.2 = ((f32[32,1,1152]{2,1,0:T(1,128)}), f32[32,1,1152]{2,1,0:T(1,128)S(1)}, u32[]{:S(2)}, u32[]{:S(2)}) async-start(f32[32,1,1152]{2,1,0:T(1,128)} %get-tuple-element.141), calls=%async_computation.2 | async-start | bytes 294912 | tf_op jit(solution)/shard_map/all_to_all | solution.py:641
  143.8 34.5 %copy-start.1 = (f32[128,512]{1,0:T(8,128)S(1)}, f32[128,512]{1,0:T(8,128)}, u32[]{:S(2)}) copy-start(f32[128,512]{1,0:T(8,128)} %get-tuple-element.153.z0) | copy-start | bytes 786436
  143.8 8.8 %collective-permute-start.25 = (f32[128,128]{1,0:T(8,128)S(1)}, f32[128,128]{1,0:T(8,128)S(1)}, u32[]{:S(2)}, u32[]{:S(2)}) collective-permute-start(f32[128,128]{1,0:T(8,128)S(1)} %get-tuple-element.142), channel_id=1, source_target_pairs={{0,15},{1,2},{2,1},{3,4},{4,3},{5,6},{6,5},{7,8},{8,7},{9,10},{10,... | collective-permute-start | bytes 196616 | tf_op jit(solution)/shard_map/ppermute | solution.py:627
  150.6 5.0 %collective-permute-start.26 = (f32[128,128]{1,0:T(8,128)S(1)}, f32[128,128]{1,0:T(8,128)S(1)}, u32[]{:S(2)}, u32[]{:S(2)}) collective-permute-start(f32[128,128]{1,0:T(8,128)S(1)} %get-tuple-element.143), channel_id=1, source_target_pairs={{0,1},{1,0},{2,3},{3,2},{4,5},{5,4},{6,7},{7,6},{8,9},{9,8},{10,11... | collective-permute-start | bytes 196616 | tf_op jit(solution)/shard_map/ppermute | solution.py:627
  156.3 22.0 %all-to-all-start.3 = ((f32[16,1,1152]{2,1,0:T(1,128)}), f32[16,1,1152]{2,1,0:T(1,128)S(1)}, u32[]{:S(2)}, u32[]{:S(2)}) async-start(f32[16,1,1152]{2,1,0:T(1,128)} %shard_map.133), calls=%async_computation.3 | async-start | bytes 147456 | tf_op jit(solution)/shard_map/all_to_all | solution.py:641
  166.6 8.2 %collective-permute-start.27 = (f32[128,128]{1,0:T(8,128)S(1)}, f32[128,128]{1,0:T(8,128)S(1)}, u32[]{:S(2)}, u32[]{:S(2)}) collective-permute-start(f32[128,128]{1,0:T(8,128)S(1)} %get-tuple-element.151), channel_id=1, source_target_pairs={{16,32},{32,16},{48,64},{64,48},{80,96},{96,80},{112,128},{128,112... | collective-permute-start | bytes 196616 | tf_op jit(solution)/shard_map/ppermute | solution.py:633
  172.1 3.1 %collective-permute-start.28 = (f32[128,128]{1,0:T(8,128)S(1)}, f32[128,128]{1,0:T(8,128)S(1)}, u32[]{:S(2)}, u32[]{:S(2)}) collective-permute-start(f32[128,128]{1,0:T(8,128)S(1)} %get-tuple-element.152), channel_id=1, source_target_pairs={{0,16},{16,0},{32,48},{48,32},{64,80},{80,64},{96,112},{112,96},{1... | collective-permute-start | bytes 196616 | tf_op jit(solution)/shard_map/ppermute | solution.py:633

commit v11 on v9

--- a/solution.py
+++ b/solution.py
@@ -146,6 +146,12 @@
 
 def held(ref):
     return [ref[n] for n in range(ref.shape[0])]
+
+
+def averages(avg, value):
+    pick = jnp.concatenate([avg, jnp.zeros_like(avg)], axis=0).astype(BF16)
+    high, middle, low = [narrow(pick, piece, True) for piece in cut(value, 3)]
+    return ((low + middle) + high)[: avg.shape[0]]
 
 
 def schur(z, diag, couple, blocks):
@@ -278,7 +284,7 @@
     r_o[...] = r
     share_o[...] = share
     weighted = share * r
-    prim_o[...] = mm_t(avg[...], weighted)
+    prim_o[...] = averages(avg[...], weighted)
     t = jnp.concatenate([share * product(weighted, held(neumann)), share * avg[...]], axis=0)
     t_o[...] = t
     put_sends(sends, t, at)
@@ -306,7 +312,7 @@
     v_o[...] = v
     weighted = share[...] * v
     pr_o[...] = jnp.concatenate(
-        [mm_t(avg[...], weighted[:rhs]), mm_t(avg[...], weighted[rhs:])], axis=1
+        [averages(avg[...], weighted[:rhs]), averages(avg[...], weighted[rhs:])], axis=1
     )
     t = share[...] * product(weighted, held(neumann))
     t_o[...] = t
@@ -317,14 +323,15 @@
     at = Place(place)
     rhs = prim0.shape[1]
     w = assembled(q[...], (g0, g1, g2, g3), at, rhs)
+    fields = w[:rhs] - SHIFT * v[:rhs, :]
+    v2_s[0:rhs, :] = fields
+    copies = begin(v2_s.at[0:rhs], v2_o.at[0:rhs], sem.at[0], 2)
+    prim2 = averages(avg[...], share[...] * fields)
     zero = jnp.zeros((16, w.shape[1]), F32)
-    older = jnp.concatenate([v[...][:rhs], zero, v[...][rhs:], zero], axis=0)
-    v2 = w - SHIFT * older
-    v2_s[...] = v2
-    copies = begin(v2_s, v2_o, sem, 4)
-    weighted = share[...] * v2
-    prim2 = mm_t(avg[...], weighted[:rhs])
-    reach2 = mm_t(avg[...], weighted[rhs:])
+    basis = w[rhs:] - SHIFT * jnp.concatenate([zero, v[rhs:, :], zero], axis=0)
+    v2_s[rhs:, :] = basis
+    copies += begin(v2_s.at[rhs:], v2_o.at[rhs:], sem.at[1], 2)
+    reach2 = averages(avg[...], share[...] * basis)
     reach1 = prim1[...][:, rhs:]
     spare = jnp.zeros((8, LANES - reach1.shape[1] - reach2.shape[1]), F32)
     tail = jnp.concatenate([reach1, reach2, spare], axis=1)
@@ -369,11 +376,17 @@
 
 def k_fourth(place, v2, share, neumann, t_o, s0, s1, s2, s3, v2_s, t_s, sem):
     at = Place(place)
-    finish(begin(v2, v2_s, sem.at[0], 4))
-    t = share[...] * product(share[...] * v2_s[...], held(neumann))
-    t_s[...] = t
-    copies = begin(t_s, t_o, sem.at[1], 4)
-    put_sends((s0, s1, s2, s3), t, at)
+    half = v2_s.shape[0] // 16 * 8
+    bands = (slice(0, half), slice(half, v2_s.shape[0]))
+    loads = [begin(v2.at[band], v2_s.at[band], sem.at[n], 2) for n, band in enumerate(bands)]
+    copies, done = [], []
+    for n, band in enumerate(bands):
+        finish(loads[n])
+        part = share[...] * product(share[...] * v2_s[band, :], held(neumann))
+        t_s[band, :] = part
+        copies += begin(t_s.at[band], t_o.at[band], sem.at[2 + n], 2)
+        done.append(part)
+    put_sends((s0, s1, s2, s3), jnp.concatenate(done, axis=0), at)
     finish(copies)
 
 
@@ -727,13 +740,13 @@
     n = rhs + 72
     v2, pay = call(
         k_third, [(n, points), (columns, 32, LANES)], place, q1, *got, v1, share, avg, prim0, prim1,
-        raw_outs=(0,), scratch=[pltpu.VMEM((n, points), F32), dma((4,))],
+        raw_outs=(0,), scratch=[pltpu.VMEM((n, points), F32), dma((2, 2))],
     )
     got = spread(pay, "circ")
     t2, *sends = call(
         k_fourth, [(n, points)] + face(n), place, v2, share, neumann,
         raw=(0,), raw_outs=(0,),
-        scratch=[pltpu.VMEM((n, points), F32)] * 2 + [dma((2, 4))],
+        scratch=[pltpu.VMEM((n, points), F32)] * 2 + [dma((4, 2))],
         flops=500_000_000,
     )
     got, t2 = lax.optimization_barrier((got, t2))

time: 183 us -> 183 us (level)
  no operation moved by 1% of the time
where the time goes in v11:
time: 183 us; the launch traced here: 181 us
  starting transfers between devices  132 us (72%)
  Pallas kernels  27.5 us (15%)
  waiting for transfers between devices  18.3 us (10%)
    ppermute x7, starting transfers between devices, exchange_columns(): lax.ppermute(sends[0], 'circ', far)  35.2 us
    ppermute x7, starting transfers between devices, exchange_rows(): lax.ppermute(sends[2], 'axial', link)  33 us
    all_to_all x4, starting transfers between devices, spread(): lax.all_to_all(value, axis, split_axis=0, concat_axis=0, tiled=True, axis...  30.7 us
    pallas_call x13, Pallas kernels, call(): pl.pallas_call(body, out_shape=[out if isinstance(out, jax.ShapeDtypeStru...  27.5 us
    ppermute x7, starting transfers between devices, exchange_columns(): lax.ppermute(sends[1], 'circ', near)  13.4 us
    ppermute x7, starting transfers between devices, exchange_rows(): lax.ppermute(sends[3], 'axial', core)  13.4 us
    all_to_all x4, waiting for transfers between devices, spread(): lax.all_to_all(value, axis, split_axis=0, concat_axis=0, tiled=True, axis...  7.25 us
    ppermute x1, starting transfers between devices, local(): other = lax.ppermute(mine, 'axial', [(i, i ^ 1) for i in range(rows)])  6.55 us
  transfers between devices with their start and end apart: 33, of which 13 were waited for; matrix products, arithmetic and copies ran while one was open for 0% of the time, Pallas kernels for 3%

profile of v11, /device:TPU:1, one launch (start us, length us, event | category | flops | bytes accessed | tf_op | source)
XLA Modules:
  0.0 180.8 jit_solution(6275531835988694239)
XLA Ops:
  0.7 2.1 %shard_map.122 = (f32[136,512]{1,0:T(8,128)S(1)}, s32[1,512]{1,0:T(1,128)S(1)}, f32[136,128]{1,0:T(8,128)S(1)}, f32[136,128]{1,0:T(8,128)S(1)}, f32[136,128]{1,0...) custom-call(s32[3]{0:T(128)S(1)} %pad_add_fusion.place, f32[128,512]{1,0:T(8,128)} %bitcast.14, ...), custom_call_target="tpu_custom_call" | custom-call | flops 1000000 | bytes 1000000 | tf_op jit(solution)/shard_map/pallas_call | solution.py:613
  2.8 7.7 %collective-permute-start = (f32[136,128]{1,0:T(8,128)S(1)}, f32[136,128]{1,0:T(8,128)S(1)}, u32[]{:S(2)}, u32[]{:S(2)}) collective-permute-start(f32[136,128]{1,0:T(8,128)S(1)} %get-tuple-element.82), channel_id=1, source_target_pairs={{0,15},{1,2},{2,1},{3,4},{4,3},{5,6},{6,5},{7,8},{8,7},{9,10},{10,... | collective-permute-start | bytes 208904 | tf_op jit(solution)/shard_map/ppermute | solution.py:635
  10.5 1.9 %collective-permute-start.1 = (f32[136,128]{1,0:T(8,128)S(1)}, f32[136,128]{1,0:T(8,128)S(1)}, u32[]{:S(2)}, u32[]{:S(2)}) collective-permute-start(f32[136,128]{1,0:T(8,128)S(1)} %get-tuple-element.83), channel_id=1, source_target_pairs={{0,1},{1,0},{2,3},{3,2},{4,5},{5,4},{6,7},{7,6},{8,9},{9,8},{10,11... | collective-permute-start | bytes 208904 | tf_op jit(solution)/shard_map/ppermute | solution.py:635
  12.4 4.4 %collective-permute-start.2 = (f32[136,128]{1,0:T(8,128)S(1)}, f32[136,128]{1,0:T(8,128)S(1)}, u32[]{:S(2)}, u32[]{:S(2)}) collective-permute-start(f32[136,128]{1,0:T(8,128)S(1)} %get-tuple-element.84), channel_id=1, source_target_pairs={{16,32},{32,16},{48,64},{64,48},{80,96},{96,80},{112,128},{128,112... | collective-permute-start | bytes 208904 | tf_op jit(solution)/shard_map/ppermute | solution.py:641
  16.8 1.9 %collective-permute-start.3 = (f32[136,128]{1,0:T(8,128)S(1)}, f32[136,128]{1,0:T(8,128)S(1)}, u32[]{:S(2)}, u32[]{:S(2)}) collective-permute-start(f32[136,128]{1,0:T(8,128)S(1)} %get-tuple-element.85), channel_id=1, source_target_pairs={{0,16},{16,0},{32,48},{48,32},{64,80},{80,64},{96,112},{112,96},{1... | collective-permute-start | bytes 208904 | tf_op jit(solution)/shard_map/ppermute | solution.py:641
  18.8 1.7 shard_map.123
  21.6 4.4 %collective-permute-start.4 = (f32[136,128]{1,0:T(8,128)S(1)}, f32[136,128]{1,0:T(8,128)S(1)}, u32[]{:S(2)}, u32[]{:S(2)}) collective-permute-start(f32[136,128]{1,0:T(8,128)S(1)} %get-tuple-element.91), channel_id=1, source_target_pairs={{0,15},{1,2},{2,1},{3,4},{4,3},{5,6},{6,5},{7,8},{8,7},{9,10},{10,... | collective-permute-start | bytes 208904 | tf_op jit(solution)/shard_map/ppermute | solution.py:635
  26.0 1.9 %collective-permute-start.5 = (f32[136,128]{1,0:T(8,128)S(1)}, f32[136,128]{1,0:T(8,128)S(1)}, u32[]{:S(2)}, u32[]{:S(2)}) collective-permute-start(f32[136,128]{1,0:T(8,128)S(1)} %get-tuple-element.92), channel_id=1, source_target_pairs={{0,1},{1,0},{2,3},{3,2},{4,5},{5,4},{6,7},{7,6},{8,9},{9,8},{10,11... | collective-permute-start | bytes 208904 | tf_op jit(solution)/shard_map/ppermute | solution.py:635
  27.9 3.5 %collective-permute-start.6 = (f32[136,128]{1,0:T(8,128)S(1)}, f32[136,128]{1,0:T(8,128)S(1)}, u32[]{:S(2)}, u32[]{:S(2)}) collective-permute-start(f32[136,128]{1,0:T(8,128)S(1)} %get-tuple-element.93), channel_id=1, source_target_pairs={{16,32},{32,16},{48,64},{64,48},{80,96},{96,80},{112,128},{128,112... | collective-permute-start | bytes 208904 | tf_op jit(solution)/shard_map/ppermute | solution.py:641
  31.4 1.9 %collective-permute-start.7 = (f32[136,128]{1,0:T(8,128)S(1)}, f32[136,128]{1,0:T(8,128)S(1)}, u32[]{:S(2)}, u32[]{:S(2)}) collective-permute-start(f32[136,128]{1,0:T(8,128)S(1)} %get-tuple-element.94), channel_id=1, source_target_pairs={{0,16},{16,0},{32,48},{48,32},{64,80},{80,64},{96,112},{112,96},{1... | collective-permute-start | bytes 208904 | tf_op jit(solution)/shard_map/ppermute | solution.py:641
  33.3 1.5 shard_map.125
  34.8 2.1 %shard_map.126 = (f32[152,512]{1,0:T(8,128)}, f32[152,512]{1,0:T(8,128)S(1)}, f32[152,128]{1,0:T(8,128)S(1)}, f32[152,128]{1,0:T(8,128)S(1)}, f32[152,128]{1,0:T(8,128)S(1)}, /*index=5*/f32[152,128]{1,0:T(8,128)S(1)}) custom-call(s32[3]{0:T(128)S(1)} %pad_add_fusion.place, f32[136,512]{1,0:T(8,128)S(1)} %get-tuple-element.90.t, ...), custom_call_target="tpu_custom_call" | custom-call | flops 1000000 | bytes 1000000 | tf_op jit(solution)/shard_map/pallas_call | solution.py:613
  37.0 5.0 %collective-permute-start.10 = (f32[152,128]{1,0:T(8,128)S(1)}, f32[152,128]{1,0:T(8,128)S(1)}, u32[]{:S(2)}, u32[]{:S(2)}) collective-permute-start(f32[152,128]{1,0:T(8,128)S(1)} %get-tuple-element.103), channel_id=1, source_target_pairs={{0,15},{1,2},{2,1},{3,4},{4,3},{5,6},{6,5},{7,8},{8,7},{9,10},{10,... | collective-permute-start | bytes 233480 | tf_op jit(solution)/shard_map/ppermute | solution.py:635
  42.0 1.9 %collective-permute-start.11 = (f32[152,128]{1,0:T(8,128)S(1)}, f32[152,128]{1,0:T(8,128)S(1)}, u32[]{:S(2)}, u32[]{:S(2)}) collective-permute-start(f32[152,128]{1,0:T(8,128)S(1)} %get-tuple-element.104), channel_id=1, source_target_pairs={{0,1},{1,0},{2,3},{3,2},{4,5},{5,4},{6,7},{7,6},{8,9},{9,8},{10,11... | collective-permute-start | bytes 233480 | tf_op jit(solution)/shard_map/ppermute | solution.py:635
  43.9 4.2 %collective-permute-start.8 = (f32[152,128]{1,0:T(8,128)S(1)}, f32[152,128]{1,0:T(8,128)S(1)}, u32[]{:S(2)}, u32[]{:S(2)}) collective-permute-start(f32[152,128]{1,0:T(8,128)S(1)} %get-tuple-element.101), channel_id=1, source_target_pairs={{16,32},{32,16},{48,64},{64,48},{80,96},{96,80},{112,128},{128,112... | collective-permute-start | bytes 233480 | tf_op jit(solution)/shard_map/ppermute | solution.py:641
  48.1 1.9 %collective-permute-start.9 = (f32[152,128]{1,0:T(8,128)S(1)}, f32[152,128]{1,0:T(8,128)S(1)}, u32[]{:S(2)}, u32[]{:S(2)}) collective-permute-start(f32[152,128]{1,0:T(8,128)S(1)} %get-tuple-element.102), channel_id=1, source_target_pairs={{0,16},{16,0},{32,48},{48,32},{64,80},{80,64},{96,112},{112,96},{1... | collective-permute-start | bytes 233480 | tf_op jit(solution)/shard_map/ppermute | solution.py:641
  51.3 1.1 shard_map.127
  52.4 3.6 %collective-permute-start.12 = (f32[168,128]{1,0:T(8,128)S(1)}, f32[168,128]{1,0:T(8,128)S(1)}, u32[]{:S(2)}, u32[]{:S(2)}) collective-permute-start(f32[168,128]{1,0:T(8,128)S(1)} %get-tuple-element.107), channel_id=1, source_target_pairs={{0,15},{1,2},{2,1},{3,4},{4,3},{5,6},{6,5},{7,8},{8,7},{9,10},{10,... | collective-permute-start | bytes 258056 | tf_op jit(solution)/shard_map/ppermute | solution.py:635
  56.1 1.9 %collective-permute-start.13 = (f32[168,128]{1,0:T(8,128)S(1)}, f32[168,128]{1,0:T(8,128)S(1)}, u32[]{:S(2)}, u32[]{:S(2)}) collective-permute-start(f32[168,128]{1,0:T(8,128)S(1)} %get-tuple-element.108), channel_id=1, source_target_pairs={{0,1},{1,0},{2,3},{3,2},{4,5},{5,4},{6,7},{7,6},{8,9},{9,8},{10,11... | collective-permute-start | bytes 258056 | tf_op jit(solution)/shard_map/ppermute | solution.py:635
  58.0 5.1 %collective-permute-start.14 = (f32[168,128]{1,0:T(8,128)S(1)}, f32[168,128]{1,0:T(8,128)S(1)}, u32[]{:S(2)}, u32[]{:S(2)}) collective-permute-start(f32[168,128]{1,0:T(8,128)S(1)} %get-tuple-element.109), channel_id=1, source_target_pairs={{16,32},{32,16},{48,64},{64,48},{80,96},{96,80},{112,128},{128,112... | collective-permute-start | bytes 258056 | tf_op jit(solution)/shard_map/ppermute | solution.py:641
  63.1 1.9 %collective-permute-start.15 = (f32[168,128]{1,0:T(8,128)S(1)}, f32[168,128]{1,0:T(8,128)S(1)}, u32[]{:S(2)}, u32[]{:S(2)}) collective-permute-start(f32[168,128]{1,0:T(8,128)S(1)} %get-tuple-element.110), channel_id=1, source_target_pairs={{0,16},{16,0},{32,48},{48,32},{64,80},{80,64},{96,112},{112,96},{1... | collective-permute-start | bytes 258056 | tf_op jit(solution)/shard_map/ppermute | solution.py:641
  66.3 2.2 %shard_map.128 = (f32[184,512]{1,0:T(8,128)}, f32[184,512]{1,0:T(8,128)S(1)}, f32[184,128]{1,0:T(8,128)S(1)}, f32[184,128]{1,0:T(8,128)S(1)}, f32[184,128]{1,0:T(8,128)S(1)}, /*index=5*/f32[184,128]{1,0:T(8,128)S(1)}) custom-call(s32[3]{0:T(128)S(1)} %pad_add_fusion.place, f32[168,512]{1,0:T(8,128)S(1)} %get-tuple-element.106.t, ...), custom_call_target="tpu_custom_call" | custom-call | flops 1000000 | bytes 1000000 | tf_op jit(solution)/shard_map/pallas_call | solution.py:613
  68.5 5.0 %collective-permute-start.16 = (f32[184,128]{1,0:T(8,128)S(1)}, f32[184,128]{1,0:T(8,128)S(1)}, u32[]{:S(2)}, u32[]{:S(2)}) collective-permute-start(f32[184,128]{1,0:T(8,128)S(1)} %get-tuple-element.112), channel_id=1, source_target_pairs={{0,15},{1,2},{2,1},{3,4},{4,3},{5,6},{6,5},{7,8},{8,7},{9,10},{10,... | collective-permute-start | bytes 282632 | tf_op jit(solution)/shard_map/ppermute | solution.py:635
  73.5 1.9 %collective-permute-start.17 = (f32[184,128]{1,0:T(8,128)S(1)}, f32[184,128]{1,0:T(8,128)S(1)}, u32[]{:S(2)}, u32[]{:S(2)}) collective-permute-start(f32[184,128]{1,0:T(8,128)S(1)} %get-tuple-element.113), channel_id=1, source_target_pairs={{0,1},{1,0},{2,3},{3,2},{4,5},{5,4},{6,7},{7,6},{8,9},{9,8},{10,11... | collective-permute-start | bytes 282632 | tf_op jit(solution)/shard_map/ppermute | solution.py:635
  75.4 3.9 %collective-permute-start.18 = (f32[184,128]{1,0:T(8,128)S(1)}, f32[184,128]{1,0:T(8,128)S(1)}, u32[]{:S(2)}, u32[]{:S(2)}) collective-permute-start(f32[184,128]{1,0:T(8,128)S(1)} %get-tuple-element.114), channel_id=1, source_target_pairs={{16,32},{32,16},{48,64},{64,48},{80,96},{96,80},{112,128},{128,112... | collective-permute-start | bytes 282632 | tf_op jit(solution)/shard_map/ppermute | solution.py:641
  79.3 1.9 %collective-permute-start.19 = (f32[184,128]{1,0:T(8,128)S(1)}, f32[184,128]{1,0:T(8,128)S(1)}, u32[]{:S(2)}, u32[]{:S(2)}) collective-permute-start(f32[184,128]{1,0:T(8,128)S(1)} %get-tuple-element.115), channel_id=1, source_target_pairs={{0,16},{16,0},{32,48},{48,32},{64,80},{80,64},{96,112},{112,96},{1... | collective-permute-start | bytes 282632 | tf_op jit(solution)/shard_map/ppermute | solution.py:641
  82.5 2.2 %shard_map.129 = (f32[200,512]{1,0:T(8,128)}, f32[16,32,128]{2,1,0:T(8,128)}) custom-call(s32[3]{0:T(128)S(1)} %pad_add_fusion.place, f32[184,512]{1,0:T(8,128)S(1)} %get-tuple-element.111.q, f32[184,128]{1,0:T(8,128)S(1)} %collective-permute-done.16.g0, f32[184,128]{1,0:T(8,128)S(1)} %collective-permute-done.17.g1, ...), custom_call_target="tpu_custom_call" | custom-call | flops 1000000 | bytes 1000000 | tf_op jit(solution)/shard_map/pallas_call | solution.py:613
  84.7 4.8 %all-to-all-start = ((f32[16,32,128]{2,1,0:T(8,128)}), f32[16,32,128]{2,1,0:T(8,128)S(1)}, u32[]{:S(2)}, u32[]{:S(2)}) async-start(f32[16,32,128]{2,1,0:T(8,128)} %get-tuple-element.119), calls=%async_computation | async-start | bytes 524288 | tf_op jit(solution)/shard_map/all_to_all | solution.py:649
  89.4 2.9 %shard_map.130 = (f32[200,512]{1,0:T(8,128)}, f32[200,128]{1,0:T(8,128)S(1)}, f32[200,128]{1,0:T(8,128)S(1)}, f32[200,128]{1,0:T(8,128)S(1)}, f32[200,128]{1,0:T(8,128)S(1)}) custom-call(s32[3]{0:T(128)S(1)} %pad_add_fusion.place, f32[200,512]{1,0:T(8,128)} %get-tuple-element.120.v2, f32[1,512]{1,0:T(1,128)S(1)} %get-tuple-element.95.after.share, ...), custom_call_target="tpu_custom_call" | custom-call | flops 500000000 | bytes 1000000 | tf_op jit(solution)/shard_map/pallas_call | solution.py:613
  93.6 4.1 %all-to-all-done.got = f32[16,32,128]{2,1,0:T(8,128)S(1)} async-done(((f32[16,32,128]{2,1,0:T(8,128)}), f32[16,32,128]{2,1,0:T(8,128)S(1)}, u32[]{:S(2)}, u32[]{:S(2)}) %all-to-all-start) | async-done | bytes 262176 | tf_op jit(solution)/shard_map/all_to_all | solution.py:649
  98.5 11.5 %all-to-all-start.1 = ((f32[16,32,128]{2,1,0:T(8,128)}), f32[16,32,128]{2,1,0:T(8,128)S(1)}, u32[]{:S(2)}, u32[]{:S(2)}) async-start(f32[16,32,128]{2,1,0:T(8,128)} %shard_map.131), calls=%async_computation.1 | async-start | bytes 524288 | tf_op jit(solution)/shard_map/all_to_all | solution.py:649
  110.1 2.8 %collective-permute-start.20 = (f32[200,128]{1,0:T(8,128)S(1)}, f32[200,128]{1,0:T(8,128)S(1)}, u32[]{:S(2)}, u32[]{:S(2)}) collective-permute-start(f32[200,128]{1,0:T(8,128)S(1)} %copy-done.6), channel_id=1, source_target_pairs={{0,15},{1,2},{2,1},{3,4},{4,3},{5,6},{6,5},{7,8},{8,7},{9,10},{10,... | collective-permute-start | bytes 307208 | tf_op jit(solution)/shard_map/ppermute | solution.py:635
  112.9 1.9 %collective-permute-start.21 = (f32[200,128]{1,0:T(8,128)S(1)}, f32[200,128]{1,0:T(8,128)S(1)}, u32[]{:S(2)}, u32[]{:S(2)}) collective-permute-start(f32[200,128]{1,0:T(8,128)S(1)} %copy-done.4), channel_id=1, source_target_pairs={{0,1},{1,0},{2,3},{3,2},{4,5},{5,4},{6,7},{7,6},{8,9},{9,8},{10,11... | collective-permute-start | bytes 307208 | tf_op jit(solution)/shard_map/ppermute | solution.py:635
  114.8 6.6 %collective-permute-start.22 = (f32[200,128]{1,0:T(8,128)S(1)}, f32[200,128]{1,0:T(8,128)S(1)}, u32[]{:S(2)}, u32[]{:S(2)}) collective-permute-start(f32[200,128]{1,0:T(8,128)S(1)} %get-tuple-element.131), channel_id=1, source_target_pairs={{16,32},{32,16},{48,64},{64,48},{80,96},{96,80},{112,128},{128,112... | collective-permute-start | bytes 307208 | tf_op jit(solution)/shard_map/ppermute | solution.py:641
  121.4 1.9 %collective-permute-start.23 = (f32[200,128]{1,0:T(8,128)S(1)}, f32[200,128]{1,0:T(8,128)S(1)}, u32[]{:S(2)}, u32[]{:S(2)}) collective-permute-start(f32[200,128]{1,0:T(8,128)S(1)} %get-tuple-element.132), channel_id=1, source_target_pairs={{0,16},{16,0},{32,48},{48,32},{64,80},{80,64},{96,112},{112,96},{1... | collective-permute-start | bytes 307208 | tf_op jit(solution)/shard_map/ppermute | solution.py:641
  123.3 1.9 %collective-permute-done.22.g2 = f32[200,128]{1,0:T(8,128)S(1)} collective-permute-done((f32[200,128]{1,0:T(8,128)S(1)}, f32[200,128]{1,0:T(8,128)S(1)}, u32[]{:S(2)}, u32[]{:S(2)}) %collective-permute-start.22) | collective-permute-done | bytes 102432 | tf_op jit(solution)/shard_map/ppermute | solution.py:641
  125.3 6.5 %collective-permute-start.24 = (f32[16,32,128]{2,1,0:T(8,128)S(1)}, f32[16,32,128]{2,1,0:T(8,128)S(1)}, u32[]{:S(2)}, u32[]{:S(2)}) collective-permute-start(f32[16,32,128]{2,1,0:T(8,128)S(1)} %all-to-all-done.1.mine), channel_id=1, source_target_pairs={{0,16},{16,0},{32,48},{48,32},{64,80},{80,64},{96,112},{112,96},{1... | collective-permute-start | bytes 786440 | tf_op jit(solution)/shard_map/ppermute | solution.py:758
  131.8 1.1 collective-permute-done.24.other
  133.0 6.0 %shard_map.132 = (f32[128,512]{1,0:T(8,128)}, f32[128,512]{1,0:T(8,128)}, f32[128,512]{1,0:T(8,128)}, f32[128,512]{1,0:T(8,128)}, f32[128,512]{1,0:T(8,128)}, /*...) custom-call(s32[3]{0:T(128)S(1)} %pad_add_fusion.place, ...), custom_call_target="tpu_custom_call" | custom-call | flops 1000000 | bytes 1000000 | tf_op jit(solution)/shard_map/pallas_call | solution.py:613
  138.9 4.1 %all-to-all-start.2 = ((f32[32,1,1152]{2,1,0:T(1,128)}), f32[32,1,1152]{2,1,0:T(1,128)S(1)}, u32[]{:S(2)}, u32[]{:S(2)}) async-start(f32[32,1,1152]{2,1,0:T(1,128)} %get-tuple-element.141), calls=%async_computation.2 | async-start | bytes 294912 | tf_op jit(solution)/shard_map/all_to_all | solution.py:649
  143.1 6.8 %collective-permute-start.25 = (f32[128,128]{1,0:T(8,128)S(1)}, f32[128,128]{1,0:T(8,128)S(1)}, u32[]{:S(2)}, u32[]{:S(2)}) collective-permute-start(f32[128,128]{1,0:T(8,128)S(1)} %get-tuple-element.142), channel_id=1, source_target_pairs={{0,15},{1,2},{2,1},{3,4},{4,3},{5,6},{6,5},{7,8},{8,7},{9,10},{10,... | collective-permute-start | bytes 196616 | tf_op jit(solution)/shard_map/ppermute | solution.py:635
  149.9 1.9 %collective-permute-start.26 = (f32[128,128]{1,0:T(8,128)S(1)}, f32[128,128]{1,0:T(8,128)S(1)}, u32[]{:S(2)}, u32[]{:S(2)}) collective-permute-start(f32[128,128]{1,0:T(8,128)S(1)} %get-tuple-element.143), channel_id=1, source_target_pairs={{0,1},{1,0},{2,3},{3,2},{4,5},{5,4},{6,7},{7,6},{8,9},{9,8},{10,11... | collective-permute-start | bytes 196616 | tf_op jit(solution)/shard_map/ppermute | solution.py:635
  151.9 3.1 %collective-permute-done.26.g1 = f32[128,128]{1,0:T(8,128)S(1)} collective-permute-done((f32[128,128]{1,0:T(8,128)S(1)}, f32[128,128]{1,0:T(8,128)S(1)}, u32[]{:S(2)}, u32[]{:S(2)}) %collective-permute-start.26) | collective-permute-done | bytes 65568 | tf_op jit(solution)/shard_map/ppermute | solution.py:635
  155.6 10.3 %all-to-all-start.3 = ((f32[16,1,1152]{2,1,0:T(1,128)}), f32[16,1,1152]{2,1,0:T(1,128)S(1)}, u32[]{:S(2)}, u32[]{:S(2)}) async-start(f32[16,1,1152]{2,1,0:T(1,128)} %shard_map.133), calls=%async_computation.3 | async-start | bytes 147456 | tf_op jit(solution)/shard_map/all_to_all | solution.py:649
  165.9 5.4 %collective-permute-start.27 = (f32[128,128]{1,0:T(8,128)S(1)}, f32[128,128]{1,0:T(8,128)S(1)}, u32[]{:S(2)}, u32[]{:S(2)}) collective-permute-start(f32[128,128]{1,0:T(8,128)S(1)} %get-tuple-element.151), channel_id=1, source_target_pairs={{16,32},{32,16},{48,64},{64,48},{80,96},{96,80},{112,128},{128,112... | collective-permute-start | bytes 196616 | tf_op jit(solution)/shard_map/ppermute | solution.py:641
  171.4 1.9 %collective-permute-start.28 = (f32[128,128]{1,0:T(8,128)S(1)}, f32[128,128]{1,0:T(8,128)S(1)}, u32[]{:S(2)}, u32[]{:S(2)}) collective-permute-start(f32[128,128]{1,0:T(8,128)S(1)} %get-tuple-element.152), channel_id=1, source_target_pairs={{0,16},{16,0},{32,48},{48,32},{64,80},{80,64},{96,112},{112,96},{1... | collective-permute-start | bytes 196616 | tf_op jit(solution)/shard_map/ppermute | solution.py:641
  174.5 3.1 %all-to-all-done.3.got = f32[16,1,1152]{2,1,0:T(1,128)S(1)} async-done(((f32[16,1,1152]{2,1,0:T(1,128)}), f32[16,1,1152]{2,1,0:T(1,128)S(1)}, u32[]{:S(2)}, u32[]{:S(2)}) %all-to-all-start.3) | async-done | bytes 73760 | tf_op jit(solution)/shard_map/all_to_all | solution.py:649
  177.6 3.2 %shard_map.134 = (f32[128,512]{1,0:T(8,128)}, f32[128,512]{1,0:T(8,128)}) custom-call(s32[3]{0:T(128)S(1)} %pad_add_fusion.place, f32[16,1,1152]{2,1,0:T(1,128)S(1)} %all-to-all-done.3.got, f32[128,512]{1,0:T(8,128)S(1)} %get-tuple-element.148.q, f32[128,128]{1,0:T(8,128)S(1)} %collective-permute-done.25.g0, f32[128,128]{1,0:T(8,128)S(1)} %collective-permute-done.26.g1, ...), custom_call_target="tpu_custom_call" | custom-call | flops 1000000 | bytes 1000000 | tf_op jit(solution)/shard_map/pallas_call | solution.py:613
  (47 shorter events, 8.8 us)
Async XLA Ops:
  2.8 17.7 %collective-permute-start = (f32[136,128]{1,0:T(8,128)S(1)}, f32[136,128]{1,0:T(8,128)S(1)}, u32[]{:S(2)}, u32[]{:S(2)}) collective-permute-start(f32[136,128]{1,0:T(8,128)S(1)} %get-tuple-element.82), channel_id=1, source_target_pairs={{0,15},{1,2},{2,1},{3,4},{4,3},{5,6},{6,5},{7,8},{8,7},{9,10},{10,... | collective-permute-start | bytes 208904 | tf_op jit(solution)/shard_map/ppermute | solution.py:635
  10.5 10.0 %collective-permute-start.1 = (f32[136,128]{1,0:T(8,128)S(1)}, f32[136,128]{1,0:T(8,128)S(1)}, u32[]{:S(2)}, u32[]{:S(2)}) collective-permute-start(f32[136,128]{1,0:T(8,128)S(1)} %get-tuple-element.83), channel_id=1, source_target_pairs={{0,1},{1,0},{2,3},{3,2},{4,5},{5,4},{6,7},{7,6},{8,9},{9,8},{10,11... | collective-permute-start | bytes 208904 | tf_op jit(solution)/shard_map/ppermute | solution.py:635
  12.4 8.1 %collective-permute-start.2 = (f32[136,128]{1,0:T(8,128)S(1)}, f32[136,128]{1,0:T(8,128)S(1)}, u32[]{:S(2)}, u32[]{:S(2)}) collective-permute-start(f32[136,128]{1,0:T(8,128)S(1)} %get-tuple-element.84), channel_id=1, source_target_pairs={{16,32},{32,16},{48,64},{64,48},{80,96},{96,80},{112,128},{128,112... | collective-permute-start | bytes 208904 | tf_op jit(solution)/shard_map/ppermute | solution.py:641
  16.8 3.7 %collective-permute-start.3 = (f32[136,128]{1,0:T(8,128)S(1)}, f32[136,128]{1,0:T(8,128)S(1)}, u32[]{:S(2)}, u32[]{:S(2)}) collective-permute-start(f32[136,128]{1,0:T(8,128)S(1)} %get-tuple-element.85), channel_id=1, source_target_pairs={{0,16},{16,0},{32,48},{48,32},{64,80},{80,64},{96,112},{112,96},{1... | collective-permute-start | bytes 208904 | tf_op jit(solution)/shard_map/ppermute | solution.py:641
  21.6 13.2 %collective-permute-start.4 = (f32[136,128]{1,0:T(8,128)S(1)}, f32[136,128]{1,0:T(8,128)S(1)}, u32[]{:S(2)}, u32[]{:S(2)}) collective-permute-start(f32[136,128]{1,0:T(8,128)S(1)} %get-tuple-element.91), channel_id=1, source_target_pairs={{0,15},{1,2},{2,1},{3,4},{4,3},{5,6},{6,5},{7,8},{8,7},{9,10},{10,... | collective-permute-start | bytes 208904 | tf_op jit(solution)/shard_map/ppermute | solution.py:635
  26.0 8.9 %collective-permute-start.5 = (f32[136,128]{1,0:T(8,128)S(1)}, f32[136,128]{1,0:T(8,128)S(1)}, u32[]{:S(2)}, u32[]{:S(2)}) collective-permute-start(f32[136,128]{1,0:T(8,128)S(1)} %get-tuple-element.92), channel_id=1, source_target_pairs={{0,1},{1,0},{2,3},{3,2},{4,5},{5,4},{6,7},{7,6},{8,9},{9,8},{10,11... | collective-permute-start | bytes 208904 | tf_op jit(solution)/shard_map/ppermute | solution.py:635
  27.9 6.9 %collective-permute-start.6 = (f32[136,128]{1,0:T(8,128)S(1)}, f32[136,128]{1,0:T(8,128)S(1)}, u32[]{:S(2)}, u32[]{:S(2)}) collective-permute-start(f32[136,128]{1,0:T(8,128)S(1)} %get-tuple-element.93), channel_id=1, source_target_pairs={{16,32},{32,16},{48,64},{64,48},{80,96},{96,80},{112,128},{128,112... | collective-permute-start | bytes 208904 | tf_op jit(solution)/shard_map/ppermute | solution.py:641
  31.4 3.5 %collective-permute-start.7 = (f32[136,128]{1,0:T(8,128)S(1)}, f32[136,128]{1,0:T(8,128)S(1)}, u32[]{:S(2)}, u32[]{:S(2)}) collective-permute-start(f32[136,128]{1,0:T(8,128)S(1)} %get-tuple-element.94), channel_id=1, source_target_pairs={{0,16},{16,0},{32,48},{48,32},{64,80},{80,64},{96,112},{112,96},{1... | collective-permute-start | bytes 208904 | tf_op jit(solution)/shard_map/ppermute | solution.py:641
  37.0 13.1 %collective-permute-start.10 = (f32[152,128]{1,0:T(8,128)S(1)}, f32[152,128]{1,0:T(8,128)S(1)}, u32[]{:S(2)}, u32[]{:S(2)}) collective-permute-start(f32[152,128]{1,0:T(8,128)S(1)} %get-tuple-element.103), channel_id=1, source_target_pairs={{0,15},{1,2},{2,1},{3,4},{4,3},{5,6},{6,5},{7,8},{8,7},{9,10},{10,... | collective-permute-start | bytes 233480 | tf_op jit(solution)/shard_map/ppermute | solution.py:635
  42.0 8.1 %collective-permute-start.11 = (f32[152,128]{1,0:T(8,128)S(1)}, f32[152,128]{1,0:T(8,128)S(1)}, u32[]{:S(2)}, u32[]{:S(2)}) collective-permute-start(f32[152,128]{1,0:T(8,128)S(1)} %get-tuple-element.104), channel_id=1, source_target_pairs={{0,1},{1,0},{2,3},{3,2},{4,5},{5,4},{6,7},{7,6},{8,9},{9,8},{10,11... | collective-permute-start | bytes 233480 | tf_op jit(solution)/shard_map/ppermute | solution.py:635
  43.9 6.3 %collective-permute-start.8 = (f32[152,128]{1,0:T(8,128)S(1)}, f32[152,128]{1,0:T(8,128)S(1)}, u32[]{:S(2)}, u32[]{:S(2)}) collective-permute-start(f32[152,128]{1,0:T(8,128)S(1)} %get-tuple-element.101), channel_id=1, source_target_pairs={{16,32},{32,16},{48,64},{64,48},{80,96},{96,80},{112,128},{128,112... | collective-permute-start | bytes 233480 | tf_op jit(solution)/shard_map/ppermute | solution.py:641
  48.1 3.2 %collective-permute-start.9 = (f32[152,128]{1,0:T(8,128)S(1)}, f32[152,128]{1,0:T(8,128)S(1)}, u32[]{:S(2)}, u32[]{:S(2)}) collective-permute-start(f32[152,128]{1,0:T(8,128)S(1)} %get-tuple-element.102), channel_id=1, source_target_pairs={{0,16},{16,0},{32,48},{48,32},{64,80},{80,64},{96,112},{112,96},{1... | collective-permute-start | bytes 233480 | tf_op jit(solution)/shard_map/ppermute | solution.py:641
  52.4 12.6 %collective-permute-start.12 = (f32[168,128]{1,0:T(8,128)S(1)}, f32[168,128]{1,0:T(8,128)S(1)}, u32[]{:S(2)}, u32[]{:S(2)}) collective-permute-start(f32[168,128]{1,0:T(8,128)S(1)} %get-tuple-element.107), channel_id=1, source_target_pairs={{0,15},{1,2},{2,1},{3,4},{4,3},{5,6},{6,5},{7,8},{8,7},{9,10},{10,... | collective-permute-start | bytes 258056 | tf_op jit(solution)/shard_map/ppermute | solution.py:635
  56.1 8.9 %collective-permute-start.13 = (f32[168,128]{1,0:T(8,128)S(1)}, f32[168,128]{1,0:T(8,128)S(1)}, u32[]{:S(2)}, u32[]{:S(2)}) collective-permute-start(f32[168,128]{1,0:T(8,128)S(1)} %get-tuple-element.108), channel_id=1, source_target_pairs={{0,1},{1,0},{2,3},{3,2},{4,5},{5,4},{6,7},{7,6},{8,9},{9,8},{10,11... | collective-permute-start | bytes 258056 | tf_op jit(solution)/shard_map/ppermute | solution.py:635
  58.0 7.2 %collective-permute-start.14 = (f32[168,128]{1,0:T(8,128)S(1)}, f32[168,128]{1,0:T(8,128)S(1)}, u32[]{:S(2)}, u32[]{:S(2)}) collective-permute-start(f32[168,128]{1,0:T(8,128)S(1)} %get-tuple-element.109), channel_id=1, source_target_pairs={{16,32},{32,16},{48,64},{64,48},{80,96},{96,80},{112,128},{128,112... | collective-permute-start | bytes 258056 | tf_op jit(solution)/shard_map/ppermute | solution.py:641
  63.1 3.2 %collective-permute-start.15 = (f32[168,128]{1,0:T(8,128)S(1)}, f32[168,128]{1,0:T(8,128)S(1)}, u32[]{:S(2)}, u32[]{:S(2)}) collective-permute-start(f32[168,128]{1,0:T(8,128)S(1)} %get-tuple-element.110), channel_id=1, source_target_pairs={{0,16},{16,0},{32,48},{48,32},{64,80},{80,64},{96,112},{112,96},{1... | collective-permute-start | bytes 258056 | tf_op jit(solution)/shard_map/ppermute | solution.py:641
  68.5 12.7 %collective-permute-start.16 = (f32[184,128]{1,0:T(8,128)S(1)}, f32[184,128]{1,0:T(8,128)S(1)}, u32[]{:S(2)}, u32[]{:S(2)}) collective-permute-start(f32[184,128]{1,0:T(8,128)S(1)} %get-tuple-element.112), channel_id=1, source_target_pairs={{0,15},{1,2},{2,1},{3,4},{4,3},{5,6},{6,5},{7,8},{8,7},{9,10},{10,... | collective-permute-start | bytes 282632 | tf_op jit(solution)/shard_map/ppermute | solution.py:635
  73.5 7.8 %collective-permute-start.17 = (f32[184,128]{1,0:T(8,128)S(1)}, f32[184,128]{1,0:T(8,128)S(1)}, u32[]{:S(2)}, u32[]{:S(2)}) collective-permute-start(f32[184,128]{1,0:T(8,128)S(1)} %get-tuple-element.113), channel_id=1, source_target_pairs={{0,1},{1,0},{2,3},{3,2},{4,5},{5,4},{6,7},{7,6},{8,9},{9,8},{10,11... | collective-permute-start | bytes 282632 | tf_op jit(solution)/shard_map/ppermute | solution.py:635
  75.4 6.1 %collective-permute-start.18 = (f32[184,128]{1,0:T(8,128)S(1)}, f32[184,128]{1,0:T(8,128)S(1)}, u32[]{:S(2)}, u32[]{:S(2)}) collective-permute-start(f32[184,128]{1,0:T(8,128)S(1)} %get-tuple-element.114), channel_id=1, source_target_pairs={{16,32},{32,16},{48,64},{64,48},{80,96},{96,80},{112,128},{128,112... | collective-permute-start | bytes 282632 | tf_op jit(solution)/shard_map/ppermute | solution.py:641
  79.3 3.2 %collective-permute-start.19 = (f32[184,128]{1,0:T(8,128)S(1)}, f32[184,128]{1,0:T(8,128)S(1)}, u32[]{:S(2)}, u32[]{:S(2)}) collective-permute-start(f32[184,128]{1,0:T(8,128)S(1)} %get-tuple-element.115), channel_id=1, source_target_pairs={{0,16},{16,0},{32,48},{48,32},{64,80},{80,64},{96,112},{112,96},{1... | collective-permute-start | bytes 282632 | tf_op jit(solution)/shard_map/ppermute | solution.py:641
  84.7 13.1 %all-to-all-start = ((f32[16,32,128]{2,1,0:T(8,128)}), f32[16,32,128]{2,1,0:T(8,128)S(1)}, u32[]{:S(2)}, u32[]{:S(2)}) async-start(f32[16,32,128]{2,1,0:T(8,128)} %get-tuple-element.119), calls=%async_computation | async-start | bytes 524288 | tf_op jit(solution)/shard_map/all_to_all | solution.py:649
  92.3 0.6 copy-start.3
  93.0 0.6 copy-start.5
  98.5 34.4 %copy-start = (f32[152,512]{1,0:T(8,128)S(1)}, f32[152,512]{1,0:T(8,128)}, u32[]{:S(2)}) copy-start(f32[152,512]{1,0:T(8,128)} %get-tuple-element.139.z0) | copy-start | bytes 933892
  98.5 11.6 %copy-start.6 = (f32[200,128]{1,0:T(8,128)S(1)}, f32[200,128]{1,0:T(8,128)}, u32[]{:S(2)}) copy-start(f32[200,128]{1,0:T(8,128)} %copy-done.5) | copy-start | bytes 307204
  98.5 14.4 %copy-start.4 = (f32[200,128]{1,0:T(8,128)S(1)}, f32[200,128]{1,0:T(8,128)}, u32[]{:S(2)}) copy-start(f32[200,128]{1,0:T(8,128)} %copy-done.3) | copy-start | bytes 307204
  98.5 26.7 %all-to-all-start.1 = ((f32[16,32,128]{2,1,0:T(8,128)}), f32[16,32,128]{2,1,0:T(8,128)S(1)}, u32[]{:S(2)}, u32[]{:S(2)}) async-start(f32[16,32,128]{2,1,0:T(8,128)} %shard_map.131), calls=%async_computation.1 | async-start | bytes 524288 | tf_op jit(solution)/shard_map/all_to_all | solution.py:649
  110.1 13.2 %collective-permute-start.20 = (f32[200,128]{1,0:T(8,128)S(1)}, f32[200,128]{1,0:T(8,128)S(1)}, u32[]{:S(2)}, u32[]{:S(2)}) collective-permute-start(f32[200,128]{1,0:T(8,128)S(1)} %copy-done.6), channel_id=1, source_target_pairs={{0,15},{1,2},{2,1},{3,4},{4,3},{5,6},{6,5},{7,8},{8,7},{9,10},{10,... | collective-permute-start | bytes 307208 | tf_op jit(solution)/shard_map/ppermute | solution.py:635
  112.9 10.4 %collective-permute-start.21 = (f32[200,128]{1,0:T(8,128)S(1)}, f32[200,128]{1,0:T(8,128)S(1)}, u32[]{:S(2)}, u32[]{:S(2)}) collective-permute-start(f32[200,128]{1,0:T(8,128)S(1)} %copy-done.4), channel_id=1, source_target_pairs={{0,1},{1,0},{2,3},{3,2},{4,5},{5,4},{6,7},{7,6},{8,9},{9,8},{10,11... | collective-permute-start | bytes 307208 | tf_op jit(solution)/shard_map/ppermute | solution.py:635
  114.8 10.4 %collective-permute-start.22 = (f32[200,128]{1,0:T(8,128)S(1)}, f32[200,128]{1,0:T(8,128)S(1)}, u32[]{:S(2)}, u32[]{:S(2)}) collective-permute-start(f32[200,128]{1,0:T(8,128)S(1)} %get-tuple-element.131), channel_id=1, source_target_pairs={{16,32},{32,16},{48,64},{64,48},{80,96},{96,80},{112,128},{128,112... | collective-permute-start | bytes 307208 | tf_op jit(solution)/shard_map/ppermute | solution.py:641
  121.4 3.9 %collective-permute-start.23 = (f32[200,128]{1,0:T(8,128)S(1)}, f32[200,128]{1,0:T(8,128)S(1)}, u32[]{:S(2)}, u32[]{:S(2)}) collective-permute-start(f32[200,128]{1,0:T(8,128)S(1)} %get-tuple-element.132), channel_id=1, source_target_pairs={{0,16},{16,0},{32,48},{48,32},{64,80},{80,64},{96,112},{112,96},{1... | collective-permute-start | bytes 307208 | tf_op jit(solution)/shard_map/ppermute | solution.py:641
  125.3 7.7 %collective-permute-start.24 = (f32[16,32,128]{2,1,0:T(8,128)S(1)}, f32[16,32,128]{2,1,0:T(8,128)S(1)}, u32[]{:S(2)}, u32[]{:S(2)}) collective-permute-start(f32[16,32,128]{2,1,0:T(8,128)S(1)} %all-to-all-done.1.mine), channel_id=1, source_target_pairs={{0,16},{16,0},{32,48},{48,32},{64,80},{80,64},{96,112},{112,96},{1... | collective-permute-start | bytes 786440 | tf_op jit(solution)/shard_map/ppermute | solution.py:758
  138.9 38.7 %copy-start.2 = (f32[128,512]{1,0:T(8,128)S(1)}, f32[128,512]{1,0:T(8,128)}, u32[]{:S(2)}) copy-start(f32[128,512]{1,0:T(8,128)} %get-tuple-element.154.z1) | copy-start | bytes 786436
  138.9 16.0 %all-to-all-start.2 = ((f32[32,1,1152]{2,1,0:T(1,128)}), f32[32,1,1152]{2,1,0:T(1,128)S(1)}, u32[]{:S(2)}, u32[]{:S(2)}) async-start(f32[32,1,1152]{2,1,0:T(1,128)} %get-tuple-element.141), calls=%async_computation.2 | async-start | bytes 294912 | tf_op jit(solution)/shard_map/all_to_all | solution.py:649
  143.1 34.5 %copy-start.1 = (f32[128,512]{1,0:T(8,128)S(1)}, f32[128,512]{1,0:T(8,128)}, u32[]{:S(2)}) copy-start(f32[128,512]{1,0:T(8,128)} %get-tuple-element.153.z0) | copy-start | bytes 786436
  143.1 8.8 %collective-permute-start.25 = (f32[128,128]{1,0:T(8,128)S(1)}, f32[128,128]{1,0:T(8,128)S(1)}, u32[]{:S(2)}, u32[]{:S(2)}) collective-permute-start(f32[128,128]{1,0:T(8,128)S(1)} %get-tuple-element.142), channel_id=1, source_target_pairs={{0,15},{1,2},{2,1},{3,4},{4,3},{5,6},{6,5},{7,8},{8,7},{9,10},{10,... | collective-permute-start | bytes 196616 | tf_op jit(solution)/shard_map/ppermute | solution.py:635
  149.9 5.0 %collective-permute-start.26 = (f32[128,128]{1,0:T(8,128)S(1)}, f32[128,128]{1,0:T(8,128)S(1)}, u32[]{:S(2)}, u32[]{:S(2)}) collective-permute-start(f32[128,128]{1,0:T(8,128)S(1)} %get-tuple-element.143), channel_id=1, source_target_pairs={{0,1},{1,0},{2,3},{3,2},{4,5},{5,4},{6,7},{7,6},{8,9},{9,8},{10,11... | collective-permute-start | bytes 196616 | tf_op jit(solution)/shard_map/ppermute | solution.py:635
  155.6 22.0 %all-to-all-start.3 = ((f32[16,1,1152]{2,1,0:T(1,128)}), f32[16,1,1152]{2,1,0:T(1,128)S(1)}, u32[]{:S(2)}, u32[]{:S(2)}) async-start(f32[16,1,1152]{2,1,0:T(1,128)} %shard_map.133), calls=%async_computation.3 | async-start | bytes 147456 | tf_op jit(solution)/shard_map/all_to_all | solution.py:649
  165.9 8.2 %collective-permute-start.27 = (f32[128,128]{1,0:T(8,128)S(1)}, f32[128,128]{1,0:T(8,128)S(1)}, u32[]{:S(2)}, u32[]{:S(2)}) collective-permute-start(f32[128,128]{1,0:T(8,128)S(1)} %get-tuple-element.151), channel_id=1, source_target_pairs={{16,32},{32,16},{48,64},{64,48},{80,96},{96,80},{112,128},{128,112... | collective-permute-start | bytes 196616 | tf_op jit(solution)/shard_map/ppermute | solution.py:641
  171.4 3.1 %collective-permute-start.28 = (f32[128,128]{1,0:T(8,128)S(1)}, f32[128,128]{1,0:T(8,128)S(1)}, u32[]{:S(2)}, u32[]{:S(2)}) collective-permute-start(f32[128,128]{1,0:T(8,128)S(1)} %get-tuple-element.152), channel_id=1, source_target_pairs={{0,16},{16,0},{32,48},{48,32},{64,80},{80,64},{96,112},{112,96},{1... | collective-permute-start | bytes 196616 | tf_op jit(solution)/shard_map/ppermute | solution.py:641

commit v12 on v11

--- a/solution.py
+++ b/solution.py
@@ -629,10 +629,13 @@
     )(*args)
 
 
-def exchange_columns(sends, columns):
-    near = [(i, i ^ 1) for i in range(columns)]
+def exchange_far(sends, columns):
     far = [(i, (i + 1 if i % 2 else i - 1) % columns) for i in range(columns)]
-    return [lax.ppermute(sends[0], "circ", far), lax.ppermute(sends[1], "circ", near)]
+    return [lax.ppermute(sends[0], "circ", far)]
+
+
+def exchange_near(sends, columns):
+    return [lax.ppermute(sends[1], "circ", [(i, i ^ 1) for i in range(columns)])]
 
 
 def exchange_rows(sends, rows):
@@ -642,7 +645,7 @@
 
 
 def exchange(sends, rows, columns):
-    return exchange_columns(sends, columns) + exchange_rows(sends, rows)
+    return exchange_far(sends, columns) + exchange_near(sends, columns) + exchange_rows(sends, rows)
 
 
 def spread(value, axis, groups=None):
@@ -774,13 +777,13 @@
         for pair in range(0, rows, 2)
     ]
     dots = spread(pay, ("axial", "circ"), chips)
-    got = exchange_columns(sends, columns)
+    got = exchange_far(sends, columns)
     dots, *got = lax.optimization_barrier((dots, *got))
     blank = jnp.zeros((1, 9 * LANES), F32)
     (pay,) = call(k_sum_spread, [(rows // 2, 1, 9 * LANES)], None, dots, blank)
     pay, *sends = lax.optimization_barrier((pay, *sends))
     dots = spread(pay, "axial", along)
-    got = got + exchange_rows(sends, rows)
+    got = got + exchange_near(sends, columns) + exchange_rows(sends, rows)
     x, r = call(
         k_final, [(rhs, points)] * 2,
         place, dots, q2, *got, order, r0, z0f, z1f, z2f, w0f, w1f,

time: 183 us -> 180 us (0.984)
  waiting for transfers between devices: 18.3 us -> 15.7 us
where the time goes in v12:
time: 180 us; the launch traced here: 178 us
  starting transfers between devices  132 us (73%)
  Pallas kernels  27.5 us (15%)
  waiting for transfers between devices  15.7 us (9%)
    ppermute x7, starting transfers between devices, exchange_far(): return [lax.ppermute(sends[0], 'circ', far)]  35.2 us
    ppermute x7, starting transfers between devices, exchange_rows(): lax.ppermute(sends[2], 'axial', link)  32.3 us
    all_to_all x4, starting transfers between devices, spread(): lax.all_to_all(value, axis, split_axis=0, concat_axis=0, tiled=True, axis...  31.1 us
    pallas_call x13, Pallas kernels, call(): pl.pallas_call(body, out_shape=[out if isinstance(out, jax.ShapeDtypeStru...  27.5 us
    ppermute x7, starting transfers between devices, exchange_rows(): lax.ppermute(sends[3], 'axial', core)  13.4 us
    ppermute x7, starting transfers between devices, exchange_near(): lax.ppermute(sends[1], 'circ', [(i, i ^ 1) for i in range(columns)])  13.4 us
    ppermute x1, starting transfers between devices, local(): other = lax.ppermute(mine, 'axial', [(i, i ^ 1) for i in range(rows)])  6.55 us
    all_to_all x4, waiting for transfers between devices, spread(): lax.all_to_all(value, axis, split_axis=0, concat_axis=0, tiled=True, axis...  6.04 us
  transfers between devices with their start and end apart: 33, of which 13 were waited for; matrix products, arithmetic and copies ran while one was open for 0% of the time, Pallas kernels for 3%

profile of v12, /device:TPU:1, one launch (start us, length us, event | category | flops | bytes accessed | tf_op | source)
XLA Modules:
  0.0 177.8 jit_solution(16330831805124207438)
XLA Ops:
  0.7 2.1 %shard_map.122 = (f32[136,512]{1,0:T(8,128)S(1)}, s32[1,512]{1,0:T(1,128)S(1)}, f32[136,128]{1,0:T(8,128)S(1)}, f32[136,128]{1,0:T(8,128)S(1)}, f32[136,128]{1,0...) custom-call(s32[3]{0:T(128)S(1)} %pad_add_fusion.place, f32[128,512]{1,0:T(8,128)} %bitcast.14, ...), custom_call_target="tpu_custom_call" | custom-call | flops 1000000 | bytes 1000000 | tf_op jit(solution)/shard_map/pallas_call | solution.py:613
  2.8 7.7 %collective-permute-start = (f32[136,128]{1,0:T(8,128)S(1)}, f32[136,128]{1,0:T(8,128)S(1)}, u32[]{:S(2)}, u32[]{:S(2)}) collective-permute-start(f32[136,128]{1,0:T(8,128)S(1)} %get-tuple-element.82), channel_id=1, source_target_pairs={{0,15},{1,2},{2,1},{3,4},{4,3},{5,6},{6,5},{7,8},{8,7},{9,10},{10,... | collective-permute-start | bytes 208904 | tf_op jit(solution)/shard_map/ppermute | solution.py:634
  10.5 1.9 %collective-permute-start.1 = (f32[136,128]{1,0:T(8,128)S(1)}, f32[136,128]{1,0:T(8,128)S(1)}, u32[]{:S(2)}, u32[]{:S(2)}) collective-permute-start(f32[136,128]{1,0:T(8,128)S(1)} %get-tuple-element.83), channel_id=1, source_target_pairs={{0,1},{1,0},{2,3},{3,2},{4,5},{5,4},{6,7},{7,6},{8,9},{9,8},{10,11... | collective-permute-start | bytes 208904 | tf_op jit(solution)/shard_map/ppermute | solution.py:638
  12.4 4.4 %collective-permute-start.2 = (f32[136,128]{1,0:T(8,128)S(1)}, f32[136,128]{1,0:T(8,128)S(1)}, u32[]{:S(2)}, u32[]{:S(2)}) collective-permute-start(f32[136,128]{1,0:T(8,128)S(1)} %get-tuple-element.84), channel_id=1, source_target_pairs={{16,32},{32,16},{48,64},{64,48},{80,96},{96,80},{112,128},{128,112... | collective-permute-start | bytes 208904 | tf_op jit(solution)/shard_map/ppermute | solution.py:644
  16.8 1.9 %collective-permute-start.3 = (f32[136,128]{1,0:T(8,128)S(1)}, f32[136,128]{1,0:T(8,128)S(1)}, u32[]{:S(2)}, u32[]{:S(2)}) collective-permute-start(f32[136,128]{1,0:T(8,128)S(1)} %get-tuple-element.85), channel_id=1, source_target_pairs={{0,16},{16,0},{32,48},{48,32},{64,80},{80,64},{96,112},{112,96},{1... | collective-permute-start | bytes 208904 | tf_op jit(solution)/shard_map/ppermute | solution.py:644
  18.8 1.7 shard_map.123
  21.6 4.4 %collective-permute-start.4 = (f32[136,128]{1,0:T(8,128)S(1)}, f32[136,128]{1,0:T(8,128)S(1)}, u32[]{:S(2)}, u32[]{:S(2)}) collective-permute-start(f32[136,128]{1,0:T(8,128)S(1)} %get-tuple-element.91), channel_id=1, source_target_pairs={{0,15},{1,2},{2,1},{3,4},{4,3},{5,6},{6,5},{7,8},{8,7},{9,10},{10,... | collective-permute-start | bytes 208904 | tf_op jit(solution)/shard_map/ppermute | solution.py:634
  26.0 1.9 %collective-permute-start.5 = (f32[136,128]{1,0:T(8,128)S(1)}, f32[136,128]{1,0:T(8,128)S(1)}, u32[]{:S(2)}, u32[]{:S(2)}) collective-permute-start(f32[136,128]{1,0:T(8,128)S(1)} %get-tuple-element.92), channel_id=1, source_target_pairs={{0,1},{1,0},{2,3},{3,2},{4,5},{5,4},{6,7},{7,6},{8,9},{9,8},{10,11... | collective-permute-start | bytes 208904 | tf_op jit(solution)/shard_map/ppermute | solution.py:638
  27.9 3.5 %collective-permute-start.6 = (f32[136,128]{1,0:T(8,128)S(1)}, f32[136,128]{1,0:T(8,128)S(1)}, u32[]{:S(2)}, u32[]{:S(2)}) collective-permute-start(f32[136,128]{1,0:T(8,128)S(1)} %get-tuple-element.93), channel_id=1, source_target_pairs={{16,32},{32,16},{48,64},{64,48},{80,96},{96,80},{112,128},{128,112... | collective-permute-start | bytes 208904 | tf_op jit(solution)/shard_map/ppermute | solution.py:644
  31.4 1.9 %collective-permute-start.7 = (f32[136,128]{1,0:T(8,128)S(1)}, f32[136,128]{1,0:T(8,128)S(1)}, u32[]{:S(2)}, u32[]{:S(2)}) collective-permute-start(f32[136,128]{1,0:T(8,128)S(1)} %get-tuple-element.94), channel_id=1, source_target_pairs={{0,16},{16,0},{32,48},{48,32},{64,80},{80,64},{96,112},{112,96},{1... | collective-permute-start | bytes 208904 | tf_op jit(solution)/shard_map/ppermute | solution.py:644
  33.3 1.5 shard_map.125
  34.8 2.1 %shard_map.126 = (f32[152,512]{1,0:T(8,128)}, f32[152,512]{1,0:T(8,128)S(1)}, f32[152,128]{1,0:T(8,128)S(1)}, f32[152,128]{1,0:T(8,128)S(1)}, f32[152,128]{1,0:T(8,128)S(1)}, /*index=5*/f32[152,128]{1,0:T(8,128)S(1)}) custom-call(s32[3]{0:T(128)S(1)} %pad_add_fusion.place, f32[136,512]{1,0:T(8,128)S(1)} %get-tuple-element.90.t, ...), custom_call_target="tpu_custom_call" | custom-call | flops 1000000 | bytes 1000000 | tf_op jit(solution)/shard_map/pallas_call | solution.py:613
  37.0 5.0 %collective-permute-start.10 = (f32[152,128]{1,0:T(8,128)S(1)}, f32[152,128]{1,0:T(8,128)S(1)}, u32[]{:S(2)}, u32[]{:S(2)}) collective-permute-start(f32[152,128]{1,0:T(8,128)S(1)} %get-tuple-element.103), channel_id=1, source_target_pairs={{0,15},{1,2},{2,1},{3,4},{4,3},{5,6},{6,5},{7,8},{8,7},{9,10},{10,... | collective-permute-start | bytes 233480 | tf_op jit(solution)/shard_map/ppermute | solution.py:634
  42.0 1.9 %collective-permute-start.11 = (f32[152,128]{1,0:T(8,128)S(1)}, f32[152,128]{1,0:T(8,128)S(1)}, u32[]{:S(2)}, u32[]{:S(2)}) collective-permute-start(f32[152,128]{1,0:T(8,128)S(1)} %get-tuple-element.104), channel_id=1, source_target_pairs={{0,1},{1,0},{2,3},{3,2},{4,5},{5,4},{6,7},{7,6},{8,9},{9,8},{10,11... | collective-permute-start | bytes 233480 | tf_op jit(solution)/shard_map/ppermute | solution.py:638
  43.9 4.2 %collective-permute-start.8 = (f32[152,128]{1,0:T(8,128)S(1)}, f32[152,128]{1,0:T(8,128)S(1)}, u32[]{:S(2)}, u32[]{:S(2)}) collective-permute-start(f32[152,128]{1,0:T(8,128)S(1)} %get-tuple-element.101), channel_id=1, source_target_pairs={{16,32},{32,16},{48,64},{64,48},{80,96},{96,80},{112,128},{128,112... | collective-permute-start | bytes 233480 | tf_op jit(solution)/shard_map/ppermute | solution.py:644
  48.1 1.9 %collective-permute-start.9 = (f32[152,128]{1,0:T(8,128)S(1)}, f32[152,128]{1,0:T(8,128)S(1)}, u32[]{:S(2)}, u32[]{:S(2)}) collective-permute-start(f32[152,128]{1,0:T(8,128)S(1)} %get-tuple-element.102), channel_id=1, source_target_pairs={{0,16},{16,0},{32,48},{48,32},{64,80},{80,64},{96,112},{112,96},{1... | collective-permute-start | bytes 233480 | tf_op jit(solution)/shard_map/ppermute | solution.py:644
  51.3 1.1 shard_map.127
  52.4 3.6 %collective-permute-start.12 = (f32[168,128]{1,0:T(8,128)S(1)}, f32[168,128]{1,0:T(8,128)S(1)}, u32[]{:S(2)}, u32[]{:S(2)}) collective-permute-start(f32[168,128]{1,0:T(8,128)S(1)} %get-tuple-element.107), channel_id=1, source_target_pairs={{0,15},{1,2},{2,1},{3,4},{4,3},{5,6},{6,5},{7,8},{8,7},{9,10},{10,... | collective-permute-start | bytes 258056 | tf_op jit(solution)/shard_map/ppermute | solution.py:634
  56.1 1.9 %collective-permute-start.13 = (f32[168,128]{1,0:T(8,128)S(1)}, f32[168,128]{1,0:T(8,128)S(1)}, u32[]{:S(2)}, u32[]{:S(2)}) collective-permute-start(f32[168,128]{1,0:T(8,128)S(1)} %get-tuple-element.108), channel_id=1, source_target_pairs={{0,1},{1,0},{2,3},{3,2},{4,5},{5,4},{6,7},{7,6},{8,9},{9,8},{10,11... | collective-permute-start | bytes 258056 | tf_op jit(solution)/shard_map/ppermute | solution.py:638
  58.0 5.1 %collective-permute-start.14 = (f32[168,128]{1,0:T(8,128)S(1)}, f32[168,128]{1,0:T(8,128)S(1)}, u32[]{:S(2)}, u32[]{:S(2)}) collective-permute-start(f32[168,128]{1,0:T(8,128)S(1)} %get-tuple-element.109), channel_id=1, source_target_pairs={{16,32},{32,16},{48,64},{64,48},{80,96},{96,80},{112,128},{128,112... | collective-permute-start | bytes 258056 | tf_op jit(solution)/shard_map/ppermute | solution.py:644
  63.1 1.9 %collective-permute-start.15 = (f32[168,128]{1,0:T(8,128)S(1)}, f32[168,128]{1,0:T(8,128)S(1)}, u32[]{:S(2)}, u32[]{:S(2)}) collective-permute-start(f32[168,128]{1,0:T(8,128)S(1)} %get-tuple-element.110), channel_id=1, source_target_pairs={{0,16},{16,0},{32,48},{48,32},{64,80},{80,64},{96,112},{112,96},{1... | collective-permute-start | bytes 258056 | tf_op jit(solution)/shard_map/ppermute | solution.py:644
  66.3 2.2 %shard_map.128 = (f32[184,512]{1,0:T(8,128)}, f32[184,512]{1,0:T(8,128)S(1)}, f32[184,128]{1,0:T(8,128)S(1)}, f32[184,128]{1,0:T(8,128)S(1)}, f32[184,128]{1,0:T(8,128)S(1)}, /*index=5*/f32[184,128]{1,0:T(8,128)S(1)}) custom-call(s32[3]{0:T(128)S(1)} %pad_add_fusion.place, f32[168,512]{1,0:T(8,128)S(1)} %get-tuple-element.106.t, ...), custom_call_target="tpu_custom_call" | custom-call | flops 1000000 | bytes 1000000 | tf_op jit(solution)/shard_map/pallas_call | solution.py:613
  68.5 5.0 %collective-permute-start.16 = (f32[184,128]{1,0:T(8,128)S(1)}, f32[184,128]{1,0:T(8,128)S(1)}, u32[]{:S(2)}, u32[]{:S(2)}) collective-permute-start(f32[184,128]{1,0:T(8,128)S(1)} %get-tuple-element.112), channel_id=1, source_target_pairs={{0,15},{1,2},{2,1},{3,4},{4,3},{5,6},{6,5},{7,8},{8,7},{9,10},{10,... | collective-permute-start | bytes 282632 | tf_op jit(solution)/shard_map/ppermute | solution.py:634
  73.5 1.9 %collective-permute-start.17 = (f32[184,128]{1,0:T(8,128)S(1)}, f32[184,128]{1,0:T(8,128)S(1)}, u32[]{:S(2)}, u32[]{:S(2)}) collective-permute-start(f32[184,128]{1,0:T(8,128)S(1)} %get-tuple-element.113), channel_id=1, source_target_pairs={{0,1},{1,0},{2,3},{3,2},{4,5},{5,4},{6,7},{7,6},{8,9},{9,8},{10,11... | collective-permute-start | bytes 282632 | tf_op jit(solution)/shard_map/ppermute | solution.py:638
  75.4 3.9 %collective-permute-start.18 = (f32[184,128]{1,0:T(8,128)S(1)}, f32[184,128]{1,0:T(8,128)S(1)}, u32[]{:S(2)}, u32[]{:S(2)}) collective-permute-start(f32[184,128]{1,0:T(8,128)S(1)} %get-tuple-element.114), channel_id=1, source_target_pairs={{16,32},{32,16},{48,64},{64,48},{80,96},{96,80},{112,128},{128,112... | collective-permute-start | bytes 282632 | tf_op jit(solution)/shard_map/ppermute | solution.py:644
  79.3 1.9 %collective-permute-start.19 = (f32[184,128]{1,0:T(8,128)S(1)}, f32[184,128]{1,0:T(8,128)S(1)}, u32[]{:S(2)}, u32[]{:S(2)}) collective-permute-start(f32[184,128]{1,0:T(8,128)S(1)} %get-tuple-element.115), channel_id=1, source_target_pairs={{0,16},{16,0},{32,48},{48,32},{64,80},{80,64},{96,112},{112,96},{1... | collective-permute-start | bytes 282632 | tf_op jit(solution)/shard_map/ppermute | solution.py:644
  82.5 2.2 %shard_map.129 = (f32[200,512]{1,0:T(8,128)}, f32[16,32,128]{2,1,0:T(8,128)}) custom-call(s32[3]{0:T(128)S(1)} %pad_add_fusion.place, f32[184,512]{1,0:T(8,128)S(1)} %get-tuple-element.111.q, f32[184,128]{1,0:T(8,128)S(1)} %collective-permute-done.16.g0, f32[184,128]{1,0:T(8,128)S(1)} %collective-permute-done.17.g1, ...), custom_call_target="tpu_custom_call" | custom-call | flops 1000000 | bytes 1000000 | tf_op jit(solution)/shard_map/pallas_call | solution.py:613
  84.7 4.8 %all-to-all-start = ((f32[16,32,128]{2,1,0:T(8,128)}), f32[16,32,128]{2,1,0:T(8,128)S(1)}, u32[]{:S(2)}, u32[]{:S(2)}) async-start(f32[16,32,128]{2,1,0:T(8,128)} %get-tuple-element.119), calls=%async_computation | async-start | bytes 524288 | tf_op jit(solution)/shard_map/all_to_all | solution.py:652
  89.4 2.9 %shard_map.130 = (f32[200,512]{1,0:T(8,128)}, f32[200,128]{1,0:T(8,128)S(1)}, f32[200,128]{1,0:T(8,128)S(1)}, f32[200,128]{1,0:T(8,128)S(1)}, f32[200,128]{1,0:T(8,128)S(1)}) custom-call(s32[3]{0:T(128)S(1)} %pad_add_fusion.place, f32[200,512]{1,0:T(8,128)} %get-tuple-element.120.v2, f32[1,512]{1,0:T(1,128)S(1)} %get-tuple-element.95.after.share, ...), custom_call_target="tpu_custom_call" | custom-call | flops 500000000 | bytes 1000000 | tf_op jit(solution)/shard_map/pallas_call | solution.py:613
  93.6 4.1 %all-to-all-done.got = f32[16,32,128]{2,1,0:T(8,128)S(1)} async-done(((f32[16,32,128]{2,1,0:T(8,128)}), f32[16,32,128]{2,1,0:T(8,128)S(1)}, u32[]{:S(2)}, u32[]{:S(2)}) %all-to-all-start) | async-done | bytes 262176 | tf_op jit(solution)/shard_map/all_to_all | solution.py:652
  98.5 11.5 %all-to-all-start.1 = ((f32[16,32,128]{2,1,0:T(8,128)}), f32[16,32,128]{2,1,0:T(8,128)S(1)}, u32[]{:S(2)}, u32[]{:S(2)}) async-start(f32[16,32,128]{2,1,0:T(8,128)} %shard_map.131), calls=%async_computation.1 | async-start | bytes 524288 | tf_op jit(solution)/shard_map/all_to_all | solution.py:652
  110.1 2.8 %collective-permute-start.20 = (f32[200,128]{1,0:T(8,128)S(1)}, f32[200,128]{1,0:T(8,128)S(1)}, u32[]{:S(2)}, u32[]{:S(2)}) collective-permute-start(f32[200,128]{1,0:T(8,128)S(1)} %copy-done.6), channel_id=1, source_target_pairs={{0,15},{1,2},{2,1},{3,4},{4,3},{5,6},{6,5},{7,8},{8,7},{9,10},{10,... | collective-permute-start | bytes 307208 | tf_op jit(solution)/shard_map/ppermute | solution.py:634
  112.9 1.9 %collective-permute-start.21 = (f32[200,128]{1,0:T(8,128)S(1)}, f32[200,128]{1,0:T(8,128)S(1)}, u32[]{:S(2)}, u32[]{:S(2)}) collective-permute-start(f32[200,128]{1,0:T(8,128)S(1)} %copy-done.4), channel_id=1, source_target_pairs={{0,1},{1,0},{2,3},{3,2},{4,5},{5,4},{6,7},{7,6},{8,9},{9,8},{10,11... | collective-permute-start | bytes 307208 | tf_op jit(solution)/shard_map/ppermute | solution.py:638
  114.8 6.6 %collective-permute-start.22 = (f32[200,128]{1,0:T(8,128)S(1)}, f32[200,128]{1,0:T(8,128)S(1)}, u32[]{:S(2)}, u32[]{:S(2)}) collective-permute-start(f32[200,128]{1,0:T(8,128)S(1)} %get-tuple-element.131), channel_id=1, source_target_pairs={{16,32},{32,16},{48,64},{64,48},{80,96},{96,80},{112,128},{128,112... | collective-permute-start | bytes 307208 | tf_op jit(solution)/shard_map/ppermute | solution.py:644
  121.4 1.9 %collective-permute-start.23 = (f32[200,128]{1,0:T(8,128)S(1)}, f32[200,128]{1,0:T(8,128)S(1)}, u32[]{:S(2)}, u32[]{:S(2)}) collective-permute-start(f32[200,128]{1,0:T(8,128)S(1)} %get-tuple-element.132), channel_id=1, source_target_pairs={{0,16},{16,0},{32,48},{48,32},{64,80},{80,64},{96,112},{112,96},{1... | collective-permute-start | bytes 307208 | tf_op jit(solution)/shard_map/ppermute | solution.py:644
  123.3 1.9 %collective-permute-done.22.g2 = f32[200,128]{1,0:T(8,128)S(1)} collective-permute-done((f32[200,128]{1,0:T(8,128)S(1)}, f32[200,128]{1,0:T(8,128)S(1)}, u32[]{:S(2)}, u32[]{:S(2)}) %collective-permute-start.22) | collective-permute-done | bytes 102432 | tf_op jit(solution)/shard_map/ppermute | solution.py:644
  125.3 6.5 %collective-permute-start.24 = (f32[16,32,128]{2,1,0:T(8,128)S(1)}, f32[16,32,128]{2,1,0:T(8,128)S(1)}, u32[]{:S(2)}, u32[]{:S(2)}) collective-permute-start(f32[16,32,128]{2,1,0:T(8,128)S(1)} %all-to-all-done.1.mine), channel_id=1, source_target_pairs={{0,16},{16,0},{32,48},{48,32},{64,80},{80,64},{96,112},{112,96},{1... | collective-permute-start | bytes 786440 | tf_op jit(solution)/shard_map/ppermute | solution.py:761
  131.8 1.1 collective-permute-done.24.other
  133.0 6.0 %shard_map.132 = (f32[128,512]{1,0:T(8,128)}, f32[128,512]{1,0:T(8,128)}, f32[128,512]{1,0:T(8,128)}, f32[128,512]{1,0:T(8,128)}, f32[128,512]{1,0:T(8,128)}, /*...) custom-call(s32[3]{0:T(128)S(1)} %pad_add_fusion.place, ...), custom_call_target="tpu_custom_call" | custom-call | flops 1000000 | bytes 1000000 | tf_op jit(solution)/shard_map/pallas_call | solution.py:613
  138.9 4.1 %all-to-all-start.2 = ((f32[32,1,1152]{2,1,0:T(1,128)}), f32[32,1,1152]{2,1,0:T(1,128)S(1)}, u32[]{:S(2)}, u32[]{:S(2)}) async-start(f32[32,1,1152]{2,1,0:T(1,128)} %get-tuple-element.141), calls=%async_computation.2 | async-start | bytes 294912 | tf_op jit(solution)/shard_map/all_to_all | solution.py:652
  143.1 6.8 %collective-permute-start.25 = (f32[128,128]{1,0:T(8,128)S(1)}, f32[128,128]{1,0:T(8,128)S(1)}, u32[]{:S(2)}, u32[]{:S(2)}) collective-permute-start(f32[128,128]{1,0:T(8,128)S(1)} %get-tuple-element.142), channel_id=1, source_target_pairs={{0,15},{1,2},{2,1},{3,4},{4,3},{5,6},{6,5},{7,8},{8,7},{9,10},{10,... | collective-permute-start | bytes 196616 | tf_op jit(solution)/shard_map/ppermute | solution.py:634
  149.9 1.6 collective-permute-done.25.g0
  152.2 10.7 %all-to-all-start.3 = ((f32[16,1,1152]{2,1,0:T(1,128)}), f32[16,1,1152]{2,1,0:T(1,128)S(1)}, u32[]{:S(2)}, u32[]{:S(2)}) async-start(f32[16,1,1152]{2,1,0:T(1,128)} %shard_map.133), calls=%async_computation.3 | async-start | bytes 147456 | tf_op jit(solution)/shard_map/all_to_all | solution.py:652
  162.9 1.9 %collective-permute-start.26 = (f32[128,128]{1,0:T(8,128)S(1)}, f32[128,128]{1,0:T(8,128)S(1)}, u32[]{:S(2)}, u32[]{:S(2)}) collective-permute-start(f32[128,128]{1,0:T(8,128)S(1)} %get-tuple-element.150), channel_id=1, source_target_pairs={{0,1},{1,0},{2,3},{3,2},{4,5},{5,4},{6,7},{7,6},{8,9},{9,8},{10,11... | collective-permute-start | bytes 196616 | tf_op jit(solution)/shard_map/ppermute | solution.py:638
  164.8 4.7 %collective-permute-start.27 = (f32[128,128]{1,0:T(8,128)S(1)}, f32[128,128]{1,0:T(8,128)S(1)}, u32[]{:S(2)}, u32[]{:S(2)}) collective-permute-start(f32[128,128]{1,0:T(8,128)S(1)} %get-tuple-element.151), channel_id=1, source_target_pairs={{16,32},{32,16},{48,64},{64,48},{80,96},{96,80},{112,128},{128,112... | collective-permute-start | bytes 196616 | tf_op jit(solution)/shard_map/ppermute | solution.py:644
  169.6 1.9 %collective-permute-start.28 = (f32[128,128]{1,0:T(8,128)S(1)}, f32[128,128]{1,0:T(8,128)S(1)}, u32[]{:S(2)}, u32[]{:S(2)}) collective-permute-start(f32[128,128]{1,0:T(8,128)S(1)} %get-tuple-element.152), channel_id=1, source_target_pairs={{0,16},{16,0},{32,48},{48,32},{64,80},{80,64},{96,112},{112,96},{1... | collective-permute-start | bytes 196616 | tf_op jit(solution)/shard_map/ppermute | solution.py:644
  172.7 1.9 %all-to-all-done.3.got = f32[16,1,1152]{2,1,0:T(1,128)S(1)} async-done(((f32[16,1,1152]{2,1,0:T(1,128)}), f32[16,1,1152]{2,1,0:T(1,128)S(1)}, u32[]{:S(2)}, u32[]{:S(2)}) %all-to-all-start.3) | async-done | bytes 73760 | tf_op jit(solution)/shard_map/all_to_all | solution.py:652
  174.6 3.2 %shard_map.134 = (f32[128,512]{1,0:T(8,128)}, f32[128,512]{1,0:T(8,128)}) custom-call(s32[3]{0:T(128)S(1)} %pad_add_fusion.place, f32[16,1,1152]{2,1,0:T(1,128)S(1)} %all-to-all-done.3.got, f32[128,512]{1,0:T(8,128)S(1)} %get-tuple-element.148.q, f32[128,128]{1,0:T(8,128)S(1)} %collective-permute-done.25.g0, f32[128,128]{1,0:T(8,128)S(1)} %collective-permute-done.26.g1, ...), custom_call_target="tpu_custom_call" | custom-call | flops 1000000 | bytes 1000000 | tf_op jit(solution)/shard_map/pallas_call | solution.py:613
  (47 shorter events, 8.8 us)
Async XLA Ops:
  2.8 17.7 %collective-permute-start = (f32[136,128]{1,0:T(8,128)S(1)}, f32[136,128]{1,0:T(8,128)S(1)}, u32[]{:S(2)}, u32[]{:S(2)}) collective-permute-start(f32[136,128]{1,0:T(8,128)S(1)} %get-tuple-element.82), channel_id=1, source_target_pairs={{0,15},{1,2},{2,1},{3,4},{4,3},{5,6},{6,5},{7,8},{8,7},{9,10},{10,... | collective-permute-start | bytes 208904 | tf_op jit(solution)/shard_map/ppermute | solution.py:634
  10.5 10.0 %collective-permute-start.1 = (f32[136,128]{1,0:T(8,128)S(1)}, f32[136,128]{1,0:T(8,128)S(1)}, u32[]{:S(2)}, u32[]{:S(2)}) collective-permute-start(f32[136,128]{1,0:T(8,128)S(1)} %get-tuple-element.83), channel_id=1, source_target_pairs={{0,1},{1,0},{2,3},{3,2},{4,5},{5,4},{6,7},{7,6},{8,9},{9,8},{10,11... | collective-permute-start | bytes 208904 | tf_op jit(solution)/shard_map/ppermute | solution.py:638
  12.4 8.1 %collective-permute-start.2 = (f32[136,128]{1,0:T(8,128)S(1)}, f32[136,128]{1,0:T(8,128)S(1)}, u32[]{:S(2)}, u32[]{:S(2)}) collective-permute-start(f32[136,128]{1,0:T(8,128)S(1)} %get-tuple-element.84), channel_id=1, source_target_pairs={{16,32},{32,16},{48,64},{64,48},{80,96},{96,80},{112,128},{128,112... | collective-permute-start | bytes 208904 | tf_op jit(solution)/shard_map/ppermute | solution.py:644
  16.8 3.7 %collective-permute-start.3 = (f32[136,128]{1,0:T(8,128)S(1)}, f32[136,128]{1,0:T(8,128)S(1)}, u32[]{:S(2)}, u32[]{:S(2)}) collective-permute-start(f32[136,128]{1,0:T(8,128)S(1)} %get-tuple-element.85), channel_id=1, source_target_pairs={{0,16},{16,0},{32,48},{48,32},{64,80},{80,64},{96,112},{112,96},{1... | collective-permute-start | bytes 208904 | tf_op jit(solution)/shard_map/ppermute | solution.py:644
  21.6 13.2 %collective-permute-start.4 = (f32[136,128]{1,0:T(8,128)S(1)}, f32[136,128]{1,0:T(8,128)S(1)}, u32[]{:S(2)}, u32[]{:S(2)}) collective-permute-start(f32[136,128]{1,0:T(8,128)S(1)} %get-tuple-element.91), channel_id=1, source_target_pairs={{0,15},{1,2},{2,1},{3,4},{4,3},{5,6},{6,5},{7,8},{8,7},{9,10},{10,... | collective-permute-start | bytes 208904 | tf_op jit(solution)/shard_map/ppermute | solution.py:634
  26.0 8.9 %collective-permute-start.5 = (f32[136,128]{1,0:T(8,128)S(1)}, f32[136,128]{1,0:T(8,128)S(1)}, u32[]{:S(2)}, u32[]{:S(2)}) collective-permute-start(f32[136,128]{1,0:T(8,128)S(1)} %get-tuple-element.92), channel_id=1, source_target_pairs={{0,1},{1,0},{2,3},{3,2},{4,5},{5,4},{6,7},{7,6},{8,9},{9,8},{10,11... | collective-permute-start | bytes 208904 | tf_op jit(solution)/shard_map/ppermute | solution.py:638
  27.9 6.9 %collective-permute-start.6 = (f32[136,128]{1,0:T(8,128)S(1)}, f32[136,128]{1,0:T(8,128)S(1)}, u32[]{:S(2)}, u32[]{:S(2)}) collective-permute-start(f32[136,128]{1,0:T(8,128)S(1)} %get-tuple-element.93), channel_id=1, source_target_pairs={{16,32},{32,16},{48,64},{64,48},{80,96},{96,80},{112,128},{128,112... | collective-permute-start | bytes 208904 | tf_op jit(solution)/shard_map/ppermute | solution.py:644
  31.4 3.5 %collective-permute-start.7 = (f32[136,128]{1,0:T(8,128)S(1)}, f32[136,128]{1,0:T(8,128)S(1)}, u32[]{:S(2)}, u32[]{:S(2)}) collective-permute-start(f32[136,128]{1,0:T(8,128)S(1)} %get-tuple-element.94), channel_id=1, source_target_pairs={{0,16},{16,0},{32,48},{48,32},{64,80},{80,64},{96,112},{112,96},{1... | collective-permute-start | bytes 208904 | tf_op jit(solution)/shard_map/ppermute | solution.py:644
  37.0 13.1 %collective-permute-start.10 = (f32[152,128]{1,0:T(8,128)S(1)}, f32[152,128]{1,0:T(8,128)S(1)}, u32[]{:S(2)}, u32[]{:S(2)}) collective-permute-start(f32[152,128]{1,0:T(8,128)S(1)} %get-tuple-element.103), channel_id=1, source_target_pairs={{0,15},{1,2},{2,1},{3,4},{4,3},{5,6},{6,5},{7,8},{8,7},{9,10},{10,... | collective-permute-start | bytes 233480 | tf_op jit(solution)/shard_map/ppermute | solution.py:634
  42.0 8.1 %collective-permute-start.11 = (f32[152,128]{1,0:T(8,128)S(1)}, f32[152,128]{1,0:T(8,128)S(1)}, u32[]{:S(2)}, u32[]{:S(2)}) collective-permute-start(f32[152,128]{1,0:T(8,128)S(1)} %get-tuple-element.104), channel_id=1, source_target_pairs={{0,1},{1,0},{2,3},{3,2},{4,5},{5,4},{6,7},{7,6},{8,9},{9,8},{10,11... | collective-permute-start | bytes 233480 | tf_op jit(solution)/shard_map/ppermute | solution.py:638
  43.9 6.3 %collective-permute-start.8 = (f32[152,128]{1,0:T(8,128)S(1)}, f32[152,128]{1,0:T(8,128)S(1)}, u32[]{:S(2)}, u32[]{:S(2)}) collective-permute-start(f32[152,128]{1,0:T(8,128)S(1)} %get-tuple-element.101), channel_id=1, source_target_pairs={{16,32},{32,16},{48,64},{64,48},{80,96},{96,80},{112,128},{128,112... | collective-permute-start | bytes 233480 | tf_op jit(solution)/shard_map/ppermute | solution.py:644
  48.1 3.2 %collective-permute-start.9 = (f32[152,128]{1,0:T(8,128)S(1)}, f32[152,128]{1,0:T(8,128)S(1)}, u32[]{:S(2)}, u32[]{:S(2)}) collective-permute-start(f32[152,128]{1,0:T(8,128)S(1)} %get-tuple-element.102), channel_id=1, source_target_pairs={{0,16},{16,0},{32,48},{48,32},{64,80},{80,64},{96,112},{112,96},{1... | collective-permute-start | bytes 233480 | tf_op jit(solution)/shard_map/ppermute | solution.py:644
  52.4 12.6 %collective-permute-start.12 = (f32[168,128]{1,0:T(8,128)S(1)}, f32[168,128]{1,0:T(8,128)S(1)}, u32[]{:S(2)}, u32[]{:S(2)}) collective-permute-start(f32[168,128]{1,0:T(8,128)S(1)} %get-tuple-element.107), channel_id=1, source_target_pairs={{0,15},{1,2},{2,1},{3,4},{4,3},{5,6},{6,5},{7,8},{8,7},{9,10},{10,... | collective-permute-start | bytes 258056 | tf_op jit(solution)/shard_map/ppermute | solution.py:634
  56.1 8.9 %collective-permute-start.13 = (f32[168,128]{1,0:T(8,128)S(1)}, f32[168,128]{1,0:T(8,128)S(1)}, u32[]{:S(2)}, u32[]{:S(2)}) collective-permute-start(f32[168,128]{1,0:T(8,128)S(1)} %get-tuple-element.108), channel_id=1, source_target_pairs={{0,1},{1,0},{2,3},{3,2},{4,5},{5,4},{6,7},{7,6},{8,9},{9,8},{10,11... | collective-permute-start | bytes 258056 | tf_op jit(solution)/shard_map/ppermute | solution.py:638
  58.0 7.2 %collective-permute-start.14 = (f32[168,128]{1,0:T(8,128)S(1)}, f32[168,128]{1,0:T(8,128)S(1)}, u32[]{:S(2)}, u32[]{:S(2)}) collective-permute-start(f32[168,128]{1,0:T(8,128)S(1)} %get-tuple-element.109), channel_id=1, source_target_pairs={{16,32},{32,16},{48,64},{64,48},{80,96},{96,80},{112,128},{128,112... | collective-permute-start | bytes 258056 | tf_op jit(solution)/shard_map/ppermute | solution.py:644
  63.1 3.2 %collective-permute-start.15 = (f32[168,128]{1,0:T(8,128)S(1)}, f32[168,128]{1,0:T(8,128)S(1)}, u32[]{:S(2)}, u32[]{:S(2)}) collective-permute-start(f32[168,128]{1,0:T(8,128)S(1)} %get-tuple-element.110), channel_id=1, source_target_pairs={{0,16},{16,0},{32,48},{48,32},{64,80},{80,64},{96,112},{112,96},{1... | collective-permute-start | bytes 258056 | tf_op jit(solution)/shard_map/ppermute | solution.py:644
  68.5 12.7 %collective-permute-start.16 = (f32[184,128]{1,0:T(8,128)S(1)}, f32[184,128]{1,0:T(8,128)S(1)}, u32[]{:S(2)}, u32[]{:S(2)}) collective-permute-start(f32[184,128]{1,0:T(8,128)S(1)} %get-tuple-element.112), channel_id=1, source_target_pairs={{0,15},{1,2},{2,1},{3,4},{4,3},{5,6},{6,5},{7,8},{8,7},{9,10},{10,... | collective-permute-start | bytes 282632 | tf_op jit(solution)/shard_map/ppermute | solution.py:634
  73.5 7.8 %collective-permute-start.17 = (f32[184,128]{1,0:T(8,128)S(1)}, f32[184,128]{1,0:T(8,128)S(1)}, u32[]{:S(2)}, u32[]{:S(2)}) collective-permute-start(f32[184,128]{1,0:T(8,128)S(1)} %get-tuple-element.113), channel_id=1, source_target_pairs={{0,1},{1,0},{2,3},{3,2},{4,5},{5,4},{6,7},{7,6},{8,9},{9,8},{10,11... | collective-permute-start | bytes 282632 | tf_op jit(solution)/shard_map/ppermute | solution.py:638
  75.4 6.1 %collective-permute-start.18 = (f32[184,128]{1,0:T(8,128)S(1)}, f32[184,128]{1,0:T(8,128)S(1)}, u32[]{:S(2)}, u32[]{:S(2)}) collective-permute-start(f32[184,128]{1,0:T(8,128)S(1)} %get-tuple-element.114), channel_id=1, source_target_pairs={{16,32},{32,16},{48,64},{64,48},{80,96},{96,80},{112,128},{128,112... | collective-permute-start | bytes 282632 | tf_op jit(solution)/shard_map/ppermute | solution.py:644
  79.3 3.2 %collective-permute-start.19 = (f32[184,128]{1,0:T(8,128)S(1)}, f32[184,128]{1,0:T(8,128)S(1)}, u32[]{:S(2)}, u32[]{:S(2)}) collective-permute-start(f32[184,128]{1,0:T(8,128)S(1)} %get-tuple-element.115), channel_id=1, source_target_pairs={{0,16},{16,0},{32,48},{48,32},{64,80},{80,64},{96,112},{112,96},{1... | collective-permute-start | bytes 282632 | tf_op jit(solution)/shard_map/ppermute | solution.py:644
  84.7 13.1 %all-to-all-start = ((f32[16,32,128]{2,1,0:T(8,128)}), f32[16,32,128]{2,1,0:T(8,128)S(1)}, u32[]{:S(2)}, u32[]{:S(2)}) async-start(f32[16,32,128]{2,1,0:T(8,128)} %get-tuple-element.119), calls=%async_computation | async-start | bytes 524288 | tf_op jit(solution)/shard_map/all_to_all | solution.py:652
  92.3 0.6 copy-start.3
  93.0 0.6 copy-start.5
  98.5 34.4 %copy-start = (f32[152,512]{1,0:T(8,128)S(1)}, f32[152,512]{1,0:T(8,128)}, u32[]{:S(2)}) copy-start(f32[152,512]{1,0:T(8,128)} %get-tuple-element.139.z0) | copy-start | bytes 933892
  98.5 11.6 %copy-start.6 = (f32[200,128]{1,0:T(8,128)S(1)}, f32[200,128]{1,0:T(8,128)}, u32[]{:S(2)}) copy-start(f32[200,128]{1,0:T(8,128)} %copy-done.5) | copy-start | bytes 307204
  98.5 14.4 %copy-start.4 = (f32[200,128]{1,0:T(8,128)S(1)}, f32[200,128]{1,0:T(8,128)}, u32[]{:S(2)}) copy-start(f32[200,128]{1,0:T(8,128)} %copy-done.3) | copy-start | bytes 307204
  98.5 26.7 %all-to-all-start.1 = ((f32[16,32,128]{2,1,0:T(8,128)}), f32[16,32,128]{2,1,0:T(8,128)S(1)}, u32[]{:S(2)}, u32[]{:S(2)}) async-start(f32[16,32,128]{2,1,0:T(8,128)} %shard_map.131), calls=%async_computation.1 | async-start | bytes 524288 | tf_op jit(solution)/shard_map/all_to_all | solution.py:652
  110.1 13.2 %collective-permute-start.20 = (f32[200,128]{1,0:T(8,128)S(1)}, f32[200,128]{1,0:T(8,128)S(1)}, u32[]{:S(2)}, u32[]{:S(2)}) collective-permute-start(f32[200,128]{1,0:T(8,128)S(1)} %copy-done.6), channel_id=1, source_target_pairs={{0,15},{1,2},{2,1},{3,4},{4,3},{5,6},{6,5},{7,8},{8,7},{9,10},{10,... | collective-permute-start | bytes 307208 | tf_op jit(solution)/shard_map/ppermute | solution.py:634
  112.9 10.4 %collective-permute-start.21 = (f32[200,128]{1,0:T(8,128)S(1)}, f32[200,128]{1,0:T(8,128)S(1)}, u32[]{:S(2)}, u32[]{:S(2)}) collective-permute-start(f32[200,128]{1,0:T(8,128)S(1)} %copy-done.4), channel_id=1, source_target_pairs={{0,1},{1,0},{2,3},{3,2},{4,5},{5,4},{6,7},{7,6},{8,9},{9,8},{10,11... | collective-permute-start | bytes 307208 | tf_op jit(solution)/shard_map/ppermute | solution.py:638
  114.8 10.4 %collective-permute-start.22 = (f32[200,128]{1,0:T(8,128)S(1)}, f32[200,128]{1,0:T(8,128)S(1)}, u32[]{:S(2)}, u32[]{:S(2)}) collective-permute-start(f32[200,128]{1,0:T(8,128)S(1)} %get-tuple-element.131), channel_id=1, source_target_pairs={{16,32},{32,16},{48,64},{64,48},{80,96},{96,80},{112,128},{128,112... | collective-permute-start | bytes 307208 | tf_op jit(solution)/shard_map/ppermute | solution.py:644
  121.4 3.9 %collective-permute-start.23 = (f32[200,128]{1,0:T(8,128)S(1)}, f32[200,128]{1,0:T(8,128)S(1)}, u32[]{:S(2)}, u32[]{:S(2)}) collective-permute-start(f32[200,128]{1,0:T(8,128)S(1)} %get-tuple-element.132), channel_id=1, source_target_pairs={{0,16},{16,0},{32,48},{48,32},{64,80},{80,64},{96,112},{112,96},{1... | collective-permute-start | bytes 307208 | tf_op jit(solution)/shard_map/ppermute | solution.py:644
  125.3 7.7 %collective-permute-start.24 = (f32[16,32,128]{2,1,0:T(8,128)S(1)}, f32[16,32,128]{2,1,0:T(8,128)S(1)}, u32[]{:S(2)}, u32[]{:S(2)}) collective-permute-start(f32[16,32,128]{2,1,0:T(8,128)S(1)} %all-to-all-done.1.mine), channel_id=1, source_target_pairs={{0,16},{16,0},{32,48},{48,32},{64,80},{80,64},{96,112},{112,96},{1... | collective-permute-start | bytes 786440 | tf_op jit(solution)/shard_map/ppermute | solution.py:761
  138.9 35.7 %copy-start.2 = (f32[128,512]{1,0:T(8,128)S(1)}, f32[128,512]{1,0:T(8,128)}, u32[]{:S(2)}) copy-start(f32[128,512]{1,0:T(8,128)} %get-tuple-element.154.z1) | copy-start | bytes 786436
  138.9 12.6 %all-to-all-start.2 = ((f32[32,1,1152]{2,1,0:T(1,128)}), f32[32,1,1152]{2,1,0:T(1,128)S(1)}, u32[]{:S(2)}, u32[]{:S(2)}) async-start(f32[32,1,1152]{2,1,0:T(1,128)} %get-tuple-element.141), calls=%async_computation.2 | async-start | bytes 294912 | tf_op jit(solution)/shard_map/all_to_all | solution.py:652
  143.1 31.6 %copy-start.1 = (f32[128,512]{1,0:T(8,128)S(1)}, f32[128,512]{1,0:T(8,128)}, u32[]{:S(2)}) copy-start(f32[128,512]{1,0:T(8,128)} %get-tuple-element.153.z0) | copy-start | bytes 786436
  143.1 8.5 %collective-permute-start.25 = (f32[128,128]{1,0:T(8,128)S(1)}, f32[128,128]{1,0:T(8,128)S(1)}, u32[]{:S(2)}, u32[]{:S(2)}) collective-permute-start(f32[128,128]{1,0:T(8,128)S(1)} %get-tuple-element.142), channel_id=1, source_target_pairs={{0,15},{1,2},{2,1},{3,4},{4,3},{5,6},{6,5},{7,8},{8,7},{9,10},{10,... | collective-permute-start | bytes 196616 | tf_op jit(solution)/shard_map/ppermute | solution.py:634
  152.2 22.4 %all-to-all-start.3 = ((f32[16,1,1152]{2,1,0:T(1,128)}), f32[16,1,1152]{2,1,0:T(1,128)S(1)}, u32[]{:S(2)}, u32[]{:S(2)}) async-start(f32[16,1,1152]{2,1,0:T(1,128)} %shard_map.133), calls=%async_computation.3 | async-start | bytes 147456 | tf_op jit(solution)/shard_map/all_to_all | solution.py:652
  162.9 8.6 %collective-permute-start.26 = (f32[128,128]{1,0:T(8,128)S(1)}, f32[128,128]{1,0:T(8,128)S(1)}, u32[]{:S(2)}, u32[]{:S(2)}) collective-permute-start(f32[128,128]{1,0:T(8,128)S(1)} %get-tuple-element.150), channel_id=1, source_target_pairs={{0,1},{1,0},{2,3},{3,2},{4,5},{5,4},{6,7},{7,6},{8,9},{9,8},{10,11... | collective-permute-start | bytes 196616 | tf_op jit(solution)/shard_map/ppermute | solution.py:638
  164.8 7.3 %collective-permute-start.27 = (f32[128,128]{1,0:T(8,128)S(1)}, f32[128,128]{1,0:T(8,128)S(1)}, u32[]{:S(2)}, u32[]{:S(2)}) collective-permute-start(f32[128,128]{1,0:T(8,128)S(1)} %get-tuple-element.151), channel_id=1, source_target_pairs={{16,32},{32,16},{48,64},{64,48},{80,96},{96,80},{112,128},{128,112... | collective-permute-start | bytes 196616 | tf_op jit(solution)/shard_map/ppermute | solution.py:644
  169.6 3.1 %collective-permute-start.28 = (f32[128,128]{1,0:T(8,128)S(1)}, f32[128,128]{1,0:T(8,128)S(1)}, u32[]{:S(2)}, u32[]{:S(2)}) collective-permute-start(f32[128,128]{1,0:T(8,128)S(1)} %get-tuple-element.152), channel_id=1, source_target_pairs={{0,16},{16,0},{32,48},{48,32},{64,80},{80,64},{96,112},{112,96},{1... | collective-permute-start | bytes 196616 | tf_op jit(solution)/shard_map/ppermute | solution.py:644
